TPU v7x, 32 devices: a whole 2x2x4 slice. The times are simulated.
32 devices in a mesh: dp: 8 (over z, y), tensor: 4 (over x, core).
Axes of the slice: x: 2, y: 2, z: 4, core: 2. Of those that a mesh axis runs over, the one named last changes fastest.
Arguments:
- tokens: bfloat16 [16384, 1024], P(('dp', 'tensor')), may hold values from -6 to 6
- output_cotangent: bfloat16 [16384, 1024], P(('dp', 'tensor')), may hold values from -6 to 6
- lengths: int32 [8], P('dp'), may hold values from 1024 to 2048, as said below
- block_place: int32 [8, 32], P('dp'), may hold values from 0 to 31, each once within a row
- random_blocks: int32 [8, 16, 32, 3], P('dp', 'tensor'), may hold values from 0 to 31
- qkv_weight: bfloat16 [1024, 3, 1024], P('dp', None, 'tensor'), may hold values from -0.1875 to 0.1875
- out_weight: bfloat16 [1024, 1024], P('dp', 'tensor'), may hold values from -0.75 to 0.75
- up_weight: bfloat16 [1024, 4096], P('dp', 'tensor'), may hold values from -0.1875 to 0.1875
- down_weight: bfloat16 [1024, 4096], P('dp', 'tensor'), may hold values from -0.09375 to 0.09375
- vectors: float32 [8, 1024], P(None, ('dp', 'tensor')), may hold values from -2 to 2
- hidden_bias: float32 [1, 4096], P(None, ('dp', 'tensor')), may hold values from -3 to 3
Outputs:
- output: bfloat16 [16384, 1024], P(('dp', 'tensor'))
- input_grad: bfloat16 [16384, 1024], P(('dp', 'tensor'))
- qkv_weight_grad: float32 [1024, 3, 1024], P('dp', None, 'tensor')
- out_weight_grad: float32 [1024, 1024], P('dp', 'tensor')
- up_weight_grad: float32 [1024, 4096], P('dp', 'tensor')
- down_weight_grad: float32 [1024, 4096], P('dp', 'tensor')
- vectors_grad: float32 [8, 1024], P(None, ('dp', 'tensor'))
- hidden_bias_grad: float32 [1, 4096], P(None, ('dp', 'tensor'))
Inputs may be any that keep to these rules, and one draw needn't show every extreme that they name: `lengths`: one sequence has exactly 2048 tokens. `block_place`: each row is a permutation.
All inputs are finite; a program needn't handle non-finite values.
Results may differ from a plain program's by a relative error of at most 0.015.
Values may be sent and summed in bfloat16 or wider, within the bound.
No kernel may reach another device: no remote copies, remote signals or barrier semaphores. Data moves between devices by JAX's collectives and lax.ppermute only.
A program may use at most 192 MiB of HBM per device.

v0:
```python
import functools

import jax
import jax.numpy as jnp
from jax import lax
from jax.experimental import pallas as pl
from jax.experimental.pallas import tpu as pltpu
from jax.sharding import PartitionSpec as P

HEAD_DIM = 64
BLOCK = 64
PAIR = 2 * HEAD_DIM
SLOTS = 8
CHUNK = 512
EPS = 1e-05
NEGATIVE = -1e30
F32 = jnp.float32
BF16 = jnp.bfloat16
NT = (((1,), (1,)), ((), ()))
NN = (((1,), (0,)), ((), ()))
TN = (((0,), (0,)), ((), ()))


def matmul(left, right, dims):
    return lax.dot_general(left, right, dims, preferred_element_type=F32)


def swapped(value, axis, bit):
    count = lax.axis_size(axis)
    return lax.ppermute(value, axis, [(i, i ^ bit) for i in range(count)])


def bits_of(axis):
    count = lax.axis_size(axis)
    return [1 << b for b in range(count.bit_length() - 1)]


def together(*values):
    return lax.optimization_barrier(values)


def far(value, axis):
    return swapped(value, axis, bits_of(axis)[-1])


def gathered_parts(value, far_value, axis):
    bits = bits_of(axis)
    parts = {0: value, bits[-1]: far_value}
    for bit in reversed(bits[:-1]):
        parts.update({k | bit: swapped(p, axis, bit) for k, p in list(parts.items())})
    return [parts[k] for k in range(len(parts))]


def summed_halves(parts, axis):
    left = dict(enumerate(parts))
    terms = [parts[0]]
    for bit in bits_of(axis)[: len(parts).bit_length() - 2]:
        kept = {}
        for k in sorted(left, reverse=True):
            if k & bit == 0:
                arrived = swapped(left[k | bit], axis, bit)
                if k == 0:
                    terms.append(arrived)
                    kept[k] = None
                else:
                    kept[k] = added(left[k], arrived)
        left = kept
    return terms, left[len(parts) // 2]


def added(left, right):
    return (left.astype(F32) + right.astype(F32)).astype(BF16)


def doubled(value, axis, order):
    blocks = value[None]
    for bit in order:
        blocks = jnp.concatenate([blocks, swapped(blocks, axis, bit)], axis=0)
    return blocks


def halved(keep, send, axis, order):
    half = send.shape[0]
    arrived = swapped(send, axis, order[half.bit_length() - 1])
    rest = half // 2
    return added(keep[: half - rest], arrived[: half - rest]), added(
        keep[half - rest :], arrived[half - rest :]
    )


def block_owners(axis, order):
    count = lax.axis_size(axis)
    device = [sum(bit for b, bit in enumerate(order) if p >> b & 1) for p in range(count)]
    return lax.axis_index(axis) ^ jnp.asarray(device, jnp.int32)


def exchanged_parts(parts, axis):
    return [p if k == 0 else swapped(p, axis, k) for k, p in enumerate(parts)]


def summed_everywhere(value, axes):
    size = value.shape[0]
    value = jnp.pad(value, (0, -size % 1024)).reshape(-1, 128)
    for axis in axes:
        for bit in bits_of(axis):
            value = value + swapped(value, axis, bit)
    return value.reshape(-1)[:size]


def sent_and_summed(value, axis):
    count = lax.axis_size(axis)
    blocks = value.reshape(count, value.shape[0] // count, *value.shape[1:])
    arrived = lax.all_to_all(blocks, axis, 0, 0, tiled=True)
    return jnp.sum(arrived.astype(F32), axis=0)


def attention_tables(length, place, chosen):
    count = place.shape[0]
    heads = chosen.shape[0]
    nblocks = (length + BLOCK - 1) // BLOCK
    last = nblocks - 1
    number = jnp.arange(count, dtype=jnp.int32)
    same = jnp.zeros_like(number)
    common = jnp.stack([same, same + last, number - 1, number, number + 1], axis=1)
    middle = (number > 0) & (number < last)
    good = jnp.stack(
        [
            middle | (number > last),
            middle | (number > last),
            (number - 1 > 0) & (number - 1 < last) & (number != last),
            middle,
            (number + 1 < last) & (number > 0),
        ],
        axis=1,
    )
    drawn = jnp.transpose(chosen, (1, 2, 0))
    away = number[:, None, None]
    fresh = (
        (drawn > 0)
        & (drawn < last)
        & (jnp.abs(drawn - away) > 1)
        & (away > 0)
        & (away != last)
    )
    first, second, third = drawn[:, 0], drawn[:, 1], drawn[:, 2]
    fresh = jnp.stack(
        [
            fresh[:, 0],
            fresh[:, 1] & (second != first),
            fresh[:, 2] & (third != first) & (third != second),
        ],
        axis=1,
    )
    flags = jnp.concatenate(
        [jnp.broadcast_to(good[:, :, None], (count, 5, heads)), fresh], axis=1
    )
    bias = jnp.where(flags, 0.0, NEGATIVE).astype(F32)
    bias = jnp.broadcast_to(bias[..., None], (*bias.shape, HEAD_DIM))
    bias = bias.reshape(count, SLOTS, heads * HEAD_DIM)
    wanted = jnp.concatenate([common, drawn.reshape(count, -1)], axis=1)
    hit = wanted[:, :, None] == place[None, None, :]
    stored = jnp.sum(jnp.where(hit, number[None, None, :], 0), axis=-1).astype(jnp.int32)
    limits = jnp.clip(length - BLOCK * place, 0, BLOCK).astype(jnp.int32)
    ends = jnp.stack([last, length - BLOCK * last]).astype(jnp.int32)
    return stored, limits, ends, bias


def block_rows(index):
    return pl.ds(pl.multiple_of(index * BLOCK, BLOCK), BLOCK)


def spread(rows, heads):
    lane = lax.broadcasted_iota(jnp.int32, (1, heads * HEAD_DIM), 1)
    zero = jnp.zeros_like(rows)
    return jnp.concatenate(
        [jnp.where(lane // HEAD_DIM == h, rows, zero) for h in range(heads)], axis=0
    )


def collapse(full, heads):
    lane = lax.broadcasted_iota(jnp.int32, (1, PAIR), 1)
    pieces = []
    for pair in range(heads // 2):
        cols = slice(PAIR * pair, PAIR * (pair + 1))
        even = full[2 * pair * HEAD_DIM : (2 * pair + 1) * HEAD_DIM, cols]
        odd = full[(2 * pair + 1) * HEAD_DIM : (2 * pair + 2) * HEAD_DIM, cols]
        pieces.append(jnp.where(lane < HEAD_DIM, even, odd))
    return jnp.concatenate(pieces, axis=1)


def gathered_keys(ref, start, stored, number, heads):
    width = heads * HEAD_DIM
    lane = lax.broadcasted_iota(jnp.int32, (1, PAIR), 1)
    parts = [ref[block_rows(stored[number, s]), start : start + width] for s in range(5)]
    for s in range(3):
        pieces = []
        for pair in range(heads // 2):
            cols = slice(start + PAIR * pair, start + PAIR * (pair + 1))
            at = 5 + heads * s + 2 * pair
            even = ref[block_rows(stored[number, at]), cols]
            odd = ref[block_rows(stored[number, at + 1]), cols]
            pieces.append(jnp.where(lane < HEAD_DIM, even, odd))
        parts.append(jnp.concatenate(pieces, axis=1))
    return jnp.concatenate(parts, axis=0)


def slot(value, index):
    return value[BLOCK * index : BLOCK * (index + 1)]


def biased(scores, bias, last_rows):
    row = lax.broadcasted_iota(jnp.int32, (BLOCK, 1), 0)
    parts = [slot(scores, s) + bias[s : s + 1] for s in range(SLOTS)]
    parts[1] = jnp.where(row < last_rows, parts[1], NEGATIVE)
    return parts


def total(parts):
    return functools.reduce(jnp.add, parts)


def attend_kernel(heads, stored, limits, ends, qkv_ref, bias_ref, out_ref, log_ref, keep_ref):
    count = bias_ref.shape[0]
    width = heads * HEAD_DIM
    scale = jnp.asarray(HEAD_DIM**-0.5, BF16)

    def item(number):
        here = block_rows(stored[number, 3])
        queries = spread(qkv_ref[here, :width] * scale, heads)
        keys = gathered_keys(qkv_ref, width, stored, number, heads)
        parts = biased(matmul(keys, queries, NT), bias_ref[number], ends[1])
        top = jnp.max(functools.reduce(jnp.maximum, parts), axis=0, keepdims=True)
        weights = [jnp.exp(p - top) for p in parts]
        row_total = jnp.sum(total(weights), axis=0, keepdims=True)
        inverse = 1.0 / row_total
        probs = jnp.concatenate([(p * inverse).astype(BF16) for p in weights], axis=0)
        values = gathered_keys(qkv_ref, 2 * width, stored, number, heads)
        out_ref[here, :] = collapse(matmul(probs, values, TN), heads).astype(BF16)
        log_ref[pl.ds(number, 1), :] = top + jnp.log(row_total)

    def step(group, carry):
        for part in range(4):
            item(1 + group * 4 + part)
        return carry

    lax.fori_loop(0, (count - 1) // 4, step, 0)
    for number in range(1 + (count - 1) // 4 * 4, count):
        item(number)

    row = lax.broadcasted_iota(jnp.int32, (BLOCK, 1), 0)
    per = CHUNK // BLOCK
    chunks = count // per

    def chunk_rows(chunk):
        return pl.ds(pl.multiple_of(chunk * CHUNK, CHUNK), CHUNK)

    numbers = [0, ends[0]]
    rows_of = [block_rows(stored[number, 3]) for number in numbers]
    queries = [spread(qkv_ref[at, :width] * scale, heads) for at in rows_of]

    def scores(chunk, tops):
        at = chunk_rows(chunk)
        keys = qkv_ref[at, width : 2 * width]
        found = []
        for end in range(2):
            raw = matmul(keys, queries[end], NT)
            parts = [
                jnp.where(row < limits[chunk * per + s], slot(raw, s), NEGATIVE)
                for s in range(per)
            ]
            keep_ref[end, at, :] = jnp.concatenate(parts, axis=0)
            found.append(jnp.maximum(tops[end], functools.reduce(jnp.maximum, parts)))
        return tuple(found)

    tops = lax.fori_loop(0, chunks, scores, (jnp.full((BLOCK, width), NEGATIVE, F32),) * 2)
    tops = [jnp.max(top, axis=0, keepdims=True) for top in tops]

    def exponents(chunk, totals):
        at = chunk_rows(chunk)
        found = []
        for end in range(2):
            weights = jnp.exp(keep_ref[end, at, :] - tops[end])
            keep_ref[end, at, :] = weights
            found.append(totals[end] + total([slot(weights, s) for s in range(per)]))
        return tuple(found)

    totals = lax.fori_loop(0, chunks, exponents, (jnp.zeros((BLOCK, width), F32),) * 2)
    totals = [jnp.sum(found, axis=0, keepdims=True) for found in totals]
    inverses = [1.0 / found for found in totals]

    def contexts(chunk, sums):
        at = chunk_rows(chunk)
        values = qkv_ref[at, 2 * width :]
        return tuple(
            sums[end] + matmul((keep_ref[end, at, :] * inverses[end]).astype(BF16), values, TN)
            for end in range(2)
        )

    sums = lax.fori_loop(0, chunks, contexts, (jnp.zeros((width, width), F32),) * 2)
    for end in range(2):
        out_ref[rows_of[end], :] = collapse(sums[end], heads).astype(BF16)
        log_ref[pl.ds(numbers[end], 1), :] = tops[end] + jnp.log(totals[end])


def attend_back_kernel(
    heads,
    stored,
    limits,
    ends,
    qkv_ref,
    grad_ref,
    bias_ref,
    log_ref,
    out_ref,
    keys_acc,
    values_acc,
    probs_ref,
    inner_ref,
):
    count = bias_ref.shape[0]
    width = heads * HEAD_DIM
    scale = jnp.asarray(HEAD_DIM**-0.5, BF16)
    lane = lax.broadcasted_iota(jnp.int32, (1, PAIR), 1)
    keys_acc[...] = jnp.zeros_like(keys_acc)
    values_acc[...] = jnp.zeros_like(values_acc)

    def accumulate(acc, value, number):
        for s in range(5):
            acc[block_rows(stored[number, s]), :] += slot(value, s)
        for s in range(3):
            for h in range(heads):
                cols = slice(PAIR * (h // 2), PAIR * (h // 2 + 1))
                mine = (lane < HEAD_DIM) == (h % 2 == 0)
                term = jnp.where(mine, slot(value, 5 + s)[:, cols], 0.0)
                acc[block_rows(stored[number, 5 + heads * s + h]), cols] += term

    def item(number):
        here = block_rows(stored[number, 3])
        queries = spread(qkv_ref[here, :width] * scale, heads)
        grads = spread(grad_ref[here, :], heads)
        keys = gathered_keys(qkv_ref, width, stored, number, heads)
        values = gathered_keys(qkv_ref, 2 * width, stored, number, heads)
        log_total = log_ref[pl.ds(number, 1), :]
        parts = biased(matmul(keys, queries, NT), bias_ref[number], ends[1])
        probs = [jnp.exp(p - log_total) for p in parts]
        found = matmul(values, grads, NT)
        found = [slot(found, s) for s in range(SLOTS)]
        inner = total([p * d for p, d in zip(probs, found)])
        inner = jnp.sum(inner, axis=0, keepdims=True)
        grad_scores = jnp.concatenate(
            [(p * (d - inner)).astype(BF16) for p, d in zip(probs, found)], axis=0
        )
        probs_low = jnp.concatenate([p.astype(BF16) for p in probs], axis=0)
        accumulate(values_acc, matmul(probs_low, grads, NN), number)
        accumulate(keys_acc, matmul(grad_scores, queries, NN), number)
        grad_queries = collapse(matmul(grad_scores, keys, TN), heads) * HEAD_DIM**-0.5
        out_ref[here, :width] = grad_queries.astype(BF16)

    def step(group, carry):
        for part in range(4):
            item(1 + group * 4 + part)
        return carry

    lax.fori_loop(0, (count - 1) // 4, step, 0)
    for number in range(1 + (count - 1) // 4 * 4, count):
        item(number)

    row = lax.broadcasted_iota(jnp.int32, (BLOCK, 1), 0)
    per = CHUNK // BLOCK
    chunks = count // per

    def chunk_rows(chunk):
        return pl.ds(pl.multiple_of(chunk * CHUNK, CHUNK), CHUNK)

    numbers = [0, ends[0]]
    rows_of = [block_rows(stored[number, 3]) for number in numbers]
    queries = [spread(qkv_ref[at, :width] * scale, heads) for at in rows_of]
    grads = [spread(grad_ref[at, :], heads) for at in rows_of]
    log_rows = [log_ref[pl.ds(number, 1), :] for number in numbers]

    def first(chunk, inners):
        at = chunk_rows(chunk)
        keys = qkv_ref[at, width : 2 * width]
        values = qkv_ref[at, 2 * width :]
        sums = []
        for end in range(2):
            scores = matmul(keys, queries[end], NT)
            parts = [
                jnp.where(row < limits[chunk * per + s], slot(scores, s), NEGATIVE)
                for s in range(per)
            ]
            probs = jnp.exp(jnp.concatenate(parts, axis=0) - log_rows[end])
            found = matmul(values, grads[end], NT)
            probs_ref[end, at, :] = probs
            inner_ref[end, at, :] = found
            both = probs * found
            sums.append(inners[end] + total([slot(both, s) for s in range(per)]))
        return tuple(sums)

    inners = lax.fori_loop(0, chunks, first, (jnp.zeros((BLOCK, width), F32),) * 2)
    inners = [jnp.sum(inner, axis=0, keepdims=True) for inner in inners]

    def second(chunk, sums):
        at = chunk_rows(chunk)
        keys = qkv_ref[at, width : 2 * width]
        found, to_values, to_keys = [], values_acc[at, :], keys_acc[at, :]
        for end in range(2):
            probs = probs_ref[end, at, :]
            grad_scores = (probs * (inner_ref[end, at, :] - inners[end])).astype(BF16)
            to_values = to_values + matmul(probs.astype(BF16), grads[end], NN)
            to_keys = to_keys + matmul(grad_scores, queries[end], NN)
            found.append(sums[end] + matmul(grad_scores, keys, TN))
        out_ref[at, width : 2 * width] = to_keys.astype(BF16)
        out_ref[at, 2 * width :] = to_values.astype(BF16)
        return tuple(found)

    sums = lax.fori_loop(0, chunks, second, (jnp.zeros((width, width), F32),) * 2)
    for end in range(2):
        grad_queries = collapse(sums[end], heads) * HEAD_DIM**-0.5
        out_ref[rows_of[end], :width] = grad_queries.astype(BF16)


def in_smem():
    return pl.BlockSpec(memory_space=pltpu.SMEM)


def in_vmem():
    return pl.BlockSpec(memory_space=pltpu.VMEM)


def attention_cost(qkv, matmuls):
    rows, width = qkv.shape
    width //= 3
    return pl.CostEstimate(
        flops=2 * matmuls * rows * CHUNK * width,
        bytes_accessed=12 * rows * width,
        transcendentals=rows * CHUNK * width // HEAD_DIM,
    )


def attend(qkv, tables, heads):
    stored, limits, ends, bias = tables
    rows, width = qkv.shape[0], heads * HEAD_DIM
    return pl.pallas_call(
        functools.partial(attend_kernel, heads),
        out_shape=(
            jax.ShapeDtypeStruct((rows, width), BF16),
            jax.ShapeDtypeStruct((rows // BLOCK, width), F32),
        ),
        grid=(1,),
        in_specs=[in_smem()] * 3 + [in_vmem()] * 2,
        out_specs=(
            pl.BlockSpec((rows, width), lambda i: (0, 0)),
            pl.BlockSpec((rows // BLOCK, width), lambda i: (0, 0)),
        ),
        scratch_shapes=[pltpu.VMEM((2, rows, width), F32)],
        compiler_params=pltpu.CompilerParams(vmem_limit_bytes=32 << 20),
        cost_estimate=attention_cost(qkv, 8),
        name="attend",
    )(stored, limits, ends, qkv, bias)


def attend_back(qkv, grad_context, log_totals, tables, heads):
    stored, limits, ends, bias = tables
    rows, width = qkv.shape[0], heads * HEAD_DIM
    return pl.pallas_call(
        functools.partial(attend_back_kernel, heads),
        out_shape=jax.ShapeDtypeStruct(qkv.shape, BF16),
        grid=(1,),
        in_specs=[in_smem()] * 3 + [in_vmem()] * 4,
        out_specs=pl.BlockSpec(qkv.shape, lambda i: (0, 0)),
        scratch_shapes=[pltpu.VMEM((rows, width), F32)] * 2
        + [pltpu.VMEM((2, rows, width), F32)] * 2,
        compiler_params=pltpu.CompilerParams(vmem_limit_bytes=32 << 20),
        cost_estimate=attention_cost(qkv, 16),
        name="attend_back",
    )(stored, limits, ends, qkv, grad_context, bias, log_totals)


TILE = 256


def gelu_and_slope(pre):
    scale = (2.0 / 3.141592653589793) ** 0.5
    square = pre * pre
    bent = jnp.tanh(scale * pre * (1.0 + 0.044715 * square))
    half = 0.5 + 0.5 * bent
    slope = half + (0.5 * scale) * pre * (1.0 - bent * bent) * (1.0 + 0.134145 * square)
    return pre * half, slope


def pick(refs):
    per = pl.num_programs(0) // len(refs)
    value = refs[0][...]
    for k, ref in enumerate(refs[1:], 1):
        value = jnp.where(pl.program_id(0) >= k * per, ref[...], value)
    return value


def put(refs, value):
    per = pl.num_programs(0) // len(refs)
    for k, ref in enumerate(refs):
        ref[...] = jnp.where(pl.program_id(0) // per == k, value, ref[...])


def feed_kernel(quarters, taken, *refs):
    normed = pick(refs[:quarters])
    grads = pick(refs[quarters : 2 * quarters])
    weight_ref, bias_ref = refs[2 * quarters : 2 * quarters + 2]
    results = refs[2 * quarters + 2 + taken :]
    units = bias_ref.shape[1]
    up = weight_ref[:, :units]
    down = weight_ref[:, units:]
    active, slope = gelu_and_slope(matmul(normed, up, NN) + bias_ref[...])
    active = active.astype(BF16)
    grad_hidden = (matmul(grads, down, NN) * slope).astype(BF16)
    put(results[:quarters], matmul(grad_hidden, up, NT).astype(BF16))
    put(results[quarters : 2 * quarters], matmul(active, down, NT).astype(BF16))
    for ref, value in zip(results[2 * quarters :], (normed, grad_hidden, grads, active)):
        ref[...] = value


def tile_specs(arrays):
    def spec(k, value):
        tiles = value.shape[0] // TILE
        return pl.BlockSpec(
            (TILE, value.shape[1]), lambda i: (jnp.clip(i - k * tiles, 0, tiles - 1), 0)
        )

    return [spec(k, value) for k, value in enumerate(arrays)]


def feed(normed, grads, weights, bias, stacks, start, quarters):
    rows, features = normed[0].shape
    units = bias.shape[1]
    here = len(normed)
    tiles = rows // TILE
    stacked = [jax.ShapeDtypeStruct((rows * quarters, n), BF16) for n in (features, units) * 2]
    once = pl.BlockSpec(weights.shape, lambda i: (0, 0), pipeline_mode=pl.Buffered(1))
    found = pl.pallas_call(
        functools.partial(feed_kernel, here, len(stacks)),
        grid=(here * tiles,),
        out_shape=[like(value) for value in normed] * 2 + stacked,
        in_specs=tile_specs(normed)
        + tile_specs(grads)
        + [once, whole_spec(bias)]
        + [pl.BlockSpec(memory_space=pl.ANY)] * len(stacks),
        out_specs=tile_specs(normed) * 2
        + [
            pl.BlockSpec((TILE, value.shape[1]), lambda i: (i + start * tiles, 0))
            for value in stacked
        ],
        input_output_aliases={2 * here + 2 + n: 2 * here + n for n in range(len(stacks))},
        compiler_params=limit(62),
        cost_estimate=pl.CostEstimate(
            flops=8 * here * rows * features * units,
            bytes_accessed=16 * here * rows * features + 4 * features * units,
            transcendentals=here * rows * units,
        ),
        name="feed",
    )(*normed, *grads, weights, bias, *stacks)
    return found[:here], found[here : 2 * here], found[2 * here :]


def feed_grads_kernel(normed_ref, grad_ref, grads_ref, active_ref, out_ref, sum_ref, acc_ref):
    units = sum_ref.shape[1]
    grad_hidden = grad_ref[...]

    @pl.when(pl.program_id(0) == 0)
    def _():
        acc_ref[...] = jnp.zeros_like(acc_ref)
        sum_ref[...] = jnp.zeros_like(sum_ref)

    acc_ref[:, :units] += matmul(normed_ref[...], grad_hidden, TN)
    acc_ref[:, units:] += matmul(grads_ref[...], active_ref[...], TN)
    sum_ref[...] += jnp.sum(grad_hidden.astype(F32), axis=0, keepdims=True)

    @pl.when(pl.program_id(0) == pl.num_programs(0) - 1)
    def _():
        out_ref[...] = acc_ref[...].astype(BF16)


def feed_grads(stacks):
    rows, features = stacks[0].shape
    units = stacks[1].shape[1]
    sums = jax.ShapeDtypeStruct((features, 2 * units), BF16)
    hidden = jax.ShapeDtypeStruct((1, units), F32)
    return pl.pallas_call(
        feed_grads_kernel,
        grid=(rows // (2 * TILE),),
        out_shape=[sums, hidden],
        in_specs=[tiled_spec(value, 2 * TILE) for value in stacks],
        out_specs=[whole_spec(sums), whole_spec(hidden)],
        scratch_shapes=[pltpu.VMEM(sums.shape, F32)],
        compiler_params=limit(62),
        cost_estimate=cost(4 * rows * features * units, 8 * rows * features),
        name="feed_grads",
    )(*stacks)


def norm_parts(rows):
    centred = rows - jnp.mean(rows, axis=-1, keepdims=True)
    inverse = lax.rsqrt(jnp.mean(centred * centred, axis=-1, keepdims=True) + EPS)
    return centred * inverse, inverse


def norm_back(grad_normed, unit, inverse, gain):
    grad_unit = grad_normed * gain
    return inverse * (
        grad_unit
        - jnp.mean(grad_unit, axis=-1, keepdims=True)
        - unit * jnp.mean(grad_unit * unit, axis=-1, keepdims=True)
    )


def whole_spec(value):
    return pl.BlockSpec(value.shape, lambda i: (0,) * value.ndim)


def tiled_spec(value, tile=TILE):
    return pl.BlockSpec((tile, value.shape[1]), lambda i: (i, 0))


def like(value, dtype=None):
    return jax.ShapeDtypeStruct(value.shape, dtype or value.dtype)


def limit(mebibytes):
    return pltpu.CompilerParams(vmem_limit_bytes=mebibytes << 20)


def cost(flops, moved):
    return pl.CostEstimate(flops=flops, bytes_accessed=moved, transcendentals=0)


def unit_kernel(rows_ref, unit_ref):
    unit_ref[...] = norm_parts(rows_ref[...].astype(F32))[0].astype(BF16)


def unit_rows(rows):
    return pl.pallas_call(
        unit_kernel,
        grid=(rows.shape[0] // TILE,),
        out_shape=like(rows),
        in_specs=[tiled_spec(rows)],
        out_specs=tiled_spec(rows),
        compiler_params=limit(62),
        cost_estimate=cost(8 * rows.size, 4 * rows.size),
        name="unit",
    )(rows)


def project_kernel(parts, owner_a, owner_b, *refs):
    unit_refs = refs[:parts]
    first_ref, last_ref, norm_ref, bias_ref, qkv_ref, weight_ref, out_ref = refs[parts:]
    count, own, split = first_ref.shape
    near = unit_refs[0].shape[0]
    rest = weight_ref.shape[1] - split

    @pl.when(pl.program_id(0) == 0)
    def _():
        for p in range(count):
            at = pl.ds(pl.multiple_of(owner_a[p] * own, own), own)
            weight_ref[at, :split] = first_ref[p]
            at = pl.ds(pl.multiple_of(owner_b[p] * own, own), own)
            weight_ref[at, split:] = last_ref[p, :, :rest]
            out_ref[at, :] = last_ref[p, :, rest:]

    for k, ref in enumerate(unit_refs):

        @pl.when(pl.program_id(0) == k)
        def _(ref=ref):
            def tile(i, carry):
                at = pl.ds(pl.multiple_of(i * TILE, TILE), TILE)
                normed = ref[at, :].astype(F32) * norm_ref[0:1, :] + norm_ref[1:2, :]
                found = matmul(normed.astype(BF16), weight_ref[...], NN) + bias_ref[...]
                qkv_ref[at, :] = found.astype(BF16)
                return carry

            lax.fori_loop(0, near // TILE, tile, 0)


def project(unit, first, last, owner_a, owner_b, norm, bias):
    rows = sum(value.shape[0] for value in unit)
    features, width = unit[0].shape[1], bias.shape[1]
    more = first.shape[2] + last.shape[2] - width
    qkv = jax.ShapeDtypeStruct((rows, width), BF16)
    weights = [jax.ShapeDtypeStruct((features, n), BF16) for n in (width, more)]
    return pl.pallas_call(
        functools.partial(project_kernel, len(unit)),
        grid=(len(unit),),
        out_shape=[qkv, *weights],
        in_specs=[in_smem()] * 2 + [in_vmem()] * (len(unit) + 4),
        out_specs=[tiled_spec(qkv, rows // len(unit))] + [whole_spec(value) for value in weights],
        compiler_params=limit(32),
        cost_estimate=cost(2 * rows * features * width, 2 * rows * (features + width)),
        name="project",
    )(owner_a, owner_b, *unit, first, last, norm, bias)


def middle_kernel(parts, *refs):
    context_refs, out_refs = refs[:parts], refs[parts : 2 * parts]
    rows_ref, vector_ref, middle_ref, normed_ref = refs[2 * parts :]
    middle = rows_ref[...].astype(F32) + vector_ref[0:1, :]
    for context_ref, out_ref in zip(context_refs, out_refs):
        middle += matmul(context_ref[...], out_ref[...], NT)
    middle_ref[...] = middle
    unit = norm_parts(middle)[0]
    normed_ref[...] = (unit * vector_ref[1:2, :] + vector_ref[2:3, :]).astype(BF16)


def middle_rows(context, out_parts, rows, vectors):
    return pl.pallas_call(
        functools.partial(middle_kernel, len(context)),
        grid=(rows.shape[0] // TILE,),
        out_shape=[like(rows, F32), like(rows)],
        in_specs=[tiled_spec(value) for value in context]
        + [whole_spec(value) for value in out_parts]
        + [tiled_spec(rows), whole_spec(vectors)],
        out_specs=[tiled_spec(rows), tiled_spec(rows)],
        compiler_params=limit(62),
        cost_estimate=cost(2 * rows.size * rows.shape[1], 12 * rows.size),
        name="middle",
    )(*context, *out_parts, rows, vectors)


def middle_back_kernel(terms, parts, owner, *refs):
    term_refs, out_refs = refs[:terms], refs[terms : terms + parts]
    context_refs = refs[terms + parts : terms + 2 * parts]
    middle_ref, cotangent_ref, vector_ref, grad_ref, sum_ref = refs[
        terms + 2 * parts : terms + 2 * parts + 5
    ]
    head_refs = refs[terms + 2 * parts + 5 : terms + 3 * parts + 5]
    block_refs = refs[terms + 3 * parts + 5 : -1]
    found_ref = refs[-1]
    first = pl.program_id(0) == 0
    last = pl.program_id(0) == pl.num_programs(0) - 1
    count, own, width = block_refs[0].shape
    grad_normed = total([ref[...].astype(F32) for ref in term_refs])
    unit, inverse = norm_parts(middle_ref[...])
    cotangent = cotangent_ref[...].astype(F32)
    grad = cotangent + norm_back(grad_normed, unit, inverse, vector_ref[1:2, :])
    grad_ref[...] = grad
    low = grad.astype(BF16)
    for head_ref, out_ref in zip(head_refs, out_refs):
        head_ref[...] = matmul(low, out_ref[...], NN).astype(BF16)
    sums = [
        jnp.sum(value, axis=0, keepdims=True)
        for value in (grad_normed * unit, grad_normed, grad, cotangent)
    ]
    sums = jnp.concatenate(sums, axis=0)

    @pl.when(first)
    def _():
        sum_ref[...] = jnp.zeros_like(sum_ref)
        found_ref[...] = jnp.zeros_like(found_ref)

    sum_ref[...] += sums
    for k, context_ref in enumerate(context_refs):
        found_ref[:, k * width : (k + 1) * width] += matmul(low, context_ref[...], TN)

    @pl.when(last)
    def _():
        for k, block_ref in enumerate(block_refs):
            for p in range(count):
                at = pl.ds(pl.multiple_of(owner[p] * own, own), own)
                block_ref[p] = found_ref[at, k * width : (k + 1) * width].astype(BF16)


def middle_back(terms, out_parts, context, middle, cotangent, vectors, owner):
    rows, features = middle.shape
    width = out_parts[0].shape[1]
    parts = len(out_parts)
    count = owner.shape[0]
    sums = jax.ShapeDtypeStruct((4, features), F32)
    head = jax.ShapeDtypeStruct((rows, width), BF16)
    blocks = jax.ShapeDtypeStruct((count, features // count, width), BF16)
    found = pl.pallas_call(
        functools.partial(middle_back_kernel, len(terms), parts),
        grid=(rows // TILE,),
        out_shape=[like(middle), sums] + [head] * parts + [blocks] * parts,
        in_specs=[in_smem()]
        + [tiled_spec(value) for value in terms]
        + [whole_spec(value) for value in out_parts]
        + [tiled_spec(value) for value in context]
        + [tiled_spec(middle), tiled_spec(cotangent), whole_spec(vectors)],
        out_specs=[tiled_spec(middle), whole_spec(sums)]
        + [tiled_spec(head)] * parts
        + [whole_spec(blocks)] * parts,
        scratch_shapes=[pltpu.VMEM((features, width * parts), F32)],
        compiler_params=limit(62),
        cost_estimate=cost(4 * middle.size * features, 20 * middle.size),
        name="middle_back",
    )(owner, *terms, *out_parts, *context, middle, cotangent, vectors)
    return found[0], found[1], found[2 : 2 + parts], found[2 + parts :]


def qkv_grads_kernel(parts, terms, owner_a, owner_b, *refs):
    unit_refs, term_refs = refs[:parts], refs[parts : parts + terms]
    grad_ref, weight_ref, *block_refs, late_ref, sum_ref = refs[parts + terms : parts + terms + 8]
    *row_refs, raw_ref = refs[parts + terms + 8 :]
    half, own, split = block_refs[0].shape
    width = weight_ref.shape[1]
    rest = width - split
    near = unit_refs[0].shape[0]
    step = 256
    sums = jnp.sum(grad_ref[...].astype(F32), axis=0, keepdims=True)
    sum_ref[...] = sums
    for i in range(weight_ref.shape[0] // step):
        at = slice(step * i, step * (i + 1))
        raw = total(
            [
                matmul(ref[:, at], grad_ref[near * k : near * (k + 1), :], TN)
                for k, ref in enumerate(unit_refs)
            ]
        )
        weight = weight_ref[at, :].astype(F32)
        raw_ref[at, :] = raw.astype(BF16)
        for row, value in enumerate((raw * weight, weight * sums)):
            lanes = total([value[:, 128 * c : 128 * (c + 1)] for c in range(width // 128)])
            for b in range(step // 128):
                turned = lanes[128 * b : 128 * (b + 1)].T
                found = jnp.sum(turned, axis=0, keepdims=True)
                start = step * i + 128 * b
                late_ref[row : row + 1, start : start + 128] = found
    for p in range(2 * half):
        first_ref, last_ref = block_refs[p // half], block_refs[2 + p // half]
        at = pl.ds(pl.multiple_of(owner_a[p] * own, own), own)
        first_ref[p % half] = raw_ref[at, :split]
        at = pl.ds(pl.multiple_of(owner_b[p] * own, own), own)
        last_ref[p % half, :, :rest] = raw_ref[at, split:]
        found = total([ref[p].astype(F32) for ref in term_refs])
        last_ref[p % half, :, rest:] = found.astype(BF16)
    for k, ref in enumerate(row_refs):

        def tile(i, carry, k=k, ref=ref):
            at = pl.ds(pl.multiple_of(i * TILE + k * near, TILE), TILE)
            to = pl.ds(pl.multiple_of(i * TILE, TILE), TILE)
            ref[to, :] = matmul(grad_ref[at, :], weight_ref[...], NT).astype(BF16)
            return carry

        lax.fori_loop(0, near // TILE, tile, 0)


def qkv_grads(unit, out_terms, grad_qkv, weight, owner_a, owner_b, split):
    features, width = weight.shape
    count, own, more = out_terms[0].shape
    first = jax.ShapeDtypeStruct((count // 2, own, split), BF16)
    last = jax.ShapeDtypeStruct((count // 2, own, width - split + more), BF16)
    return pl.pallas_call(
        functools.partial(qkv_grads_kernel, len(unit), len(out_terms)),
        grid=(1,),
        out_shape=[
            first,
            first,
            last,
            last,
            jax.ShapeDtypeStruct((2, features), F32),
            jax.ShapeDtypeStruct((1, width), F32),
        ]
        + [like(value) for value in unit],
        in_specs=[in_smem()] * 2 + [in_vmem()] * (len(unit) + len(out_terms) + 2),
        out_specs=[whole_spec(value) for value in (first, first, last, last)]
        + [pl.BlockSpec((2, features), lambda i: (0, 0)), pl.BlockSpec((1, width), lambda i: (0, 0))]
        + [whole_spec(value) for value in unit],
        scratch_shapes=[pltpu.VMEM((features, width), BF16)],
        compiler_params=limit(32),
        cost_estimate=cost(4 * grad_qkv.size * features, 4 * grad_qkv.size + 8 * weight.size),
        name="qkv_grads",
    )(owner_a, owner_b, *unit, *out_terms, grad_qkv, weight)


def input_back_kernel(terms, *refs):
    *term_refs, first_ref, last_ref = refs[:terms]
    rows_ref, middle_ref, vector_ref, out_ref = refs[terms:]
    half = jnp.where(pl.program_id(0) == 0, first_ref[...], last_ref[...])
    grad_normed = total([ref[...].astype(F32) for ref in term_refs]) + half.astype(F32)
    unit, inverse = norm_parts(rows_ref[...].astype(F32))
    grad = norm_back(grad_normed, unit, inverse, vector_ref[0:1, :])
    out_ref[...] = (middle_ref[...] + grad).astype(BF16)


def input_back(terms, rows, grad_middle, vectors):
    tile = rows.shape[0] // 2
    return pl.pallas_call(
        functools.partial(input_back_kernel, len(terms)),
        grid=(2,),
        out_shape=like(rows),
        in_specs=[tiled_spec(value, tile) for value in terms[:-2]]
        + [whole_spec(value) for value in terms[-2:]]
        + [tiled_spec(rows, tile), tiled_spec(grad_middle, tile), whole_spec(vectors)],
        out_specs=tiled_spec(rows, tile),
        compiler_params=limit(62),
        cost_estimate=cost(20 * rows.size, 14 * rows.size),
        name="input_back",
    )(*terms, rows, grad_middle, vectors)


def per_device(
    tokens,
    output_cotangent,
    lengths,
    block_place,
    random_blocks,
    qkv_weight,
    out_weight,
    up_weight,
    down_weight,
    vectors,
    hidden_bias,
):
    ways = lax.axis_size("tensor")
    spread_ways = lax.axis_size("dp")
    position = lax.axis_index("tensor")
    index = lax.axis_index("dp") * ways + position
    near = tokens.shape[0]
    rows = near * ways
    features = tokens.shape[1]
    width = qkv_weight.shape[2]
    heads = width // HEAD_DIM
    units = up_weight.shape[1]
    own = features // spread_ways
    piece = vectors.shape[1]
    unit_piece = hidden_bias.shape[1]

    def quarters(value):
        return [value[k * near : (k + 1) * near] for k in range(ways)]

    small = jnp.zeros((8, features), F32)
    small = lax.dynamic_update_slice(small, vectors, (0, index * piece))
    small_hidden = jnp.zeros((1, units * ways), F32)
    small_hidden = lax.dynamic_update_slice(small_hidden, hidden_bias, (0, index * unit_piece))
    packed = jnp.concatenate([small.reshape(-1), small_hidden.reshape(-1)])
    packed = summed_everywhere(packed, ("tensor",))

    unit_near = unit_rows(tokens)
    unit_near, packed = together(unit_near, packed)
    unit_far = far(unit_near, "tensor")

    bits = bits_of("dp")
    order_a = bits[::-1]
    order_b = bits[:1] + bits[:0:-1]
    owner_a = block_owners("dp", order_a)
    owner_b = block_owners("dp", order_b)
    split = 2 * width
    qkv_flat = qkv_weight.reshape(own, 3 * width)
    first_blocks = doubled(qkv_flat[:, :split], "dp", order_a)
    last_flat = jnp.concatenate([qkv_flat[:, split:], out_weight], axis=1)
    last_blocks = doubled(last_flat, "dp", order_b)
    packed = summed_everywhere(packed, ("dp",))
    feed_flat = jnp.concatenate([up_weight, down_weight], axis=1)
    cotangent_near, unit_far = together(output_cotangent, unit_far)
    feed_flat, first_blocks, last_blocks, _here, packed = together(
        feed_flat, first_blocks, last_blocks, unit_far, packed
    )
    feed_full = lax.all_gather(feed_flat, "dp", axis=0, tiled=True)
    cotangent_far = far(cotangent_near, "tensor")
    unit_parts = gathered_parts(unit_near, unit_far, "tensor")

    vectors_full = packed[: 8 * features].reshape(8, features)
    hidden_full = packed[8 * features :]
    bias_query = lax.dynamic_slice_in_dim(vectors_full[6], position * width, width)
    bias_value = lax.dynamic_slice_in_dim(vectors_full[7], position * width, width)
    bias_qkv = jnp.concatenate([bias_query, jnp.zeros_like(bias_query), bias_value])[None]
    bias_hidden = lax.dynamic_slice_in_dim(hidden_full, position * units, units)[None]
    norm_one = vectors_full[:2]
    norm_two = jnp.stack([vectors_full[4], vectors_full[2], vectors_full[3]])

    placed = block_place[0].reshape(ways, -1)
    order = position ^ jnp.arange(ways, dtype=jnp.int32)
    chosen_rows = order[:, None, None] == jnp.arange(ways, dtype=jnp.int32)[None, :, None]
    place = jnp.sum(jnp.where(chosen_rows, placed[None], 0), axis=1).reshape(-1)
    tables = attention_tables(lengths[0], place, random_blocks[0])

    qkv, qkv_full, out_group = project(
        unit_parts, first_blocks, last_blocks, owner_a, owner_b, norm_one, bias_qkv
    )
    context, log_totals = attend(qkv, tables, heads)
    out_far = far(out_group, "tensor")
    context, out_far, cotangent_far = together(context, out_far, cotangent_far)
    grad_parts = gathered_parts(output_cotangent, cotangent_far, "tensor")

    out_parts = gathered_parts(out_group, out_far, "tensor")
    context_near = exchanged_parts(quarters(context), "tensor")
    middle, normed_two = middle_rows(context_near, out_parts, tokens, norm_two)

    half = ways // 2
    normed_far = far(normed_two, "tensor")
    normed_parts = gathered_parts(normed_two, normed_far, "tensor")
    near_back, near_out, stacks = feed(
        normed_parts[:half], grad_parts[:half], feed_full, bias_hidden, (), 0, ways
    )
    normed_far, *stacks = together(normed_far, *stacks)
    normed_parts = gathered_parts(normed_two, normed_far, "tensor")
    far_back, far_out, stacks = feed(
        normed_parts[half:], grad_parts[half:], feed_full, bias_hidden, stacks, half, ways
    )
    back_parts, feed_parts = near_back + far_back, near_out + far_out
    back_terms, far_sum = summed_halves(back_parts, "tensor")
    back_terms.append(far(far_sum, "tensor"))
    feed_sums, sum_hidden = feed_grads(stacks)
    feed_weight_grads = lax.psum_scatter(feed_sums, "dp", scatter_dimension=0, tiled=True)
    feed_weight_grads = feed_weight_grads.astype(F32)
    *back_terms, sum_hidden = together(*back_terms, sum_hidden)

    grad_middle, sums_two, grad_heads, out_blocks = middle_back(
        back_terms, out_parts, context_near, middle, output_cotangent, norm_two, owner_b
    )
    grad_heads = exchanged_parts(grad_heads, "tensor")
    grad_context = jnp.concatenate(grad_heads, axis=0)

    out_terms, out_far = summed_halves(out_blocks, "tensor")
    feed_terms, feed_far = summed_halves(feed_parts, "tensor")
    early, late_rows = feed_far[: near // 2], feed_far[near // 2 :]
    grad_context, out_far, early = together(grad_context, out_far, early)
    out_terms.append(far(out_far, "tensor"))
    early = far(early, "tensor")
    grad_qkv = attend_back(qkv, grad_context, log_totals, tables, heads)
    grad_qkv, early, late_rows, *out_terms = together(grad_qkv, early, late_rows, *out_terms)
    late_rows = far(late_rows, "tensor")
    first_keep, first_send, last_keep, last_send, late, sum_qkv, *back_parts = qkv_grads(
        unit_parts, out_terms, grad_qkv, qkv_full, owner_a, owner_b, split
    )
    near_rows, far_rows = back_parts[:half], back_parts[half:]
    head_sums = lax.dynamic_update_slice(
        jnp.zeros((3, features), F32), sum_qkv.reshape(3, width), (0, position * width)
    )
    hidden_sums = lax.dynamic_update_slice(
        jnp.zeros((1, units * ways), F32), sum_hidden, (0, position * units)
    )
    packed = jnp.concatenate(
        [late.reshape(-1), sums_two.reshape(-1), head_sums.reshape(-1), hidden_sums.reshape(-1)]
    )
    far_sum = added(far_rows[0], swapped(far_rows[1], "tensor", 1))
    packed, far_sum, first_keep, last_keep, *near_rows = together(
        packed, far_sum, first_keep, last_keep, *near_rows
    )
    far_first = far(far_sum[: near // 2], "tensor")
    far_last = far(far_sum[near // 2 :], "tensor")
    first_keep, first_send = halved(first_keep, first_send, "dp", order_a)
    last_keep, last_send = halved(last_keep, last_send, "dp", order_b)
    first_send, last_send, far_first = together(first_send, last_send, far_first)
    while first_send.shape[0] > 1:
        first_keep, first_send = halved(first_keep, first_send, "dp", order_a)
        last_keep, last_send = halved(last_keep, last_send, "dp", order_b)
    first_send, last_send, far_last = together(first_send, last_send, far_last)
    near_terms = [near_rows[0], swapped(near_rows[1], "tensor", 1), far_first, far_last]
    first_raw = halved(first_keep, first_send, "dp", order_a)[0][0].astype(F32)
    last_raw = halved(last_keep, last_send, "dp", order_b)[0][0].astype(F32)
    out_weight_grad = last_raw[:, width:]
    last_raw = last_raw[:, :width]
    input_grad = input_back(near_terms, tokens, grad_middle, norm_one)
    feed_terms.append(jnp.concatenate([early, late_rows], axis=0))
    output = total([term.astype(F32) for term in feed_terms]) + middle + vectors_full[5]
    output = output.astype(BF16)

    packed = summed_everywhere(packed, ("tensor", "dp"))
    by_feature = packed[: 9 * features].reshape(9, features)
    hidden_sums = packed[9 * features :]
    vectors_grad = lax.dynamic_slice_in_dim(by_feature, index * piece, piece, axis=1)
    vectors_grad = jnp.concatenate([vectors_grad[:7], vectors_grad[8:]], axis=0)
    hidden_bias_grad = lax.dynamic_slice_in_dim(hidden_sums, index * unit_piece, unit_piece)

    sum_qkv = lax.dynamic_slice_in_dim(by_feature[6:], position * width, width, axis=1)
    mine = lax.dynamic_slice_in_dim(norm_one, lax.axis_index("dp") * own, own, axis=1)
    raw = jnp.concatenate([first_raw, last_raw], axis=1).reshape(own, 3, width)
    qkv_weight_grad = mine[0][:, None, None] * raw + mine[1][:, None, None] * sum_qkv
    return (
        output,
        input_grad,
        qkv_weight_grad,
        out_weight_grad,
        feed_weight_grads[:, :units],
        feed_weight_grads[:, units:],
        vectors_grad,
        hidden_bias_grad[None, :],
    )


def solution(mesh):
    placed = (
        P(("dp", "tensor"), None),
        P(("dp", "tensor"), None),
        P("dp"),
        P("dp", None),
        P("dp", "tensor", None, None),
        P("dp", None, "tensor"),
        P("dp", "tensor"),
        P("dp", "tensor"),
        P("dp", "tensor"),
        P(None, ("dp", "tensor")),
        P(None, ("dp", "tensor")),
    )
    return jax.shard_map(
        per_device,
        mesh=mesh,
        in_specs=placed,
        out_specs=(
            P(("dp", "tensor"), None),
            P(("dp", "tensor"), None),
            P("dp", None, "tensor"),
            P("dp", "tensor"),
            P("dp", "tensor"),
            P("dp", "tensor"),
            P(None, ("dp", "tensor")),
            P(None, ("dp", "tensor")),
        ),
        check_vma=False,
    )
```

profile of v0, /device:TPU:0, one launch (start us, length us, event | category | flops | bytes accessed | tf_op | source)
XLA Modules:
  0.0 339.0 jit_solution(11147725981156379391)
XLA Ops:
  9.5 1.1 copy.64
  10.7 3.6 %collective-permute-start.5 = (bf16[1,128,512]{2,1,0:T(8,128)(2,1)S(1)}, bf16[1,128,512]{2,1,0:T(8,128)(2,1)S(1)}, u32[]{:S(2)}, u32[]{:S(2)}) collective-permute-start(bf16[1,128,512]{2,1,0:T(8,128)(2,1)S(1)} %bitcast.77), channel_id=1, source_target_pairs={{0,16},{4,20},{8,24},{12,28},{16,0},{20,4},{24,8},{28,12},{1,17},{... | collective-permute-start | bytes 393224 | tf_op jit(solution)/shard_map/ppermute | solution.py:30
  15.2 1.6 collective-permute-start.8
  16.8 1.6 collective-permute-start.1
  18.5 1.9 pad_maximum_fusion.3
  20.4 2.5 unit.1.refs_0_
  23.9 1.6 collective-permute-start.6
  25.6 1.9 collective-permute-done.11
  27.5 1.6 collective-permute-start.12
  29.6 4.7 %collective-permute-done.12 = f32[96,128]{1,0:T(8,128)S(1)} collective-permute-done((f32[96,128]{1,0:T(8,128)S(1)}, f32[96,128]{1,0:T(8,128)S(1)}, u32[]{:S(2)}, u32[]{:S(2)}) %collective-permute-start.12) | collective-permute-done | bytes 49184 | tf_op jit(solution)/shard_map/ppermute | solution.py:30
  34.3 2.9 collective-permute-start.13
  37.2 2.4 collective-permute-start.7
  39.6 3.9 %collective-permute-done.9 = bf16[2,128,512]{2,1,0:T(8,128)(2,1)S(1)} collective-permute-done((bf16[2,128,512]{2,1,0:T(8,128)(2,1)S(1)}, bf16[2,128,512]{2,1,0:T(8,128)(2,1)S(1)}, u32[]{:S(2)}, u32[]{:S(2)}) %collective-permute-start.9) | collective-permute-done | bytes 262176 | tf_op jit(solution)/shard_map/ppermute | solution.py:30
  44.1 5.8 %collective-permute-done.7 = bf16[4,128,512]{2,1,0:T(8,128)(2,1)S(1)} collective-permute-done((bf16[4,128,512]{2,1,0:T(8,128)(2,1)S(1)}, bf16[4,128,512]{2,1,0:T(8,128)(2,1)S(1)}, u32[]{:S(2)}, u32[]{:S(2)}) %collective-permute-start.7) | collective-permute-done | bytes 524320 | tf_op jit(solution)/shard_map/ppermute | solution.py:30
  50.1 5.2 %collective-permute-done.10 = bf16[4,128,512]{2,1,0:T(8,128)(2,1)S(1)} collective-permute-done((bf16[4,128,512]{2,1,0:T(8,128)(2,1)S(1)}, bf16[4,128,512]{2,1,0:T(8,128)(2,1)S(1)}, u32[]{:S(2)}, u32[]{:S(2)}) %collective-permute-start.10) | collective-permute-done | bytes 524320 | tf_op jit(solution)/shard_map/ppermute | solution.py:30
  55.2 1.1 pad_maximum_fusion.1.refs_5_
  60.6 2.4 collective-permute-start.15
  63.4 1.0 collective-permute-done.4.refs_3_
  64.4 1.2 copy-done.2
  65.6 6.9 %project.1 = (bf16[2048,768]{1,0:T(8,128)(2,1)S(1)}, bf16[1024,768]{1,0:T(8,128)(2,1)S(1)}, bf16[1024,256]{1,0:T(8,128)(2,1)S(1)}) custom-call(s32[8]{0:T(128)S(1)} %get-tuple-element.240.owner_a, s32[8]{0:T(128)S(1)} %get-tuple-element.239.owner_b.owner, bf16[512,1024]{1,0:T(8,128)(2,1)S(1)} %copy-done.1, bf16[512,1024]{1,0:T(8,128)(2,1)} %collective-permute-done.2.refs_1_, ...), custom_call_target="tpu_custom_call" | custom-call | flops 3221225472 | bytes 7340032 | tf_op jit(solution)/shard_map/project/pallas_call | solution.py:689
  72.6 1.7 copy-done.16
  74.3 1.2 copy-done.19
  75.5 2.3 collective-permute-start.14
  78.9 1.9 copy-done.17
  80.8 17.3 %attend.1 = (bf16[2048,256]{1,0:T(8,128)(2,1)S(1)}, f32[32,256]{1,0:T(8,128)S(1)}) custom-call(s32[32,17]{1,0:T(8,128)S(1)} %copy.68.stored, s32[32]{0:T(128)S(1)} %subtract_clamp_fusion.limits, s32[2]{0:T(128)S(1)} %pad_add_fusion.ends, bf16[2048,768]{1,0:T(8,128)(2,1)S(1)} %copy-done.17, f32[32,8,256]{2,1,0:T(8,128)S(1)} %reshape.250.bias_ref), custom_call_target="tpu_custom_call" | custom-call | flops 4294967296 | bytes 6291456 | tf_op jit(solution)/shard_map/attend/pallas_call | solution.py:444
  99.5 1.3 collective-permute-start.17
  102.4 6.3 %collective-permute-done.17.refs_2_.refs_9_ = bf16[512,256]{1,0:T(8,128)(2,1)S(1)} collective-permute-done((bf16[512,256]{1,0:T(8,128)(2,1)S(1)}, bf16[512,256]{1,0:T(8,128)(2,1)S(1)}, u32[]{:S(2)}, u32[]{:S(2)}) %collective-permute-start.17) | collective-permute-done | bytes 262176 | tf_op jit(solution)/shard_map/ppermute | solution.py:30
  108.7 4.8 %collective-permute-done.18.refs_3_.refs_10_ = bf16[512,256]{1,0:T(8,128)(2,1)S(1)} collective-permute-done((bf16[512,256]{1,0:T(8,128)(2,1)S(1)}, bf16[512,256]{1,0:T(8,128)(2,1)S(1)}, u32[]{:S(2)}, u32[]{:S(2)}) %collective-permute-start.18) | collective-permute-done | bytes 262176 | tf_op jit(solution)/shard_map/ppermute | solution.py:30
  115.0 5.0 %middle.1 = (f32[512,1024]{1,0:T(8,128)}, bf16[512,1024]{1,0:T(8,128)(2,1)}) custom-call(bf16[512,256]{1,0:T(8,128)(2,1)} %get-tuple-element.223.refs_0_.refs_7_, bf16[512,256]{1,0:T(8,128)(2,1)} %copy-done.25, bf16[512,256]{1,0:T(8,128)(2,1)} %copy-done.26, bf16[512,256]{1,0:T(8,128)(2,1)} %copy-done.27, bf16[1024,256]{1,0:T(8,128)(2,1)} %copy-done, ...), custom_call_target="tpu_custom_call" | custom-call | flops 1073741824 | bytes 6291456 | tf_op jit(solution)/shard_map/middle/pallas_call | solution.py:713
  122.2 1.1 collective-permute-done.21.refs_1_
  123.3 4.8 %all-gather.2.cloned.1.call-done.refs_4_ = bf16[1024,2048]{1,0:T(8,128)(2,1)} async-done(((bf16[128,2048]{1,0:T(8,128)(2,1)}), bf16[1024,2048]{1,0:T(8,128)(2,1)}) %all-gather.2.cloned.1.call-update) | async-done | bytes 4194320 | tf_op jit(solution)/shard_map/all_gather | solution.py:956
  128.0 15.0 %feed.2 = (bf16[512,1024]{1,0:T(8,128)(2,1)}, bf16[512,1024]{1,0:T(8,128)(2,1)}, bf16[512,1024]{1,0:T(8,128)(2,1)}, bf16[512,1024]{1,0:T(8,128)(2,1)}, bf16[2048...) custom-call(bf16[512,1024]{1,0:T(8,128)(2,1)} %get-tuple-element.106.re, ...), custom_call_target="tpu_custom_call" | custom-call | flops 8589934592 | bytes 20971520 | tf_op jit(solution)/shard_map/feed/pallas_call | solution.py:540
  143.0 3.1 collective-permute-done.25.refs_0_
  146.1 3.0 collective-permute-done.26.refs_1_
  149.1 15.2 %feed.3 = (bf16[512,1024]{1,0:T(8,128)(2,1)}, bf16[512,1024]{1,0:T(8,128)(2,1)}, bf16[512,1024]{1,0:T(8,128)(2,1)}, bf16[512,1024]{1,0:T(8,128)(2,1)}, bf16[2048...) custom-call(bf16[512,1024]{1,0:T(8,128)(2,1)} %collective-permute-do, ...), custom_call_target="tpu_custom_call", output_to_operand_aliasing={{4}: (6, {}), {5}: (7, {}), {6}: (8, {}), {7}: (9, {})} | custom-call | flops 8589934592 | bytes 20971520 | tf_op jit(solution)/shard_map/feed/pallas_call | solution.py:540
  165.0 2.4 collective-permute-done.28
  167.4 2.6 add_convert_fusion.3
  170.9 15.4 %feed_grads.1 = (bf16[1024,2048]{1,0:T(8,128)(2,1)}, f32[1,1024]{1,0:T(1,128)}) custom-call(bf16[2048,1024]{1,0:T(8,128)(2,1)} %get-tuple-element.124.normed_ref, bf16[2048,1024]{1,0:T(8,128)(2,1)} %get-tuple-element.125.grad_ref, bf16[2048,1024]{1,0:T(8,128)(2,1)} %get-tuple-element.126.grads_ref, bf16[2048,1024]{1,0:T(8,128)(2,1)} %get-tuple-element.127.active_ref), custom_call_target="tpu_custom_call" | custom-call | flops 8589934592 | bytes 16777216 | tf_op jit(solution)/shard_map/feed_grads/pallas_call | solution.py:588
  186.3 9.2 %collective-permute-done.29.refs_2_ = bf16[512,1024]{1,0:T(8,128)(2,1)} collective-permute-done((bf16[512,1024]{1,0:T(8,128)(2,1)}, bf16[512,1024]{1,0:T(8,128)(2,1)}, u32[]{:S(2)}, u32[]{:S(2)}) %collective-permute-start.29) | collective-permute-done | bytes 1048608 | tf_op jit(solution)/shard_map/ppermute | solution.py:30
  195.5 10.3 %middle_back.1 = (f32[512,1024]{1,0:T(8,128)}, f32[4,1024]{1,0:T(4,128)}, bf16[512,256]{1,0:T(8,128)(2,1)}, bf16[512,256]{1,0:T(8,128)(2,1)}, bf16[512,256]{1,0:...) custom-call(s32[8]{0:T(128)} %copy-done.7, ...), custom_call_target="tpu_custom_call" | custom-call | flops 2147483648 | bytes 10485760 | tf_op jit(solution)/shard_map/middle_back/pallas_call | solution.py:778
  206.0 2.1 add_convert_fusion.2
  208.0 1.1 collective-permute-start.32
  209.1 1.1 collective-permute-start.31
  211.6 4.6 %collective-permute-done.32 = bf16[512,256]{1,0:T(8,128)(2,1)S(1)} collective-permute-done((bf16[512,256]{1,0:T(8,128)(2,1)S(1)}, bf16[512,256]{1,0:T(8,128)(2,1)S(1)}, u32[]{:S(2)}, u32[]{:S(2)}) %collective-permute-start.32) | collective-permute-done | bytes 262176 | tf_op jit(solution)/shard_map/ppermute | solution.py:30
  216.1 6.2 %collective-permute-done.31 = bf16[512,256]{1,0:T(8,128)(2,1)S(1)} collective-permute-done((bf16[512,256]{1,0:T(8,128)(2,1)S(1)}, bf16[512,256]{1,0:T(8,128)(2,1)S(1)}, u32[]{:S(2)}, u32[]{:S(2)}) %collective-permute-start.31) | collective-permute-done | bytes 262176 | tf_op jit(solution)/shard_map/ppermute | solution.py:30
  223.5 1.2 collective-permute-start.37
  224.7 23.3 %attend_back.1.refs_7_ = bf16[2048,768]{1,0:T(8,128)(2,1)S(1)} custom-call(s32[32,17]{1,0:T(8,128)S(1)} %copy.68.stored, s32[32]{0:T(128)S(1)} %subtract_clamp_fusion.limits, s32[2]{0:T(128)S(1)} %pad_add_fusion.ends, bf16[2048,768]{1,0:T(8,128)(2,1)S(1)} %copy-done.18, bf16[2048,256]{1,0:T(8,128)(2,1)S(1)} %pad_maximum_fusion.2.grad_ref, ...), custom_call_target="tpu_custom_call" | custom-call | flops 8589934592 | bytes 6291456 | tf_op jit(solution)/shard_map/attend_back/pallas_call | solution.py:466
  248.0 12.6 %qkv_grads.1 = (bf16[4,128,512]{2,1,0:T(8,128)(2,1)S(1)}, bf16[4,128,512]{2,1,0:T(8,128)(2,1)S(1)}, bf16[4,128,512]{2,1,0:T(8,128)(2,1)S(1)}, bf16[4,128,512]{2,...) custom-call(s32[8]{0:T(128)S(1)} %get-tuple-element.240.owner_a, ...), custom_call_target="tpu_custom_call" | custom-call | flops 6442450944 | bytes 12582912 | tf_op jit(solution)/shard_map/qkv_grads/pallas_call | solution.py:850
  260.6 1.0 copy-done.3
  262.4 1.0 copy-done.9
  266.3 1.8 collective-permute-done.39
  268.1 1.8 add_convert_fusion
  273.3 12.4 %collective-permute-done.50 = f32[104,128]{1,0:T(8,128)S(1)} collective-permute-done((f32[104,128]{1,0:T(8,128)S(1)}, f32[104,128]{1,0:T(8,128)S(1)}, u32[]{:S(2)}, u32[]{:S(2)}) %collective-permute-start.50) | collective-permute-done | bytes 53280 | tf_op jit(solution)/shard_map/ppermute | solution.py:30
  286.9 3.1 add_convert_fusion.1
  290.7 1.2 collective-permute-start.46
  292.3 3.9 %collective-permute-done.52 = f32[104,128]{1,0:T(8,128)S(1)} collective-permute-done((f32[104,128]{1,0:T(8,128)S(1)}, f32[104,128]{1,0:T(8,128)S(1)}, u32[]{:S(2)}, u32[]{:S(2)}) %collective-permute-start.52) | collective-permute-done | bytes 53280 | tf_op jit(solution)/shard_map/ppermute | solution.py:30
  297.1 4.3 %collective-permute-done.53 = f32[104,128]{1,0:T(8,128)S(1)} collective-permute-done((f32[104,128]{1,0:T(8,128)S(1)}, f32[104,128]{1,0:T(8,128)S(1)}, u32[]{:S(2)}, u32[]{:S(2)}) %collective-permute-start.53) | collective-permute-done | bytes 53280 | tf_op jit(solution)/shard_map/ppermute | solution.py:30
  302.3 8.8 %collective-permute-done.44 = bf16[2,128,512]{2,1,0:T(8,128)(2,1)S(1)} collective-permute-done((bf16[2,128,512]{2,1,0:T(8,128)(2,1)S(1)}, bf16[2,128,512]{2,1,0:T(8,128)(2,1)S(1)}, u32[]{:S(2)}, u32[]{:S(2)}) %collective-permute-start.44) | collective-permute-done | bytes 262176 | tf_op jit(solution)/shard_map/ppermute | solution.py:30
  311.2 3.0 collective-permute-done.45
  314.2 2.0 collective-permute-start.48
  317.4 1.8 collective-permute-done.48
  320.0 3.8 %collective-permute-done.47 = bf16[1,128,512]{2,1,0:T(8,128)(2,1)S(1)} collective-permute-done((bf16[1,128,512]{2,1,0:T(8,128)(2,1)S(1)}, bf16[1,128,512]{2,1,0:T(8,128)(2,1)S(1)}, u32[]{:S(2)}, u32[]{:S(2)}) %collective-permute-start.47) | collective-permute-done | bytes 131104 | tf_op jit(solution)/shard_map/ppermute | solution.py:30
  325.1 4.7 %input_back.1 = bf16[512,1024]{1,0:T(8,128)(2,1)} custom-call(bf16[512,1024]{1,0:T(8,128)(2,1)} %copy-done.3, bf16[512,1024]{1,0:T(8,128)(2,1)} %collective-permute-done.40.refs_1_, bf16[256,1024]{1,0:T(8,128)(2,1)} %copy-done.29, bf16[256,1024]{1,0:T(8,128)(2,1)} %collective-permute-done.46.refs_3_, bf16[512,1024]{1,0:T(8,128)(2,1)} %refs_4_.1, ...), custom_call_target="tpu_custom_call" | custom-call | flops 10485760 | bytes 7340032 | tf_op jit(solution)/shard_map/input_back/pallas_call | solution.py:885
  329.8 2.1 fusion.10
  (262 shorter events, 35.9 us)
Async XLA Ops:
  7.2 120.8 %all-gather.2.cloned.1.call-start = ((), (), s32[]{:S(2)}) async-start(), calls=%async_computation.1 | async-start | bytes 4718592 | tf_op jit(solution)/shard_map/all_gather | solution.py:956
  8.9 8.0 %collective-permute-start = (f32[96,128]{1,0:T(8,128)S(1)}, f32[96,128]{1,0:T(8,128)S(1)}, u32[]{:S(2)}, u32[]{:S(2)}) collective-permute-start(f32[96,128]{1,0:T(8,128)S(1)} %maximum_bitcast_fusion.1), channel_id=1, source_target_pairs={{0,1},{1,0},{2,3},{3,2},{4,5},{5,4},{6,7},{7,6},{8,9},{9,8},{10,11... | collective-permute-start | bytes 147464 | tf_op jit(solution)/shard_map/ppermute | solution.py:30
  10.7 13.2 %collective-permute-start.5 = (bf16[1,128,512]{2,1,0:T(8,128)(2,1)S(1)}, bf16[1,128,512]{2,1,0:T(8,128)(2,1)S(1)}, u32[]{:S(2)}, u32[]{:S(2)}) collective-permute-start(bf16[1,128,512]{2,1,0:T(8,128)(2,1)S(1)} %bitcast.77), channel_id=1, source_target_pairs={{0,16},{4,20},{8,24},{12,28},{16,0},{20,4},{24,8},{28,12},{1,17},{... | collective-permute-start | bytes 393224 | tf_op jit(solution)/shard_map/ppermute | solution.py:30
  15.2 13.9 %collective-permute-start.8 = (bf16[1,128,512]{2,1,0:T(8,128)(2,1)S(1)}, bf16[1,128,512]{2,1,0:T(8,128)(2,1)S(1)}, u32[]{:S(2)}, u32[]{:S(2)}) collective-permute-start(bf16[1,128,512]{2,1,0:T(8,128)(2,1)S(1)} %maximum_bitcast_fusion), channel_id=1, source_target_pairs={{0,4},{4,0},{8,12},{12,8},{16,20},{20,16},{24,28},{28,24},{1,5},{5... | collective-permute-start | bytes 393224 | tf_op jit(solution)/shard_map/ppermute | solution.py:30
  16.8 6.0 %collective-permute-start.1 = (f32[96,128]{1,0:T(8,128)S(1)}, f32[96,128]{1,0:T(8,128)S(1)}, u32[]{:S(2)}, u32[]{:S(2)}) collective-permute-start(f32[96,128]{1,0:T(8,128)S(1)} %fusion.6), channel_id=1, source_target_pairs={{0,2},{1,3},{2,0},{3,1},{4,6},{5,7},{6,4},{7,5},{8,10},{9,11},{10,... | collective-permute-start | bytes 147464 | tf_op jit(solution)/shard_map/ppermute | solution.py:30
  22.9 33.4 %collective-permute-start.3 = (bf16[512,1024]{1,0:T(8,128)(2,1)}, bf16[512,1024]{1,0:T(8,128)(2,1)}, u32[]{:S(2)}, u32[]{:S(2)}) collective-permute-start(bf16[512,1024]{1,0:T(8,128)(2,1)} %unit.1.refs_0_), channel_id=1, source_target_pairs={{0,2},{1,3},{2,0},{3,1},{4,6},{5,7},{6,4},{7,5},{8,10},{9,11},{10,... | collective-permute-start | bytes 3145736 | tf_op jit(solution)/shard_map/ppermute | solution.py:30
  23.4 4.1 %collective-permute-start.11 = (f32[96,128]{1,0:T(8,128)S(1)}, f32[96,128]{1,0:T(8,128)S(1)}, u32[]{:S(2)}, u32[]{:S(2)}) collective-permute-start(f32[96,128]{1,0:T(8,128)S(1)} %bitcast.88), channel_id=1, source_target_pairs={{0,4},{4,0},{8,12},{12,8},{16,20},{20,16},{24,28},{28,24},{1,5},{5... | collective-permute-start | bytes 147464 | tf_op jit(solution)/shard_map/ppermute | solution.py:30
  23.9 13.2 %collective-permute-start.6 = (bf16[2,128,512]{2,1,0:T(8,128)(2,1)S(1)}, bf16[2,128,512]{2,1,0:T(8,128)(2,1)S(1)}, u32[]{:S(2)}, u32[]{:S(2)}) collective-permute-start(bf16[2,128,512]{2,1,0:T(8,128)(2,1)S(1)} %pad_maximum_fusion.7), channel_id=1, source_target_pairs={{0,8},{4,12},{8,0},{12,4},{16,24},{20,28},{24,16},{28,20},{1,9},{5... | collective-permute-start | bytes 786440 | tf_op jit(solution)/shard_map/ppermute | solution.py:30
  27.5 6.8 %collective-permute-start.12 = (f32[96,128]{1,0:T(8,128)S(1)}, f32[96,128]{1,0:T(8,128)S(1)}, u32[]{:S(2)}, u32[]{:S(2)}) collective-permute-start(f32[96,128]{1,0:T(8,128)S(1)} %bitcast_add_fusion.1), channel_id=1, source_target_pairs={{0,8},{4,12},{8,0},{12,4},{16,24},{20,28},{24,16},{28,20},{1,9},{5... | collective-permute-start | bytes 147464 | tf_op jit(solution)/shard_map/ppermute | solution.py:30
  29.2 14.3 %collective-permute-start.9 = (bf16[2,128,512]{2,1,0:T(8,128)(2,1)S(1)}, bf16[2,128,512]{2,1,0:T(8,128)(2,1)S(1)}, u32[]{:S(2)}, u32[]{:S(2)}) collective-permute-start(bf16[2,128,512]{2,1,0:T(8,128)(2,1)S(1)} %pad_maximum_fusion.8), channel_id=1, source_target_pairs={{0,16},{4,20},{8,24},{12,28},{16,0},{20,4},{24,8},{28,12},{1,17},{... | collective-permute-start | bytes 786440 | tf_op jit(solution)/shard_map/ppermute | solution.py:30
  34.3 9.8 %collective-permute-start.13 = (f32[96,128]{1,0:T(8,128)S(1)}, f32[96,128]{1,0:T(8,128)S(1)}, u32[]{:S(2)}, u32[]{:S(2)}) collective-permute-start(f32[96,128]{1,0:T(8,128)S(1)} %fusion.14), channel_id=1, source_target_pairs={{0,16},{4,20},{8,24},{12,28},{16,0},{20,4},{24,8},{28,12},{1,17},{... | collective-permute-start | bytes 147464 | tf_op jit(solution)/shard_map/ppermute | solution.py:30
  37.2 12.7 %collective-permute-start.7 = (bf16[4,128,512]{2,1,0:T(8,128)(2,1)S(1)}, bf16[4,128,512]{2,1,0:T(8,128)(2,1)S(1)}, u32[]{:S(2)}, u32[]{:S(2)}) collective-permute-start(bf16[4,128,512]{2,1,0:T(8,128)(2,1)S(1)} %pad_maximum_fusion.4), channel_id=1, source_target_pairs={{0,4},{4,0},{8,12},{12,8},{16,20},{20,16},{24,28},{28,24},{1,5},{5... | collective-permute-start | bytes 1572872 | tf_op jit(solution)/shard_map/ppermute | solution.py:30
  43.5 11.7 %collective-permute-start.10 = (bf16[4,128,512]{2,1,0:T(8,128)(2,1)S(1)}, bf16[4,128,512]{2,1,0:T(8,128)(2,1)S(1)}, u32[]{:S(2)}, u32[]{:S(2)}) collective-permute-start(bf16[4,128,512]{2,1,0:T(8,128)(2,1)S(1)} %pad_maximum_fusion.5), channel_id=1, source_target_pairs={{0,8},{4,12},{8,0},{12,4},{16,24},{20,28},{24,16},{28,20},{1,9},{5... | collective-permute-start | bytes 1572872 | tf_op jit(solution)/shard_map/ppermute | solution.py:30
  56.3 273.5 %reduce-scatter.2.cloned.1.call-start = ((), (), s32[]{:S(2)}) async-start(), calls=%async_computation.2 | async-start | bytes 4718592 | tf_op jit(solution)/shard_map/reduce_scatter | solution.py:1002
  59.9 3.6 %collective-permute-start.2 = (bf16[512,1024]{1,0:T(8,128)(2,1)S(1)}, bf16[512,1024]{1,0:T(8,128)(2,1)}, u32[]{:S(2)}, u32[]{:S(2)}) collective-permute-start(bf16[512,1024]{1,0:T(8,128)(2,1)S(1)} %copy-done.1), channel_id=1, source_target_pairs={{0,1},{1,0},{2,3},{3,2},{4,5},{5,4},{6,7},{7,6},{8,9},{9,8},{10,11... | collective-permute-start | bytes 3145736 | tf_op jit(solution)/shard_map/ppermute | solution.py:30
  59.9 4.5 %collective-permute-start.4 = (bf16[512,1024]{1,0:T(8,128)(2,1)}, bf16[512,1024]{1,0:T(8,128)(2,1)}, u32[]{:S(2)}, u32[]{:S(2)}) collective-permute-start(bf16[512,1024]{1,0:T(8,128)(2,1)} %collective-permute-done.3.refs_2_), channel_id=1, source_target_pairs={{0,1},{1,0},{2,3},{3,2},{4,5},{5,4},{6,7},{7,6},{8,9},{9,8},{10,11... | collective-permute-start | bytes 3145736 | tf_op jit(solution)/shard_map/ppermute | solution.py:30
  60.6 37.6 %collective-permute-start.15 = (bf16[512,1024]{1,0:T(8,128)(2,1)}, bf16[512,1024]{1,0:T(8,128)(2,1)}, u32[]{:S(2)}, u32[]{:S(2)}) collective-permute-start(bf16[512,1024]{1,0:T(8,128)(2,1)} %refs_12_.1), channel_id=1, source_target_pairs={{0,2},{1,3},{2,0},{3,1},{4,6},{5,7},{6,4},{7,5},{8,10},{9,11},{10,... | collective-permute-start | bytes 3145736 | tf_op jit(solution)/shard_map/ppermute | solution.py:30
  63.0 202.1 %copy-start.6 = (f32[2,1024]{1,0:T(2,128)}, f32[2,1024]{1,0:T(2,128)S(1)}, u32[]{:S(2)}) copy-start(f32[2,1024]{1,0:T(2,128)S(1)} %slice.195.refs_6_) | copy-start | bytes 24580
  75.5 22.6 %copy-start = (bf16[1024,256]{1,0:T(8,128)(2,1)}, bf16[1024,256]{1,0:T(8,128)(2,1)S(1)}, u32[]{:S(2)}) copy-start(bf16[1024,256]{1,0:T(8,128)(2,1)S(1)} %get-tuple-element.102.refs_4_.refs_3_) | copy-start | bytes 1572868
  75.5 22.6 %collective-permute-start.14 = (bf16[1024,256]{1,0:T(8,128)(2,1)S(1)}, bf16[1024,256]{1,0:T(8,128)(2,1)S(1)}, u32[]{:S(2)}, u32[]{:S(2)}) collective-permute-start(bf16[1024,256]{1,0:T(8,128)(2,1)S(1)} %get-tuple-element.102.refs_4_.refs_3_), channel_id=1, source_target_pairs={{0,2},{1,3},{2,0},{3,1},{4,6},{5,7},{6,4},{7,5},{8,10},{9,11},{10,... | collective-permute-start | bytes 1572872 | tf_op jit(solution)/shard_map/ppermute | solution.py:30
  78.9 23.1 %collective-permute-start.19 = (bf16[1024,256]{1,0:T(8,128)(2,1)S(1)}, bf16[1024,256]{1,0:T(8,128)(2,1)S(1)}, u32[]{:S(2)}, u32[]{:S(2)}) collective-permute-start(bf16[1024,256]{1,0:T(8,128)(2,1)S(1)} %get-tuple-element.102.refs_4_.refs_3_), channel_id=1, source_target_pairs={{0,1},{1,0},{2,3},{3,2},{4,5},{5,4},{6,7},{7,6},{8,9},{9,8},{10,11... | collective-permute-start | bytes 1572872 | tf_op jit(solution)/shard_map/ppermute | solution.py:30
  98.2 15.3 %collective-permute-start.20 = (bf16[1024,256]{1,0:T(8,128)(2,1)S(1)}, bf16[1024,256]{1,0:T(8,128)(2,1)S(1)}, u32[]{:S(2)}, u32[]{:S(2)}) collective-permute-start(bf16[1024,256]{1,0:T(8,128)(2,1)S(1)} %collective-permute-done.14.refs_6_.refs_5_), channel_id=1, source_target_pairs={{0,1},{1,0},{2,3},{3,2},{4,5},{5,4},{6,7},{7,6},{8,9},{9,8},{10,11... | collective-permute-start | bytes 1572872 | tf_op jit(solution)/shard_map/ppermute | solution.py:30
  99.5 2.9 collective-permute-start.16
  99.5 9.1 %collective-permute-start.17 = (bf16[512,256]{1,0:T(8,128)(2,1)S(1)}, bf16[512,256]{1,0:T(8,128)(2,1)S(1)}, u32[]{:S(2)}, u32[]{:S(2)}) collective-permute-start(bf16[512,256]{1,0:T(8,128)(2,1)S(1)} %get-tuple-element.221), channel_id=1, source_target_pairs={{0,2},{1,3},{2,0},{3,1},{4,6},{5,7},{6,4},{7,5},{8,10},{9,11},{10,... | collective-permute-start | bytes 786440 | tf_op jit(solution)/shard_map/ppermute | solution.py:30
  100.9 12.6 %collective-permute-start.18 = (bf16[512,256]{1,0:T(8,128)(2,1)S(1)}, bf16[512,256]{1,0:T(8,128)(2,1)S(1)}, u32[]{:S(2)}, u32[]{:S(2)}) collective-permute-start(bf16[512,256]{1,0:T(8,128)(2,1)S(1)} %get-tuple-element.220), channel_id=1, source_target_pairs={{0,3},{1,2},{2,1},{3,0},{4,7},{5,6},{6,5},{7,4},{8,11},{9,10},{10,... | collective-permute-start | bytes 786440 | tf_op jit(solution)/shard_map/ppermute | solution.py:30
  102.0 20.2 %collective-permute-start.22 = (bf16[512,1024]{1,0:T(8,128)(2,1)}, bf16[512,1024]{1,0:T(8,128)(2,1)}, u32[]{:S(2)}, u32[]{:S(2)}) collective-permute-start(bf16[512,1024]{1,0:T(8,128)(2,1)} %refs_12_.1), channel_id=1, source_target_pairs={{0,1},{1,0},{2,3},{3,2},{4,5},{5,4},{6,7},{7,6},{8,9},{9,8},{10,11... | collective-permute-start | bytes 3145736 | tf_op jit(solution)/shard_map/ppermute | solution.py:30
  120.0 3.3 collective-permute-start.21
  120.6 25.5 %collective-permute-start.25 = (bf16[512,1024]{1,0:T(8,128)(2,1)}, bf16[512,1024]{1,0:T(8,128)(2,1)}, u32[]{:S(2)}, u32[]{:S(2)}) collective-permute-start(bf16[512,1024]{1,0:T(8,128)(2,1)} %get-tuple-element.106.refs_0_), channel_id=1, source_target_pairs={{0,2},{1,3},{2,0},{3,1},{4,6},{5,7},{6,4},{7,5},{8,10},{9,11},{10,... | collective-permute-start | bytes 3145736 | tf_op jit(solution)/shard_map/ppermute | solution.py:30
  122.2 23.9 %collective-permute-start.27 = (bf16[512,1024]{1,0:T(8,128)(2,1)}, bf16[512,1024]{1,0:T(8,128)(2,1)}, u32[]{:S(2)}, u32[]{:S(2)}) collective-permute-start(bf16[512,1024]{1,0:T(8,128)(2,1)} %collective-permute-done.15.refs_2_), channel_id=1, source_target_pairs={{0,1},{1,0},{2,3},{3,2},{4,5},{5,4},{6,7},{7,6},{8,9},{9,8},{10,11... | collective-permute-start | bytes 3145736 | tf_op jit(solution)/shard_map/ppermute | solution.py:30
  146.1 3.0 collective-permute-start.26
  164.3 3.1 collective-permute-start.28
  164.5 21.8 %collective-permute-start.24 = (bf16[512,1024]{1,0:T(8,128)(2,1)}, bf16[512,1024]{1,0:T(8,128)(2,1)}, u32[]{:S(2)}, u32[]{:S(2)}) collective-permute-start(bf16[512,1024]{1,0:T(8,128)(2,1)} %get-tuple-element.111), channel_id=1, source_target_pairs={{0,1},{1,0},{2,3},{3,2},{4,5},{5,4},{6,7},{7,6},{8,9},{9,8},{10,11... | collective-permute-start | bytes 3145736 | tf_op jit(solution)/shard_map/ppermute | solution.py:30
  164.8 41.1 %collective-permute-start.34 = (bf16[512,1024]{1,0:T(8,128)(2,1)}, bf16[512,1024]{1,0:T(8,128)(2,1)}, u32[]{:S(2)}, u32[]{:S(2)}) collective-permute-start(bf16[512,1024]{1,0:T(8,128)(2,1)} %get-tuple-element.140), channel_id=1, source_target_pairs={{0,1},{1,0},{2,3},{3,2},{4,5},{5,4},{6,7},{7,6},{8,9},{9,8},{10,11... | collective-permute-start | bytes 3145736 | tf_op jit(solution)/shard_map/ppermute | solution.py:30
  170.0 25.5 %collective-permute-start.29 = (bf16[512,1024]{1,0:T(8,128)(2,1)}, bf16[512,1024]{1,0:T(8,128)(2,1)}, u32[]{:S(2)}, u32[]{:S(2)}) collective-permute-start(bf16[512,1024]{1,0:T(8,128)(2,1)} %add_convert_fusion.3), channel_id=1, source_target_pairs={{0,2},{1,3},{2,0},{3,1},{4,6},{5,7},{6,4},{7,5},{8,10},{9,11},{10,... | collective-permute-start | bytes 3145736 | tf_op jit(solution)/shard_map/ppermute | solution.py:30
  205.9 16.6 %collective-permute-start.33 = (bf16[8,128,256]{2,1,0:T(8,128)(2,1)}, bf16[8,128,256]{2,1,0:T(8,128)(2,1)S(1)}, u32[]{:S(2)}, u32[]{:S(2)}) collective-permute-start(bf16[8,128,256]{2,1,0:T(8,128)(2,1)} %get-tuple-element.138), channel_id=1, source_target_pairs={{0,1},{1,0},{2,3},{3,2},{4,5},{5,4},{6,7},{7,6},{8,9},{9,8},{10,11... | collective-permute-start | bytes 1572872 | tf_op jit(solution)/shard_map/ppermute | solution.py:30
  208.0 8.1 %collective-permute-start.32 = (bf16[512,256]{1,0:T(8,128)(2,1)S(1)}, bf16[512,256]{1,0:T(8,128)(2,1)S(1)}, u32[]{:S(2)}, u32[]{:S(2)}) collective-permute-start(bf16[512,256]{1,0:T(8,128)(2,1)S(1)} %copy-done.42), channel_id=1, source_target_pairs={{0,3},{1,2},{2,1},{3,0},{4,7},{5,6},{6,5},{7,4},{8,11},{9,10},{10,... | collective-permute-start | bytes 786440 | tf_op jit(solution)/shard_map/ppermute | solution.py:30
  209.1 13.2 %collective-permute-start.31 = (bf16[512,256]{1,0:T(8,128)(2,1)S(1)}, bf16[512,256]{1,0:T(8,128)(2,1)S(1)}, u32[]{:S(2)}, u32[]{:S(2)}) collective-permute-start(bf16[512,256]{1,0:T(8,128)(2,1)S(1)} %copy-done.41), channel_id=1, source_target_pairs={{0,2},{1,3},{2,0},{3,1},{4,6},{5,7},{6,4},{7,5},{8,10},{9,11},{10,... | collective-permute-start | bytes 786440 | tf_op jit(solution)/shard_map/ppermute | solution.py:30
  210.2 12.1 %collective-permute-start.30 = (bf16[512,256]{1,0:T(8,128)(2,1)S(1)}, bf16[512,256]{1,0:T(8,128)(2,1)S(1)}, u32[]{:S(2)}, u32[]{:S(2)}) collective-permute-start(bf16[512,256]{1,0:T(8,128)(2,1)S(1)} %copy-done.40), channel_id=1, source_target_pairs={{0,1},{1,0},{2,3},{3,2},{4,5},{5,4},{6,7},{7,6},{8,9},{9,8},{10,11... | collective-permute-start | bytes 786440 | tf_op jit(solution)/shard_map/ppermute | solution.py:30
  211.1 36.9 %collective-permute-start.36 = (bf16[8,128,256]{2,1,0:T(8,128)(2,1)S(1)}, bf16[8,128,256]{2,1,0:T(8,128)(2,1)S(1)}, u32[]{:S(2)}, u32[]{:S(2)}) collective-permute-start(bf16[8,128,256]{2,1,0:T(8,128)(2,1)S(1)} %copy-done.39), channel_id=1, source_target_pairs={{0,1},{1,0},{2,3},{3,2},{4,5},{5,4},{6,7},{7,6},{8,9},{9,8},{10,11... | collective-permute-start | bytes 1572872 | tf_op jit(solution)/shard_map/ppermute | solution.py:30
  222.6 25.4 %collective-permute-start.35 = (bf16[256,1024]{1,0:T(8,128)(2,1)S(1)}, bf16[256,1024]{1,0:T(8,128)(2,1)S(1)}, u32[]{:S(2)}, u32[]{:S(2)}) collective-permute-start(bf16[256,1024]{1,0:T(8,128)(2,1)S(1)} %get-tuple-element.143), channel_id=1, source_target_pairs={{0,2},{1,3},{2,0},{3,1},{4,6},{5,7},{6,4},{7,5},{8,10},{9,11},{10,... | collective-permute-start | bytes 1572872 | tf_op jit(solution)/shard_map/ppermute | solution.py:30
  223.5 24.5 %collective-permute-start.37 = (bf16[8,128,256]{2,1,0:T(8,128)(2,1)S(1)}, bf16[8,128,256]{2,1,0:T(8,128)(2,1)S(1)}, u32[]{:S(2)}, u32[]{:S(2)}) collective-permute-start(bf16[8,128,256]{2,1,0:T(8,128)(2,1)S(1)} %add_convert_fusion.4), channel_id=1, source_target_pairs={{0,2},{1,3},{2,0},{3,1},{4,6},{5,7},{6,4},{7,5},{8,10},{9,11},{10,... | collective-permute-start | bytes 1572872 | tf_op jit(solution)/shard_map/ppermute | solution.py:30
  224.7 23.3 %copy-start.8 = (s32[8]{0:T(128)S(1)}, s32[8]{0:T(128)}, u32[]{:S(2)}) copy-start(s32[8]{0:T(128)} %copy-done.7) | copy-start | bytes 100
  224.7 23.3 %copy-start.15 = (bf16[8,128,256]{2,1,0:T(8,128)(2,1)S(1)}, bf16[8,128,256]{2,1,0:T(8,128)(2,1)}, u32[]{:S(2)}) copy-start(bf16[8,128,256]{2,1,0:T(8,128)(2,1)} %get-tuple-element.149.refs_4_) | copy-start | bytes 1572868
  224.7 23.3 %copy-start.20 = (bf16[1024,768]{1,0:T(8,128)(2,1)S(1)}, bf16[1024,768]{1,0:T(8,128)(2,1)}, u32[]{:S(2)}) copy-start(bf16[1024,768]{1,0:T(8,128)(2,1)} %copy-done.19) | copy-start | bytes 4718596
  265.1 3.0 collective-permute-start.39
  265.1 21.4 %collective-permute-start.23 = (bf16[512,1024]{1,0:T(8,128)(2,1)}, bf16[512,1024]{1,0:T(8,128)(2,1)}, u32[]{:S(2)}, u32[]{:S(2)}) collective-permute-start(bf16[512,1024]{1,0:T(8,128)(2,1)} %get-tuple-element.109), channel_id=1, source_target_pairs={{0,1},{1,0},{2,3},{3,2},{4,5},{5,4},{6,7},{7,6},{8,9},{9,8},{10,11... | collective-permute-start | bytes 3145736 | tf_op jit(solution)/shard_map/ppermute | solution.py:30
  268.1 18.7 %copy-start.28 = (bf16[512,1024]{1,0:T(8,128)(2,1)S(1)}, bf16[512,1024]{1,0:T(8,128)(2,1)}, u32[]{:S(2)}) copy-start(bf16[512,1024]{1,0:T(8,128)(2,1)} %get-tuple-element.108) | copy-start | bytes 3145732
  268.1 18.7 %copy-start.32 = (bf16[256,1024]{1,0:T(8,128)(2,1)S(1)}, bf16[256,1024]{1,0:T(8,128)(2,1)}, u32[]{:S(2)}) copy-start(bf16[256,1024]{1,0:T(8,128)(2,1)} %copy-done.31) | copy-start | bytes 1572868
  269.9 1.7 collective-permute-start.49
  270.1 16.7 %collective-permute-start.38 = (bf16[256,1024]{1,0:T(8,128)(2,1)}, bf16[256,1024]{1,0:T(8,128)(2,1)S(1)}, u32[]{:S(2)}, u32[]{:S(2)}) collective-permute-start(bf16[256,1024]{1,0:T(8,128)(2,1)} %get-tuple-element.148), channel_id=1, source_target_pairs={{0,2},{1,3},{2,0},{3,1},{4,6},{5,7},{6,4},{7,5},{8,10},{9,11},{10,... | collective-permute-start | bytes 1572872 | tf_op jit(solution)/shard_map/ppermute | solution.py:30
  271.0 20.9 %collective-permute-start.41 = (bf16[4,128,512]{2,1,0:T(8,128)(2,1)S(1)}, bf16[4,128,512]{2,1,0:T(8,128)(2,1)S(1)}, u32[]{:S(2)}, u32[]{:S(2)}) collective-permute-start(bf16[4,128,512]{2,1,0:T(8,128)(2,1)S(1)} %copy-done.14), channel_id=1, source_target_pairs={{0,4},{4,0},{8,12},{12,8},{16,20},{20,16},{24,28},{28,24},{1,5},{5... | collective-permute-start | bytes 1572872 | tf_op jit(solution)/shard_map/ppermute | solution.py:30
  271.2 25.0 %collective-permute-start.42 = (bf16[4,128,512]{2,1,0:T(8,128)(2,1)S(1)}, bf16[4,128,512]{2,1,0:T(8,128)(2,1)S(1)}, u32[]{:S(2)}, u32[]{:S(2)}) collective-permute-start(bf16[4,128,512]{2,1,0:T(8,128)(2,1)S(1)} %copy-done.12), channel_id=1, source_target_pairs={{0,8},{4,12},{8,0},{12,4},{16,24},{20,28},{24,16},{28,20},{1,9},{5... | collective-permute-start | bytes 1572872 | tf_op jit(solution)/shard_map/ppermute | solution.py:30
  271.6 14.1 %collective-permute-start.50 = (f32[104,128]{1,0:T(8,128)S(1)}, f32[104,128]{1,0:T(8,128)S(1)}, u32[]{:S(2)}, u32[]{:S(2)}) collective-permute-start(f32[104,128]{1,0:T(8,128)S(1)} %bitcast_add_fusion), channel_id=1, source_target_pairs={{0,2},{1,3},{2,0},{3,1},{4,6},{5,7},{6,4},{7,5},{8,10},{9,11},{10,... | collective-permute-start | bytes 159752 | tf_op jit(solution)/shard_map/ppermute | solution.py:30
  285.7 15.7 %collective-permute-start.43 = (bf16[256,1024]{1,0:T(8,128)(2,1)S(1)}, bf16[256,1024]{1,0:T(8,128)(2,1)S(1)}, u32[]{:S(2)}, u32[]{:S(2)}) collective-permute-start(bf16[256,1024]{1,0:T(8,128)(2,1)S(1)} %get-tuple-element.213), channel_id=1, source_target_pairs={{0,2},{1,3},{2,0},{3,1},{4,6},{5,7},{6,4},{7,5},{8,10},{9,11},{10,... | collective-permute-start | bytes 1572872 | tf_op jit(solution)/shard_map/ppermute | solution.py:30
  286.5 4.2 %collective-permute-start.51 = (f32[104,128]{1,0:T(8,128)S(1)}, f32[104,128]{1,0:T(8,128)S(1)}, u32[]{:S(2)}, u32[]{:S(2)}) collective-permute-start(f32[104,128]{1,0:T(8,128)S(1)} %fusion.13), channel_id=1, source_target_pairs={{0,4},{4,0},{8,12},{12,8},{16,20},{20,16},{24,28},{28,24},{1,5},{5... | collective-permute-start | bytes 159752 | tf_op jit(solution)/shard_map/ppermute | solution.py:30
  290.0 35.1 %collective-permute-start.40 = (bf16[512,1024]{1,0:T(8,128)(2,1)S(1)}, bf16[512,1024]{1,0:T(8,128)(2,1)}, u32[]{:S(2)}, u32[]{:S(2)}) collective-permute-start(bf16[512,1024]{1,0:T(8,128)(2,1)S(1)} %copy-done.10), channel_id=1, source_target_pairs={{0,1},{1,0},{2,3},{3,2},{4,5},{5,4},{6,7},{7,6},{8,9},{9,8},{10,11... | collective-permute-start | bytes 3145736 | tf_op jit(solution)/shard_map/ppermute | solution.py:30
  290.7 23.5 %collective-permute-start.46 = (bf16[256,1024]{1,0:T(8,128)(2,1)}, bf16[256,1024]{1,0:T(8,128)(2,1)}, u32[]{:S(2)}, u32[]{:S(2)}) collective-permute-start(bf16[256,1024]{1,0:T(8,128)(2,1)} %get-tuple-element.212), channel_id=1, source_target_pairs={{0,2},{1,3},{2,0},{3,1},{4,6},{5,7},{6,4},{7,5},{8,10},{9,11},{10,... | collective-permute-start | bytes 1572872 | tf_op jit(solution)/shard_map/ppermute | solution.py:30
  291.9 4.2 %collective-permute-start.52 = (f32[104,128]{1,0:T(8,128)S(1)}, f32[104,128]{1,0:T(8,128)S(1)}, u32[]{:S(2)}, u32[]{:S(2)}) collective-permute-start(f32[104,128]{1,0:T(8,128)S(1)} %add.187), channel_id=1, source_target_pairs={{0,8},{4,12},{8,0},{12,4},{16,24},{20,28},{24,16},{28,20},{1,9},{5... | collective-permute-start | bytes 159752 | tf_op jit(solution)/shard_map/ppermute | solution.py:30
  296.1 5.2 %collective-permute-start.53 = (f32[104,128]{1,0:T(8,128)S(1)}, f32[104,128]{1,0:T(8,128)S(1)}, u32[]{:S(2)}, u32[]{:S(2)}) collective-permute-start(f32[104,128]{1,0:T(8,128)S(1)} %add.188), channel_id=1, source_target_pairs={{0,16},{4,20},{8,24},{12,28},{16,0},{20,4},{24,8},{28,12},{1,17},{... | collective-permute-start | bytes 159752 | tf_op jit(solution)/shard_map/ppermute | solution.py:30
  301.4 22.6 %copy-start.29 = (bf16[256,1024]{1,0:T(8,128)(2,1)}, bf16[256,1024]{1,0:T(8,128)(2,1)S(1)}, u32[]{:S(2)}) copy-start(bf16[256,1024]{1,0:T(8,128)(2,1)S(1)} %collective-permute-done.43.refs_2_) | copy-start | bytes 1572868
  301.4 9.7 %collective-permute-start.44 = (bf16[2,128,512]{2,1,0:T(8,128)(2,1)S(1)}, bf16[2,128,512]{2,1,0:T(8,128)(2,1)S(1)}, u32[]{:S(2)}, u32[]{:S(2)}) collective-permute-start(bf16[2,128,512]{2,1,0:T(8,128)(2,1)S(1)} %get-tuple-element.172), channel_id=1, source_target_pairs={{0,8},{4,12},{8,0},{12,4},{16,24},{20,28},{24,16},{28,20},{1,9},{5... | collective-permute-start | bytes 786440 | tf_op jit(solution)/shard_map/ppermute | solution.py:30
  301.6 12.6 %collective-permute-start.45 = (bf16[2,128,512]{2,1,0:T(8,128)(2,1)}, bf16[2,128,512]{2,1,0:T(8,128)(2,1)S(1)}, u32[]{:S(2)}, u32[]{:S(2)}) collective-permute-start(bf16[2,128,512]{2,1,0:T(8,128)(2,1)} %get-tuple-element.173), channel_id=1, source_target_pairs={{0,16},{4,20},{8,24},{12,28},{16,0},{20,4},{24,8},{28,12},{1,17},{... | collective-permute-start | bytes 786440 | tf_op jit(solution)/shard_map/ppermute | solution.py:30
  314.2 5.0 %collective-permute-start.48 = (bf16[1,128,512]{2,1,0:T(8,128)(2,1)S(1)}, bf16[1,128,512]{2,1,0:T(8,128)(2,1)S(1)}, u32[]{:S(2)}, u32[]{:S(2)}) collective-permute-start(bf16[1,128,512]{2,1,0:T(8,128)(2,1)S(1)} %add_convert_fusion.13), channel_id=1, source_target_pairs={{0,4},{4,0},{8,12},{12,8},{16,20},{20,16},{24,28},{28,24},{1,5},{5... | collective-permute-start | bytes 393224 | tf_op jit(solution)/shard_map/ppermute | solution.py:30
  317.4 6.3 %collective-permute-start.47 = (bf16[1,128,512]{2,1,0:T(8,128)(2,1)S(1)}, bf16[1,128,512]{2,1,0:T(8,128)(2,1)S(1)}, u32[]{:S(2)}, u32[]{:S(2)}) collective-permute-start(bf16[1,128,512]{2,1,0:T(8,128)(2,1)S(1)} %add_convert_fusion.14), channel_id=1, source_target_pairs={{0,16},{4,20},{8,24},{12,28},{16,0},{20,4},{24,8},{28,12},{1,17},{... | collective-permute-start | bytes 393224 | tf_op jit(solution)/shard_map/ppermute | solution.py:30
  (36 other events, 276.9 us)
Sparse Core Ops, SparseCore 0:
  56.5 71.5 all-gather.1
  186.4 84.8 reduce-scatter.1
where the time goes:
time: 342 us; the launch traced here: 339 us
  Pallas kernels  128 us (37%)
  waiting for transfers between devices  109 us (32%)
  starting transfers between devices  42.5 us (12%)
  local copies, waits for them, and re-layouts  25.3 us (7%)
  other arithmetic  18 us (5%)
  between operations  15.9 us (5%)
    ppermute x54, waiting for transfers between devices, swapped(): return lax.ppermute(value, axis, [(i, i ^ bit) for i in range(count)])  104 us
    ppermute x54, starting transfers between devices, swapped(): return lax.ppermute(value, axis, [(i, i ^ bit) for i in range(count)])  41.9 us
    pallas_call x2, Pallas kernels, feed(): pl.pallas_call(functools.partial(feed_kernel, here, len(stacks)), grid=(h...  30.2 us
    pallas_call x1, Pallas kernels, attend_back(): pl.pallas_call(functools.partial(attend_back_kernel, heads), out_shape=ja...  23.3 us
    pallas_call x1, Pallas kernels, attend(): pl.pallas_call(functools.partial(attend_kernel, heads), out_shape=(jax.Sh...  17.3 us
    pallas_call x1, Pallas kernels, feed_grads(): pl.pallas_call(feed_grads_kernel, grid=(rows // (2 * TILE),), out_shape=[...  15.4 us
    unnamed x97, local copies, waits for them, and re-layouts  14.9 us
    pallas_call x1, Pallas kernels, qkv_grads(): pl.pallas_call(functools.partial(qkv_grads_kernel, len(unit), len(out_ter...  12.6 us
  transfers between devices with their start and end apart: 56, of which 27 were waited for; matrix products, arithmetic and copies ran while one was open for 8% of the time, Pallas kernels for 33%

commit v1 on v0

--- a/solution.py
+++ b/solution.py
@@ -114,55 +114,64 @@
     return jnp.sum(arrived.astype(F32), axis=0)
 
 
-def attention_tables(length, place, chosen):
-    count = place.shape[0]
-    heads = chosen.shape[0]
-    nblocks = (length + BLOCK - 1) // BLOCK
-    last = nblocks - 1
-    number = jnp.arange(count, dtype=jnp.int32)
-    same = jnp.zeros_like(number)
-    common = jnp.stack([same, same + last, number - 1, number, number + 1], axis=1)
-    middle = (number > 0) & (number < last)
-    good = jnp.stack(
-        [
-            middle | (number > last),
-            middle | (number > last),
-            (number - 1 > 0) & (number - 1 < last) & (number != last),
-            middle,
-            (number + 1 < last) & (number > 0),
-        ],
-        axis=1,
-    )
-    drawn = jnp.transpose(chosen, (1, 2, 0))
-    away = number[:, None, None]
-    fresh = (
-        (drawn > 0)
-        & (drawn < last)
-        & (jnp.abs(drawn - away) > 1)
-        & (away > 0)
-        & (away != last)
-    )
-    first, second, third = drawn[:, 0], drawn[:, 1], drawn[:, 2]
-    fresh = jnp.stack(
-        [
-            fresh[:, 0],
-            fresh[:, 1] & (second != first),
-            fresh[:, 2] & (third != first) & (third != second),
-        ],
-        axis=1,
-    )
-    flags = jnp.concatenate(
-        [jnp.broadcast_to(good[:, :, None], (count, 5, heads)), fresh], axis=1
-    )
-    bias = jnp.where(flags, 0.0, NEGATIVE).astype(F32)
-    bias = jnp.broadcast_to(bias[..., None], (*bias.shape, HEAD_DIM))
-    bias = bias.reshape(count, SLOTS, heads * HEAD_DIM)
-    wanted = jnp.concatenate([common, drawn.reshape(count, -1)], axis=1)
-    hit = wanted[:, :, None] == place[None, None, :]
-    stored = jnp.sum(jnp.where(hit, number[None, None, :], 0), axis=-1).astype(jnp.int32)
-    limits = jnp.clip(length - BLOCK * place, 0, BLOCK).astype(jnp.int32)
-    ends = jnp.stack([last, length - BLOCK * last]).astype(jnp.int32)
-    return stored, limits, ends, bias
+def attention_facts(length, position, placing, chosen):
+    head = jnp.stack([length, position]).astype(jnp.int32)
+    return jnp.concatenate([head, placing.reshape(-1), chosen.reshape(-1)])
+
+
+class Blocks:
+    def __init__(self, facts, stored, limits, heads, quarters):
+        self.facts, self.stored, self.limits = facts, stored, limits
+        self.heads, self.quarters = heads, quarters
+        self.count = stored.shape[0]
+        self.length = facts[0]
+        self.last = (self.length + BLOCK - 1) // BLOCK - 1
+        self.last_rows = self.length - BLOCK * self.last
+
+    def find(self):
+        per = self.count // self.quarters
+        for quarter in range(self.quarters):
+            start = (self.facts[1] ^ quarter) * per
+            for n in range(per):
+                number = self.facts[2 + start + n]
+                self.stored[number] = quarter * per + n
+                rows = self.length - BLOCK * number
+                self.limits[quarter * per + n] = jnp.clip(rows, 0, BLOCK)
+
+    def item(self, number):
+        last = self.last
+        alive = number != last
+        before, behind = number - 1, number + 1
+        common = [0, last, before, number, jnp.minimum(behind, self.count - 1)]
+        good = [
+            alive,
+            alive,
+            alive & (before > 0) & (before < last),
+            alive & (number < last),
+            alive & (behind < last),
+        ]
+        places = [self.stored[block] for block in common]
+        lane = lax.broadcasted_iota(jnp.int32, (1, self.heads * HEAD_DIM), 1)
+        added_scores = [jnp.where(flag, 0.0, NEGATIVE).astype(F32) for flag in good]
+        drawn = [
+            [
+                self.facts[2 + self.count + (h * self.count + number) * 3 + s]
+                for h in range(self.heads)
+            ]
+            for s in range(3)
+        ]
+        random = []
+        for s in range(3):
+            random.append([self.stored[block] for block in drawn[s]])
+            row = jnp.zeros((1, self.heads * HEAD_DIM), F32)
+            for h, block in enumerate(drawn[s]):
+                fresh = alive & (block > 0) & (block < last) & (jnp.abs(block - number) > 1)
+                for other in range(s):
+                    fresh = fresh & (block != drawn[other][h])
+                score = jnp.where(fresh, 0.0, NEGATIVE).astype(F32)
+                row = jnp.where(lane // HEAD_DIM == h, score, row)
+            added_scores.append(row)
+        return places, random, added_scores
 
 
 def block_rows(index):
@@ -188,17 +197,16 @@
     return jnp.concatenate(pieces, axis=1)
 
 
-def gathered_keys(ref, start, stored, number, heads):
+def gathered_keys(ref, start, places, random, heads):
     width = heads * HEAD_DIM
     lane = lax.broadcasted_iota(jnp.int32, (1, PAIR), 1)
-    parts = [ref[block_rows(stored[number, s]), start : start + width] for s in range(5)]
-    for s in range(3):
+    parts = [ref[block_rows(place), start : start + width] for place in places]
+    for drawn in random:
         pieces = []
         for pair in range(heads // 2):
             cols = slice(start + PAIR * pair, start + PAIR * (pair + 1))
-            at = 5 + heads * s + 2 * pair
-            even = ref[block_rows(stored[number, at]), cols]
-            odd = ref[block_rows(stored[number, at + 1]), cols]
+            even = ref[block_rows(drawn[2 * pair]), cols]
+            odd = ref[block_rows(drawn[2 * pair + 1]), cols]
             pieces.append(jnp.where(lane < HEAD_DIM, even, odd))
         parts.append(jnp.concatenate(pieces, axis=1))
     return jnp.concatenate(parts, axis=0)
@@ -210,7 +218,7 @@
 
 def biased(scores, bias, last_rows):
     row = lax.broadcasted_iota(jnp.int32, (BLOCK, 1), 0)
-    parts = [slot(scores, s) + bias[s : s + 1] for s in range(SLOTS)]
+    parts = [slot(scores, s) + bias[s] for s in range(SLOTS)]
     parts[1] = jnp.where(row < last_rows, parts[1], NEGATIVE)
     return parts
 
@@ -219,32 +227,34 @@
     return functools.reduce(jnp.add, parts)
 
 
-def attend_kernel(heads, stored, limits, ends, qkv_ref, bias_ref, out_ref, log_ref, keep_ref):
-    count = bias_ref.shape[0]
+def attend_body(heads, blocks, qkv_ref, out_ref, log_ref, keep_ref):
+    count = blocks.count
+    stored, limits = blocks.stored, blocks.limits
     width = heads * HEAD_DIM
     scale = jnp.asarray(HEAD_DIM**-0.5, BF16)
 
     def item(number):
-        here = block_rows(stored[number, 3])
+        places, random, scores = blocks.item(number)
+        here = block_rows(places[3])
         queries = spread(qkv_ref[here, :width] * scale, heads)
-        keys = gathered_keys(qkv_ref, width, stored, number, heads)
-        parts = biased(matmul(keys, queries, NT), bias_ref[number], ends[1])
+        keys = gathered_keys(qkv_ref, width, places, random, heads)
+        parts = biased(matmul(keys, queries, NT), scores, blocks.last_rows)
         top = jnp.max(functools.reduce(jnp.maximum, parts), axis=0, keepdims=True)
         weights = [jnp.exp(p - top) for p in parts]
         row_total = jnp.sum(total(weights), axis=0, keepdims=True)
         inverse = 1.0 / row_total
         probs = jnp.concatenate([(p * inverse).astype(BF16) for p in weights], axis=0)
-        values = gathered_keys(qkv_ref, 2 * width, stored, number, heads)
+        values = gathered_keys(qkv_ref, 2 * width, places, random, heads)
         out_ref[here, :] = collapse(matmul(probs, values, TN), heads).astype(BF16)
         log_ref[pl.ds(number, 1), :] = top + jnp.log(row_total)
 
     def step(group, carry):
-        for part in range(4):
-            item(1 + group * 4 + part)
+        for part in range(10):
+            item(1 + group * 10 + part)
         return carry
 
-    lax.fori_loop(0, (count - 1) // 4, step, 0)
-    for number in range(1 + (count - 1) // 4 * 4, count):
+    lax.fori_loop(0, (count - 1) // 10, step, 0)
+    for number in range(1 + (count - 1) // 10 * 10, count):
         item(number)
 
     row = lax.broadcasted_iota(jnp.int32, (BLOCK, 1), 0)
@@ -254,8 +264,8 @@
     def chunk_rows(chunk):
         return pl.ds(pl.multiple_of(chunk * CHUNK, CHUNK), CHUNK)
 
-    numbers = [0, ends[0]]
-    rows_of = [block_rows(stored[number, 3]) for number in numbers]
+    numbers = [0, blocks.last]
+    rows_of = [block_rows(stored[number]) for number in numbers]
     queries = [spread(qkv_ref[at, :width] * scale, heads) for at in rows_of]
 
     def scores(chunk, tops):
@@ -302,14 +312,11 @@
         log_ref[pl.ds(numbers[end], 1), :] = tops[end] + jnp.log(totals[end])
 
 
-def attend_back_kernel(
+def attend_back_body(
     heads,
-    stored,
-    limits,
-    ends,
+    blocks,
     qkv_ref,
     grad_ref,
-    bias_ref,
     log_ref,
     out_ref,
     keys_acc,
@@ -317,31 +324,33 @@
     probs_ref,
     inner_ref,
 ):
-    count = bias_ref.shape[0]
+    count = blocks.count
+    stored, limits = blocks.stored, blocks.limits
     width = heads * HEAD_DIM
     scale = jnp.asarray(HEAD_DIM**-0.5, BF16)
     lane = lax.broadcasted_iota(jnp.int32, (1, PAIR), 1)
     keys_acc[...] = jnp.zeros_like(keys_acc)
     values_acc[...] = jnp.zeros_like(values_acc)
 
-    def accumulate(acc, value, number):
+    def accumulate(acc, value, places, random):
         for s in range(5):
-            acc[block_rows(stored[number, s]), :] += slot(value, s)
+            acc[block_rows(places[s]), :] += slot(value, s)
         for s in range(3):
             for h in range(heads):
                 cols = slice(PAIR * (h // 2), PAIR * (h // 2 + 1))
                 mine = (lane < HEAD_DIM) == (h % 2 == 0)
                 term = jnp.where(mine, slot(value, 5 + s)[:, cols], 0.0)
-                acc[block_rows(stored[number, 5 + heads * s + h]), cols] += term
+                acc[block_rows(random[s][h]), cols] += term
 
     def item(number):
-        here = block_rows(stored[number, 3])
+        places, random, scores = blocks.item(number)
+        here = block_rows(places[3])
         queries = spread(qkv_ref[here, :width] * scale, heads)
         grads = spread(grad_ref[here, :], heads)
-        keys = gathered_keys(qkv_ref, width, stored, number, heads)
-        values = gathered_keys(qkv_ref, 2 * width, stored, number, heads)
+        keys = gathered_keys(qkv_ref, width, places, random, heads)
+        values = gathered_keys(qkv_ref, 2 * width, places, random, heads)
         log_total = log_ref[pl.ds(number, 1), :]
-        parts = biased(matmul(keys, queries, NT), bias_ref[number], ends[1])
+        parts = biased(matmul(keys, queries, NT), scores, blocks.last_rows)
         probs = [jnp.exp(p - log_total) for p in parts]
         found = matmul(values, grads, NT)
         found = [slot(found, s) for s in range(SLOTS)]
@@ -351,18 +360,18 @@
             [(p * (d - inner)).astype(BF16) for p, d in zip(probs, found)], axis=0
         )
         probs_low = jnp.concatenate([p.astype(BF16) for p in probs], axis=0)
-        accumulate(values_acc, matmul(probs_low, grads, NN), number)
-        accumulate(keys_acc, matmul(grad_scores, queries, NN), number)
+        accumulate(values_acc, matmul(probs_low, grads, NN), places, random)
+        accumulate(keys_acc, matmul(grad_scores, queries, NN), places, random)
         grad_queries = collapse(matmul(grad_scores, keys, TN), heads) * HEAD_DIM**-0.5
         out_ref[here, :width] = grad_queries.astype(BF16)
 
     def step(group, carry):
-        for part in range(4):
-            item(1 + group * 4 + part)
+        for part in range(6):
+            item(1 + group * 6 + part)
         return carry
 
-    lax.fori_loop(0, (count - 1) // 4, step, 0)
-    for number in range(1 + (count - 1) // 4 * 4, count):
+    lax.fori_loop(0, (count - 1) // 6, step, 0)
+    for number in range(1 + (count - 1) // 6 * 6, count):
         item(number)
 
     row = lax.broadcasted_iota(jnp.int32, (BLOCK, 1), 0)
@@ -372,8 +381,8 @@
     def chunk_rows(chunk):
         return pl.ds(pl.multiple_of(chunk * CHUNK, CHUNK), CHUNK)
 
-    numbers = [0, ends[0]]
-    rows_of = [block_rows(stored[number, 3]) for number in numbers]
+    numbers = [0, blocks.last]
+    rows_of = [block_rows(stored[number]) for number in numbers]
     queries = [spread(qkv_ref[at, :width] * scale, heads) for at in rows_of]
     grads = [spread(grad_ref[at, :], heads) for at in rows_of]
     log_rows = [log_ref[pl.ds(number, 1), :] for number in numbers]
@@ -428,53 +437,216 @@
     return pl.BlockSpec(memory_space=pltpu.VMEM)
 
 
-def attention_cost(qkv, matmuls):
-    rows, width = qkv.shape
-    width //= 3
-    return pl.CostEstimate(
-        flops=2 * matmuls * rows * CHUNK * width,
-        bytes_accessed=12 * rows * width,
-        transcendentals=rows * CHUNK * width // HEAD_DIM,
-    )
-
-
-def attend(qkv, tables, heads):
-    stored, limits, ends, bias = tables
+def project_attend_kernel(heads, parts, owner_a, owner_b, facts, *refs):
+    unit_refs = refs[:parts]
+    first_ref, last_ref, norm_ref, bias_ref = refs[parts : parts + 4]
+    *quarter_refs, kept_ref, weight_out_ref, log_ref = refs[parts + 4 : 2 * parts + 7]
+    qkv_ref, weight_ref, out_ref, keep_ref, stored, limits, sems = refs[2 * parts + 7 :]
+    blocks = Blocks(facts, stored, limits, heads, parts)
+    blocks.find()
+    count, own, split = first_ref.shape
+    near = unit_refs[0].shape[0]
+    rest = weight_ref.shape[1] - split
+    for p in range(count):
+        at = pl.ds(pl.multiple_of(owner_a[p] * own, own), own)
+        weight_ref[at, :split] = first_ref[p]
+        at = pl.ds(pl.multiple_of(owner_b[p] * own, own), own)
+        weight_ref[at, split:] = last_ref[p, :, :rest]
+    copies = [pltpu.make_async_copy(weight_ref, weight_out_ref, sems.at[0])]
+    copies[0].start()
+    for k, ref in enumerate(unit_refs):
+        normed = ref[...].astype(F32) * norm_ref[0:1, :] + norm_ref[1:2, :]
+        found = matmul(normed.astype(BF16), weight_ref[...], NN) + bias_ref[...]
+        qkv_ref[near * k : near * (k + 1), :] = found.astype(BF16)
+    copies.append(pltpu.make_async_copy(qkv_ref, kept_ref, sems.at[1]))
+    copies[1].start()
+    attend_body(heads, blocks, qkv_ref, out_ref, log_ref, keep_ref)
+    for k, ref in enumerate(quarter_refs):
+        part = out_ref.at[near * k : near * (k + 1), :]
+        copies.append(pltpu.make_async_copy(part, ref, sems.at[2 + k]))
+        copies[-1].start()
+    for copy in copies:
+        copy.wait()
+
+
+def in_hbm():
+    return pl.BlockSpec(memory_space=pltpu.HBM)
+
+
+def project_attend(unit, first, last, owner_a, owner_b, norm, bias, facts, heads):
+    rows = sum(value.shape[0] for value in unit)
+    features = unit[0].shape[1]
+    width = heads * HEAD_DIM
+    log_shape = jax.ShapeDtypeStruct((rows // BLOCK, width), F32)
+    quarter = [jax.ShapeDtypeStruct((value.shape[0], width), BF16) for value in unit]
+    qkv = jax.ShapeDtypeStruct((rows, 3 * width), BF16)
+    weight = jax.ShapeDtypeStruct((features, 3 * width), BF16)
+    found = pl.pallas_call(
+        functools.partial(project_attend_kernel, heads, len(unit)),
+        grid=(1,),
+        out_shape=[*quarter, qkv, weight, log_shape],
+        in_specs=[in_smem()] * 3 + [in_vmem()] * (len(unit) + 4),
+        out_specs=[in_hbm()] * (len(unit) + 2)
+        + [pl.BlockSpec(log_shape.shape, lambda i: (0, 0))],
+        scratch_shapes=[
+            pltpu.VMEM(qkv.shape, BF16),
+            pltpu.VMEM(weight.shape, BF16),
+            pltpu.VMEM((rows, width), BF16),
+            pltpu.VMEM((2, rows, width), F32),
+            pltpu.SMEM((rows // BLOCK,), jnp.int32),
+            pltpu.SMEM((rows // BLOCK,), jnp.int32),
+            pltpu.SemaphoreType.DMA((len(unit) + 2,)),
+        ],
+        compiler_params=pltpu.CompilerParams(vmem_limit_bytes=56 << 20),
+        cost_estimate=pl.CostEstimate(
+            flops=20 * rows * CHUNK * width,
+            bytes_accessed=20 * rows * width,
+            transcendentals=rows * CHUNK * width // HEAD_DIM,
+        ),
+        name="project_attend",
+    )(owner_a, owner_b, facts, *unit, first, last, norm, bias)
+    return found[: len(unit)], *found[len(unit) :]
+
+
+def place_kernel(owner, blocks_ref, out_ref):
+    count, own, _ = blocks_ref.shape
+    width = out_ref.shape[1]
+    for p in range(count):
+        at = pl.ds(pl.multiple_of(owner[p] * own, own), own)
+        out_ref[at, :] = blocks_ref[p, :, -width:]
+
+
+def placed_rows(blocks, owner, width):
+    out = jax.ShapeDtypeStruct((blocks.shape[0] * blocks.shape[1], width), blocks.dtype)
+    return pl.pallas_call(
+        place_kernel,
+        grid=(1,),
+        out_shape=out,
+        in_specs=[in_smem(), in_vmem()],
+        out_specs=pl.BlockSpec(out.shape, lambda i: (0, 0)),
+        name="placed_rows",
+    )(owner, blocks)
+
+
+def attend_back_kernel(heads, parts, owner_a, owner_b, facts, *refs):
+    qkv_ref, log_ref, weight_ref = refs[:3]
+    part_refs, unit_refs = refs[3 : 3 + parts], refs[3 + parts : 3 + 2 * parts]
+    outs = refs[3 + 2 * parts :]
+    block_outs, row_outs, late_ref, sum_ref = outs[:4], outs[4 : 4 + parts], *outs[4 + parts :][:2]
+    grads_ref, grad_ref, keys_acc, values_acc, probs_ref, inner_ref = outs[6 + parts :][:6]
+    raw_ref, *block_refs, rows_ref, stored, limits, sems = outs[12 + parts :]
+    blocks = Blocks(facts, stored, limits, heads, parts)
+    blocks.find()
+    half, own, split = block_refs[0].shape
+    width = weight_ref.shape[1]
+    near = unit_refs[0].shape[0]
+    step = 2 * TILE
+    for k, ref in enumerate(part_refs):
+        grads_ref[near * k : near * (k + 1), :] = ref[...]
+    attend_back_body(
+        heads,
+        blocks,
+        qkv_ref,
+        grads_ref,
+        log_ref,
+        grad_ref,
+        keys_acc,
+        values_acc,
+        probs_ref,
+        inner_ref,
+    )
+    copies = []
+
+    def leave(source, target):
+        copies.append(pltpu.make_async_copy(source, target, sems.at[len(copies)]))
+        copies[-1].start()
+
+    sums = jnp.sum(grad_ref[...].astype(F32), axis=0, keepdims=True)
+    sum_ref[...] = sums
+    for i in range(weight_ref.shape[0] // step):
+        at = slice(step * i, step * (i + 1))
+        raw = total(
+            [
+                matmul(ref[:, at], grad_ref[near * k : near * (k + 1), :], TN)
+                for k, ref in enumerate(unit_refs)
+            ]
+        )
+        weight = weight_ref[at, :].astype(F32)
+        raw_ref[at, :] = raw.astype(BF16)
+        for row, value in enumerate((raw * weight, weight * sums)):
+            lanes = total([value[:, 128 * c : 128 * (c + 1)] for c in range(width // 128)])
+            for b in range(step // 128):
+                turned = lanes[128 * b : 128 * (b + 1)].T
+                found = jnp.sum(turned, axis=0, keepdims=True)
+                start = step * i + 128 * b
+                late_ref[row : row + 1, start : start + 128] = found
+    for p in range(2 * half):
+        at = pl.ds(pl.multiple_of(owner_a[p] * own, own), own)
+        block_refs[p // half][p % half] = raw_ref[at, :split]
+        at = pl.ds(pl.multiple_of(owner_b[p] * own, own), own)
+        block_refs[2 + p // half][p % half] = raw_ref[at, split:]
+    for source, target in zip(block_refs, block_outs):
+        leave(source, target)
+    for k in range(parts - 1, -1, -1):
+        at = slice(near * k, near * (k + 1))
+        rows_ref[at, :] = matmul(grad_ref[at, :], weight_ref[...], NT).astype(BF16)
+        leave(rows_ref.at[at, :], row_outs[k])
+    for copy in copies:
+        copy.wait()
+
+
+def attend_back(
+    qkv, grad_context, log_totals, unit, weight, owner_a, owner_b, split, facts, heads
+):
     rows, width = qkv.shape[0], heads * HEAD_DIM
+    features = weight.shape[0]
+    count = owner_a.shape[0]
+    own = features // count
+    first = jax.ShapeDtypeStruct((count // 2, own, split), BF16)
+    last = jax.ShapeDtypeStruct((count // 2, own, 3 * width - split), BF16)
+    small = [
+        jax.ShapeDtypeStruct((2, features), F32),
+        jax.ShapeDtypeStruct((1, 3 * width), F32),
+    ]
+    blocks = [first, first, last, last]
     return pl.pallas_call(
-        functools.partial(attend_kernel, heads),
-        out_shape=(
-            jax.ShapeDtypeStruct((rows, width), BF16),
-            jax.ShapeDtypeStruct((rows // BLOCK, width), F32),
+        functools.partial(attend_back_kernel, heads, len(unit)),
+        grid=(1,),
+        out_shape=[*blocks, *[like(value) for value in unit], *small],
+        in_specs=[in_smem()] * 3 + [in_vmem()] * (3 + 2 * len(unit)),
+        out_specs=[in_hbm()] * (4 + len(unit))
+        + [pl.BlockSpec(value.shape, lambda i: (0, 0)) for value in small],
+        scratch_shapes=[
+            pltpu.VMEM((rows, width), BF16),
+            pltpu.VMEM(qkv.shape, BF16),
+            pltpu.VMEM((rows, width), F32),
+            pltpu.VMEM((rows, width), F32),
+            pltpu.VMEM((2, rows, width), F32),
+            pltpu.VMEM((2, rows, width), F32),
+            pltpu.VMEM(weight.shape, BF16),
+            *[pltpu.VMEM(value.shape, BF16) for value in blocks],
+            pltpu.VMEM((rows, features), BF16),
+            pltpu.SMEM((rows // BLOCK,), jnp.int32),
+            pltpu.SMEM((rows // BLOCK,), jnp.int32),
+            pltpu.SemaphoreType.DMA((4 + len(unit),)),
+        ],
+        compiler_params=pltpu.CompilerParams(vmem_limit_bytes=53 << 20),
+        cost_estimate=pl.CostEstimate(
+            flops=40 * rows * CHUNK * width,
+            bytes_accessed=40 * rows * width,
+            transcendentals=rows * CHUNK * width // HEAD_DIM,
         ),
-        grid=(1,),
-        in_specs=[in_smem()] * 3 + [in_vmem()] * 2,
-        out_specs=(
-            pl.BlockSpec((rows, width), lambda i: (0, 0)),
-            pl.BlockSpec((rows // BLOCK, width), lambda i: (0, 0)),
-        ),
-        scratch_shapes=[pltpu.VMEM((2, rows, width), F32)],
-        compiler_params=pltpu.CompilerParams(vmem_limit_bytes=32 << 20),
-        cost_estimate=attention_cost(qkv, 8),
-        name="attend",
-    )(stored, limits, ends, qkv, bias)
-
-
-def attend_back(qkv, grad_context, log_totals, tables, heads):
-    stored, limits, ends, bias = tables
-    rows, width = qkv.shape[0], heads * HEAD_DIM
-    return pl.pallas_call(
-        functools.partial(attend_back_kernel, heads),
-        out_shape=jax.ShapeDtypeStruct(qkv.shape, BF16),
-        grid=(1,),
-        in_specs=[in_smem()] * 3 + [in_vmem()] * 4,
-        out_specs=pl.BlockSpec(qkv.shape, lambda i: (0, 0)),
-        scratch_shapes=[pltpu.VMEM((rows, width), F32)] * 2
-        + [pltpu.VMEM((2, rows, width), F32)] * 2,
-        compiler_params=pltpu.CompilerParams(vmem_limit_bytes=32 << 20),
-        cost_estimate=attention_cost(qkv, 16),
         name="attend_back",
-    )(stored, limits, ends, qkv, grad_context, bias, log_totals)
+    )(
+        owner_a,
+        owner_b,
+        facts,
+        qkv,
+        log_totals,
+        weight,
+        *grad_context,
+        *unit,
+    )
 
 
 TILE = 256
@@ -536,14 +708,13 @@
     here = len(normed)
     tiles = rows // TILE
     stacked = [jax.ShapeDtypeStruct((rows * quarters, n), BF16) for n in (features, units) * 2]
-    once = pl.BlockSpec(weights.shape, lambda i: (0, 0), pipeline_mode=pl.Buffered(1))
     found = pl.pallas_call(
         functools.partial(feed_kernel, here, len(stacks)),
         grid=(here * tiles,),
         out_shape=[like(value) for value in normed] * 2 + stacked,
         in_specs=tile_specs(normed)
         + tile_specs(grads)
-        + [once, whole_spec(bias)]
+        + [in_vmem(), whole_spec(bias)]
         + [pl.BlockSpec(memory_space=pl.ANY)] * len(stacks),
         out_specs=tile_specs(normed) * 2
         + [
@@ -551,7 +722,7 @@
             for value in stacked
         ],
         input_output_aliases={2 * here + 2 + n: 2 * here + n for n in range(len(stacks))},
-        compiler_params=limit(62),
+        compiler_params=limit(56),
         cost_estimate=pl.CostEstimate(
             flops=8 * here * rows * features * units,
             bytes_accessed=16 * here * rows * features + 4 * features * units,
@@ -650,61 +821,13 @@
     )(rows)
 
 
-def project_kernel(parts, owner_a, owner_b, *refs):
-    unit_refs = refs[:parts]
-    first_ref, last_ref, norm_ref, bias_ref, qkv_ref, weight_ref, out_ref = refs[parts:]
-    count, own, split = first_ref.shape
-    near = unit_refs[0].shape[0]
-    rest = weight_ref.shape[1] - split
-
-    @pl.when(pl.program_id(0) == 0)
-    def _():
-        for p in range(count):
-            at = pl.ds(pl.multiple_of(owner_a[p] * own, own), own)
-            weight_ref[at, :split] = first_ref[p]
-            at = pl.ds(pl.multiple_of(owner_b[p] * own, own), own)
-            weight_ref[at, split:] = last_ref[p, :, :rest]
-            out_ref[at, :] = last_ref[p, :, rest:]
-
-    for k, ref in enumerate(unit_refs):
-
-        @pl.when(pl.program_id(0) == k)
-        def _(ref=ref):
-            def tile(i, carry):
-                at = pl.ds(pl.multiple_of(i * TILE, TILE), TILE)
-                normed = ref[at, :].astype(F32) * norm_ref[0:1, :] + norm_ref[1:2, :]
-                found = matmul(normed.astype(BF16), weight_ref[...], NN) + bias_ref[...]
-                qkv_ref[at, :] = found.astype(BF16)
-                return carry
-
-            lax.fori_loop(0, near // TILE, tile, 0)
-
-
-def project(unit, first, last, owner_a, owner_b, norm, bias):
-    rows = sum(value.shape[0] for value in unit)
-    features, width = unit[0].shape[1], bias.shape[1]
-    more = first.shape[2] + last.shape[2] - width
-    qkv = jax.ShapeDtypeStruct((rows, width), BF16)
-    weights = [jax.ShapeDtypeStruct((features, n), BF16) for n in (width, more)]
-    return pl.pallas_call(
-        functools.partial(project_kernel, len(unit)),
-        grid=(len(unit),),
-        out_shape=[qkv, *weights],
-        in_specs=[in_smem()] * 2 + [in_vmem()] * (len(unit) + 4),
-        out_specs=[tiled_spec(qkv, rows // len(unit))] + [whole_spec(value) for value in weights],
-        compiler_params=limit(32),
-        cost_estimate=cost(2 * rows * features * width, 2 * rows * (features + width)),
-        name="project",
-    )(owner_a, owner_b, *unit, first, last, norm, bias)
-
-
 def middle_kernel(parts, *refs):
     context_refs, out_refs = refs[:parts], refs[parts : 2 * parts]
     rows_ref, vector_ref, middle_ref, normed_ref = refs[2 * parts :]
     middle = rows_ref[...].astype(F32) + vector_ref[0:1, :]
     for context_ref, out_ref in zip(context_refs, out_refs):
         middle += matmul(context_ref[...], out_ref[...], NT)
-    middle_ref[...] = middle
+    middle_ref[...] = middle.astype(BF16)
     unit = norm_parts(middle)[0]
     normed_ref[...] = (unit * vector_ref[1:2, :] + vector_ref[2:3, :]).astype(BF16)
 
@@ -713,7 +836,7 @@
     return pl.pallas_call(
         functools.partial(middle_kernel, len(context)),
         grid=(rows.shape[0] // TILE,),
-        out_shape=[like(rows, F32), like(rows)],
+        out_shape=[like(rows), like(rows)],
         in_specs=[tiled_spec(value) for value in context]
         + [whole_spec(value) for value in out_parts]
         + [tiled_spec(rows), whole_spec(vectors)],
@@ -737,11 +860,11 @@
     last = pl.program_id(0) == pl.num_programs(0) - 1
     count, own, width = block_refs[0].shape
     grad_normed = total([ref[...].astype(F32) for ref in term_refs])
-    unit, inverse = norm_parts(middle_ref[...])
+    unit, inverse = norm_parts(middle_ref[...].astype(F32))
     cotangent = cotangent_ref[...].astype(F32)
     grad = cotangent + norm_back(grad_normed, unit, inverse, vector_ref[1:2, :])
-    grad_ref[...] = grad
     low = grad.astype(BF16)
+    grad_ref[...] = low
     for head_ref, out_ref in zip(head_refs, out_refs):
         head_ref[...] = matmul(low, out_ref[...], NN).astype(BF16)
     sums = [
@@ -795,81 +918,6 @@
     return found[0], found[1], found[2 : 2 + parts], found[2 + parts :]
 
 
-def qkv_grads_kernel(parts, terms, owner_a, owner_b, *refs):
-    unit_refs, term_refs = refs[:parts], refs[parts : parts + terms]
-    grad_ref, weight_ref, *block_refs, late_ref, sum_ref = refs[parts + terms : parts + terms + 8]
-    *row_refs, raw_ref = refs[parts + terms + 8 :]
-    half, own, split = block_refs[0].shape
-    width = weight_ref.shape[1]
-    rest = width - split
-    near = unit_refs[0].shape[0]
-    step = 256
-    sums = jnp.sum(grad_ref[...].astype(F32), axis=0, keepdims=True)
-    sum_ref[...] = sums
-    for i in range(weight_ref.shape[0] // step):
-        at = slice(step * i, step * (i + 1))
-        raw = total(
-            [
-                matmul(ref[:, at], grad_ref[near * k : near * (k + 1), :], TN)
-                for k, ref in enumerate(unit_refs)
-            ]
-        )
-        weight = weight_ref[at, :].astype(F32)
-        raw_ref[at, :] = raw.astype(BF16)
-        for row, value in enumerate((raw * weight, weight * sums)):
-            lanes = total([value[:, 128 * c : 128 * (c + 1)] for c in range(width // 128)])
-            for b in range(step // 128):
-                turned = lanes[128 * b : 128 * (b + 1)].T
-                found = jnp.sum(turned, axis=0, keepdims=True)
-                start = step * i + 128 * b
-                late_ref[row : row + 1, start : start + 128] = found
-    for p in range(2 * half):
-        first_ref, last_ref = block_refs[p // half], block_refs[2 + p // half]
-        at = pl.ds(pl.multiple_of(owner_a[p] * own, own), own)
-        first_ref[p % half] = raw_ref[at, :split]
-        at = pl.ds(pl.multiple_of(owner_b[p] * own, own), own)
-        last_ref[p % half, :, :rest] = raw_ref[at, split:]
-        found = total([ref[p].astype(F32) for ref in term_refs])
-        last_ref[p % half, :, rest:] = found.astype(BF16)
-    for k, ref in enumerate(row_refs):
-
-        def tile(i, carry, k=k, ref=ref):
-            at = pl.ds(pl.multiple_of(i * TILE + k * near, TILE), TILE)
-            to = pl.ds(pl.multiple_of(i * TILE, TILE), TILE)
-            ref[to, :] = matmul(grad_ref[at, :], weight_ref[...], NT).astype(BF16)
-            return carry
-
-        lax.fori_loop(0, near // TILE, tile, 0)
-
-
-def qkv_grads(unit, out_terms, grad_qkv, weight, owner_a, owner_b, split):
-    features, width = weight.shape
-    count, own, more = out_terms[0].shape
-    first = jax.ShapeDtypeStruct((count // 2, own, split), BF16)
-    last = jax.ShapeDtypeStruct((count // 2, own, width - split + more), BF16)
-    return pl.pallas_call(
-        functools.partial(qkv_grads_kernel, len(unit), len(out_terms)),
-        grid=(1,),
-        out_shape=[
-            first,
-            first,
-            last,
-            last,
-            jax.ShapeDtypeStruct((2, features), F32),
-            jax.ShapeDtypeStruct((1, width), F32),
-        ]
-        + [like(value) for value in unit],
-        in_specs=[in_smem()] * 2 + [in_vmem()] * (len(unit) + len(out_terms) + 2),
-        out_specs=[whole_spec(value) for value in (first, first, last, last)]
-        + [pl.BlockSpec((2, features), lambda i: (0, 0)), pl.BlockSpec((1, width), lambda i: (0, 0))]
-        + [whole_spec(value) for value in unit],
-        scratch_shapes=[pltpu.VMEM((features, width), BF16)],
-        compiler_params=limit(32),
-        cost_estimate=cost(4 * grad_qkv.size * features, 4 * grad_qkv.size + 8 * weight.size),
-        name="qkv_grads",
-    )(owner_a, owner_b, *unit, *out_terms, grad_qkv, weight)
-
-
 def input_back_kernel(terms, *refs):
     *term_refs, first_ref, last_ref = refs[:terms]
     rows_ref, middle_ref, vector_ref, out_ref = refs[terms:]
@@ -877,7 +925,7 @@
     grad_normed = total([ref[...].astype(F32) for ref in term_refs]) + half.astype(F32)
     unit, inverse = norm_parts(rows_ref[...].astype(F32))
     grad = norm_back(grad_normed, unit, inverse, vector_ref[0:1, :])
-    out_ref[...] = (middle_ref[...] + grad).astype(BF16)
+    out_ref[...] = (middle_ref[...].astype(F32) + grad).astype(BF16)
 
 
 def input_back(terms, rows, grad_middle, vectors):
@@ -923,9 +971,6 @@
     piece = vectors.shape[1]
     unit_piece = hidden_bias.shape[1]
 
-    def quarters(value):
-        return [value[k * near : (k + 1) * near] for k in range(ways)]
-
     small = jnp.zeros((8, features), F32)
     small = lax.dynamic_update_slice(small, vectors, (0, index * piece))
     small_hidden = jnp.zeros((1, units * ways), F32)
@@ -936,6 +981,8 @@
     unit_near = unit_rows(tokens)
     unit_near, packed = together(unit_near, packed)
     unit_far = far(unit_near, "tensor")
+
+    facts = attention_facts(lengths[0], position, block_place, random_blocks)
 
     bits = bits_of("dp")
     order_a = bits[::-1]
@@ -949,12 +996,13 @@
     last_blocks = doubled(last_flat, "dp", order_b)
     packed = summed_everywhere(packed, ("dp",))
     feed_flat = jnp.concatenate([up_weight, down_weight], axis=1)
-    cotangent_near, unit_far = together(output_cotangent, unit_far)
-    feed_flat, first_blocks, last_blocks, _here, packed = together(
-        feed_flat, first_blocks, last_blocks, unit_far, packed
+    first_going, last_going = output_cotangent[: near // 2], output_cotangent[near // 2 :]
+    first_going, unit_far = together(first_going, unit_far)
+    cotangent_first = far(first_going, "tensor")
+    feed_flat, first_blocks, last_blocks, cotangent_first, packed = together(
+        feed_flat, first_blocks, last_blocks, cotangent_first, packed
     )
     feed_full = lax.all_gather(feed_flat, "dp", axis=0, tiled=True)
-    cotangent_far = far(cotangent_near, "tensor")
     unit_parts = gathered_parts(unit_near, unit_far, "tensor")
 
     vectors_full = packed[: 8 * features].reshape(8, features)
@@ -966,22 +1014,29 @@
     norm_one = vectors_full[:2]
     norm_two = jnp.stack([vectors_full[4], vectors_full[2], vectors_full[3]])
 
-    placed = block_place[0].reshape(ways, -1)
-    order = position ^ jnp.arange(ways, dtype=jnp.int32)
-    chosen_rows = order[:, None, None] == jnp.arange(ways, dtype=jnp.int32)[None, :, None]
-    place = jnp.sum(jnp.where(chosen_rows, placed[None], 0), axis=1).reshape(-1)
-    tables = attention_tables(lengths[0], place, random_blocks[0])
-
-    qkv, qkv_full, out_group = project(
-        unit_parts, first_blocks, last_blocks, owner_a, owner_b, norm_one, bias_qkv
-    )
-    context, log_totals = attend(qkv, tables, heads)
+
+    out_group = placed_rows(last_blocks, owner_b, width)
     out_far = far(out_group, "tensor")
-    context, out_far, cotangent_far = together(context, out_far, cotangent_far)
+    last_going, out_group = together(last_going, out_group)
+    cotangent_last = far(last_going, "tensor")
+    *context, qkv, qkv_full, log_totals = project_attend(
+        unit_parts,
+        first_blocks,
+        last_blocks,
+        owner_a,
+        owner_b,
+        norm_one,
+        bias_qkv,
+        facts,
+        heads,
+    )
+    context = context[0]
+    *context, out_far, cotangent_last = together(*context, out_far, cotangent_last)
+    cotangent_far = jnp.concatenate([cotangent_first, cotangent_last], axis=0)
     grad_parts = gathered_parts(output_cotangent, cotangent_far, "tensor")
 
     out_parts = gathered_parts(out_group, out_far, "tensor")
-    context_near = exchanged_parts(quarters(context), "tensor")
+    context_near = exchanged_parts(context, "tensor")
     middle, normed_two = middle_rows(context_near, out_parts, tokens, norm_two)
 
     half = ways // 2
@@ -999,29 +1054,46 @@
     back_terms, far_sum = summed_halves(back_parts, "tensor")
     back_terms.append(far(far_sum, "tensor"))
     feed_sums, sum_hidden = feed_grads(stacks)
+    feed_terms, feed_far = summed_halves(feed_parts, "tensor")
+    early, late_rows = feed_far[: near // 2], feed_far[near // 2 :]
+    *back_terms, feed_sums, early = together(*back_terms, feed_sums, early)
+    early = far(early, "tensor")
     feed_weight_grads = lax.psum_scatter(feed_sums, "dp", scatter_dimension=0, tiled=True)
     feed_weight_grads = feed_weight_grads.astype(F32)
-    *back_terms, sum_hidden = together(*back_terms, sum_hidden)
 
     grad_middle, sums_two, grad_heads, out_blocks = middle_back(
         back_terms, out_parts, context_near, middle, output_cotangent, norm_two, owner_b
     )
-    grad_heads = exchanged_parts(grad_heads, "tensor")
-    grad_context = jnp.concatenate(grad_heads, axis=0)
-
+    grad_context = exchanged_parts(grad_heads, "tensor")
+
+    *out_blocks, early = together(*out_blocks, early)
     out_terms, out_far = summed_halves(out_blocks, "tensor")
-    feed_terms, feed_far = summed_halves(feed_parts, "tensor")
-    early, late_rows = feed_far[: near // 2], feed_far[near // 2 :]
-    grad_context, out_far, early = together(grad_context, out_far, early)
+    *grad_context, out_far, late_rows = together(*grad_context, out_far, late_rows)
     out_terms.append(far(out_far, "tensor"))
-    early = far(early, "tensor")
-    grad_qkv = attend_back(qkv, grad_context, log_totals, tables, heads)
-    grad_qkv, early, late_rows, *out_terms = together(grad_qkv, early, late_rows, *out_terms)
     late_rows = far(late_rows, "tensor")
-    first_keep, first_send, last_keep, last_send, late, sum_qkv, *back_parts = qkv_grads(
-        unit_parts, out_terms, grad_qkv, qkv_full, owner_a, owner_b, split
-    )
+    first_keep, first_send, last_keep, last_send, *back_parts, late, sum_qkv = attend_back(
+        qkv,
+        grad_context,
+        log_totals,
+        unit_parts,
+        qkv_full,
+        owner_a,
+        owner_b,
+        split,
+        facts,
+        heads,
+    )
+    first_send, last_send, late, late_rows, *rest = together(
+        first_send, last_send, late, late_rows, *out_terms, *back_parts
+    )
+    out_terms, back_parts = rest[: len(out_terms)], rest[len(out_terms) :]
     near_rows, far_rows = back_parts[:half], back_parts[half:]
+    feed_terms.append(jnp.concatenate([early, late_rows], axis=0))
+    output = total([term.astype(F32) for term in (*feed_terms, middle)]) + vectors_full[5]
+    output = output.astype(BF16)
+    out_sums = total([term.astype(F32) for term in out_terms]).astype(BF16)
+    last_keep = jnp.concatenate([last_keep, out_sums[: spread_ways // 2]], axis=2)
+    last_send = jnp.concatenate([last_send, out_sums[spread_ways // 2 :]], axis=2)
     head_sums = lax.dynamic_update_slice(
         jnp.zeros((3, features), F32), sum_qkv.reshape(3, width), (0, position * width)
     )
@@ -1031,6 +1103,7 @@
     packed = jnp.concatenate(
         [late.reshape(-1), sums_two.reshape(-1), head_sums.reshape(-1), hidden_sums.reshape(-1)]
     )
+    packed = summed_everywhere(packed, ("tensor",))
     far_sum = added(far_rows[0], swapped(far_rows[1], "tensor", 1))
     packed, far_sum, first_keep, last_keep, *near_rows = together(
         packed, far_sum, first_keep, last_keep, *near_rows
@@ -1043,18 +1116,18 @@
     while first_send.shape[0] > 1:
         first_keep, first_send = halved(first_keep, first_send, "dp", order_a)
         last_keep, last_send = halved(last_keep, last_send, "dp", order_b)
-    first_send, last_send, far_last = together(first_send, last_send, far_last)
+    first_send, last_send, far_last, feed_weight_grads, output = together(
+        first_send, last_send, far_last, feed_weight_grads, output
+    )
     near_terms = [near_rows[0], swapped(near_rows[1], "tensor", 1), far_first, far_last]
+    input_grad = input_back(near_terms, tokens, grad_middle, norm_one)
+    first_keep, last_keep, input_grad = together(first_keep, last_keep, input_grad)
     first_raw = halved(first_keep, first_send, "dp", order_a)[0][0].astype(F32)
     last_raw = halved(last_keep, last_send, "dp", order_b)[0][0].astype(F32)
     out_weight_grad = last_raw[:, width:]
     last_raw = last_raw[:, :width]
-    input_grad = input_back(near_terms, tokens, grad_middle, norm_one)
-    feed_terms.append(jnp.concatenate([early, late_rows], axis=0))
-    output = total([term.astype(F32) for term in feed_terms]) + middle + vectors_full[5]
-    output = output.astype(BF16)
-
-    packed = summed_everywhere(packed, ("tensor", "dp"))
+
+    packed = summed_everywhere(packed, ("dp",))
     by_feature = packed[: 9 * features].reshape(9, features)
     hidden_sums = packed[9 * features :]
     vectors_grad = lax.dynamic_slice_in_dim(by_feature, index * piece, piece, axis=1)

time: 342 us -> 341 us (level)
  waiting for transfers between devices: 109 us -> 99.7 us
  starting transfers between devices: 42.5 us -> 49.4 us
  local copies, waits for them, and re-layouts: 25.3 us -> 19.3 us
  other arithmetic: 18 us -> 22.8 us
    ppermute x54 -> x55, waiting for transfers between devices: 104 us -> 82.8 us  [swapped(): return lax.ppermute(value, axis, [(i, i ^ bit) for i in range(count)])]
    all_gather x1, waiting for transfers between devices: 4.76 us -> 16.9 us  [per_device(): feed_full = lax.all_gather(feed_flat, 'dp', axis=0, tiled=True)]
    ppermute x54 -> x55, starting transfers between devices: 41.9 us -> 49.3 us  [swapped(): return lax.ppermute(value, axis, [(i, i ^ bit) for i in range(count)])]
    unnamed x97 -> x67, local copies, waits for them, and re-layouts: 14.9 us -> 7.67 us
    pallas_call x4 -> x3, Pallas kernels: 60.1 us -> 60.5 us  [the longest x1 36.9 us: attend_back(): pl.pallas_call(functools.partial(attend_back_kernel, heads, len(unit)), g...]
  transfers between devices with their start and end apart: 56 -> 57, of which waited for: 27 -> 23; matrix products, arithmetic and copies ran while one was open for 8% -> 10% of each run, Pallas kernels for 33% -> 34%
where the time goes in v1:
time: 341 us; the launch traced here: 335 us
  Pallas kernels  128 us (38%)
  waiting for transfers between devices  99.7 us (29%)
  starting transfers between devices  49.4 us (14%)
  other arithmetic  22.8 us (7%)
  local copies, waits for them, and re-layouts  19.3 us (6%)
  between operations  15.6 us (5%)
    ppermute x55, waiting for transfers between devices, swapped(): return lax.ppermute(value, axis, [(i, i ^ bit) for i in range(count)])  82.8 us
    ppermute x55, starting transfers between devices, swapped(): return lax.ppermute(value, axis, [(i, i ^ bit) for i in range(count)])  49.3 us
    pallas_call x1, Pallas kernels, attend_back(): pl.pallas_call(functools.partial(attend_back_kernel, heads, len(unit)), g...  36.9 us
    pallas_call x2, Pallas kernels, feed(): pl.pallas_call(functools.partial(feed_kernel, here, len(stacks)), grid=(h...  29.9 us
    pallas_call x1, Pallas kernels, project_attend(): pl.pallas_call(functools.partial(project_attend_kernel, heads, len(unit))...  21.5 us
    all_gather x1, waiting for transfers between devices, per_device(): feed_full = lax.all_gather(feed_flat, 'dp', axis=0, tiled=True)  16.9 us
    pallas_call x1, Pallas kernels, feed_grads(): pl.pallas_call(feed_grads_kernel, grid=(rows // (2 * TILE),), out_shape=[...  15.8 us
    pallas_call x1, Pallas kernels, middle_back(): pl.pallas_call(functools.partial(middle_back_kernel, len(terms), parts),...  9.88 us
  transfers between devices with their start and end apart: 57, of which 23 were waited for; matrix products, arithmetic and copies ran while one was open for 10% of the time, Pallas kernels for 34%

profile of v1, /device:TPU:0, one launch (start us, length us, event | category | flops | bytes accessed | tf_op | source)
XLA Modules:
  0.0 334.9 jit_solution(11727009050992170845)
XLA Ops:
  9.5 1.1 copy.28
  10.8 3.6 %collective-permute-start.5 = (bf16[1,128,512]{2,1,0:T(8,128)(2,1)S(1)}, bf16[1,128,512]{2,1,0:T(8,128)(2,1)S(1)}, u32[]{:S(2)}, u32[]{:S(2)}) collective-permute-start(bf16[1,128,512]{2,1,0:T(8,128)(2,1)S(1)} %bitcast.73), channel_id=1, source_target_pairs={{0,16},{4,20},{8,24},{12,28},{16,0},{20,4},{24,8},{28,12},{1,17},{... | collective-permute-start | bytes 393224 | tf_op jit(solution)/shard_map/ppermute | solution.py:30
  15.3 1.6 collective-permute-start.8
  16.9 1.7 collective-permute-start.1
  19.6 2.5 unit.1.refs_0_.refs_7_
  22.7 1.8 pad_maximum_fusion.2
  25.1 1.6 collective-permute-start.6
  26.7 1.9 collective-permute-done.12
  28.6 1.6 collective-permute-start.13
  30.7 4.0 %collective-permute-done.13 = f32[96,128]{1,0:T(8,128)S(1)} collective-permute-done((f32[96,128]{1,0:T(8,128)S(1)}, f32[96,128]{1,0:T(8,128)S(1)}, u32[]{:S(2)}, u32[]{:S(2)}) %collective-permute-start.13) | collective-permute-done | bytes 49184 | tf_op jit(solution)/shard_map/ppermute | solution.py:30
  34.7 2.9 collective-permute-start.14
  37.6 2.6 collective-permute-start.7
  40.2 4.6 %collective-permute-done.9 = bf16[2,128,512]{2,1,0:T(8,128)(2,1)S(1)} collective-permute-done((bf16[2,128,512]{2,1,0:T(8,128)(2,1)S(1)}, bf16[2,128,512]{2,1,0:T(8,128)(2,1)S(1)}, u32[]{:S(2)}, u32[]{:S(2)}) %collective-permute-start.9) | collective-permute-done | bytes 262176 | tf_op jit(solution)/shard_map/ppermute | solution.py:30
  44.9 2.2 collective-permute-done.3.refs_2_.refs_9_
  48.9 1.1 pad_maximum_fusion.refs_4_
  50.0 7.0 %collective-permute-done.10 = bf16[4,128,512]{2,1,0:T(8,128)(2,1)S(1)} collective-permute-done((bf16[4,128,512]{2,1,0:T(8,128)(2,1)S(1)}, bf16[4,128,512]{2,1,0:T(8,128)(2,1)S(1)}, u32[]{:S(2)}, u32[]{:S(2)}) %collective-permute-start.10) | collective-permute-done | bytes 524320 | tf_op jit(solution)/shard_map/ppermute | solution.py:30
  57.0 1.1 pad_maximum_fusion.1.refs_5_.blocks_ref
  58.1 2.0 collective-permute-done.11
  63.6 2.1 placed_rows.1.refs_4_.refs_3_
  66.0 1.8 collective-permute-start.16
  69.0 21.5 %project_attend.1 = (bf16[512,256]{1,0:T(8,128)(2,1)}, bf16[512,256]{1,0:T(8,128)(2,1)}, bf16[512,256]{1,0:T(8,128)(2,1)}, bf16[512,256]{1,0:T(8,128)(2,1)}, bf1...) custom-call(s32[8]{0:T(128)} %broadcast_xor_fusion.1.owner_a, ...), custom_call_target="tpu_custom_call" | custom-call | flops 5368709120 | bytes 10485760 | tf_op jit(solution)/shard_map/project_attend/pallas_call | solution.py:484
  94.5 6.7 %collective-permute-done.18.refs_2_.refs_9_ = bf16[512,256]{1,0:T(8,128)(2,1)} collective-permute-done((bf16[512,256]{1,0:T(8,128)(2,1)}, bf16[512,256]{1,0:T(8,128)(2,1)}, u32[]{:S(2)}, u32[]{:S(2)}) %collective-permute-start.18) | collective-permute-done | bytes 262176 | tf_op jit(solution)/shard_map/ppermute | solution.py:30
  101.2 3.7 %collective-permute-done.19.refs_3_.refs_10_ = bf16[512,256]{1,0:T(8,128)(2,1)} collective-permute-done((bf16[512,256]{1,0:T(8,128)(2,1)}, bf16[512,256]{1,0:T(8,128)(2,1)}, u32[]{:S(2)}, u32[]{:S(2)}) %collective-permute-start.19) | collective-permute-done | bytes 262176 | tf_op jit(solution)/shard_map/ppermute | solution.py:30
  104.9 5.0 %middle.1 = (bf16[512,1024]{1,0:T(8,128)(2,1)}, bf16[512,1024]{1,0:T(8,128)(2,1)}) custom-call(bf16[512,256]{1,0:T(8,128)(2,1)} %get-tuple-element.136.refs_0_.refs_7_, bf16[512,256]{1,0:T(8,128)(2,1)} %copy-done.11, bf16[512,256]{1,0:T(8,128)(2,1)} %collective-permute-done.18.refs_2_.refs_9_, bf16[512,256]{1,0:T(8,128)(2,1)} %collective-permute-done.19.refs_3_.refs_10_, ...), custom_call_target="tpu_custom_call" | custom-call | flops 1073741824 | bytes 6291456 | tf_op jit(solution)/shard_map/middle/pallas_call | solution.py:836
  111.8 1.1 constant_dynamic-update-slice_fusion.1
  112.9 1.1 constant_dynamic-update-slice_fusion.refs_2_
  114.1 16.9 %all-gather.2.cloned.1.call-done.refs_4_ = bf16[1024,2048]{1,0:T(8,128)(2,1)} async-done(((bf16[128,2048]{1,0:T(8,128)(2,1)}), bf16[1024,2048]{1,0:T(8,128)(2,1)}) %all-gather.2.cloned.1.call-update) | async-done | bytes 4194320 | tf_op jit(solution)/shard_map/all_gather | solution.py:1005
  131.0 14.9 %feed.2 = (bf16[512,1024]{1,0:T(8,128)(2,1)}, bf16[512,1024]{1,0:T(8,128)(2,1)}, bf16[512,1024]{1,0:T(8,128)(2,1)}, bf16[512,1024]{1,0:T(8,128)(2,1)}, bf16[2048...) custom-call(bf16[512,1024]{1,0:T(8,128)(2,1)} %get-tuple-element.142.re, ...), custom_call_target="tpu_custom_call" | custom-call | flops 8589934592 | bytes 20971520 | tf_op jit(solution)/shard_map/feed/pallas_call | solution.py:711
  146.0 2.8 collective-permute-done.26.refs_1_
  149.8 14.9 %feed.3 = (bf16[512,1024]{1,0:T(8,128)(2,1)}, bf16[512,1024]{1,0:T(8,128)(2,1)}, bf16[512,1024]{1,0:T(8,128)(2,1)}, bf16[512,1024]{1,0:T(8,128)(2,1)}, bf16[2048...) custom-call(bf16[512,1024]{1,0:T(8,128)(2,1)} %collective-permute-do, ...), custom_call_target="tpu_custom_call", output_to_operand_aliasing={{4}: (6, {}), {5}: (7, {}), {6}: (8, {}), {7}: (9, {})} | custom-call | flops 8589934592 | bytes 20971520 | tf_op jit(solution)/shard_map/feed/pallas_call | solution.py:711
  165.5 2.2 collective-permute-done.28
  167.7 2.6 add_convert_fusion.3
  170.3 1.5 collective-permute-start.29
  171.8 15.8 %feed_grads.1 = (bf16[1024,2048]{1,0:T(8,128)(2,1)}, f32[1,1024]{1,0:T(1,128)}) custom-call(bf16[2048,1024]{1,0:T(8,128)(2,1)} %get-tuple-element.159.normed_ref, bf16[2048,1024]{1,0:T(8,128)(2,1)} %get-tuple-element.160.grad_ref, bf16[2048,1024]{1,0:T(8,128)(2,1)} %get-tuple-element.161.grads_ref, bf16[2048,1024]{1,0:T(8,128)(2,1)} %get-tuple-element.162.active_ref), custom_call_target="tpu_custom_call" | custom-call | flops 8589934592 | bytes 16777216 | tf_op jit(solution)/shard_map/feed_grads/pallas_call | solution.py:759
  187.6 1.9 add_convert_fusion.2
  189.5 1.1 fusion.8
  190.6 5.2 %collective-permute-done.29.refs_2_ = bf16[512,1024]{1,0:T(8,128)(2,1)} collective-permute-done((bf16[512,1024]{1,0:T(8,128)(2,1)}, bf16[512,1024]{1,0:T(8,128)(2,1)}, u32[]{:S(2)}, u32[]{:S(2)}) %collective-permute-start.29) | collective-permute-done | bytes 1048608 | tf_op jit(solution)/shard_map/ppermute | solution.py:30
  195.9 1.5 collective-permute-start.34
  197.4 9.9 %middle_back.1 = (bf16[512,1024]{1,0:T(8,128)(2,1)}, f32[4,1024]{1,0:T(4,128)}, bf16[512,256]{1,0:T(8,128)(2,1)}, bf16[512,256]{1,0:T(8,128)(2,1)}, bf16[512,256...) custom-call(s32[8]{0:T(128)} %broadcast_xor_fusion.owner_b.owner, ...), custom_call_target="tpu_custom_call" | custom-call | flops 2147483648 | bytes 10485760 | tf_op jit(solution)/shard_map/middle_back/pallas_call | solution.py:901
  207.3 2.0 collective-permute-done.34
  210.8 1.4 collective-permute-start.32
  213.7 2.0 add_convert_fusion.5
  215.7 4.5 %collective-permute-done.32.refs_5_ = bf16[512,256]{1,0:T(8,128)(2,1)S(1)} collective-permute-done((bf16[512,256]{1,0:T(8,128)(2,1)}, bf16[512,256]{1,0:T(8,128)(2,1)S(1)}, u32[]{:S(2)}, u32[]{:S(2)}) %collective-permute-start.32) | collective-permute-done | bytes 262176 | tf_op jit(solution)/shard_map/ppermute | solution.py:30
  220.2 4.7 %collective-permute-done.33.refs_6_ = bf16[512,256]{1,0:T(8,128)(2,1)S(1)} collective-permute-done((bf16[512,256]{1,0:T(8,128)(2,1)}, bf16[512,256]{1,0:T(8,128)(2,1)S(1)}, u32[]{:S(2)}, u32[]{:S(2)}) %collective-permute-start.33) | collective-permute-done | bytes 262176 | tf_op jit(solution)/shard_map/ppermute | solution.py:30
  224.8 1.5 collective-permute-start.36
  227.9 36.9 %attend_back.1 = (bf16[4,128,512]{2,1,0:T(8,128)(2,1)}, bf16[4,128,512]{2,1,0:T(8,128)(2,1)}, bf16[4,128,256]{2,1,0:T(8,128)(2,1)S(1)}, bf16[4,128,256]{2,1,0:T(...) custom-call(s32[8]{0:T(128)S(1)} %copy-done.3, ...), custom_call_target="tpu_custom_call" | custom-call | flops 10737418240 | bytes 20971520 | tf_op jit(solution)/shard_map/attend_back/pallas_call | solution.py:612
  266.0 1.6 add_convert_fusion.4
  268.6 1.9 add_convert_fusion
  270.5 1.5 collective-permute-start.40
  272.1 2.6 collective-permute-done.40
  275.2 1.6 collective-permute-start.52
  277.8 1.5 collective-permute-start.44
  279.8 2.2 collective-permute-done.52
  282.1 1.6 collective-permute-start.53
  283.8 9.5 %collective-permute-done.53 = f32[104,128]{1,0:T(8,128)S(1)} collective-permute-done((f32[104,128]{1,0:T(8,128)S(1)}, f32[104,128]{1,0:T(8,128)S(1)}, u32[]{:S(2)}, u32[]{:S(2)}) %collective-permute-start.53) | collective-permute-done | bytes 53280 | tf_op jit(solution)/shard_map/ppermute | solution.py:30
  293.3 2.5 collective-permute-start.54
  296.6 2.3 collective-permute-done.54
  299.9 2.9 collective-permute-start.46
  303.3 7.9 %collective-permute-done.45 = bf16[2,128,512]{2,1,0:T(8,128)(2,1)S(1)} collective-permute-done((bf16[2,128,512]{2,1,0:T(8,128)(2,1)S(1)}, bf16[2,128,512]{2,1,0:T(8,128)(2,1)S(1)}, u32[]{:S(2)}, u32[]{:S(2)}) %collective-permute-start.45) | collective-permute-done | bytes 262176 | tf_op jit(solution)/shard_map/ppermute | solution.py:30
  311.3 3.3 collective-permute-done.46
  315.3 1.1 convert_element_type.202
  316.6 1.7 collective-permute-start.51
  318.2 1.1 fusion.6
  320.3 4.6 %input_back.1 = bf16[512,1024]{1,0:T(8,128)(2,1)} custom-call(bf16[512,1024]{1,0:T(8,128)(2,1)} %get-tuple-element.222.refs_0_, bf16[512,1024]{1,0:T(8,128)(2,1)} %copy-done.14, bf16[256,1024]{1,0:T(8,128)(2,1)} %copy-done.16, bf16[256,1024]{1,0:T(8,128)(2,1)} %collective-permute-done.47.refs_3_, bf16[512,1024]{1,0:T(8,128)(2,1)} %refs_4_.1, ...), custom_call_target="tpu_custom_call" | custom-call | flops 10485760 | bytes 7340032 | tf_op jit(solution)/shard_map/input_back/pallas_call | solution.py:933
  (213 shorter events, 36.1 us)
Async XLA Ops:
  7.2 123.8 %all-gather.2.cloned.1.call-start = ((), (), s32[]{:S(2)}) async-start(), calls=%async_computation.1 | async-start | bytes 4718592 | tf_op jit(solution)/shard_map/all_gather | solution.py:1005
  8.9 8.0 %collective-permute-start = (f32[96,128]{1,0:T(8,128)S(1)}, f32[96,128]{1,0:T(8,128)S(1)}, u32[]{:S(2)}, u32[]{:S(2)}) collective-permute-start(f32[96,128]{1,0:T(8,128)S(1)} %maximum_bitcast_fusion.2), channel_id=1, source_target_pairs={{0,1},{1,0},{2,3},{3,2},{4,5},{5,4},{6,7},{7,6},{8,9},{9,8},{10,11... | collective-permute-start | bytes 147464 | tf_op jit(solution)/shard_map/ppermute | solution.py:30
  10.8 14.3 %collective-permute-start.5 = (bf16[1,128,512]{2,1,0:T(8,128)(2,1)S(1)}, bf16[1,128,512]{2,1,0:T(8,128)(2,1)S(1)}, u32[]{:S(2)}, u32[]{:S(2)}) collective-permute-start(bf16[1,128,512]{2,1,0:T(8,128)(2,1)S(1)} %bitcast.73), channel_id=1, source_target_pairs={{0,16},{4,20},{8,24},{12,28},{16,0},{20,4},{24,8},{28,12},{1,17},{... | collective-permute-start | bytes 393224 | tf_op jit(solution)/shard_map/ppermute | solution.py:30
  15.3 15.0 %collective-permute-start.8 = (bf16[1,128,512]{2,1,0:T(8,128)(2,1)S(1)}, bf16[1,128,512]{2,1,0:T(8,128)(2,1)S(1)}, u32[]{:S(2)}, u32[]{:S(2)}) collective-permute-start(bf16[1,128,512]{2,1,0:T(8,128)(2,1)S(1)} %maximum_bitcast_fusion), channel_id=1, source_target_pairs={{0,4},{4,0},{8,12},{12,8},{16,20},{20,16},{24,28},{28,24},{1,5},{5... | collective-permute-start | bytes 393224 | tf_op jit(solution)/shard_map/ppermute | solution.py:30
  16.9 5.2 %collective-permute-start.1 = (f32[96,128]{1,0:T(8,128)S(1)}, f32[96,128]{1,0:T(8,128)S(1)}, u32[]{:S(2)}, u32[]{:S(2)}) collective-permute-start(f32[96,128]{1,0:T(8,128)S(1)} %fusion.4), channel_id=1, source_target_pairs={{0,2},{1,3},{2,0},{3,1},{4,6},{5,7},{6,4},{7,5},{8,10},{9,11},{10,... | collective-permute-start | bytes 147464 | tf_op jit(solution)/shard_map/ppermute | solution.py:30
  22.1 25.0 %collective-permute-start.3 = (bf16[512,1024]{1,0:T(8,128)(2,1)}, bf16[512,1024]{1,0:T(8,128)(2,1)S(1)}, u32[]{:S(2)}, u32[]{:S(2)}) collective-permute-start(bf16[512,1024]{1,0:T(8,128)(2,1)} %unit.1.refs_0_.refs_7_), channel_id=1, source_target_pairs={{0,2},{1,3},{2,0},{3,1},{4,6},{5,7},{6,4},{7,5},{8,10},{9,11},{10,... | collective-permute-start | bytes 3145736 | tf_op jit(solution)/shard_map/ppermute | solution.py:30
  24.5 4.1 %collective-permute-start.12 = (f32[96,128]{1,0:T(8,128)S(1)}, f32[96,128]{1,0:T(8,128)S(1)}, u32[]{:S(2)}, u32[]{:S(2)}) collective-permute-start(f32[96,128]{1,0:T(8,128)S(1)} %bitcast.84), channel_id=1, source_target_pairs={{0,4},{4,0},{8,12},{12,8},{16,20},{20,16},{24,28},{28,24},{1,5},{5... | collective-permute-start | bytes 147464 | tf_op jit(solution)/shard_map/ppermute | solution.py:30
  25.1 12.5 %collective-permute-start.6 = (bf16[2,128,512]{2,1,0:T(8,128)(2,1)S(1)}, bf16[2,128,512]{2,1,0:T(8,128)(2,1)S(1)}, u32[]{:S(2)}, u32[]{:S(2)}) collective-permute-start(bf16[2,128,512]{2,1,0:T(8,128)(2,1)S(1)} %pad_maximum_fusion.8), channel_id=1, source_target_pairs={{0,8},{4,12},{8,0},{12,4},{16,24},{20,28},{24,16},{28,20},{1,9},{5... | collective-permute-start | bytes 786440 | tf_op jit(solution)/shard_map/ppermute | solution.py:30
  28.6 6.0 %collective-permute-start.13 = (f32[96,128]{1,0:T(8,128)S(1)}, f32[96,128]{1,0:T(8,128)S(1)}, u32[]{:S(2)}, u32[]{:S(2)}) collective-permute-start(f32[96,128]{1,0:T(8,128)S(1)} %bitcast_add_fusion.1), channel_id=1, source_target_pairs={{0,8},{4,12},{8,0},{12,4},{16,24},{20,28},{24,16},{28,20},{1,9},{5... | collective-permute-start | bytes 147464 | tf_op jit(solution)/shard_map/ppermute | solution.py:30
  30.3 14.5 %collective-permute-start.9 = (bf16[2,128,512]{2,1,0:T(8,128)(2,1)S(1)}, bf16[2,128,512]{2,1,0:T(8,128)(2,1)S(1)}, u32[]{:S(2)}, u32[]{:S(2)}) collective-permute-start(bf16[2,128,512]{2,1,0:T(8,128)(2,1)S(1)} %pad_maximum_fusion.9), channel_id=1, source_target_pairs={{0,16},{4,20},{8,24},{12,28},{16,0},{20,4},{24,8},{28,12},{1,17},{... | collective-permute-start | bytes 786440 | tf_op jit(solution)/shard_map/ppermute | solution.py:30
  34.7 12.9 %collective-permute-start.14 = (f32[96,128]{1,0:T(8,128)S(1)}, f32[96,128]{1,0:T(8,128)S(1)}, u32[]{:S(2)}, u32[]{:S(2)}) collective-permute-start(f32[96,128]{1,0:T(8,128)S(1)} %fusion.14), channel_id=1, source_target_pairs={{0,16},{4,20},{8,24},{12,28},{16,0},{20,4},{24,8},{28,12},{1,17},{... | collective-permute-start | bytes 147464 | tf_op jit(solution)/shard_map/ppermute | solution.py:30
  37.6 11.3 %collective-permute-start.7 = (bf16[4,128,512]{2,1,0:T(8,128)(2,1)S(1)}, bf16[4,128,512]{2,1,0:T(8,128)(2,1)S(1)}, u32[]{:S(2)}, u32[]{:S(2)}) collective-permute-start(bf16[4,128,512]{2,1,0:T(8,128)(2,1)S(1)} %pad_maximum_fusion.3), channel_id=1, source_target_pairs={{0,4},{4,0},{8,12},{12,8},{16,20},{20,16},{24,28},{28,24},{1,5},{5... | collective-permute-start | bytes 1572872 | tf_op jit(solution)/shard_map/ppermute | solution.py:30
  44.8 12.1 %collective-permute-start.10 = (bf16[4,128,512]{2,1,0:T(8,128)(2,1)S(1)}, bf16[4,128,512]{2,1,0:T(8,128)(2,1)S(1)}, u32[]{:S(2)}, u32[]{:S(2)}) collective-permute-start(bf16[4,128,512]{2,1,0:T(8,128)(2,1)S(1)} %pad_maximum_fusion.4), channel_id=1, source_target_pairs={{0,8},{4,12},{8,0},{12,4},{16,24},{20,28},{24,16},{28,20},{1,9},{5... | collective-permute-start | bytes 1572872 | tf_op jit(solution)/shard_map/ppermute | solution.py:30
  47.1 12.9 %collective-permute-start.11 = (bf16[256,1024]{1,0:T(8,128)(2,1)}, bf16[256,1024]{1,0:T(8,128)(2,1)}, u32[]{:S(2)}, u32[]{:S(2)}) collective-permute-start(bf16[256,1024]{1,0:T(8,128)(2,1)} %get-tuple-element.123), channel_id=1, source_target_pairs={{0,2},{1,3},{2,0},{3,1},{4,6},{5,7},{6,4},{7,5},{8,10},{9,11},{10,... | collective-permute-start | bytes 1572872 | tf_op jit(solution)/shard_map/ppermute | solution.py:30
  48.2 14.7 %copy-start.27 = (s32[8]{0:T(128)S(1)}, s32[8]{0:T(128)}, u32[]{:S(2)}) copy-start(s32[8]{0:T(128)} %constant.37.clone) | copy-start | bytes 100
  60.1 255.3 %reduce-scatter.2.cloned.1.call-start = ((), (), s32[]{:S(2)}) async-start(), calls=%async_computation.2 | async-start | bytes 4718592 | tf_op jit(solution)/shard_map/reduce_scatter | solution.py:1061
  60.1 8.9 %collective-permute-start.2 = (bf16[512,1024]{1,0:T(8,128)(2,1)S(1)}, bf16[512,1024]{1,0:T(8,128)(2,1)}, u32[]{:S(2)}, u32[]{:S(2)}) collective-permute-start(bf16[512,1024]{1,0:T(8,128)(2,1)S(1)} %copy-done.12), channel_id=1, source_target_pairs={{0,1},{1,0},{2,3},{3,2},{4,5},{5,4},{6,7},{7,6},{8,9},{9,8},{10,11... | collective-permute-start | bytes 3145736 | tf_op jit(solution)/shard_map/ppermute | solution.py:30
  60.2 8.8 %collective-permute-start.4 = (bf16[512,1024]{1,0:T(8,128)(2,1)}, bf16[512,1024]{1,0:T(8,128)(2,1)}, u32[]{:S(2)}, u32[]{:S(2)}) collective-permute-start(bf16[512,1024]{1,0:T(8,128)(2,1)} %copy-done.22), channel_id=1, source_target_pairs={{0,1},{1,0},{2,3},{3,2},{4,5},{5,4},{6,7},{7,6},{8,9},{9,8},{10,11... | collective-permute-start | bytes 3145736 | tf_op jit(solution)/shard_map/ppermute | solution.py:30
  65.7 24.8 %collective-permute-start.15 = (bf16[1024,256]{1,0:T(8,128)(2,1)}, bf16[1024,256]{1,0:T(8,128)(2,1)S(1)}, u32[]{:S(2)}, u32[]{:S(2)}) collective-permute-start(bf16[1024,256]{1,0:T(8,128)(2,1)} %placed_rows.1.refs_4_.refs_3_), channel_id=1, source_target_pairs={{0,2},{1,3},{2,0},{3,1},{4,6},{5,7},{6,4},{7,5},{8,10},{9,11},{10,... | collective-permute-start | bytes 1572872 | tf_op jit(solution)/shard_map/ppermute | solution.py:30
  66.0 25.2 %collective-permute-start.16 = (bf16[256,1024]{1,0:T(8,128)(2,1)}, bf16[256,1024]{1,0:T(8,128)(2,1)}, u32[]{:S(2)}, u32[]{:S(2)}) collective-permute-start(bf16[256,1024]{1,0:T(8,128)(2,1)} %get-tuple-element.135), channel_id=1, source_target_pairs={{0,2},{1,3},{2,0},{3,1},{4,6},{5,7},{6,4},{7,5},{8,10},{9,11},{10,... | collective-permute-start | bytes 1572872 | tf_op jit(solution)/shard_map/ppermute | solution.py:30
  69.0 24.7 %collective-permute-start.20 = (bf16[1024,256]{1,0:T(8,128)(2,1)}, bf16[1024,256]{1,0:T(8,128)(2,1)S(1)}, u32[]{:S(2)}, u32[]{:S(2)}) collective-permute-start(bf16[1024,256]{1,0:T(8,128)(2,1)} %placed_rows.1.refs_4_.refs_3_), channel_id=1, source_target_pairs={{0,1},{1,0},{2,3},{3,2},{4,5},{5,4},{6,7},{7,6},{8,9},{9,8},{10,11... | collective-permute-start | bytes 1572872 | tf_op jit(solution)/shard_map/ppermute | solution.py:30
  91.2 13.7 %collective-permute-start.21 = (bf16[1024,256]{1,0:T(8,128)(2,1)S(1)}, bf16[1024,256]{1,0:T(8,128)(2,1)}, u32[]{:S(2)}, u32[]{:S(2)}) collective-permute-start(bf16[1024,256]{1,0:T(8,128)(2,1)S(1)} %collective-permute-done.15.refs_6_.refs_5_), channel_id=1, source_target_pairs={{0,1},{1,0},{2,3},{3,2},{4,5},{5,4},{6,7},{7,6},{8,9},{9,8},{10,11... | collective-permute-start | bytes 1572872 | tf_op jit(solution)/shard_map/ppermute | solution.py:30
  91.2 3.3 collective-permute-start.17
  91.7 9.5 %collective-permute-start.18 = (bf16[512,256]{1,0:T(8,128)(2,1)}, bf16[512,256]{1,0:T(8,128)(2,1)}, u32[]{:S(2)}, u32[]{:S(2)}) collective-permute-start(bf16[512,256]{1,0:T(8,128)(2,1)} %get-tuple-element.138), channel_id=1, source_target_pairs={{0,2},{1,3},{2,0},{3,1},{4,6},{5,7},{6,4},{7,5},{8,10},{9,11},{10,... | collective-permute-start | bytes 786440 | tf_op jit(solution)/shard_map/ppermute | solution.py:30
  92.0 12.9 %collective-permute-start.19 = (bf16[512,256]{1,0:T(8,128)(2,1)}, bf16[512,256]{1,0:T(8,128)(2,1)}, u32[]{:S(2)}, u32[]{:S(2)}) collective-permute-start(bf16[512,256]{1,0:T(8,128)(2,1)} %get-tuple-element.139), channel_id=1, source_target_pairs={{0,3},{1,2},{2,1},{3,0},{4,7},{5,6},{6,5},{7,4},{8,11},{9,10},{10,... | collective-permute-start | bytes 786440 | tf_op jit(solution)/shard_map/ppermute | solution.py:30
  93.7 20.4 %collective-permute-start.23 = (bf16[512,1024]{1,0:T(8,128)(2,1)S(1)}, bf16[512,1024]{1,0:T(8,128)(2,1)}, u32[]{:S(2)}, u32[]{:S(2)}) collective-permute-start(bf16[512,1024]{1,0:T(8,128)(2,1)S(1)} %copy-done.5), channel_id=1, source_target_pairs={{0,1},{1,0},{2,3},{3,2},{4,5},{5,4},{6,7},{7,6},{8,9},{9,8},{10,11... | collective-permute-start | bytes 3145736 | tf_op jit(solution)/shard_map/ppermute | solution.py:30
  109.9 4.2 %collective-permute-start.22 = (bf16[512,1024]{1,0:T(8,128)(2,1)}, bf16[512,1024]{1,0:T(8,128)(2,1)}, u32[]{:S(2)}, u32[]{:S(2)}) collective-permute-start(bf16[512,1024]{1,0:T(8,128)(2,1)} %get-tuple-element.142.refs_0_), channel_id=1, source_target_pairs={{0,1},{1,0},{2,3},{3,2},{4,5},{5,4},{6,7},{7,6},{8,9},{9,8},{10,11... | collective-permute-start | bytes 3145736 | tf_op jit(solution)/shard_map/ppermute | solution.py:30
  111.5 34.4 %collective-permute-start.25 = (bf16[512,1024]{1,0:T(8,128)(2,1)}, bf16[512,1024]{1,0:T(8,128)(2,1)}, u32[]{:S(2)}, u32[]{:S(2)}) collective-permute-start(bf16[512,1024]{1,0:T(8,128)(2,1)} %get-tuple-element.142.refs_0_), channel_id=1, source_target_pairs={{0,2},{1,3},{2,0},{3,1},{4,6},{5,7},{6,4},{7,5},{8,10},{9,11},{10,... | collective-permute-start | bytes 3145736 | tf_op jit(solution)/shard_map/ppermute | solution.py:30
  114.0 31.9 %copy-start.17 = (bf16[512,1024]{1,0:T(8,128)(2,1)}, bf16[512,1024]{1,0:T(8,128)(2,1)S(1)}, u32[]{:S(2)}) copy-start(bf16[512,1024]{1,0:T(8,128)(2,1)S(1)} %constant_dynamic-update-slice_fusion.refs_2_) | copy-start | bytes 3145732
  114.0 32.0 %collective-permute-start.27 = (bf16[512,1024]{1,0:T(8,128)(2,1)S(1)}, bf16[512,1024]{1,0:T(8,128)(2,1)}, u32[]{:S(2)}, u32[]{:S(2)}) collective-permute-start(bf16[512,1024]{1,0:T(8,128)(2,1)S(1)} %constant_dynamic-update-slice_fusion.refs_2_), channel_id=1, source_target_pairs={{0,1},{1,0},{2,3},{3,2},{4,5},{5,4},{6,7},{7,6},{8,9},{9,8},{10,11... | collective-permute-start | bytes 3145736 | tf_op jit(solution)/shard_map/ppermute | solution.py:30
  145.9 2.9 collective-permute-start.26
  164.8 2.9 collective-permute-start.28
  165.0 25.6 %collective-permute-start.24 = (bf16[512,1024]{1,0:T(8,128)(2,1)}, bf16[512,1024]{1,0:T(8,128)(2,1)S(1)}, u32[]{:S(2)}, u32[]{:S(2)}) collective-permute-start(bf16[512,1024]{1,0:T(8,128)(2,1)} %get-tuple-element.145), channel_id=1, source_target_pairs={{0,1},{1,0},{2,3},{3,2},{4,5},{5,4},{6,7},{7,6},{8,9},{9,8},{10,11... | collective-permute-start | bytes 3145736 | tf_op jit(solution)/shard_map/ppermute | solution.py:30
  165.4 22.2 %collective-permute-start.30 = (bf16[512,1024]{1,0:T(8,128)(2,1)}, bf16[512,1024]{1,0:T(8,128)(2,1)}, u32[]{:S(2)}, u32[]{:S(2)}) collective-permute-start(bf16[512,1024]{1,0:T(8,128)(2,1)} %get-tuple-element.165), channel_id=1, source_target_pairs={{0,1},{1,0},{2,3},{3,2},{4,5},{5,4},{6,7},{7,6},{8,9},{9,8},{10,11... | collective-permute-start | bytes 3145736 | tf_op jit(solution)/shard_map/ppermute | solution.py:30
  170.3 25.5 %collective-permute-start.29 = (bf16[512,1024]{1,0:T(8,128)(2,1)}, bf16[512,1024]{1,0:T(8,128)(2,1)}, u32[]{:S(2)}, u32[]{:S(2)}) collective-permute-start(bf16[512,1024]{1,0:T(8,128)(2,1)} %add_convert_fusion.3), channel_id=1, source_target_pairs={{0,2},{1,3},{2,0},{3,1},{4,6},{5,7},{6,4},{7,5},{8,10},{9,11},{10,... | collective-permute-start | bytes 3145736 | tf_op jit(solution)/shard_map/ppermute | solution.py:30
  195.9 13.4 %collective-permute-start.34 = (bf16[256,1024]{1,0:T(8,128)(2,1)}, bf16[256,1024]{1,0:T(8,128)(2,1)S(1)}, u32[]{:S(2)}, u32[]{:S(2)}) collective-permute-start(bf16[256,1024]{1,0:T(8,128)(2,1)} %get-tuple-element.178), channel_id=1, source_target_pairs={{0,2},{1,3},{2,0},{3,1},{4,6},{5,7},{6,4},{7,5},{8,10},{9,11},{10,... | collective-permute-start | bytes 1572872 | tf_op jit(solution)/shard_map/ppermute | solution.py:30
  197.4 29.5 %copy-start = (s32[8]{0:T(128)S(1)}, s32[8]{0:T(128)}, u32[]{:S(2)}) copy-start(s32[8]{0:T(128)} %broadcast_xor_fusion.owner_b.owner) | copy-start | bytes 100
  197.4 29.5 %copy-start.1 = (s32[418]{0:T(512)S(1)}, s32[418]{0:T(512)}, u32[]{:S(2)}) copy-start(s32[418]{0:T(512)} %pad_add_fusion.facts) | copy-start | bytes 5020
  197.4 29.5 %copy-start.3 = (s32[8]{0:T(128)S(1)}, s32[8]{0:T(128)}, u32[]{:S(2)}) copy-start(s32[8]{0:T(128)} %broadcast_xor_fusion.1.owner_a) | copy-start | bytes 100
  197.4 29.5 %copy-start.4 = (f32[32,256]{1,0:T(8,128)S(1)}, f32[32,256]{1,0:T(8,128)}, u32[]{:S(2)}) copy-start(f32[32,256]{1,0:T(8,128)} %get-tuple-element.129.refs_1_) | copy-start | bytes 98308
  209.3 4.0 %collective-permute-start.35 = (bf16[8,128,256]{2,1,0:T(8,128)(2,1)}, bf16[8,128,256]{2,1,0:T(8,128)(2,1)S(1)}, u32[]{:S(2)}, u32[]{:S(2)}) collective-permute-start(bf16[8,128,256]{2,1,0:T(8,128)(2,1)} %get-tuple-element.180), channel_id=1, source_target_pairs={{0,1},{1,0},{2,3},{3,2},{4,5},{5,4},{6,7},{7,6},{8,9},{9,8},{10,11... | collective-permute-start | bytes 1572872 | tf_op jit(solution)/shard_map/ppermute | solution.py:30
  210.0 58.6 %collective-permute-start.48 = (bf16[512,1024]{1,0:T(8,128)(2,1)}, bf16[512,1024]{1,0:T(8,128)(2,1)S(1)}, u32[]{:S(2)}, u32[]{:S(2)}) collective-permute-start(bf16[512,1024]{1,0:T(8,128)(2,1)} %get-tuple-element.218), channel_id=1, source_target_pairs={{0,1},{1,0},{2,3},{3,2},{4,5},{5,4},{6,7},{7,6},{8,9},{9,8},{10,11... | collective-permute-start | bytes 3145736 | tf_op jit(solution)/shard_map/ppermute | solution.py:30
  210.7 5.0 %collective-permute-start.31 = (bf16[512,256]{1,0:T(8,128)(2,1)}, bf16[512,256]{1,0:T(8,128)(2,1)S(1)}, u32[]{:S(2)}, u32[]{:S(2)}) collective-permute-start(bf16[512,256]{1,0:T(8,128)(2,1)} %get-tuple-element.171), channel_id=1, source_target_pairs={{0,1},{1,0},{2,3},{3,2},{4,5},{5,4},{6,7},{7,6},{8,9},{9,8},{10,11... | collective-permute-start | bytes 786440 | tf_op jit(solution)/shard_map/ppermute | solution.py:30
  210.8 9.3 %collective-permute-start.32 = (bf16[512,256]{1,0:T(8,128)(2,1)}, bf16[512,256]{1,0:T(8,128)(2,1)S(1)}, u32[]{:S(2)}, u32[]{:S(2)}) collective-permute-start(bf16[512,256]{1,0:T(8,128)(2,1)} %get-tuple-element.172), channel_id=1, source_target_pairs={{0,2},{1,3},{2,0},{3,1},{4,6},{5,7},{6,4},{7,5},{8,10},{9,11},{10,... | collective-permute-start | bytes 786440 | tf_op jit(solution)/shard_map/ppermute | solution.py:30
  212.3 12.6 %collective-permute-start.33 = (bf16[512,256]{1,0:T(8,128)(2,1)}, bf16[512,256]{1,0:T(8,128)(2,1)S(1)}, u32[]{:S(2)}, u32[]{:S(2)}) collective-permute-start(bf16[512,256]{1,0:T(8,128)(2,1)} %get-tuple-element.173), channel_id=1, source_target_pairs={{0,3},{1,2},{2,1},{3,0},{4,7},{5,6},{6,5},{7,4},{8,11},{9,10},{10,... | collective-permute-start | bytes 786440 | tf_op jit(solution)/shard_map/ppermute | solution.py:30
  213.3 51.5 %collective-permute-start.37 = (bf16[8,128,256]{2,1,0:T(8,128)(2,1)}, bf16[8,128,256]{2,1,0:T(8,128)(2,1)}, u32[]{:S(2)}, u32[]{:S(2)}) collective-permute-start(bf16[8,128,256]{2,1,0:T(8,128)(2,1)} %get-tuple-element.190), channel_id=1, source_target_pairs={{0,1},{1,0},{2,3},{3,2},{4,5},{5,4},{6,7},{7,6},{8,9},{9,8},{10,11... | collective-permute-start | bytes 1572872 | tf_op jit(solution)/shard_map/ppermute | solution.py:30
  224.8 40.0 %collective-permute-start.36 = (bf16[256,1024]{1,0:T(8,128)(2,1)}, bf16[256,1024]{1,0:T(8,128)(2,1)S(1)}, u32[]{:S(2)}, u32[]{:S(2)}) collective-permute-start(bf16[256,1024]{1,0:T(8,128)(2,1)} %get-tuple-element.188), channel_id=1, source_target_pairs={{0,2},{1,3},{2,0},{3,1},{4,6},{5,7},{6,4},{7,5},{8,10},{9,11},{10,... | collective-permute-start | bytes 1572872 | tf_op jit(solution)/shard_map/ppermute | solution.py:30
  226.3 38.5 %collective-permute-start.38 = (bf16[8,128,256]{2,1,0:T(8,128)(2,1)}, bf16[8,128,256]{2,1,0:T(8,128)(2,1)}, u32[]{:S(2)}, u32[]{:S(2)}) collective-permute-start(bf16[8,128,256]{2,1,0:T(8,128)(2,1)} %add_convert_fusion.5), channel_id=1, source_target_pairs={{0,2},{1,3},{2,0},{3,1},{4,6},{5,7},{6,4},{7,5},{8,10},{9,11},{10,... | collective-permute-start | bytes 1572872 | tf_op jit(solution)/shard_map/ppermute | solution.py:30
  264.8 17.2 %collective-permute-start.42 = (bf16[4,128,512]{2,1,0:T(8,128)(2,1)}, bf16[4,128,512]{2,1,0:T(8,128)(2,1)S(1)}, u32[]{:S(2)}, u32[]{:S(2)}) collective-permute-start(bf16[4,128,512]{2,1,0:T(8,128)(2,1)} %get-tuple-element.210), channel_id=1, source_target_pairs={{0,4},{4,0},{8,12},{12,8},{16,20},{20,16},{24,28},{28,24},{1,5},{5... | collective-permute-start | bytes 1572872 | tf_op jit(solution)/shard_map/ppermute | solution.py:30
  265.4 5.1 %collective-permute-start.39 = (f32[104,128]{1,0:T(8,128)S(1)}, f32[104,128]{1,0:T(8,128)S(1)}, u32[]{:S(2)}, u32[]{:S(2)}) collective-permute-start(f32[104,128]{1,0:T(8,128)S(1)} %maximum_bitcast_fusion.1), channel_id=1, source_target_pairs={{0,1},{1,0},{2,3},{3,2},{4,5},{5,4},{6,7},{7,6},{8,9},{9,8},{10,11... | collective-permute-start | bytes 159752 | tf_op jit(solution)/shard_map/ppermute | solution.py:30
  265.5 9.2 %collective-permute-start.41 = (bf16[512,1024]{1,0:T(8,128)(2,1)}, bf16[512,1024]{1,0:T(8,128)(2,1)S(1)}, u32[]{:S(2)}, u32[]{:S(2)}) collective-permute-start(bf16[512,1024]{1,0:T(8,128)(2,1)} %get-tuple-element.201), channel_id=1, source_target_pairs={{0,1},{1,0},{2,3},{3,2},{4,5},{5,4},{6,7},{7,6},{8,9},{9,8},{10,11... | collective-permute-start | bytes 3145736 | tf_op jit(solution)/shard_map/ppermute | solution.py:30
  267.7 28.1 %collective-permute-start.43 = (bf16[4,128,512]{2,1,0:T(8,128)(2,1)S(1)}, bf16[4,128,512]{2,1,0:T(8,128)(2,1)S(1)}, u32[]{:S(2)}, u32[]{:S(2)}) collective-permute-start(bf16[4,128,512]{2,1,0:T(8,128)(2,1)S(1)} %pad_maximum_fusion.6), channel_id=1, source_target_pairs={{0,8},{4,12},{8,0},{12,4},{16,24},{20,28},{24,16},{28,20},{1,9},{5... | collective-permute-start | bytes 1572872 | tf_op jit(solution)/shard_map/ppermute | solution.py:30
  270.5 4.2 %collective-permute-start.40 = (f32[104,128]{1,0:T(8,128)S(1)}, f32[104,128]{1,0:T(8,128)S(1)}, u32[]{:S(2)}, u32[]{:S(2)}) collective-permute-start(f32[104,128]{1,0:T(8,128)S(1)} %fusion.5), channel_id=1, source_target_pairs={{0,2},{1,3},{2,0},{3,1},{4,6},{5,7},{6,4},{7,5},{8,10},{9,11},{10,... | collective-permute-start | bytes 159752 | tf_op jit(solution)/shard_map/ppermute | solution.py:30
  275.2 6.9 %collective-permute-start.52 = (f32[104,128]{1,0:T(8,128)S(1)}, f32[104,128]{1,0:T(8,128)S(1)}, u32[]{:S(2)}, u32[]{:S(2)}) collective-permute-start(f32[104,128]{1,0:T(8,128)S(1)} %bitcast.83), channel_id=1, source_target_pairs={{0,4},{4,0},{8,12},{12,8},{16,20},{20,16},{24,28},{28,24},{1,5},{5... | collective-permute-start | bytes 159752 | tf_op jit(solution)/shard_map/ppermute | solution.py:30
  277.8 21.2 %collective-permute-start.44 = (bf16[256,1024]{1,0:T(8,128)(2,1)}, bf16[256,1024]{1,0:T(8,128)(2,1)S(1)}, u32[]{:S(2)}, u32[]{:S(2)}) collective-permute-start(bf16[256,1024]{1,0:T(8,128)(2,1)} %get-tuple-element.245), channel_id=1, source_target_pairs={{0,2},{1,3},{2,0},{3,1},{4,6},{5,7},{6,4},{7,5},{8,10},{9,11},{10,... | collective-permute-start | bytes 1572872 | tf_op jit(solution)/shard_map/ppermute | solution.py:30
  279.3 37.2 %collective-permute-start.47 = (bf16[256,1024]{1,0:T(8,128)(2,1)}, bf16[256,1024]{1,0:T(8,128)(2,1)}, u32[]{:S(2)}, u32[]{:S(2)}) collective-permute-start(bf16[256,1024]{1,0:T(8,128)(2,1)} %get-tuple-element.244), channel_id=1, source_target_pairs={{0,2},{1,3},{2,0},{3,1},{4,6},{5,7},{6,4},{7,5},{8,10},{9,11},{10,... | collective-permute-start | bytes 1572872 | tf_op jit(solution)/shard_map/ppermute | solution.py:30
  282.1 37.3 %collective-permute-start.49 = (bf16[512,1024]{1,0:T(8,128)(2,1)}, bf16[512,1024]{1,0:T(8,128)(2,1)S(1)}, u32[]{:S(2)}, u32[]{:S(2)}) collective-permute-start(bf16[512,1024]{1,0:T(8,128)(2,1)} %get-tuple-element.223), channel_id=1, source_target_pairs={{0,1},{1,0},{2,3},{3,2},{4,5},{5,4},{6,7},{7,6},{8,9},{9,8},{10,11... | collective-permute-start | bytes 3145736 | tf_op jit(solution)/shard_map/ppermute | solution.py:30
  282.1 11.2 %collective-permute-start.53 = (f32[104,128]{1,0:T(8,128)S(1)}, f32[104,128]{1,0:T(8,128)S(1)}, u32[]{:S(2)}, u32[]{:S(2)}) collective-permute-start(f32[104,128]{1,0:T(8,128)S(1)} %bitcast_add_fusion), channel_id=1, source_target_pairs={{0,8},{4,12},{8,0},{12,4},{16,24},{20,28},{24,16},{28,20},{1,9},{5... | collective-permute-start | bytes 159752 | tf_op jit(solution)/shard_map/ppermute | solution.py:30
  293.3 5.6 %collective-permute-start.54 = (f32[104,128]{1,0:T(8,128)S(1)}, f32[104,128]{1,0:T(8,128)S(1)}, u32[]{:S(2)}, u32[]{:S(2)}) collective-permute-start(f32[104,128]{1,0:T(8,128)S(1)} %fusion.13), channel_id=1, source_target_pairs={{0,16},{4,20},{8,24},{12,28},{16,0},{20,4},{24,8},{28,12},{1,17},{... | collective-permute-start | bytes 159752 | tf_op jit(solution)/shard_map/ppermute | solution.py:30
  299.0 20.3 %copy-start.16 = (bf16[256,1024]{1,0:T(8,128)(2,1)}, bf16[256,1024]{1,0:T(8,128)(2,1)S(1)}, u32[]{:S(2)}) copy-start(bf16[256,1024]{1,0:T(8,128)(2,1)S(1)} %collective-permute-done.44.refs_2_) | copy-start | bytes 1572868
  299.0 12.2 %collective-permute-start.45 = (bf16[2,128,512]{2,1,0:T(8,128)(2,1)S(1)}, bf16[2,128,512]{2,1,0:T(8,128)(2,1)S(1)}, u32[]{:S(2)}, u32[]{:S(2)}) collective-permute-start(bf16[2,128,512]{2,1,0:T(8,128)(2,1)S(1)} %get-tuple-element.214), channel_id=1, source_target_pairs={{0,8},{4,12},{8,0},{12,4},{16,24},{20,28},{24,16},{28,20},{1,9},{5... | collective-permute-start | bytes 786440 | tf_op jit(solution)/shard_map/ppermute | solution.py:30
  299.9 14.7 %collective-permute-start.46 = (bf16[2,128,512]{2,1,0:T(8,128)(2,1)}, bf16[2,128,512]{2,1,0:T(8,128)(2,1)S(1)}, u32[]{:S(2)}, u32[]{:S(2)}) collective-permute-start(bf16[2,128,512]{2,1,0:T(8,128)(2,1)} %get-tuple-element.215), channel_id=1, source_target_pairs={{0,16},{4,20},{8,24},{12,28},{16,0},{20,4},{24,8},{28,12},{1,17},{... | collective-permute-start | bytes 786440 | tf_op jit(solution)/shard_map/ppermute | solution.py:30
  316.5 8.4 %collective-permute-start.50 = (bf16[1,128,512]{2,1,0:T(8,128)(2,1)S(1)}, bf16[1,128,512]{2,1,0:T(8,128)(2,1)}, u32[]{:S(2)}, u32[]{:S(2)}) collective-permute-start(bf16[1,128,512]{2,1,0:T(8,128)(2,1)S(1)} %get-tuple-element.229), channel_id=1, source_target_pairs={{0,16},{4,20},{8,24},{12,28},{16,0},{20,4},{24,8},{28,12},{1,17},{... | collective-permute-start | bytes 393224 | tf_op jit(solution)/shard_map/ppermute | solution.py:30
  316.6 8.3 %collective-permute-start.51 = (bf16[1,128,512]{2,1,0:T(8,128)(2,1)}, bf16[1,128,512]{2,1,0:T(8,128)(2,1)}, u32[]{:S(2)}, u32[]{:S(2)}) collective-permute-start(bf16[1,128,512]{2,1,0:T(8,128)(2,1)} %get-tuple-element.231), channel_id=1, source_target_pairs={{0,4},{4,0},{8,12},{12,8},{16,20},{20,16},{24,28},{28,24},{1,5},{5... | collective-permute-start | bytes 393224 | tf_op jit(solution)/shard_map/ppermute | solution.py:30
  (22 other events, 158.7 us)
Sparse Core Ops, SparseCore 0:
  60.2 70.7 all-gather.1
  196.0 93.6 reduce-scatter.1

commit v2 on v1

--- a/solution.py
+++ b/solution.py
@@ -102,8 +102,11 @@
     size = value.shape[0]
     value = jnp.pad(value, (0, -size % 1024)).reshape(-1, 128)
     for axis in axes:
-        for bit in bits_of(axis):
-            value = value + swapped(value, axis, bit)
+        if lax.axis_size(axis) <= 4:
+            value = total([value] + [swapped(value, axis, k) for k in range(1, lax.axis_size(axis))])
+        else:
+            for bit in bits_of(axis):
+                value = value + swapped(value, axis, bit)
     return value.reshape(-1)[:size]
 
 
@@ -1056,10 +1059,10 @@
     feed_sums, sum_hidden = feed_grads(stacks)
     feed_terms, feed_far = summed_halves(feed_parts, "tensor")
     early, late_rows = feed_far[: near // 2], feed_far[near // 2 :]
-    *back_terms, feed_sums, early = together(*back_terms, feed_sums, early)
-    early = far(early, "tensor")
     feed_weight_grads = lax.psum_scatter(feed_sums, "dp", scatter_dimension=0, tiled=True)
     feed_weight_grads = feed_weight_grads.astype(F32)
+    *back_terms, sum_hidden, early = together(*back_terms, sum_hidden, early)
+    early = far(early, "tensor")
 
     grad_middle, sums_two, grad_heads, out_blocks = middle_back(
         back_terms, out_parts, context_near, middle, output_cotangent, norm_two, owner_b
@@ -1105,8 +1108,8 @@
     )
     packed = summed_everywhere(packed, ("tensor",))
     far_sum = added(far_rows[0], swapped(far_rows[1], "tensor", 1))
-    packed, far_sum, first_keep, last_keep, *near_rows = together(
-        packed, far_sum, first_keep, last_keep, *near_rows
+    far_sum, first_keep, last_keep, *near_rows = together(
+        far_sum, first_keep, last_keep, *near_rows
     )
     far_first = far(far_sum[: near // 2], "tensor")
     far_last = far(far_sum[near // 2 :], "tensor")
@@ -1116,12 +1119,12 @@
     while first_send.shape[0] > 1:
         first_keep, first_send = halved(first_keep, first_send, "dp", order_a)
         last_keep, last_send = halved(last_keep, last_send, "dp", order_b)
-    first_send, last_send, far_last, feed_weight_grads, output = together(
-        first_send, last_send, far_last, feed_weight_grads, output
-    )
+    first_send, last_send, far_last, output = together(first_send, last_send, far_last, output)
     near_terms = [near_rows[0], swapped(near_rows[1], "tensor", 1), far_first, far_last]
     input_grad = input_back(near_terms, tokens, grad_middle, norm_one)
-    first_keep, last_keep, input_grad = together(first_keep, last_keep, input_grad)
+    first_keep, last_keep, input_grad, packed = together(
+        first_keep, last_keep, input_grad, packed
+    )
     first_raw = halved(first_keep, first_send, "dp", order_a)[0][0].astype(F32)
     last_raw = halved(last_keep, last_send, "dp", order_b)[0][0].astype(F32)
     out_weight_grad = last_raw[:, width:]

time: 341 us -> 340 us (level)
  waiting for transfers between devices: 99.7 us -> 105 us
  other arithmetic: 22.8 us -> 18.9 us
    ppermute x55 -> x57, waiting for transfers between devices: 82.8 us -> 87.9 us  [swapped(): return lax.ppermute(value, axis, [(i, i ^ bit) for i in range(count)])]
    ppermute x55 -> x57, starting transfers between devices: 49.3 us -> 47.4 us  [swapped(): return lax.ppermute(value, axis, [(i, i ^ bit) for i in range(count)])]
    unnamed x67 -> x79, local copies, waits for them, and re-layouts: 7.67 us -> 7.27 us
  transfers between devices with their start and end apart: 57 -> 59, of which waited for: 23 -> 27; matrix products, arithmetic and copies ran while one was open for 10% -> 9% of each run, Pallas kernels for 34% -> 34%
where the time goes in v2:
time: 340 us; the launch traced here: 334 us
  Pallas kernels  128 us (38%)
  waiting for transfers between devices  105 us (31%)
  starting transfers between devices  47.5 us (14%)
  local copies, waits for them, and re-layouts  19.1 us (6%)
  other arithmetic  18.9 us (6%)
  between operations  15.7 us (5%)
    ppermute x57, waiting for transfers between devices, swapped(): return lax.ppermute(value, axis, [(i, i ^ bit) for i in range(count)])  87.9 us
    ppermute x57, starting transfers between devices, swapped(): return lax.ppermute(value, axis, [(i, i ^ bit) for i in range(count)])  47.4 us
    pallas_call x1, Pallas kernels, attend_back(): pl.pallas_call(functools.partial(attend_back_kernel, heads, len(unit)), g...  37 us
    pallas_call x2, Pallas kernels, feed(): pl.pallas_call(functools.partial(feed_kernel, here, len(stacks)), grid=(h...  29.9 us
    pallas_call x1, Pallas kernels, project_attend(): pl.pallas_call(functools.partial(project_attend_kernel, heads, len(unit))...  21.5 us
    all_gather x1, waiting for transfers between devices, per_device(): feed_full = lax.all_gather(feed_flat, 'dp', axis=0, tiled=True)  16.6 us
    pallas_call x1, Pallas kernels, feed_grads(): pl.pallas_call(feed_grads_kernel, grid=(rows // (2 * TILE),), out_shape=[...  15.8 us
    pallas_call x1, Pallas kernels, middle_back(): pl.pallas_call(functools.partial(middle_back_kernel, len(terms), parts),...  9.9 us
  transfers between devices with their start and end apart: 59, of which 27 were waited for; matrix products, arithmetic and copies ran while one was open for 9% of the time, Pallas kernels for 34%

profile of v2, /device:TPU:0, one launch (start us, length us, event | category | flops | bytes accessed | tf_op | source)
XLA Modules:
  0.0 334.0 jit_solution(12128341401213173663)
XLA Ops:
  8.9 2.5 collective-permute-start.2
  12.1 1.1 copy.28
  13.4 2.8 collective-permute-start.6
  17.2 1.6 collective-permute-start.9
  19.8 2.5 unit.1.refs_0_.refs_7_
  23.1 1.7 collective-permute-start.4
  25.3 1.8 pad_maximum_fusion.2
  27.1 1.8 collective-permute-done.13
  28.9 1.6 collective-permute-start.14
  31.5 5.4 %collective-permute-done.14 = f32[96,128]{1,0:T(8,128)S(1)} collective-permute-done((f32[96,128]{1,0:T(8,128)S(1)}, f32[96,128]{1,0:T(8,128)S(1)}, u32[]{:S(2)}, u32[]{:S(2)}) %collective-permute-start.14) | collective-permute-done | bytes 49184 | tf_op jit(solution)/shard_map/ppermute | solution.py:30
  37.2 5.1 %collective-permute-done.7 = bf16[2,128,512]{2,1,0:T(8,128)(2,1)S(1)} collective-permute-done((bf16[2,128,512]{2,1,0:T(8,128)(2,1)S(1)}, bf16[2,128,512]{2,1,0:T(8,128)(2,1)S(1)}, u32[]{:S(2)}, u32[]{:S(2)}) %collective-permute-start.7) | collective-permute-done | bytes 262176 | tf_op jit(solution)/shard_map/ppermute | solution.py:30
  42.9 2.6 collective-permute-done.10
  45.6 2.6 collective-permute-done.4.refs_2_.refs_9_
  48.2 1.4 collective-permute-start.12
  49.7 4.9 %collective-permute-done.8 = bf16[4,128,512]{2,1,0:T(8,128)(2,1)S(1)} collective-permute-done((bf16[4,128,512]{2,1,0:T(8,128)(2,1)S(1)}, bf16[4,128,512]{2,1,0:T(8,128)(2,1)S(1)}, u32[]{:S(2)}, u32[]{:S(2)}) %collective-permute-start.8) | collective-permute-done | bytes 524320 | tf_op jit(solution)/shard_map/ppermute | solution.py:30
  55.7 1.2 collective-permute-done.11
  58.0 3.3 collective-permute-done.12
  64.8 2.1 placed_rows.1.refs_4_.refs_3_
  66.9 1.2 collective-permute-start.16
  70.1 21.5 %project_attend.1 = (bf16[512,256]{1,0:T(8,128)(2,1)}, bf16[512,256]{1,0:T(8,128)(2,1)}, bf16[512,256]{1,0:T(8,128)(2,1)}, bf16[512,256]{1,0:T(8,128)(2,1)}, bf1...) custom-call(s32[8]{0:T(128)} %broadcast_xor_fusion.1.owner_a, ...), custom_call_target="tpu_custom_call" | custom-call | flops 5368709120 | bytes 10485760 | tf_op jit(solution)/shard_map/project_attend/pallas_call | solution.py:487
  92.9 1.2 collective-permute-start.19
  95.6 6.7 %collective-permute-done.19.refs_2_.refs_9_ = bf16[512,256]{1,0:T(8,128)(2,1)} collective-permute-done((bf16[512,256]{1,0:T(8,128)(2,1)}, bf16[512,256]{1,0:T(8,128)(2,1)}, u32[]{:S(2)}, u32[]{:S(2)}) %collective-permute-start.19) | collective-permute-done | bytes 262176 | tf_op jit(solution)/shard_map/ppermute | solution.py:30
  102.4 3.7 %collective-permute-done.20.refs_3_.refs_10_ = bf16[512,256]{1,0:T(8,128)(2,1)} collective-permute-done((bf16[512,256]{1,0:T(8,128)(2,1)}, bf16[512,256]{1,0:T(8,128)(2,1)}, u32[]{:S(2)}, u32[]{:S(2)}) %collective-permute-start.20) | collective-permute-done | bytes 262176 | tf_op jit(solution)/shard_map/ppermute | solution.py:30
  106.1 5.0 %middle.1 = (bf16[512,1024]{1,0:T(8,128)(2,1)}, bf16[512,1024]{1,0:T(8,128)(2,1)}) custom-call(bf16[512,256]{1,0:T(8,128)(2,1)} %get-tuple-element.135.refs_0_.refs_7_, bf16[512,256]{1,0:T(8,128)(2,1)} %copy-done.12, bf16[512,256]{1,0:T(8,128)(2,1)} %collective-permute-done.19.refs_2_.refs_9_, bf16[512,256]{1,0:T(8,128)(2,1)} %collective-permute-done.20.refs_3_.refs_10_, ...), custom_call_target="tpu_custom_call" | custom-call | flops 1073741824 | bytes 6291456 | tf_op jit(solution)/shard_map/middle/pallas_call | solution.py:839
  112.7 1.2 collective-permute-start.26
  116.2 16.6 %all-gather.2.cloned.1.call-done.refs_4_ = bf16[1024,2048]{1,0:T(8,128)(2,1)} async-done(((bf16[128,2048]{1,0:T(8,128)(2,1)}), bf16[1024,2048]{1,0:T(8,128)(2,1)}) %all-gather.2.cloned.1.call-update) | async-done | bytes 4194320 | tf_op jit(solution)/shard_map/all_gather | solution.py:1008
  132.8 14.9 %feed.2 = (bf16[512,1024]{1,0:T(8,128)(2,1)}, bf16[512,1024]{1,0:T(8,128)(2,1)}, bf16[512,1024]{1,0:T(8,128)(2,1)}, bf16[512,1024]{1,0:T(8,128)(2,1)}, bf16[2048...) custom-call(bf16[512,1024]{1,0:T(8,128)(2,1)} %get-tuple-element.141.re, ...), custom_call_target="tpu_custom_call" | custom-call | flops 8589934592 | bytes 20971520 | tf_op jit(solution)/shard_map/feed/pallas_call | solution.py:714
  147.8 2.8 collective-permute-done.27.refs_1_
  151.6 14.9 %feed.3 = (bf16[512,1024]{1,0:T(8,128)(2,1)}, bf16[512,1024]{1,0:T(8,128)(2,1)}, bf16[512,1024]{1,0:T(8,128)(2,1)}, bf16[512,1024]{1,0:T(8,128)(2,1)}, bf16[2048...) custom-call(bf16[512,1024]{1,0:T(8,128)(2,1)} %collective-permute-do, ...), custom_call_target="tpu_custom_call", output_to_operand_aliasing={{4}: (6, {}), {5}: (7, {}), {6}: (8, {}), {7}: (9, {})} | custom-call | flops 8589934592 | bytes 20971520 | tf_op jit(solution)/shard_map/feed/pallas_call | solution.py:714
  167.3 2.2 collective-permute-done.29
  169.5 2.6 add_convert_fusion.3
  172.1 1.5 collective-permute-start.30
  173.6 15.8 %feed_grads.1 = (bf16[1024,2048]{1,0:T(8,128)(2,1)}, f32[1,1024]{1,0:T(1,128)}) custom-call(bf16[2048,1024]{1,0:T(8,128)(2,1)} %get-tuple-element.158.normed_ref, bf16[2048,1024]{1,0:T(8,128)(2,1)} %get-tuple-element.159.grad_ref, bf16[2048,1024]{1,0:T(8,128)(2,1)} %get-tuple-element.160.grads_ref, bf16[2048,1024]{1,0:T(8,128)(2,1)} %get-tuple-element.161.active_ref), custom_call_target="tpu_custom_call" | custom-call | flops 8589934592 | bytes 16777216 | tf_op jit(solution)/shard_map/feed_grads/pallas_call | solution.py:762
  189.4 1.2 copy-done.11
  190.6 1.6 add_convert_fusion.2
  193.3 4.3 %collective-permute-done.30.refs_2_ = bf16[512,1024]{1,0:T(8,128)(2,1)} collective-permute-done((bf16[512,1024]{1,0:T(8,128)(2,1)}, bf16[512,1024]{1,0:T(8,128)(2,1)}, u32[]{:S(2)}, u32[]{:S(2)}) %collective-permute-start.30) | collective-permute-done | bytes 1048608 | tf_op jit(solution)/shard_map/ppermute | solution.py:30
  197.6 1.5 collective-permute-start.35
  199.1 9.9 %middle_back.1 = (bf16[512,1024]{1,0:T(8,128)(2,1)}, f32[4,1024]{1,0:T(4,128)}, bf16[512,256]{1,0:T(8,128)(2,1)}, bf16[512,256]{1,0:T(8,128)(2,1)}, bf16[512,256...) custom-call(s32[8]{0:T(128)} %broadcast_xor_fusion.owner_b.owner, ...), custom_call_target="tpu_custom_call" | custom-call | flops 2147483648 | bytes 10485760 | tf_op jit(solution)/shard_map/middle_back/pallas_call | solution.py:904
  209.1 1.9 collective-permute-done.35
  212.2 1.5 collective-permute-start.33
  214.3 1.2 add_convert_fusion.5
  215.5 6.0 %collective-permute-done.33.refs_5_ = bf16[512,256]{1,0:T(8,128)(2,1)S(1)} collective-permute-done((bf16[512,256]{1,0:T(8,128)(2,1)}, bf16[512,256]{1,0:T(8,128)(2,1)S(1)}, u32[]{:S(2)}, u32[]{:S(2)}) %collective-permute-start.33) | collective-permute-done | bytes 262176 | tf_op jit(solution)/shard_map/ppermute | solution.py:30
  221.6 3.8 %collective-permute-done.34.refs_6_ = bf16[512,256]{1,0:T(8,128)(2,1)S(1)} collective-permute-done((bf16[512,256]{1,0:T(8,128)(2,1)}, bf16[512,256]{1,0:T(8,128)(2,1)S(1)}, u32[]{:S(2)}, u32[]{:S(2)}) %collective-permute-start.34) | collective-permute-done | bytes 262176 | tf_op jit(solution)/shard_map/ppermute | solution.py:30
  225.3 1.4 collective-permute-start.37
  228.4 37.0 %attend_back.1 = (bf16[4,128,512]{2,1,0:T(8,128)(2,1)}, bf16[4,128,512]{2,1,0:T(8,128)(2,1)}, bf16[4,128,256]{2,1,0:T(8,128)(2,1)S(1)}, bf16[4,128,256]{2,1,0:T(...) custom-call(s32[8]{0:T(128)S(1)} %copy-done.3, ...), custom_call_target="tpu_custom_call" | custom-call | flops 10737418240 | bytes 20971520 | tf_op jit(solution)/shard_map/attend_back/pallas_call | solution.py:615
  267.8 1.6 add_convert_fusion.4
  271.2 1.5 collective-permute-start.43
  272.7 8.7 %collective-permute-done.41 = bf16[4,128,512]{2,1,0:T(8,128)(2,1)S(1)} collective-permute-done((bf16[4,128,512]{2,1,0:T(8,128)(2,1)}, bf16[4,128,512]{2,1,0:T(8,128)(2,1)S(1)}, u32[]{:S(2)}, u32[]{:S(2)}) %collective-permute-start.41) | collective-permute-done | bytes 524320 | tf_op jit(solution)/shard_map/ppermute | solution.py:30
  281.5 1.5 collective-permute-start.46
  283.1 1.8 collective-permute-done.42
  287.1 1.5 collective-permute-start.45
  288.6 1.9 add_convert_fusion
  290.6 8.9 %collective-permute-done.44 = bf16[2,128,512]{2,1,0:T(8,128)(2,1)S(1)} collective-permute-done((bf16[2,128,512]{2,1,0:T(8,128)(2,1)S(1)}, bf16[2,128,512]{2,1,0:T(8,128)(2,1)S(1)}, u32[]{:S(2)}, u32[]{:S(2)}) %collective-permute-start.44) | collective-permute-done | bytes 262176 | tf_op jit(solution)/shard_map/ppermute | solution.py:30
  299.5 1.5 collective-permute-start.50
  301.3 1.5 collective-permute-start.53
  303.7 4.6 %input_back.1 = bf16[512,1024]{1,0:T(8,128)(2,1)} custom-call(bf16[512,1024]{1,0:T(8,128)(2,1)} %get-tuple-element.216.refs_0_, bf16[512,1024]{1,0:T(8,128)(2,1)} %collective-permute-done.48.refs_1_, bf16[256,1024]{1,0:T(8,128)(2,1)} %copy-done.17, bf16[256,1024]{1,0:T(8,128)(2,1)} %collective-permute-done.46.refs_3_, bf16[512,1024]{1,0:T(8,128)(2,1)} %refs_4_.1, ...), custom_call_target="tpu_custom_call" | custom-call | flops 10485760 | bytes 7340032 | tf_op jit(solution)/shard_map/input_back/pallas_call | solution.py:936
  308.3 1.5 collective-permute-start.54
  309.8 1.1 collective-permute-done.52
  310.9 1.5 collective-permute-done.54
  312.4 2.7 collective-permute-start.55
  315.8 1.4 collective-permute-done.55
  317.2 1.5 collective-permute-start.56
  319.0 3.4 %collective-permute-done.56 = f32[104,128]{1,0:T(8,128)S(1)} collective-permute-done((f32[104,128]{1,0:T(8,128)S(1)}, f32[104,128]{1,0:T(8,128)S(1)}, u32[]{:S(2)}, u32[]{:S(2)}) %collective-permute-start.56) | collective-permute-done | bytes 53280 | tf_op jit(solution)/shard_map/ppermute | solution.py:30
  324.8 2.1 fusion.7
  (226 shorter events, 39.0 us)
Async XLA Ops:
  7.2 125.6 %all-gather.2.cloned.1.call-start = ((), (), s32[]{:S(2)}) async-start(), calls=%async_computation.1 | async-start | bytes 4718592 | tf_op jit(solution)/shard_map/all_gather | solution.py:1008
  8.9 13.4 %collective-permute-start.2 = (f32[96,128]{1,0:T(8,128)S(1)}, f32[96,128]{1,0:T(8,128)S(1)}, u32[]{:S(2)}, u32[]{:S(2)}) collective-permute-start(f32[96,128]{1,0:T(8,128)S(1)} %maximum_bitcast_fusion.2), channel_id=1, source_target_pairs={{0,3},{1,2},{2,1},{3,0},{4,7},{5,6},{6,5},{7,4},{8,11},{9,10},{10,... | collective-permute-start | bytes 147464 | tf_op jit(solution)/shard_map/ppermute | solution.py:30
  11.5 10.8 %collective-permute-start.1 = (f32[96,128]{1,0:T(8,128)S(1)}, f32[96,128]{1,0:T(8,128)S(1)}, u32[]{:S(2)}, u32[]{:S(2)}) collective-permute-start(f32[96,128]{1,0:T(8,128)S(1)} %maximum_bitcast_fusion.2), channel_id=1, source_target_pairs={{0,2},{1,3},{2,0},{3,1},{4,6},{5,7},{6,4},{7,5},{8,10},{9,11},{10,... | collective-permute-start | bytes 147464 | tf_op jit(solution)/shard_map/ppermute | solution.py:30
  12.1 10.2 %collective-permute-start = (f32[96,128]{1,0:T(8,128)S(1)}, f32[96,128]{1,0:T(8,128)}, u32[]{:S(2)}, u32[]{:S(2)}) collective-permute-start(f32[96,128]{1,0:T(8,128)S(1)} %maximum_bitcast_fusion.2), channel_id=1, source_target_pairs={{0,1},{1,0},{2,3},{3,2},{4,5},{5,4},{6,7},{7,6},{8,9},{9,8},{10,11... | collective-permute-start | bytes 147464 | tf_op jit(solution)/shard_map/ppermute | solution.py:30
  13.4 17.1 %collective-permute-start.6 = (bf16[1,128,512]{2,1,0:T(8,128)(2,1)S(1)}, bf16[1,128,512]{2,1,0:T(8,128)(2,1)S(1)}, u32[]{:S(2)}, u32[]{:S(2)}) collective-permute-start(bf16[1,128,512]{2,1,0:T(8,128)(2,1)S(1)} %bitcast.69), channel_id=1, source_target_pairs={{0,16},{4,20},{8,24},{12,28},{16,0},{20,4},{24,8},{28,12},{1,17},{... | collective-permute-start | bytes 393224 | tf_op jit(solution)/shard_map/ppermute | solution.py:30
  17.2 13.9 %collective-permute-start.9 = (bf16[1,128,512]{2,1,0:T(8,128)(2,1)S(1)}, bf16[1,128,512]{2,1,0:T(8,128)(2,1)S(1)}, u32[]{:S(2)}, u32[]{:S(2)}) collective-permute-start(bf16[1,128,512]{2,1,0:T(8,128)(2,1)S(1)} %maximum_bitcast_fusion), channel_id=1, source_target_pairs={{0,4},{4,0},{8,12},{12,8},{16,20},{20,16},{24,28},{28,24},{1,5},{5... | collective-permute-start | bytes 393224 | tf_op jit(solution)/shard_map/ppermute | solution.py:30
  23.1 25.1 %collective-permute-start.4 = (bf16[512,1024]{1,0:T(8,128)(2,1)}, bf16[512,1024]{1,0:T(8,128)(2,1)S(1)}, u32[]{:S(2)}, u32[]{:S(2)}) collective-permute-start(bf16[512,1024]{1,0:T(8,128)(2,1)} %unit.1.refs_0_.refs_7_), channel_id=1, source_target_pairs={{0,2},{1,3},{2,0},{3,1},{4,6},{5,7},{6,4},{7,5},{8,10},{9,11},{10,... | collective-permute-start | bytes 3145736 | tf_op jit(solution)/shard_map/ppermute | solution.py:30
  24.8 4.1 %collective-permute-start.13 = (f32[96,128]{1,0:T(8,128)S(1)}, f32[96,128]{1,0:T(8,128)S(1)}, u32[]{:S(2)}, u32[]{:S(2)}) collective-permute-start(f32[96,128]{1,0:T(8,128)S(1)} %bitcast.77), channel_id=1, source_target_pairs={{0,4},{4,0},{8,12},{12,8},{16,20},{20,16},{24,28},{28,24},{1,5},{5... | collective-permute-start | bytes 147464 | tf_op jit(solution)/shard_map/ppermute | solution.py:30
  28.9 8.0 %collective-permute-start.14 = (f32[96,128]{1,0:T(8,128)S(1)}, f32[96,128]{1,0:T(8,128)S(1)}, u32[]{:S(2)}, u32[]{:S(2)}) collective-permute-start(f32[96,128]{1,0:T(8,128)S(1)} %bitcast_add_fusion.1), channel_id=1, source_target_pairs={{0,8},{4,12},{8,0},{12,4},{16,24},{20,28},{24,16},{28,20},{1,9},{5... | collective-permute-start | bytes 147464 | tf_op jit(solution)/shard_map/ppermute | solution.py:30
  30.5 11.7 %collective-permute-start.7 = (bf16[2,128,512]{2,1,0:T(8,128)(2,1)S(1)}, bf16[2,128,512]{2,1,0:T(8,128)(2,1)S(1)}, u32[]{:S(2)}, u32[]{:S(2)}) collective-permute-start(bf16[2,128,512]{2,1,0:T(8,128)(2,1)S(1)} %pad_maximum_fusion.8), channel_id=1, source_target_pairs={{0,8},{4,12},{8,0},{12,4},{16,24},{20,28},{24,16},{28,20},{1,9},{5... | collective-permute-start | bytes 786440 | tf_op jit(solution)/shard_map/ppermute | solution.py:30
  31.1 14.4 %collective-permute-start.10 = (bf16[2,128,512]{2,1,0:T(8,128)(2,1)S(1)}, bf16[2,128,512]{2,1,0:T(8,128)(2,1)S(1)}, u32[]{:S(2)}, u32[]{:S(2)}) collective-permute-start(bf16[2,128,512]{2,1,0:T(8,128)(2,1)S(1)} %pad_maximum_fusion.9), channel_id=1, source_target_pairs={{0,16},{4,20},{8,24},{12,28},{16,0},{20,4},{24,8},{28,12},{1,17},{... | collective-permute-start | bytes 786440 | tf_op jit(solution)/shard_map/ppermute | solution.py:30
  36.9 12.7 %collective-permute-start.15 = (f32[96,128]{1,0:T(8,128)S(1)}, f32[96,128]{1,0:T(8,128)S(1)}, u32[]{:S(2)}, u32[]{:S(2)}) collective-permute-start(f32[96,128]{1,0:T(8,128)S(1)} %fusion.12), channel_id=1, source_target_pairs={{0,16},{4,20},{8,24},{12,28},{16,0},{20,4},{24,8},{28,12},{1,17},{... | collective-permute-start | bytes 147464 | tf_op jit(solution)/shard_map/ppermute | solution.py:30
  42.3 12.3 %collective-permute-start.8 = (bf16[4,128,512]{2,1,0:T(8,128)(2,1)S(1)}, bf16[4,128,512]{2,1,0:T(8,128)(2,1)S(1)}, u32[]{:S(2)}, u32[]{:S(2)}) collective-permute-start(bf16[4,128,512]{2,1,0:T(8,128)(2,1)S(1)} %pad_maximum_fusion.3), channel_id=1, source_target_pairs={{0,4},{4,0},{8,12},{12,8},{16,20},{20,16},{24,28},{28,24},{1,5},{5... | collective-permute-start | bytes 1572872 | tf_op jit(solution)/shard_map/ppermute | solution.py:30
  45.5 11.3 %collective-permute-start.11 = (bf16[4,128,512]{2,1,0:T(8,128)(2,1)S(1)}, bf16[4,128,512]{2,1,0:T(8,128)(2,1)S(1)}, u32[]{:S(2)}, u32[]{:S(2)}) collective-permute-start(bf16[4,128,512]{2,1,0:T(8,128)(2,1)S(1)} %pad_maximum_fusion.4), channel_id=1, source_target_pairs={{0,8},{4,12},{8,0},{12,4},{16,24},{20,28},{24,16},{28,20},{1,9},{5... | collective-permute-start | bytes 1572872 | tf_op jit(solution)/shard_map/ppermute | solution.py:30
  48.2 13.0 %collective-permute-start.12 = (bf16[256,1024]{1,0:T(8,128)(2,1)}, bf16[256,1024]{1,0:T(8,128)(2,1)}, u32[]{:S(2)}, u32[]{:S(2)}) collective-permute-start(bf16[256,1024]{1,0:T(8,128)(2,1)} %get-tuple-element.122), channel_id=1, source_target_pairs={{0,2},{1,3},{2,0},{3,1},{4,6},{5,7},{6,4},{7,5},{8,10},{9,11},{10,... | collective-permute-start | bytes 1572872 | tf_op jit(solution)/shard_map/ppermute | solution.py:30
  61.3 263.6 %reduce-scatter.2.cloned.1.call-start = ((), (), s32[]{:S(2)}) async-start(), calls=%async_computation.2 | async-start | bytes 4718592 | tf_op jit(solution)/shard_map/reduce_scatter | solution.py:1062
  61.3 8.8 %collective-permute-start.3 = (bf16[512,1024]{1,0:T(8,128)(2,1)S(1)}, bf16[512,1024]{1,0:T(8,128)(2,1)}, u32[]{:S(2)}, u32[]{:S(2)}) collective-permute-start(bf16[512,1024]{1,0:T(8,128)(2,1)S(1)} %copy-done.13), channel_id=1, source_target_pairs={{0,1},{1,0},{2,3},{3,2},{4,5},{5,4},{6,7},{7,6},{8,9},{9,8},{10,11... | collective-permute-start | bytes 3145736 | tf_op jit(solution)/shard_map/ppermute | solution.py:30
  61.4 8.7 %collective-permute-start.5 = (bf16[512,1024]{1,0:T(8,128)(2,1)}, bf16[512,1024]{1,0:T(8,128)(2,1)}, u32[]{:S(2)}, u32[]{:S(2)}) collective-permute-start(bf16[512,1024]{1,0:T(8,128)(2,1)} %copy-done.27), channel_id=1, source_target_pairs={{0,1},{1,0},{2,3},{3,2},{4,5},{5,4},{6,7},{7,6},{8,9},{9,8},{10,11... | collective-permute-start | bytes 3145736 | tf_op jit(solution)/shard_map/ppermute | solution.py:30
  66.9 24.7 %collective-permute-start.16 = (bf16[1024,256]{1,0:T(8,128)(2,1)}, bf16[1024,256]{1,0:T(8,128)(2,1)S(1)}, u32[]{:S(2)}, u32[]{:S(2)}) collective-permute-start(bf16[1024,256]{1,0:T(8,128)(2,1)} %placed_rows.1.refs_4_.refs_3_), channel_id=1, source_target_pairs={{0,2},{1,3},{2,0},{3,1},{4,6},{5,7},{6,4},{7,5},{8,10},{9,11},{10,... | collective-permute-start | bytes 1572872 | tf_op jit(solution)/shard_map/ppermute | solution.py:30
  68.1 24.3 %collective-permute-start.17 = (bf16[256,1024]{1,0:T(8,128)(2,1)}, bf16[256,1024]{1,0:T(8,128)(2,1)}, u32[]{:S(2)}, u32[]{:S(2)}) collective-permute-start(bf16[256,1024]{1,0:T(8,128)(2,1)} %get-tuple-element.134), channel_id=1, source_target_pairs={{0,2},{1,3},{2,0},{3,1},{4,6},{5,7},{6,4},{7,5},{8,10},{9,11},{10,... | collective-permute-start | bytes 1572872 | tf_op jit(solution)/shard_map/ppermute | solution.py:30
  70.1 24.7 %collective-permute-start.21 = (bf16[1024,256]{1,0:T(8,128)(2,1)}, bf16[1024,256]{1,0:T(8,128)(2,1)S(1)}, u32[]{:S(2)}, u32[]{:S(2)}) collective-permute-start(bf16[1024,256]{1,0:T(8,128)(2,1)} %placed_rows.1.refs_4_.refs_3_), channel_id=1, source_target_pairs={{0,1},{1,0},{2,3},{3,2},{4,5},{5,4},{6,7},{7,6},{8,9},{9,8},{10,11... | collective-permute-start | bytes 1572872 | tf_op jit(solution)/shard_map/ppermute | solution.py:30
  92.4 13.7 %collective-permute-start.22 = (bf16[1024,256]{1,0:T(8,128)(2,1)S(1)}, bf16[1024,256]{1,0:T(8,128)(2,1)}, u32[]{:S(2)}, u32[]{:S(2)}) collective-permute-start(bf16[1024,256]{1,0:T(8,128)(2,1)S(1)} %collective-permute-done.16.refs_6_.refs_5_), channel_id=1, source_target_pairs={{0,1},{1,0},{2,3},{3,2},{4,5},{5,4},{6,7},{7,6},{8,9},{9,8},{10,11... | collective-permute-start | bytes 1572872 | tf_op jit(solution)/shard_map/ppermute | solution.py:30
  92.4 3.3 collective-permute-start.18
  92.9 9.5 %collective-permute-start.19 = (bf16[512,256]{1,0:T(8,128)(2,1)}, bf16[512,256]{1,0:T(8,128)(2,1)}, u32[]{:S(2)}, u32[]{:S(2)}) collective-permute-start(bf16[512,256]{1,0:T(8,128)(2,1)} %get-tuple-element.137), channel_id=1, source_target_pairs={{0,2},{1,3},{2,0},{3,1},{4,6},{5,7},{6,4},{7,5},{8,10},{9,11},{10,... | collective-permute-start | bytes 786440 | tf_op jit(solution)/shard_map/ppermute | solution.py:30
  94.0 12.0 %collective-permute-start.20 = (bf16[512,256]{1,0:T(8,128)(2,1)}, bf16[512,256]{1,0:T(8,128)(2,1)}, u32[]{:S(2)}, u32[]{:S(2)}) collective-permute-start(bf16[512,256]{1,0:T(8,128)(2,1)} %get-tuple-element.138), channel_id=1, source_target_pairs={{0,3},{1,2},{2,1},{3,0},{4,7},{5,6},{6,5},{7,4},{8,11},{9,10},{10,... | collective-permute-start | bytes 786440 | tf_op jit(solution)/shard_map/ppermute | solution.py:30
  94.8 21.3 %collective-permute-start.24 = (bf16[512,1024]{1,0:T(8,128)(2,1)S(1)}, bf16[512,1024]{1,0:T(8,128)(2,1)}, u32[]{:S(2)}, u32[]{:S(2)}) collective-permute-start(bf16[512,1024]{1,0:T(8,128)(2,1)S(1)} %copy-done.5), channel_id=1, source_target_pairs={{0,1},{1,0},{2,3},{3,2},{4,5},{5,4},{6,7},{7,6},{8,9},{9,8},{10,11... | collective-permute-start | bytes 3145736 | tf_op jit(solution)/shard_map/ppermute | solution.py:30
  111.1 5.1 %collective-permute-start.23 = (bf16[512,1024]{1,0:T(8,128)(2,1)}, bf16[512,1024]{1,0:T(8,128)(2,1)}, u32[]{:S(2)}, u32[]{:S(2)}) collective-permute-start(bf16[512,1024]{1,0:T(8,128)(2,1)} %get-tuple-element.141.refs_0_), channel_id=1, source_target_pairs={{0,1},{1,0},{2,3},{3,2},{4,5},{5,4},{6,7},{7,6},{8,9},{9,8},{10,11... | collective-permute-start | bytes 3145736 | tf_op jit(solution)/shard_map/ppermute | solution.py:30
  112.7 35.0 %collective-permute-start.26 = (bf16[512,1024]{1,0:T(8,128)(2,1)}, bf16[512,1024]{1,0:T(8,128)(2,1)}, u32[]{:S(2)}, u32[]{:S(2)}) collective-permute-start(bf16[512,1024]{1,0:T(8,128)(2,1)} %get-tuple-element.141.refs_0_), channel_id=1, source_target_pairs={{0,2},{1,3},{2,0},{3,1},{4,6},{5,7},{6,4},{7,5},{8,10},{9,11},{10,... | collective-permute-start | bytes 3145736 | tf_op jit(solution)/shard_map/ppermute | solution.py:30
  116.1 31.6 %copy-start.21 = (bf16[512,1024]{1,0:T(8,128)(2,1)}, bf16[512,1024]{1,0:T(8,128)(2,1)S(1)}, u32[]{:S(2)}) copy-start(bf16[512,1024]{1,0:T(8,128)(2,1)S(1)} %constant_dynamic-update-slice_fusion.refs_2_) | copy-start | bytes 3145732
  116.1 31.7 %collective-permute-start.28 = (bf16[512,1024]{1,0:T(8,128)(2,1)S(1)}, bf16[512,1024]{1,0:T(8,128)(2,1)}, u32[]{:S(2)}, u32[]{:S(2)}) collective-permute-start(bf16[512,1024]{1,0:T(8,128)(2,1)S(1)} %constant_dynamic-update-slice_fusion.refs_2_), channel_id=1, source_target_pairs={{0,1},{1,0},{2,3},{3,2},{4,5},{5,4},{6,7},{7,6},{8,9},{9,8},{10,11... | collective-permute-start | bytes 3145736 | tf_op jit(solution)/shard_map/ppermute | solution.py:30
  147.7 2.9 collective-permute-start.27
  166.6 2.9 collective-permute-start.29
  166.8 26.5 %collective-permute-start.25 = (bf16[512,1024]{1,0:T(8,128)(2,1)}, bf16[512,1024]{1,0:T(8,128)(2,1)S(1)}, u32[]{:S(2)}, u32[]{:S(2)}) collective-permute-start(bf16[512,1024]{1,0:T(8,128)(2,1)} %get-tuple-element.144), channel_id=1, source_target_pairs={{0,1},{1,0},{2,3},{3,2},{4,5},{5,4},{6,7},{7,6},{8,9},{9,8},{10,11... | collective-permute-start | bytes 3145736 | tf_op jit(solution)/shard_map/ppermute | solution.py:30
  167.1 22.3 %collective-permute-start.31 = (bf16[512,1024]{1,0:T(8,128)(2,1)}, bf16[512,1024]{1,0:T(8,128)(2,1)}, u32[]{:S(2)}, u32[]{:S(2)}) collective-permute-start(bf16[512,1024]{1,0:T(8,128)(2,1)} %get-tuple-element.164), channel_id=1, source_target_pairs={{0,1},{1,0},{2,3},{3,2},{4,5},{5,4},{6,7},{7,6},{8,9},{9,8},{10,11... | collective-permute-start | bytes 3145736 | tf_op jit(solution)/shard_map/ppermute | solution.py:30
  172.1 25.5 %collective-permute-start.30 = (bf16[512,1024]{1,0:T(8,128)(2,1)}, bf16[512,1024]{1,0:T(8,128)(2,1)}, u32[]{:S(2)}, u32[]{:S(2)}) collective-permute-start(bf16[512,1024]{1,0:T(8,128)(2,1)} %add_convert_fusion.3), channel_id=1, source_target_pairs={{0,2},{1,3},{2,0},{3,1},{4,6},{5,7},{6,4},{7,5},{8,10},{9,11},{10,... | collective-permute-start | bytes 3145736 | tf_op jit(solution)/shard_map/ppermute | solution.py:30
  197.6 13.4 %collective-permute-start.35 = (bf16[256,1024]{1,0:T(8,128)(2,1)}, bf16[256,1024]{1,0:T(8,128)(2,1)S(1)}, u32[]{:S(2)}, u32[]{:S(2)}) collective-permute-start(bf16[256,1024]{1,0:T(8,128)(2,1)} %get-tuple-element.177), channel_id=1, source_target_pairs={{0,2},{1,3},{2,0},{3,1},{4,6},{5,7},{6,4},{7,5},{8,10},{9,11},{10,... | collective-permute-start | bytes 1572872 | tf_op jit(solution)/shard_map/ppermute | solution.py:30
  199.1 28.3 %copy-start.3 = (s32[8]{0:T(128)S(1)}, s32[8]{0:T(128)}, u32[]{:S(2)}) copy-start(s32[8]{0:T(128)} %broadcast_xor_fusion.1.owner_a) | copy-start | bytes 100
  199.1 28.3 %copy-start.4 = (f32[32,256]{1,0:T(8,128)S(1)}, f32[32,256]{1,0:T(8,128)}, u32[]{:S(2)}) copy-start(f32[32,256]{1,0:T(8,128)} %get-tuple-element.128.refs_1_) | copy-start | bytes 98308
  211.0 3.3 collective-permute-start.36
  211.7 3.8 %collective-permute-start.32 = (bf16[512,256]{1,0:T(8,128)(2,1)}, bf16[512,256]{1,0:T(8,128)(2,1)S(1)}, u32[]{:S(2)}, u32[]{:S(2)}) collective-permute-start(bf16[512,256]{1,0:T(8,128)(2,1)} %get-tuple-element.170), channel_id=1, source_target_pairs={{0,1},{1,0},{2,3},{3,2},{4,5},{5,4},{6,7},{7,6},{8,9},{9,8},{10,11... | collective-permute-start | bytes 786440 | tf_op jit(solution)/shard_map/ppermute | solution.py:30
  212.2 9.4 %collective-permute-start.33 = (bf16[512,256]{1,0:T(8,128)(2,1)}, bf16[512,256]{1,0:T(8,128)(2,1)S(1)}, u32[]{:S(2)}, u32[]{:S(2)}) collective-permute-start(bf16[512,256]{1,0:T(8,128)(2,1)} %get-tuple-element.171), channel_id=1, source_target_pairs={{0,2},{1,3},{2,0},{3,1},{4,6},{5,7},{6,4},{7,5},{8,10},{9,11},{10,... | collective-permute-start | bytes 786440 | tf_op jit(solution)/shard_map/ppermute | solution.py:30
  213.7 11.7 %collective-permute-start.34 = (bf16[512,256]{1,0:T(8,128)(2,1)}, bf16[512,256]{1,0:T(8,128)(2,1)S(1)}, u32[]{:S(2)}, u32[]{:S(2)}) collective-permute-start(bf16[512,256]{1,0:T(8,128)(2,1)} %get-tuple-element.172), channel_id=1, source_target_pairs={{0,3},{1,2},{2,1},{3,0},{4,7},{5,6},{6,5},{7,4},{8,11},{9,10},{10,... | collective-permute-start | bytes 786440 | tf_op jit(solution)/shard_map/ppermute | solution.py:30
  213.7 51.7 %collective-permute-start.38 = (bf16[8,128,256]{2,1,0:T(8,128)(2,1)}, bf16[8,128,256]{2,1,0:T(8,128)(2,1)S(1)}, u32[]{:S(2)}, u32[]{:S(2)}) collective-permute-start(bf16[8,128,256]{2,1,0:T(8,128)(2,1)} %get-tuple-element.189), channel_id=1, source_target_pairs={{0,1},{1,0},{2,3},{3,2},{4,5},{5,4},{6,7},{7,6},{8,9},{9,8},{10,11... | collective-permute-start | bytes 1572872 | tf_op jit(solution)/shard_map/ppermute | solution.py:30
  225.3 40.0 %collective-permute-start.37 = (bf16[256,1024]{1,0:T(8,128)(2,1)}, bf16[256,1024]{1,0:T(8,128)(2,1)S(1)}, u32[]{:S(2)}, u32[]{:S(2)}) collective-permute-start(bf16[256,1024]{1,0:T(8,128)(2,1)} %get-tuple-element.187), channel_id=1, source_target_pairs={{0,2},{1,3},{2,0},{3,1},{4,6},{5,7},{6,4},{7,5},{8,10},{9,11},{10,... | collective-permute-start | bytes 1572872 | tf_op jit(solution)/shard_map/ppermute | solution.py:30
  226.7 38.6 %collective-permute-start.39 = (bf16[8,128,256]{2,1,0:T(8,128)(2,1)S(1)}, bf16[8,128,256]{2,1,0:T(8,128)(2,1)S(1)}, u32[]{:S(2)}, u32[]{:S(2)}) collective-permute-start(bf16[8,128,256]{2,1,0:T(8,128)(2,1)S(1)} %add_convert_fusion.5), channel_id=1, source_target_pairs={{0,2},{1,3},{2,0},{3,1},{4,6},{5,7},{6,4},{7,5},{8,10},{9,11},{10,... | collective-permute-start | bytes 1572872 | tf_op jit(solution)/shard_map/ppermute | solution.py:30
  228.4 38.4 %copy-start.23 = (f32[4,1024]{1,0:T(4,128)S(1)}, f32[4,1024]{1,0:T(4,128)}, u32[]{:S(2)}) copy-start(f32[4,1024]{1,0:T(4,128)} %get-tuple-element.222) | copy-start | bytes 49156
  228.4 38.5 %copy-start.25 = (f32[1,1024]{1,0:T(1,128)S(1)}, f32[1,1024]{1,0:T(1,128)}, u32[]{:S(2)}) copy-start(f32[1,1024]{1,0:T(1,128)} %get-tuple-element.224) | copy-start | bytes 12292
  265.4 5.0 %collective-permute-start.40 = (bf16[512,1024]{1,0:T(8,128)(2,1)}, bf16[512,1024]{1,0:T(8,128)(2,1)S(1)}, u32[]{:S(2)}, u32[]{:S(2)}) collective-permute-start(bf16[512,1024]{1,0:T(8,128)(2,1)} %get-tuple-element.196), channel_id=1, source_target_pairs={{0,1},{1,0},{2,3},{3,2},{4,5},{5,4},{6,7},{7,6},{8,9},{9,8},{10,11... | collective-permute-start | bytes 3145736 | tf_op jit(solution)/shard_map/ppermute | solution.py:30
  266.3 20.8 %collective-permute-start.47 = (bf16[512,1024]{1,0:T(8,128)(2,1)}, bf16[512,1024]{1,0:T(8,128)(2,1)S(1)}, u32[]{:S(2)}, u32[]{:S(2)}) collective-permute-start(bf16[512,1024]{1,0:T(8,128)(2,1)} %get-tuple-element.212), channel_id=1, source_target_pairs={{0,1},{1,0},{2,3},{3,2},{4,5},{5,4},{6,7},{7,6},{8,9},{9,8},{10,11... | collective-permute-start | bytes 3145736 | tf_op jit(solution)/shard_map/ppermute | solution.py:30
  267.2 14.3 %collective-permute-start.41 = (bf16[4,128,512]{2,1,0:T(8,128)(2,1)}, bf16[4,128,512]{2,1,0:T(8,128)(2,1)S(1)}, u32[]{:S(2)}, u32[]{:S(2)}) collective-permute-start(bf16[4,128,512]{2,1,0:T(8,128)(2,1)} %get-tuple-element.205), channel_id=1, source_target_pairs={{0,4},{4,0},{8,12},{12,8},{16,20},{20,16},{24,28},{28,24},{1,5},{5... | collective-permute-start | bytes 1572872 | tf_op jit(solution)/shard_map/ppermute | solution.py:30
  269.5 15.4 %collective-permute-start.42 = (bf16[4,128,512]{2,1,0:T(8,128)(2,1)S(1)}, bf16[4,128,512]{2,1,0:T(8,128)(2,1)S(1)}, u32[]{:S(2)}, u32[]{:S(2)}) collective-permute-start(bf16[4,128,512]{2,1,0:T(8,128)(2,1)S(1)} %pad_maximum_fusion.6), channel_id=1, source_target_pairs={{0,8},{4,12},{8,0},{12,4},{16,24},{20,28},{24,16},{28,20},{1,9},{5... | collective-permute-start | bytes 1572872 | tf_op jit(solution)/shard_map/ppermute | solution.py:30
  271.2 14.9 %collective-permute-start.43 = (bf16[256,1024]{1,0:T(8,128)(2,1)S(1)}, bf16[256,1024]{1,0:T(8,128)(2,1)S(1)}, u32[]{:S(2)}, u32[]{:S(2)}) collective-permute-start(bf16[256,1024]{1,0:T(8,128)(2,1)S(1)} %get-tuple-element.241), channel_id=1, source_target_pairs={{0,2},{1,3},{2,0},{3,1},{4,6},{5,7},{6,4},{7,5},{8,10},{9,11},{10,... | collective-permute-start | bytes 1572872 | tf_op jit(solution)/shard_map/ppermute | solution.py:30
  272.7 28.6 %collective-permute-start.51 = (f32[104,128]{1,0:T(8,128)S(1)}, f32[104,128]{1,0:T(8,128)S(1)}, u32[]{:S(2)}, u32[]{:S(2)}) collective-permute-start(f32[104,128]{1,0:T(8,128)S(1)} %maximum_bitcast_fusion.1), channel_id=1, source_target_pairs={{0,3},{1,2},{2,1},{3,0},{4,7},{5,6},{6,5},{7,4},{8,11},{9,10},{10,... | collective-permute-start | bytes 159752 | tf_op jit(solution)/shard_map/ppermute | solution.py:30
  281.5 19.7 %collective-permute-start.46 = (bf16[256,1024]{1,0:T(8,128)(2,1)S(1)}, bf16[256,1024]{1,0:T(8,128)(2,1)}, u32[]{:S(2)}, u32[]{:S(2)}) collective-permute-start(bf16[256,1024]{1,0:T(8,128)(2,1)S(1)} %get-tuple-element.240), channel_id=1, source_target_pairs={{0,2},{1,3},{2,0},{3,1},{4,6},{5,7},{6,4},{7,5},{8,10},{9,11},{10,... | collective-permute-start | bytes 1572872 | tf_op jit(solution)/shard_map/ppermute | solution.py:30
  284.9 18.7 %collective-permute-start.48 = (bf16[512,1024]{1,0:T(8,128)(2,1)S(1)}, bf16[512,1024]{1,0:T(8,128)(2,1)}, u32[]{:S(2)}, u32[]{:S(2)}) collective-permute-start(bf16[512,1024]{1,0:T(8,128)(2,1)S(1)} %copy-done.28), channel_id=1, source_target_pairs={{0,1},{1,0},{2,3},{3,2},{4,5},{5,4},{6,7},{7,6},{8,9},{9,8},{10,11... | collective-permute-start | bytes 3145736 | tf_op jit(solution)/shard_map/ppermute | solution.py:30
  286.1 13.4 %collective-permute-start.44 = (bf16[2,128,512]{2,1,0:T(8,128)(2,1)S(1)}, bf16[2,128,512]{2,1,0:T(8,128)(2,1)S(1)}, u32[]{:S(2)}, u32[]{:S(2)}) collective-permute-start(bf16[2,128,512]{2,1,0:T(8,128)(2,1)S(1)} %get-tuple-element.209), channel_id=1, source_target_pairs={{0,8},{4,12},{8,0},{12,4},{16,24},{20,28},{24,16},{28,20},{1,9},{5... | collective-permute-start | bytes 786440 | tf_op jit(solution)/shard_map/ppermute | solution.py:30
  287.1 13.9 %collective-permute-start.45 = (bf16[2,128,512]{2,1,0:T(8,128)(2,1)S(1)}, bf16[2,128,512]{2,1,0:T(8,128)(2,1)S(1)}, u32[]{:S(2)}, u32[]{:S(2)}) collective-permute-start(bf16[2,128,512]{2,1,0:T(8,128)(2,1)S(1)} %get-tuple-element.210), channel_id=1, source_target_pairs={{0,16},{4,20},{8,24},{12,28},{16,0},{20,4},{24,8},{28,12},{1,17},{... | collective-permute-start | bytes 786440 | tf_op jit(solution)/shard_map/ppermute | solution.py:30
  299.5 4.1 %collective-permute-start.50 = (f32[104,128]{1,0:T(8,128)S(1)}, f32[104,128]{1,0:T(8,128)S(1)}, u32[]{:S(2)}, u32[]{:S(2)}) collective-permute-start(f32[104,128]{1,0:T(8,128)S(1)} %maximum_bitcast_fusion.1), channel_id=1, source_target_pairs={{0,2},{1,3},{2,0},{3,1},{4,6},{5,7},{6,4},{7,5},{8,10},{9,11},{10,... | collective-permute-start | bytes 159752 | tf_op jit(solution)/shard_map/ppermute | solution.py:30
  301.0 2.6 collective-permute-start.49
  301.2 9.7 %collective-permute-start.52 = (bf16[1,128,512]{2,1,0:T(8,128)(2,1)S(1)}, bf16[1,128,512]{2,1,0:T(8,128)(2,1)S(1)}, u32[]{:S(2)}, u32[]{:S(2)}) collective-permute-start(bf16[1,128,512]{2,1,0:T(8,128)(2,1)S(1)} %get-tuple-element.227), channel_id=1, source_target_pairs={{0,16},{4,20},{8,24},{12,28},{16,0},{20,4},{24,8},{28,12},{1,17},{... | collective-permute-start | bytes 393224 | tf_op jit(solution)/shard_map/ppermute | solution.py:30
  301.3 9.6 %collective-permute-start.53 = (bf16[1,128,512]{2,1,0:T(8,128)(2,1)S(1)}, bf16[1,128,512]{2,1,0:T(8,128)(2,1)S(1)}, u32[]{:S(2)}, u32[]{:S(2)}) collective-permute-start(bf16[1,128,512]{2,1,0:T(8,128)(2,1)S(1)} %get-tuple-element.229), channel_id=1, source_target_pairs={{0,4},{4,0},{8,12},{12,8},{16,20},{20,16},{24,28},{28,24},{1,5},{5... | collective-permute-start | bytes 393224 | tf_op jit(solution)/shard_map/ppermute | solution.py:30
  308.3 4.1 %collective-permute-start.54 = (f32[104,128]{1,0:T(8,128)S(1)}, f32[104,128]{1,0:T(8,128)S(1)}, u32[]{:S(2)}, u32[]{:S(2)}) collective-permute-start(f32[104,128]{1,0:T(8,128)S(1)} %bitcast.76), channel_id=1, source_target_pairs={{0,4},{4,0},{8,12},{12,8},{16,20},{20,16},{24,28},{28,24},{1,5},{5... | collective-permute-start | bytes 159752 | tf_op jit(solution)/shard_map/ppermute | solution.py:30
  312.4 4.8 %collective-permute-start.55 = (f32[104,128]{1,0:T(8,128)S(1)}, f32[104,128]{1,0:T(8,128)S(1)}, u32[]{:S(2)}, u32[]{:S(2)}) collective-permute-start(f32[104,128]{1,0:T(8,128)S(1)} %bitcast_add_fusion), channel_id=1, source_target_pairs={{0,8},{4,12},{8,0},{12,4},{16,24},{20,28},{24,16},{28,20},{1,9},{5... | collective-permute-start | bytes 159752 | tf_op jit(solution)/shard_map/ppermute | solution.py:30
  317.2 5.1 %collective-permute-start.56 = (f32[104,128]{1,0:T(8,128)S(1)}, f32[104,128]{1,0:T(8,128)S(1)}, u32[]{:S(2)}, u32[]{:S(2)}) collective-permute-start(f32[104,128]{1,0:T(8,128)S(1)} %fusion.11), channel_id=1, source_target_pairs={{0,16},{4,20},{8,24},{12,28},{16,0},{20,4},{24,8},{28,12},{1,17},{... | collective-permute-start | bytes 159752 | tf_op jit(solution)/shard_map/ppermute | solution.py:30
  (30 other events, 281.6 us)
Sparse Core Ops, SparseCore 0:
  61.4 71.3 all-gather.1
  189.5 85.6 reduce-scatter.1

commit v3 on v2

--- a/solution.py
+++ b/solution.py
@@ -98,11 +98,11 @@
     return [p if k == 0 else swapped(p, axis, k) for k, p in enumerate(parts)]
 
 
-def summed_everywhere(value, axes):
+def summed_everywhere(value, axes, direct=False):
     size = value.shape[0]
     value = jnp.pad(value, (0, -size % 1024)).reshape(-1, 128)
     for axis in axes:
-        if lax.axis_size(axis) <= 4:
+        if direct:
             value = total([value] + [swapped(value, axis, k) for k in range(1, lax.axis_size(axis))])
         else:
             for bit in bits_of(axis):
@@ -1002,8 +1002,8 @@
     first_going, last_going = output_cotangent[: near // 2], output_cotangent[near // 2 :]
     first_going, unit_far = together(first_going, unit_far)
     cotangent_first = far(first_going, "tensor")
-    feed_flat, first_blocks, last_blocks, cotangent_first, packed = together(
-        feed_flat, first_blocks, last_blocks, cotangent_first, packed
+    feed_flat, first_blocks, last_blocks, packed, unit_far = together(
+        feed_flat, first_blocks, last_blocks, packed, unit_far
     )
     feed_full = lax.all_gather(feed_flat, "dp", axis=0, tiled=True)
     unit_parts = gathered_parts(unit_near, unit_far, "tensor")
@@ -1018,6 +1018,7 @@
     norm_two = jnp.stack([vectors_full[4], vectors_full[2], vectors_full[3]])
 
 
+    last_blocks, cotangent_first = together(last_blocks, cotangent_first)
     out_group = placed_rows(last_blocks, owner_b, width)
     out_far = far(out_group, "tensor")
     last_going, out_group = together(last_going, out_group)
@@ -1106,7 +1107,7 @@
     packed = jnp.concatenate(
         [late.reshape(-1), sums_two.reshape(-1), head_sums.reshape(-1), hidden_sums.reshape(-1)]
     )
-    packed = summed_everywhere(packed, ("tensor",))
+    packed = summed_everywhere(packed, ("dp",))
     far_sum = added(far_rows[0], swapped(far_rows[1], "tensor", 1))
     far_sum, first_keep, last_keep, *near_rows = together(
         far_sum, first_keep, last_keep, *near_rows
@@ -1130,7 +1131,7 @@
     out_weight_grad = last_raw[:, width:]
     last_raw = last_raw[:, :width]
 
-    packed = summed_everywhere(packed, ("dp",))
+    packed = summed_everywhere(packed, ("tensor",), direct=True)
     by_feature = packed[: 9 * features].reshape(9, features)
     hidden_sums = packed[9 * features :]
     vectors_grad = lax.dynamic_slice_in_dim(by_feature, index * piece, piece, axis=1)

time: 340 us -> 334 us (0.982)
  starting transfers between devices: 47.5 us -> 41.7 us
    all_gather x1, waiting for transfers between devices: 16.6 us -> 3.78 us  [per_device(): feed_full = lax.all_gather(feed_flat, 'dp', axis=0, tiled=True)]
    ppermute x57 -> x56, waiting for transfers between devices: 87.9 us -> 99.3 us  [swapped(): return lax.ppermute(value, axis, [(i, i ^ bit) for i in range(count)])]
    ppermute x57 -> x56, starting transfers between devices: 47.4 us -> 41.7 us  [swapped(): return lax.ppermute(value, axis, [(i, i ^ bit) for i in range(count)])]
    unnamed x79 -> x83, local copies, waits for them, and re-layouts: 7.27 us -> 8.61 us
  transfers between devices with their start and end apart: 59 -> 58, of which waited for: 27 -> 23; matrix products, arithmetic and copies ran while one was open for 9% -> 9% of each run, Pallas kernels for 34% -> 35%
where the time goes in v3:
time: 334 us; the launch traced here: 328 us
  Pallas kernels  128 us (38%)
  waiting for transfers between devices  103 us (31%)
  starting transfers between devices  41.7 us (12%)
  local copies, waits for them, and re-layouts  20.5 us (6%)
  other arithmetic  18.7 us (6%)
  between operations  15.6 us (5%)
    ppermute x56, waiting for transfers between devices, swapped(): return lax.ppermute(value, axis, [(i, i ^ bit) for i in range(count)])  99.3 us
    ppermute x56, starting transfers between devices, swapped(): return lax.ppermute(value, axis, [(i, i ^ bit) for i in range(count)])  41.7 us
    pallas_call x1, Pallas kernels, attend_back(): pl.pallas_call(functools.partial(attend_back_kernel, heads, len(unit)), g...  36.9 us
    pallas_call x2, Pallas kernels, feed(): pl.pallas_call(functools.partial(feed_kernel, here, len(stacks)), grid=(h...  29.9 us
    pallas_call x1, Pallas kernels, project_attend(): pl.pallas_call(functools.partial(project_attend_kernel, heads, len(unit))...  21.5 us
    pallas_call x1, Pallas kernels, feed_grads(): pl.pallas_call(feed_grads_kernel, grid=(rows // (2 * TILE),), out_shape=[...  15.8 us
    pallas_call x1, Pallas kernels, middle_back(): pl.pallas_call(functools.partial(middle_back_kernel, len(terms), parts),...  9.9 us
    unnamed x83, local copies, waits for them, and re-layouts  8.61 us
  transfers between devices with their start and end apart: 58, of which 23 were waited for; matrix products, arithmetic and copies ran while one was open for 9% of the time, Pallas kernels for 35%

profile of v3, /device:TPU:0, one launch (start us, length us, event | category | flops | bytes accessed | tf_op | source)
XLA Modules:
  0.0 327.8 jit_solution(9096813050939321791)
XLA Ops:
  9.6 1.1 copy.28
  10.8 3.6 %collective-permute-start.3 = (bf16[1,128,512]{2,1,0:T(8,128)(2,1)S(1)}, bf16[1,128,512]{2,1,0:T(8,128)(2,1)S(1)}, u32[]{:S(2)}, u32[]{:S(2)}) collective-permute-start(bf16[1,128,512]{2,1,0:T(8,128)(2,1)S(1)} %bitcast.71), channel_id=1, source_target_pairs={{0,16},{4,20},{8,24},{12,28},{16,0},{20,4},{24,8},{28,12},{1,17},{... | collective-permute-start | bytes 393224 | tf_op jit(solution)/shard_map/ppermute | solution.py:30
  15.4 1.6 collective-permute-start.6
  16.9 1.0 fusion.8
  18.0 1.7 collective-permute-start.1
  20.5 2.5 unit.1.refs_0_.refs_7_
  24.4 1.6 collective-permute-start.4
  26.0 1.2 collective-permute-done.9
  27.2 1.6 collective-permute-start.10
  29.3 5.1 %collective-permute-done.10 = f32[96,128]{1,0:T(8,128)S(1)} collective-permute-done((f32[96,128]{1,0:T(8,128)S(1)}, f32[96,128]{1,0:T(8,128)S(1)}, u32[]{:S(2)}, u32[]{:S(2)}) %collective-permute-start.10) | collective-permute-done | bytes 49184 | tf_op jit(solution)/shard_map/ppermute | solution.py:30
  34.4 3.1 collective-permute-start.11
  37.6 2.1 collective-permute-start.5
  39.7 3.7 %collective-permute-done.7 = bf16[2,128,512]{2,1,0:T(8,128)(2,1)S(1)} collective-permute-done((bf16[2,128,512]{2,1,0:T(8,128)(2,1)S(1)}, bf16[2,128,512]{2,1,0:T(8,128)(2,1)S(1)}, u32[]{:S(2)}, u32[]{:S(2)}) %collective-permute-start.7) | collective-permute-done | bytes 262176 | tf_op jit(solution)/shard_map/ppermute | solution.py:30
  44.1 5.4 %collective-permute-done.5 = bf16[4,128,512]{2,1,0:T(8,128)(2,1)S(1)} collective-permute-done((bf16[4,128,512]{2,1,0:T(8,128)(2,1)S(1)}, bf16[4,128,512]{2,1,0:T(8,128)(2,1)S(1)}, u32[]{:S(2)}, u32[]{:S(2)}) %collective-permute-start.5) | collective-permute-done | bytes 524320 | tf_op jit(solution)/shard_map/ppermute | solution.py:30
  49.5 1.1 pad_maximum_fusion.refs_4_
  50.6 4.7 %collective-permute-done.8 = bf16[4,128,512]{2,1,0:T(8,128)(2,1)S(1)} collective-permute-done((bf16[4,128,512]{2,1,0:T(8,128)(2,1)S(1)}, bf16[4,128,512]{2,1,0:T(8,128)(2,1)S(1)}, u32[]{:S(2)}, u32[]{:S(2)}) %collective-permute-start.8) | collective-permute-done | bytes 524320 | tf_op jit(solution)/shard_map/ppermute | solution.py:30
  55.2 1.1 pad_maximum_fusion.1.refs_5_.blocks_ref
  59.8 12.9 %collective-permute-done.14 = bf16[256,1024]{1,0:T(8,128)(2,1)} collective-permute-done((bf16[256,1024]{1,0:T(8,128)(2,1)}, bf16[256,1024]{1,0:T(8,128)(2,1)}, u32[]{:S(2)}, u32[]{:S(2)}) %collective-permute-start.14) | collective-permute-done | bytes 524320 | tf_op jit(solution)/shard_map/ppermute | solution.py:30
  72.7 2.1 placed_rows.1.refs_4_.refs_3_
  75.0 1.7 collective-permute-start.16
  78.0 21.5 %project_attend.1 = (bf16[512,256]{1,0:T(8,128)(2,1)}, bf16[512,256]{1,0:T(8,128)(2,1)}, bf16[512,256]{1,0:T(8,128)(2,1)}, bf16[512,256]{1,0:T(8,128)(2,1)}, bf1...) custom-call(s32[8]{0:T(128)} %broadcast_xor_fusion.1.owner_a, ...), custom_call_target="tpu_custom_call" | custom-call | flops 5368709120 | bytes 10485760 | tf_op jit(solution)/shard_map/project_attend/pallas_call | solution.py:487
  100.5 1.5 collective-permute-start.19
  103.4 6.2 %collective-permute-done.18.refs_2_.refs_9_ = bf16[512,256]{1,0:T(8,128)(2,1)} collective-permute-done((bf16[512,256]{1,0:T(8,128)(2,1)}, bf16[512,256]{1,0:T(8,128)(2,1)}, u32[]{:S(2)}, u32[]{:S(2)}) %collective-permute-start.18) | collective-permute-done | bytes 262176 | tf_op jit(solution)/shard_map/ppermute | solution.py:30
  109.6 4.7 %collective-permute-done.19.refs_3_.refs_10_ = bf16[512,256]{1,0:T(8,128)(2,1)} collective-permute-done((bf16[512,256]{1,0:T(8,128)(2,1)}, bf16[512,256]{1,0:T(8,128)(2,1)}, u32[]{:S(2)}, u32[]{:S(2)}) %collective-permute-start.19) | collective-permute-done | bytes 262176 | tf_op jit(solution)/shard_map/ppermute | solution.py:30
  114.3 5.0 %middle.1 = (bf16[512,1024]{1,0:T(8,128)(2,1)}, bf16[512,1024]{1,0:T(8,128)(2,1)}) custom-call(bf16[512,256]{1,0:T(8,128)(2,1)} %get-tuple-element.139.refs_0_.refs_7_, bf16[512,256]{1,0:T(8,128)(2,1)} %copy-done.12, bf16[512,256]{1,0:T(8,128)(2,1)} %collective-permute-done.18.refs_2_.refs_9_, bf16[512,256]{1,0:T(8,128)(2,1)} %collective-permute-done.19.refs_3_.refs_10_, ...), custom_call_target="tpu_custom_call" | custom-call | flops 1073741824 | bytes 6291456 | tf_op jit(solution)/shard_map/middle/pallas_call | solution.py:839
  120.5 1.1 constant_dynamic-update-slice_fusion.1
  121.6 1.1 constant_dynamic-update-slice_fusion.refs_2_
  122.7 3.8 %all-gather.2.cloned.1.call-done.refs_4_ = bf16[1024,2048]{1,0:T(8,128)(2,1)} async-done(((bf16[128,2048]{1,0:T(8,128)(2,1)}), bf16[1024,2048]{1,0:T(8,128)(2,1)}) %all-gather.2.cloned.1.call-update) | async-done | bytes 4194320 | tf_op jit(solution)/shard_map/all_gather | solution.py:1008
  126.5 14.9 %feed.2 = (bf16[512,1024]{1,0:T(8,128)(2,1)}, bf16[512,1024]{1,0:T(8,128)(2,1)}, bf16[512,1024]{1,0:T(8,128)(2,1)}, bf16[512,1024]{1,0:T(8,128)(2,1)}, bf16[2048...) custom-call(bf16[512,1024]{1,0:T(8,128)(2,1)} %get-tuple-element.145.re, ...), custom_call_target="tpu_custom_call" | custom-call | flops 8589934592 | bytes 20971520 | tf_op jit(solution)/shard_map/feed/pallas_call | solution.py:714
  141.5 4.3 %collective-permute-done.25.refs_0_ = bf16[512,1024]{1,0:T(8,128)(2,1)} collective-permute-done((bf16[512,1024]{1,0:T(8,128)(2,1)}, bf16[512,1024]{1,0:T(8,128)(2,1)}, u32[]{:S(2)}, u32[]{:S(2)}) %collective-permute-start.25) | collective-permute-done | bytes 1048608 | tf_op jit(solution)/shard_map/ppermute | solution.py:30
  145.8 2.9 collective-permute-done.26.refs_1_
  148.7 1.0 copy-done.31
  149.6 15.0 %feed.3 = (bf16[512,1024]{1,0:T(8,128)(2,1)}, bf16[512,1024]{1,0:T(8,128)(2,1)}, bf16[512,1024]{1,0:T(8,128)(2,1)}, bf16[512,1024]{1,0:T(8,128)(2,1)}, bf16[2048...) custom-call(bf16[512,1024]{1,0:T(8,128)(2,1)} %collective-permute-do, ...), custom_call_target="tpu_custom_call", output_to_operand_aliasing={{4}: (6, {}), {5}: (7, {}), {6}: (8, {}), {7}: (9, {})} | custom-call | flops 8589934592 | bytes 20971520 | tf_op jit(solution)/shard_map/feed/pallas_call | solution.py:714
  165.4 2.2 collective-permute-done.28
  167.6 2.6 add_convert_fusion.3
  170.4 15.8 %feed_grads.1 = (bf16[1024,2048]{1,0:T(8,128)(2,1)}, f32[1,1024]{1,0:T(1,128)}) custom-call(bf16[2048,1024]{1,0:T(8,128)(2,1)} %get-tuple-element.162.normed_ref, bf16[2048,1024]{1,0:T(8,128)(2,1)} %get-tuple-element.163.grad_ref, bf16[2048,1024]{1,0:T(8,128)(2,1)} %get-tuple-element.164.grads_ref, bf16[2048,1024]{1,0:T(8,128)(2,1)} %get-tuple-element.165.active_ref), custom_call_target="tpu_custom_call" | custom-call | flops 8589934592 | bytes 16777216 | tf_op jit(solution)/shard_map/feed_grads/pallas_call | solution.py:762
  186.3 1.2 copy-done.11
  187.5 1.6 add_convert_fusion.2
  189.1 1.1 fusion.7
  190.2 5.5 %collective-permute-done.29.refs_2_ = bf16[512,1024]{1,0:T(8,128)(2,1)} collective-permute-done((bf16[512,1024]{1,0:T(8,128)(2,1)}, bf16[512,1024]{1,0:T(8,128)(2,1)}, u32[]{:S(2)}, u32[]{:S(2)}) %collective-permute-start.29) | collective-permute-done | bytes 1048608 | tf_op jit(solution)/shard_map/ppermute | solution.py:30
  196.0 9.9 %middle_back.1 = (bf16[512,1024]{1,0:T(8,128)(2,1)}, f32[4,1024]{1,0:T(4,128)}, bf16[512,256]{1,0:T(8,128)(2,1)}, bf16[512,256]{1,0:T(8,128)(2,1)}, bf16[512,256...) custom-call(s32[8]{0:T(128)} %broadcast_xor_fusion.owner_b.owner, ...), custom_call_target="tpu_custom_call" | custom-call | flops 2147483648 | bytes 10485760 | tf_op jit(solution)/shard_map/middle_back/pallas_call | solution.py:904
  205.9 3.1 collective-permute-done.34
  210.5 1.1 collective-permute-start.33
  212.4 1.2 add_convert_fusion.5
  213.6 6.0 %collective-permute-done.32.refs_5_ = bf16[512,256]{1,0:T(8,128)(2,1)S(1)} collective-permute-done((bf16[512,256]{1,0:T(8,128)(2,1)}, bf16[512,256]{1,0:T(8,128)(2,1)S(1)}, u32[]{:S(2)}, u32[]{:S(2)}) %collective-permute-start.32) | collective-permute-done | bytes 262176 | tf_op jit(solution)/shard_map/ppermute | solution.py:30
  219.6 3.7 %collective-permute-done.33.refs_6_ = bf16[512,256]{1,0:T(8,128)(2,1)S(1)} collective-permute-done((bf16[512,256]{1,0:T(8,128)(2,1)}, bf16[512,256]{1,0:T(8,128)(2,1)S(1)}, u32[]{:S(2)}, u32[]{:S(2)}) %collective-permute-start.33) | collective-permute-done | bytes 262176 | tf_op jit(solution)/shard_map/ppermute | solution.py:30
  223.9 1.4 collective-permute-start.38
  225.4 0.9 copy-done.2
  226.4 36.9 %attend_back.1 = (bf16[4,128,512]{2,1,0:T(8,128)(2,1)}, bf16[4,128,512]{2,1,0:T(8,128)(2,1)}, bf16[4,128,256]{2,1,0:T(8,128)(2,1)S(1)}, bf16[4,128,256]{2,1,0:T(...) custom-call(s32[8]{0:T(128)S(1)} %copy-done.3, ...), custom_call_target="tpu_custom_call" | custom-call | flops 10737418240 | bytes 20971520 | tf_op jit(solution)/shard_map/attend_back/pallas_call | solution.py:615
  265.7 1.6 add_convert_fusion.4
  267.5 1.9 collective-permute-start.48
  270.6 10.0 %collective-permute-done.48 = f32[104,128]{1,0:T(8,128)S(1)} collective-permute-done((f32[104,128]{1,0:T(8,128)S(1)}, f32[104,128]{1,0:T(8,128)S(1)}, u32[]{:S(2)}, u32[]{:S(2)}) %collective-permute-start.48) | collective-permute-done | bytes 53280 | tf_op jit(solution)/shard_map/ppermute | solution.py:30
  281.9 1.3 collective-permute-done.42.refs_2_
  283.2 1.7 collective-permute-start.43
  284.9 1.9 add_convert_fusion
  287.4 1.4 collective-permute-start.44
  288.9 1.6 collective-permute-start.50
  290.5 13.6 %collective-permute-done.44 = bf16[2,128,512]{2,1,0:T(8,128)(2,1)S(1)} collective-permute-done((bf16[2,128,512]{2,1,0:T(8,128)(2,1)S(1)}, bf16[2,128,512]{2,1,0:T(8,128)(2,1)S(1)}, u32[]{:S(2)}, u32[]{:S(2)}) %collective-permute-start.44) | collective-permute-done | bytes 262176 | tf_op jit(solution)/shard_map/ppermute | solution.py:30
  306.4 4.6 %input_back.1 = bf16[512,1024]{1,0:T(8,128)(2,1)} custom-call(bf16[512,1024]{1,0:T(8,128)(2,1)} %get-tuple-element.220.refs_0_, bf16[512,1024]{1,0:T(8,128)(2,1)} %copy-done.15, bf16[256,1024]{1,0:T(8,128)(2,1)} %copy-done.18, bf16[256,1024]{1,0:T(8,128)(2,1)} %copy-done.20, bf16[512,1024]{1,0:T(8,128)(2,1)} %refs_4_.1, ...), custom_call_target="tpu_custom_call" | custom-call | flops 10485760 | bytes 7340032 | tf_op jit(solution)/shard_map/input_back/pallas_call | solution.py:936
  311.4 1.0 collective-permute-start.54
  313.2 1.0 fusion.1
  315.1 1.0 collective-permute-done.54
  316.4 0.9 copy.32
  318.6 2.1 fusion.9
  (229 shorter events, 30.6 us)
Async XLA Ops:
  7.2 119.3 %all-gather.2.cloned.1.call-start = ((), (), s32[]{:S(2)}) async-start(), calls=%async_computation.1 | async-start | bytes 4718592 | tf_op jit(solution)/shard_map/all_gather | solution.py:1008
  9.0 9.0 %collective-permute-start = (f32[96,128]{1,0:T(8,128)S(1)}, f32[96,128]{1,0:T(8,128)S(1)}, u32[]{:S(2)}, u32[]{:S(2)}) collective-permute-start(f32[96,128]{1,0:T(8,128)S(1)} %maximum_bitcast_fusion.2), channel_id=1, source_target_pairs={{0,1},{1,0},{2,3},{3,2},{4,5},{5,4},{6,7},{7,6},{8,9},{9,8},{10,11... | collective-permute-start | bytes 147464 | tf_op jit(solution)/shard_map/ppermute | solution.py:30
  10.8 13.5 %collective-permute-start.3 = (bf16[1,128,512]{2,1,0:T(8,128)(2,1)S(1)}, bf16[1,128,512]{2,1,0:T(8,128)(2,1)S(1)}, u32[]{:S(2)}, u32[]{:S(2)}) collective-permute-start(bf16[1,128,512]{2,1,0:T(8,128)(2,1)S(1)} %bitcast.71), channel_id=1, source_target_pairs={{0,16},{4,20},{8,24},{12,28},{16,0},{20,4},{24,8},{28,12},{1,17},{... | collective-permute-start | bytes 393224 | tf_op jit(solution)/shard_map/ppermute | solution.py:30
  15.4 13.5 %collective-permute-start.6 = (bf16[1,128,512]{2,1,0:T(8,128)(2,1)S(1)}, bf16[1,128,512]{2,1,0:T(8,128)(2,1)S(1)}, u32[]{:S(2)}, u32[]{:S(2)}) collective-permute-start(bf16[1,128,512]{2,1,0:T(8,128)(2,1)S(1)} %maximum_bitcast_fusion), channel_id=1, source_target_pairs={{0,4},{4,0},{8,12},{12,8},{16,20},{20,16},{24,28},{28,24},{1,5},{5... | collective-permute-start | bytes 393224 | tf_op jit(solution)/shard_map/ppermute | solution.py:30
  18.0 5.0 %collective-permute-start.1 = (f32[96,128]{1,0:T(8,128)S(1)}, f32[96,128]{1,0:T(8,128)S(1)}, u32[]{:S(2)}, u32[]{:S(2)}) collective-permute-start(f32[96,128]{1,0:T(8,128)S(1)} %fusion.4), channel_id=1, source_target_pairs={{0,2},{1,3},{2,0},{3,1},{4,6},{5,7},{6,4},{7,5},{8,10},{9,11},{10,... | collective-permute-start | bytes 147464 | tf_op jit(solution)/shard_map/ppermute | solution.py:30
  23.0 4.2 %collective-permute-start.9 = (f32[96,128]{1,0:T(8,128)S(1)}, f32[96,128]{1,0:T(8,128)S(1)}, u32[]{:S(2)}, u32[]{:S(2)}) collective-permute-start(f32[96,128]{1,0:T(8,128)S(1)} %bitcast.81), channel_id=1, source_target_pairs={{0,4},{4,0},{8,12},{12,8},{16,20},{20,16},{24,28},{28,24},{1,5},{5... | collective-permute-start | bytes 147464 | tf_op jit(solution)/shard_map/ppermute | solution.py:30
  23.6 32.7 %collective-permute-start.12 = (bf16[512,1024]{1,0:T(8,128)(2,1)}, bf16[512,1024]{1,0:T(8,128)(2,1)}, u32[]{:S(2)}, u32[]{:S(2)}) collective-permute-start(bf16[512,1024]{1,0:T(8,128)(2,1)} %unit.1.refs_0_.refs_7_), channel_id=1, source_target_pairs={{0,2},{1,3},{2,0},{3,1},{4,6},{5,7},{6,4},{7,5},{8,10},{9,11},{10,... | collective-permute-start | bytes 3145736 | tf_op jit(solution)/shard_map/ppermute | solution.py:30
  24.4 13.2 %collective-permute-start.4 = (bf16[2,128,512]{2,1,0:T(8,128)(2,1)S(1)}, bf16[2,128,512]{2,1,0:T(8,128)(2,1)S(1)}, u32[]{:S(2)}, u32[]{:S(2)}) collective-permute-start(bf16[2,128,512]{2,1,0:T(8,128)(2,1)S(1)} %pad_maximum_fusion.8), channel_id=1, source_target_pairs={{0,8},{4,12},{8,0},{12,4},{16,24},{20,28},{24,16},{28,20},{1,9},{5... | collective-permute-start | bytes 786440 | tf_op jit(solution)/shard_map/ppermute | solution.py:30
  27.2 7.2 %collective-permute-start.10 = (f32[96,128]{1,0:T(8,128)S(1)}, f32[96,128]{1,0:T(8,128)S(1)}, u32[]{:S(2)}, u32[]{:S(2)}) collective-permute-start(f32[96,128]{1,0:T(8,128)S(1)} %bitcast_add_fusion), channel_id=1, source_target_pairs={{0,8},{4,12},{8,0},{12,4},{16,24},{20,28},{24,16},{28,20},{1,9},{5... | collective-permute-start | bytes 147464 | tf_op jit(solution)/shard_map/ppermute | solution.py:30
  28.9 14.6 %collective-permute-start.7 = (bf16[2,128,512]{2,1,0:T(8,128)(2,1)S(1)}, bf16[2,128,512]{2,1,0:T(8,128)(2,1)S(1)}, u32[]{:S(2)}, u32[]{:S(2)}) collective-permute-start(bf16[2,128,512]{2,1,0:T(8,128)(2,1)S(1)} %pad_maximum_fusion.9), channel_id=1, source_target_pairs={{0,16},{4,20},{8,24},{12,28},{16,0},{20,4},{24,8},{28,12},{1,17},{... | collective-permute-start | bytes 786440 | tf_op jit(solution)/shard_map/ppermute | solution.py:30
  34.4 9.6 %collective-permute-start.11 = (f32[96,128]{1,0:T(8,128)S(1)}, f32[96,128]{1,0:T(8,128)S(1)}, u32[]{:S(2)}, u32[]{:S(2)}) collective-permute-start(f32[96,128]{1,0:T(8,128)S(1)} %fusion.14), channel_id=1, source_target_pairs={{0,16},{4,20},{8,24},{12,28},{16,0},{20,4},{24,8},{28,12},{1,17},{... | collective-permute-start | bytes 147464 | tf_op jit(solution)/shard_map/ppermute | solution.py:30
  37.6 11.9 %collective-permute-start.5 = (bf16[4,128,512]{2,1,0:T(8,128)(2,1)S(1)}, bf16[4,128,512]{2,1,0:T(8,128)(2,1)S(1)}, u32[]{:S(2)}, u32[]{:S(2)}) collective-permute-start(bf16[4,128,512]{2,1,0:T(8,128)(2,1)S(1)} %pad_maximum_fusion.3), channel_id=1, source_target_pairs={{0,4},{4,0},{8,12},{12,8},{16,20},{20,16},{24,28},{28,24},{1,5},{5... | collective-permute-start | bytes 1572872 | tf_op jit(solution)/shard_map/ppermute | solution.py:30
  43.5 11.7 %collective-permute-start.8 = (bf16[4,128,512]{2,1,0:T(8,128)(2,1)S(1)}, bf16[4,128,512]{2,1,0:T(8,128)(2,1)S(1)}, u32[]{:S(2)}, u32[]{:S(2)}) collective-permute-start(bf16[4,128,512]{2,1,0:T(8,128)(2,1)S(1)} %pad_maximum_fusion.4), channel_id=1, source_target_pairs={{0,8},{4,12},{8,0},{12,4},{16,24},{20,28},{24,16},{28,20},{1,9},{5... | collective-permute-start | bytes 1572872 | tf_op jit(solution)/shard_map/ppermute | solution.py:30
  56.3 262.3 %reduce-scatter.2.cloned.1.call-start = ((), (), s32[]{:S(2)}) async-start(), calls=%async_computation.2 | async-start | bytes 4718592 | tf_op jit(solution)/shard_map/reduce_scatter | solution.py:1063
  56.4 21.6 %collective-permute-start.2 = (bf16[512,1024]{1,0:T(8,128)(2,1)S(1)}, bf16[512,1024]{1,0:T(8,128)(2,1)}, u32[]{:S(2)}, u32[]{:S(2)}) collective-permute-start(bf16[512,1024]{1,0:T(8,128)(2,1)S(1)} %copy-done.13), channel_id=1, source_target_pairs={{0,1},{1,0},{2,3},{3,2},{4,5},{5,4},{6,7},{7,6},{8,9},{9,8},{10,11... | collective-permute-start | bytes 3145736 | tf_op jit(solution)/shard_map/ppermute | solution.py:30
  56.5 21.5 %collective-permute-start.13 = (bf16[512,1024]{1,0:T(8,128)(2,1)}, bf16[512,1024]{1,0:T(8,128)(2,1)}, u32[]{:S(2)}, u32[]{:S(2)}) collective-permute-start(bf16[512,1024]{1,0:T(8,128)(2,1)} %collective-permute-done.12.refs_2_.refs_9_), channel_id=1, source_target_pairs={{0,1},{1,0},{2,3},{3,2},{4,5},{5,4},{6,7},{7,6},{8,9},{9,8},{10,11... | collective-permute-start | bytes 3145736 | tf_op jit(solution)/shard_map/ppermute | solution.py:30
  58.5 14.2 %collective-permute-start.14 = (bf16[256,1024]{1,0:T(8,128)(2,1)}, bf16[256,1024]{1,0:T(8,128)(2,1)}, u32[]{:S(2)}, u32[]{:S(2)}) collective-permute-start(bf16[256,1024]{1,0:T(8,128)(2,1)} %get-tuple-element.128), channel_id=1, source_target_pairs={{0,2},{1,3},{2,0},{3,1},{4,6},{5,7},{6,4},{7,5},{8,10},{9,11},{10,... | collective-permute-start | bytes 1572872 | tf_op jit(solution)/shard_map/ppermute | solution.py:30
  74.8 24.7 %collective-permute-start.15 = (bf16[1024,256]{1,0:T(8,128)(2,1)}, bf16[1024,256]{1,0:T(8,128)(2,1)S(1)}, u32[]{:S(2)}, u32[]{:S(2)}) collective-permute-start(bf16[1024,256]{1,0:T(8,128)(2,1)} %placed_rows.1.refs_4_.refs_3_), channel_id=1, source_target_pairs={{0,2},{1,3},{2,0},{3,1},{4,6},{5,7},{6,4},{7,5},{8,10},{9,11},{10,... | collective-permute-start | bytes 1572872 | tf_op jit(solution)/shard_map/ppermute | solution.py:30
  75.0 24.5 %collective-permute-start.16 = (bf16[256,1024]{1,0:T(8,128)(2,1)}, bf16[256,1024]{1,0:T(8,128)(2,1)}, u32[]{:S(2)}, u32[]{:S(2)}) collective-permute-start(bf16[256,1024]{1,0:T(8,128)(2,1)} %get-tuple-element.138), channel_id=1, source_target_pairs={{0,2},{1,3},{2,0},{3,1},{4,6},{5,7},{6,4},{7,5},{8,10},{9,11},{10,... | collective-permute-start | bytes 1572872 | tf_op jit(solution)/shard_map/ppermute | solution.py:30
  78.0 24.6 %collective-permute-start.20 = (bf16[1024,256]{1,0:T(8,128)(2,1)}, bf16[1024,256]{1,0:T(8,128)(2,1)S(1)}, u32[]{:S(2)}, u32[]{:S(2)}) collective-permute-start(bf16[1024,256]{1,0:T(8,128)(2,1)} %placed_rows.1.refs_4_.refs_3_), channel_id=1, source_target_pairs={{0,1},{1,0},{2,3},{3,2},{4,5},{5,4},{6,7},{7,6},{8,9},{9,8},{10,11... | collective-permute-start | bytes 1572872 | tf_op jit(solution)/shard_map/ppermute | solution.py:30
  99.5 14.8 %collective-permute-start.21 = (bf16[1024,256]{1,0:T(8,128)(2,1)S(1)}, bf16[1024,256]{1,0:T(8,128)(2,1)}, u32[]{:S(2)}, u32[]{:S(2)}) collective-permute-start(bf16[1024,256]{1,0:T(8,128)(2,1)S(1)} %collective-permute-done.15.refs_6_.refs_5_), channel_id=1, source_target_pairs={{0,1},{1,0},{2,3},{3,2},{4,5},{5,4},{6,7},{7,6},{8,9},{9,8},{10,11... | collective-permute-start | bytes 1572872 | tf_op jit(solution)/shard_map/ppermute | solution.py:30
  100.1 3.3 %collective-permute-start.17 = (bf16[512,256]{1,0:T(8,128)(2,1)}, bf16[512,256]{1,0:T(8,128)(2,1)S(1)}, u32[]{:S(2)}, u32[]{:S(2)}) collective-permute-start(bf16[512,256]{1,0:T(8,128)(2,1)} %get-tuple-element.140), channel_id=1, source_target_pairs={{0,1},{1,0},{2,3},{3,2},{4,5},{5,4},{6,7},{7,6},{8,9},{9,8},{10,11... | collective-permute-start | bytes 786440 | tf_op jit(solution)/shard_map/ppermute | solution.py:30
  100.2 9.4 %collective-permute-start.18 = (bf16[512,256]{1,0:T(8,128)(2,1)}, bf16[512,256]{1,0:T(8,128)(2,1)}, u32[]{:S(2)}, u32[]{:S(2)}) collective-permute-start(bf16[512,256]{1,0:T(8,128)(2,1)} %get-tuple-element.141), channel_id=1, source_target_pairs={{0,2},{1,3},{2,0},{3,1},{4,6},{5,7},{6,4},{7,5},{8,10},{9,11},{10,... | collective-permute-start | bytes 786440 | tf_op jit(solution)/shard_map/ppermute | solution.py:30
  100.5 13.8 %collective-permute-start.19 = (bf16[512,256]{1,0:T(8,128)(2,1)}, bf16[512,256]{1,0:T(8,128)(2,1)}, u32[]{:S(2)}, u32[]{:S(2)}) collective-permute-start(bf16[512,256]{1,0:T(8,128)(2,1)} %get-tuple-element.142), channel_id=1, source_target_pairs={{0,3},{1,2},{2,1},{3,0},{4,7},{5,6},{6,5},{7,4},{8,11},{9,10},{10,... | collective-permute-start | bytes 786440 | tf_op jit(solution)/shard_map/ppermute | solution.py:30
  102.6 20.2 %collective-permute-start.23 = (bf16[512,1024]{1,0:T(8,128)(2,1)S(1)}, bf16[512,1024]{1,0:T(8,128)(2,1)}, u32[]{:S(2)}, u32[]{:S(2)}) collective-permute-start(bf16[512,1024]{1,0:T(8,128)(2,1)S(1)} %copy-done.5), channel_id=1, source_target_pairs={{0,1},{1,0},{2,3},{3,2},{4,5},{5,4},{6,7},{7,6},{8,9},{9,8},{10,11... | collective-permute-start | bytes 3145736 | tf_op jit(solution)/shard_map/ppermute | solution.py:30
  119.3 3.4 %collective-permute-start.22 = (bf16[512,1024]{1,0:T(8,128)(2,1)}, bf16[512,1024]{1,0:T(8,128)(2,1)}, u32[]{:S(2)}, u32[]{:S(2)}) collective-permute-start(bf16[512,1024]{1,0:T(8,128)(2,1)} %get-tuple-element.145.refs_0_), channel_id=1, source_target_pairs={{0,1},{1,0},{2,3},{3,2},{4,5},{5,4},{6,7},{7,6},{8,9},{9,8},{10,11... | collective-permute-start | bytes 3145736 | tf_op jit(solution)/shard_map/ppermute | solution.py:30
  120.2 25.6 %collective-permute-start.25 = (bf16[512,1024]{1,0:T(8,128)(2,1)}, bf16[512,1024]{1,0:T(8,128)(2,1)}, u32[]{:S(2)}, u32[]{:S(2)}) collective-permute-start(bf16[512,1024]{1,0:T(8,128)(2,1)} %get-tuple-element.145.refs_0_), channel_id=1, source_target_pairs={{0,2},{1,3},{2,0},{3,1},{4,6},{5,7},{6,4},{7,5},{8,10},{9,11},{10,... | collective-permute-start | bytes 3145736 | tf_op jit(solution)/shard_map/ppermute | solution.py:30
  122.6 23.1 %collective-permute-start.27 = (bf16[512,1024]{1,0:T(8,128)(2,1)S(1)}, bf16[512,1024]{1,0:T(8,128)(2,1)}, u32[]{:S(2)}, u32[]{:S(2)}) collective-permute-start(bf16[512,1024]{1,0:T(8,128)(2,1)S(1)} %constant_dynamic-update-slice_fusion.refs_2_), channel_id=1, source_target_pairs={{0,1},{1,0},{2,3},{3,2},{4,5},{5,4},{6,7},{7,6},{8,9},{9,8},{10,11... | collective-permute-start | bytes 3145736 | tf_op jit(solution)/shard_map/ppermute | solution.py:30
  145.8 2.9 collective-permute-start.26
  164.6 2.9 collective-permute-start.28
  164.8 25.3 %collective-permute-start.24 = (bf16[512,1024]{1,0:T(8,128)(2,1)}, bf16[512,1024]{1,0:T(8,128)(2,1)S(1)}, u32[]{:S(2)}, u32[]{:S(2)}) collective-permute-start(bf16[512,1024]{1,0:T(8,128)(2,1)} %get-tuple-element.148), channel_id=1, source_target_pairs={{0,1},{1,0},{2,3},{3,2},{4,5},{5,4},{6,7},{7,6},{8,9},{9,8},{10,11... | collective-permute-start | bytes 3145736 | tf_op jit(solution)/shard_map/ppermute | solution.py:30
  165.2 21.1 %collective-permute-start.30 = (bf16[512,1024]{1,0:T(8,128)(2,1)}, bf16[512,1024]{1,0:T(8,128)(2,1)}, u32[]{:S(2)}, u32[]{:S(2)}) collective-permute-start(bf16[512,1024]{1,0:T(8,128)(2,1)} %get-tuple-element.168), channel_id=1, source_target_pairs={{0,1},{1,0},{2,3},{3,2},{4,5},{5,4},{6,7},{7,6},{8,9},{9,8},{10,11... | collective-permute-start | bytes 3145736 | tf_op jit(solution)/shard_map/ppermute | solution.py:30
  170.1 25.5 %collective-permute-start.29 = (bf16[512,1024]{1,0:T(8,128)(2,1)}, bf16[512,1024]{1,0:T(8,128)(2,1)}, u32[]{:S(2)}, u32[]{:S(2)}) collective-permute-start(bf16[512,1024]{1,0:T(8,128)(2,1)} %add_convert_fusion.3), channel_id=1, source_target_pairs={{0,2},{1,3},{2,0},{3,1},{4,6},{5,7},{6,4},{7,5},{8,10},{9,11},{10,... | collective-permute-start | bytes 3145736 | tf_op jit(solution)/shard_map/ppermute | solution.py:30
  195.7 13.4 %collective-permute-start.34 = (bf16[256,1024]{1,0:T(8,128)(2,1)}, bf16[256,1024]{1,0:T(8,128)(2,1)S(1)}, u32[]{:S(2)}, u32[]{:S(2)}) collective-permute-start(bf16[256,1024]{1,0:T(8,128)(2,1)} %get-tuple-element.181), channel_id=1, source_target_pairs={{0,2},{1,3},{2,0},{3,1},{4,6},{5,7},{6,4},{7,5},{8,10},{9,11},{10,... | collective-permute-start | bytes 1572872 | tf_op jit(solution)/shard_map/ppermute | solution.py:30
  196.0 29.4 %copy-start = (s32[8]{0:T(128)S(1)}, s32[8]{0:T(128)}, u32[]{:S(2)}) copy-start(s32[8]{0:T(128)} %broadcast_xor_fusion.owner_b.owner) | copy-start | bytes 100
  196.0 29.4 %copy-start.1 = (s32[418]{0:T(512)S(1)}, s32[418]{0:T(512)}, u32[]{:S(2)}) copy-start(s32[418]{0:T(512)} %pad_add_fusion.facts) | copy-start | bytes 5020
  196.0 29.4 %copy-start.3 = (s32[8]{0:T(128)S(1)}, s32[8]{0:T(128)}, u32[]{:S(2)}) copy-start(s32[8]{0:T(128)} %broadcast_xor_fusion.1.owner_a) | copy-start | bytes 100
  196.0 29.4 %copy-start.4 = (f32[32,256]{1,0:T(8,128)S(1)}, f32[32,256]{1,0:T(8,128)}, u32[]{:S(2)}) copy-start(f32[32,256]{1,0:T(8,128)} %get-tuple-element.132.refs_1_) | copy-start | bytes 98308
  209.0 3.3 %collective-permute-start.35 = (bf16[8,128,256]{2,1,0:T(8,128)(2,1)}, bf16[8,128,256]{2,1,0:T(8,128)(2,1)S(1)}, u32[]{:S(2)}, u32[]{:S(2)}) collective-permute-start(bf16[8,128,256]{2,1,0:T(8,128)(2,1)} %get-tuple-element.183), channel_id=1, source_target_pairs={{0,1},{1,0},{2,3},{3,2},{4,5},{5,4},{6,7},{7,6},{8,9},{9,8},{10,11... | collective-permute-start | bytes 1572872 | tf_op jit(solution)/shard_map/ppermute | solution.py:30
  209.7 3.8 %collective-permute-start.31 = (bf16[512,256]{1,0:T(8,128)(2,1)}, bf16[512,256]{1,0:T(8,128)(2,1)S(1)}, u32[]{:S(2)}, u32[]{:S(2)}) collective-permute-start(bf16[512,256]{1,0:T(8,128)(2,1)} %get-tuple-element.174), channel_id=1, source_target_pairs={{0,1},{1,0},{2,3},{3,2},{4,5},{5,4},{6,7},{7,6},{8,9},{9,8},{10,11... | collective-permute-start | bytes 786440 | tf_op jit(solution)/shard_map/ppermute | solution.py:30
  210.2 9.4 %collective-permute-start.32 = (bf16[512,256]{1,0:T(8,128)(2,1)}, bf16[512,256]{1,0:T(8,128)(2,1)S(1)}, u32[]{:S(2)}, u32[]{:S(2)}) collective-permute-start(bf16[512,256]{1,0:T(8,128)(2,1)} %get-tuple-element.175), channel_id=1, source_target_pairs={{0,2},{1,3},{2,0},{3,1},{4,6},{5,7},{6,4},{7,5},{8,10},{9,11},{10,... | collective-permute-start | bytes 786440 | tf_op jit(solution)/shard_map/ppermute | solution.py:30
  210.5 12.8 %collective-permute-start.33 = (bf16[512,256]{1,0:T(8,128)(2,1)}, bf16[512,256]{1,0:T(8,128)(2,1)S(1)}, u32[]{:S(2)}, u32[]{:S(2)}) collective-permute-start(bf16[512,256]{1,0:T(8,128)(2,1)} %get-tuple-element.176), channel_id=1, source_target_pairs={{0,3},{1,2},{2,1},{3,0},{4,7},{5,6},{6,5},{7,4},{8,11},{9,10},{10,... | collective-permute-start | bytes 786440 | tf_op jit(solution)/shard_map/ppermute | solution.py:30
  211.6 51.7 %collective-permute-start.37 = (bf16[8,128,256]{2,1,0:T(8,128)(2,1)}, bf16[8,128,256]{2,1,0:T(8,128)(2,1)S(1)}, u32[]{:S(2)}, u32[]{:S(2)}) collective-permute-start(bf16[8,128,256]{2,1,0:T(8,128)(2,1)} %get-tuple-element.193), channel_id=1, source_target_pairs={{0,1},{1,0},{2,3},{3,2},{4,5},{5,4},{6,7},{7,6},{8,9},{9,8},{10,11... | collective-permute-start | bytes 1572872 | tf_op jit(solution)/shard_map/ppermute | solution.py:30
  223.3 40.0 %collective-permute-start.36 = (bf16[256,1024]{1,0:T(8,128)(2,1)}, bf16[256,1024]{1,0:T(8,128)(2,1)S(1)}, u32[]{:S(2)}, u32[]{:S(2)}) collective-permute-start(bf16[256,1024]{1,0:T(8,128)(2,1)} %get-tuple-element.191), channel_id=1, source_target_pairs={{0,2},{1,3},{2,0},{3,1},{4,6},{5,7},{6,4},{7,5},{8,10},{9,11},{10,... | collective-permute-start | bytes 1572872 | tf_op jit(solution)/shard_map/ppermute | solution.py:30
  223.9 39.4 %collective-permute-start.38 = (bf16[8,128,256]{2,1,0:T(8,128)(2,1)S(1)}, bf16[8,128,256]{2,1,0:T(8,128)(2,1)S(1)}, u32[]{:S(2)}, u32[]{:S(2)}) collective-permute-start(bf16[8,128,256]{2,1,0:T(8,128)(2,1)S(1)} %add_convert_fusion.5), channel_id=1, source_target_pairs={{0,2},{1,3},{2,0},{3,1},{4,6},{5,7},{6,4},{7,5},{8,10},{9,11},{10,... | collective-permute-start | bytes 1572872 | tf_op jit(solution)/shard_map/ppermute | solution.py:30
  226.3 38.6 %copy-start.26 = (f32[4,1024]{1,0:T(4,128)S(1)}, f32[4,1024]{1,0:T(4,128)}, u32[]{:S(2)}) copy-start(f32[4,1024]{1,0:T(4,128)} %get-tuple-element.226) | copy-start | bytes 49156
  226.4 38.6 %copy-start.28 = (f32[1,1024]{1,0:T(1,128)S(1)}, f32[1,1024]{1,0:T(1,128)}, u32[]{:S(2)}) copy-start(f32[1,1024]{1,0:T(1,128)} %get-tuple-element.228) | copy-start | bytes 12292
  263.3 6.1 %collective-permute-start.39 = (bf16[512,1024]{1,0:T(8,128)(2,1)}, bf16[512,1024]{1,0:T(8,128)(2,1)S(1)}, u32[]{:S(2)}, u32[]{:S(2)}) collective-permute-start(bf16[512,1024]{1,0:T(8,128)(2,1)} %get-tuple-element.200), channel_id=1, source_target_pairs={{0,1},{1,0},{2,3},{3,2},{4,5},{5,4},{6,7},{7,6},{8,9},{9,8},{10,11... | collective-permute-start | bytes 3145736 | tf_op jit(solution)/shard_map/ppermute | solution.py:30
  264.4 20.5 %collective-permute-start.46 = (bf16[512,1024]{1,0:T(8,128)(2,1)}, bf16[512,1024]{1,0:T(8,128)(2,1)S(1)}, u32[]{:S(2)}, u32[]{:S(2)}) collective-permute-start(bf16[512,1024]{1,0:T(8,128)(2,1)} %get-tuple-element.216), channel_id=1, source_target_pairs={{0,1},{1,0},{2,3},{3,2},{4,5},{5,4},{6,7},{7,6},{8,9},{9,8},{10,11... | collective-permute-start | bytes 3145736 | tf_op jit(solution)/shard_map/ppermute | solution.py:30
  265.4 15.5 %collective-permute-start.40 = (bf16[4,128,512]{2,1,0:T(8,128)(2,1)}, bf16[4,128,512]{2,1,0:T(8,128)(2,1)S(1)}, u32[]{:S(2)}, u32[]{:S(2)}) collective-permute-start(bf16[4,128,512]{2,1,0:T(8,128)(2,1)} %get-tuple-element.209), channel_id=1, source_target_pairs={{0,4},{4,0},{8,12},{12,8},{16,20},{20,16},{24,28},{28,24},{1,5},{5... | collective-permute-start | bytes 1572872 | tf_op jit(solution)/shard_map/ppermute | solution.py:30
  267.3 14.4 %collective-permute-start.41 = (bf16[4,128,512]{2,1,0:T(8,128)(2,1)S(1)}, bf16[4,128,512]{2,1,0:T(8,128)(2,1)S(1)}, u32[]{:S(2)}, u32[]{:S(2)}) collective-permute-start(bf16[4,128,512]{2,1,0:T(8,128)(2,1)S(1)} %pad_maximum_fusion.6), channel_id=1, source_target_pairs={{0,8},{4,12},{8,0},{12,4},{16,24},{20,28},{24,16},{28,20},{1,9},{5... | collective-permute-start | bytes 1572872 | tf_op jit(solution)/shard_map/ppermute | solution.py:30
  267.5 13.1 %collective-permute-start.48 = (f32[104,128]{1,0:T(8,128)S(1)}, f32[104,128]{1,0:T(8,128)S(1)}, u32[]{:S(2)}, u32[]{:S(2)}) collective-permute-start(f32[104,128]{1,0:T(8,128)S(1)} %maximum_bitcast_fusion.1), channel_id=1, source_target_pairs={{0,4},{4,0},{8,12},{12,8},{16,20},{20,16},{24,28},{28,24},{1,5},{5... | collective-permute-start | bytes 159752 | tf_op jit(solution)/shard_map/ppermute | solution.py:30
  270.0 13.3 %collective-permute-start.42 = (bf16[256,1024]{1,0:T(8,128)(2,1)S(1)}, bf16[256,1024]{1,0:T(8,128)(2,1)S(1)}, u32[]{:S(2)}, u32[]{:S(2)}) collective-permute-start(bf16[256,1024]{1,0:T(8,128)(2,1)S(1)} %get-tuple-element.245), channel_id=1, source_target_pairs={{0,2},{1,3},{2,0},{3,1},{4,6},{5,7},{6,4},{7,5},{8,10},{9,11},{10,... | collective-permute-start | bytes 1572872 | tf_op jit(solution)/shard_map/ppermute | solution.py:30
  280.6 8.2 %collective-permute-start.49 = (f32[104,128]{1,0:T(8,128)S(1)}, f32[104,128]{1,0:T(8,128)S(1)}, u32[]{:S(2)}, u32[]{:S(2)}) collective-permute-start(f32[104,128]{1,0:T(8,128)S(1)} %fusion.5), channel_id=1, source_target_pairs={{0,8},{4,12},{8,0},{12,4},{16,24},{20,28},{24,16},{28,20},{1,9},{5... | collective-permute-start | bytes 159752 | tf_op jit(solution)/shard_map/ppermute | solution.py:30
  283.2 7.2 %collective-permute-start.43 = (bf16[2,128,512]{2,1,0:T(8,128)(2,1)S(1)}, bf16[2,128,512]{2,1,0:T(8,128)(2,1)S(1)}, u32[]{:S(2)}, u32[]{:S(2)}) collective-permute-start(bf16[2,128,512]{2,1,0:T(8,128)(2,1)S(1)} %get-tuple-element.213), channel_id=1, source_target_pairs={{0,8},{4,12},{8,0},{12,4},{16,24},{20,28},{24,16},{28,20},{1,9},{5... | collective-permute-start | bytes 786440 | tf_op jit(solution)/shard_map/ppermute | solution.py:30
  286.8 18.0 %collective-permute-start.45 = (bf16[256,1024]{1,0:T(8,128)(2,1)S(1)}, bf16[256,1024]{1,0:T(8,128)(2,1)S(1)}, u32[]{:S(2)}, u32[]{:S(2)}) collective-permute-start(bf16[256,1024]{1,0:T(8,128)(2,1)S(1)} %get-tuple-element.244), channel_id=1, source_target_pairs={{0,2},{1,3},{2,0},{3,1},{4,6},{5,7},{6,4},{7,5},{8,10},{9,11},{10,... | collective-permute-start | bytes 1572872 | tf_op jit(solution)/shard_map/ppermute | solution.py:30
  287.4 17.9 %collective-permute-start.47 = (bf16[512,1024]{1,0:T(8,128)(2,1)S(1)}, bf16[512,1024]{1,0:T(8,128)(2,1)S(1)}, u32[]{:S(2)}, u32[]{:S(2)}) collective-permute-start(bf16[512,1024]{1,0:T(8,128)(2,1)S(1)} %copy-done.30), channel_id=1, source_target_pairs={{0,1},{1,0},{2,3},{3,2},{4,5},{5,4},{6,7},{7,6},{8,9},{9,8},{10,11... | collective-permute-start | bytes 3145736 | tf_op jit(solution)/shard_map/ppermute | solution.py:30
  287.4 16.7 %collective-permute-start.44 = (bf16[2,128,512]{2,1,0:T(8,128)(2,1)S(1)}, bf16[2,128,512]{2,1,0:T(8,128)(2,1)S(1)}, u32[]{:S(2)}, u32[]{:S(2)}) collective-permute-start(bf16[2,128,512]{2,1,0:T(8,128)(2,1)S(1)} %get-tuple-element.214), channel_id=1, source_target_pairs={{0,16},{4,20},{8,24},{12,28},{16,0},{20,4},{24,8},{28,12},{1,17},{... | collective-permute-start | bytes 786440 | tf_op jit(solution)/shard_map/ppermute | solution.py:30
  288.9 16.5 %collective-permute-start.50 = (f32[104,128]{1,0:T(8,128)S(1)}, f32[104,128]{1,0:T(8,128)S(1)}, u32[]{:S(2)}, u32[]{:S(2)}) collective-permute-start(f32[104,128]{1,0:T(8,128)S(1)} %fusion.13), channel_id=1, source_target_pairs={{0,16},{4,20},{8,24},{12,28},{16,0},{20,4},{24,8},{28,12},{1,17},{... | collective-permute-start | bytes 159752 | tf_op jit(solution)/shard_map/ppermute | solution.py:30
  304.8 8.3 %collective-permute-start.51 = (bf16[1,128,512]{2,1,0:T(8,128)(2,1)S(1)}, bf16[1,128,512]{2,1,0:T(8,128)(2,1)}, u32[]{:S(2)}, u32[]{:S(2)}) collective-permute-start(bf16[1,128,512]{2,1,0:T(8,128)(2,1)S(1)} %get-tuple-element.231), channel_id=1, source_target_pairs={{0,16},{4,20},{8,24},{12,28},{16,0},{20,4},{24,8},{28,12},{1,17},{... | collective-permute-start | bytes 393224 | tf_op jit(solution)/shard_map/ppermute | solution.py:30
  304.8 8.3 %collective-permute-start.52 = (bf16[1,128,512]{2,1,0:T(8,128)(2,1)}, bf16[1,128,512]{2,1,0:T(8,128)(2,1)}, u32[]{:S(2)}, u32[]{:S(2)}) collective-permute-start(bf16[1,128,512]{2,1,0:T(8,128)(2,1)} %get-tuple-element.233), channel_id=1, source_target_pairs={{0,4},{4,0},{8,12},{12,8},{16,20},{20,16},{24,28},{28,24},{1,5},{5... | collective-permute-start | bytes 393224 | tf_op jit(solution)/shard_map/ppermute | solution.py:30
  310.9 4.2 %collective-permute-start.55 = (f32[104,128]{1,0:T(8,128)S(1)}, f32[104,128]{1,0:T(8,128)S(1)}, u32[]{:S(2)}, u32[]{:S(2)}) collective-permute-start(f32[104,128]{1,0:T(8,128)S(1)} %bitcast.85), channel_id=1, source_target_pairs={{0,3},{1,2},{2,1},{3,0},{4,7},{5,6},{6,5},{7,4},{8,11},{9,10},{10,... | collective-permute-start | bytes 159752 | tf_op jit(solution)/shard_map/ppermute | solution.py:30
  311.4 4.7 %collective-permute-start.54 = (f32[104,128]{1,0:T(8,128)S(1)}, f32[104,128]{1,0:T(8,128)S(1)}, u32[]{:S(2)}, u32[]{:S(2)}) collective-permute-start(f32[104,128]{1,0:T(8,128)S(1)} %bitcast.86), channel_id=1, source_target_pairs={{0,2},{1,3},{2,0},{3,1},{4,6},{5,7},{6,4},{7,5},{8,10},{9,11},{10,... | collective-permute-start | bytes 159752 | tf_op jit(solution)/shard_map/ppermute | solution.py:30
  312.4 3.7 %collective-permute-start.53 = (f32[104,128]{1,0:T(8,128)S(1)}, f32[104,128]{1,0:T(8,128)S(1)}, u32[]{:S(2)}, u32[]{:S(2)}) collective-permute-start(f32[104,128]{1,0:T(8,128)S(1)} %bitcast.87), channel_id=1, source_target_pairs={{0,1},{1,0},{2,3},{3,2},{4,5},{5,4},{6,7},{7,6},{8,9},{9,8},{10,11... | collective-permute-start | bytes 159752 | tf_op jit(solution)/shard_map/ppermute | solution.py:30
  (31 other events, 244.7 us)
Sparse Core Ops, SparseCore 0:
  56.4 70.0 all-gather.1
  186.4 85.3 reduce-scatter.1

commit v4 on v3

--- a/solution.py
+++ b/solution.py
@@ -999,12 +999,15 @@
     last_blocks = doubled(last_flat, "dp", order_b)
     packed = summed_everywhere(packed, ("dp",))
     feed_flat = jnp.concatenate([up_weight, down_weight], axis=1)
-    first_going, last_going = output_cotangent[: near // 2], output_cotangent[near // 2 :]
+    piece_rows = near // 4
+    first_going, next_going = output_cotangent[:piece_rows], output_cotangent[piece_rows:]
+    next_going, last_going = next_going[:piece_rows], next_going[piece_rows:]
     first_going, unit_far = together(first_going, unit_far)
     cotangent_first = far(first_going, "tensor")
-    feed_flat, first_blocks, last_blocks, packed, unit_far = together(
-        feed_flat, first_blocks, last_blocks, packed, unit_far
-    )
+    feed_flat, first_blocks, last_blocks, packed, cotangent_first, next_going = together(
+        feed_flat, first_blocks, last_blocks, packed, cotangent_first, next_going
+    )
+    cotangent_next = far(next_going, "tensor")
     feed_full = lax.all_gather(feed_flat, "dp", axis=0, tiled=True)
     unit_parts = gathered_parts(unit_near, unit_far, "tensor")
 
@@ -1018,7 +1021,7 @@
     norm_two = jnp.stack([vectors_full[4], vectors_full[2], vectors_full[3]])
 
 
-    last_blocks, cotangent_first = together(last_blocks, cotangent_first)
+    last_blocks, cotangent_next = together(last_blocks, cotangent_next)
     out_group = placed_rows(last_blocks, owner_b, width)
     out_far = far(out_group, "tensor")
     last_going, out_group = together(last_going, out_group)
@@ -1036,7 +1039,7 @@
     )
     context = context[0]
     *context, out_far, cotangent_last = together(*context, out_far, cotangent_last)
-    cotangent_far = jnp.concatenate([cotangent_first, cotangent_last], axis=0)
+    cotangent_far = jnp.concatenate([cotangent_first, cotangent_next, cotangent_last], axis=0)
     grad_parts = gathered_parts(output_cotangent, cotangent_far, "tensor")
 
     out_parts = gathered_parts(out_group, out_far, "tensor")

time: 334 us -> 333 us (level)
  waiting for transfers between devices: 103 us -> 89.8 us
  starting transfers between devices: 41.7 us -> 50.1 us
    ppermute x56 -> x57, waiting for transfers between devices: 99.3 us -> 82.5 us  [swapped(): return lax.ppermute(value, axis, [(i, i ^ bit) for i in range(count)])]
    ppermute x56 -> x57, starting transfers between devices: 41.7 us -> 50 us  [swapped(): return lax.ppermute(value, axis, [(i, i ^ bit) for i in range(count)])]
    all_gather x1, waiting for transfers between devices: 3.78 us -> 7.25 us  [per_device(): feed_full = lax.all_gather(feed_flat, 'dp', axis=0, tiled=True)]
    unnamed x83 -> x90, local copies, waits for them, and re-layouts: 8.61 us -> 10.2 us
  transfers between devices with their start and end apart: 58 -> 59, of which waited for: 23 -> 21; matrix products, arithmetic and copies ran while one was open for 9% -> 10% of each run, Pallas kernels for 35% -> 35%
where the time goes in v4:
time: 333 us; the launch traced here: 326 us
  Pallas kernels  128 us (38%)
  waiting for transfers between devices  89.8 us (27%)
  starting transfers between devices  50.1 us (15%)
  local copies, waits for them, and re-layouts  23.5 us (7%)
  other arithmetic  18.7 us (6%)
  between operations  15.7 us (5%)
    ppermute x57, waiting for transfers between devices, swapped(): return lax.ppermute(value, axis, [(i, i ^ bit) for i in range(count)])  82.5 us
    ppermute x57, starting transfers between devices, swapped(): return lax.ppermute(value, axis, [(i, i ^ bit) for i in range(count)])  50 us
    pallas_call x1, Pallas kernels, attend_back(): pl.pallas_call(functools.partial(attend_back_kernel, heads, len(unit)), g...  37 us
    pallas_call x2, Pallas kernels, feed(): pl.pallas_call(functools.partial(feed_kernel, here, len(stacks)), grid=(h...  29.9 us
    pallas_call x1, Pallas kernels, project_attend(): pl.pallas_call(functools.partial(project_attend_kernel, heads, len(unit))...  21.5 us
    pallas_call x1, Pallas kernels, feed_grads(): pl.pallas_call(feed_grads_kernel, grid=(rows // (2 * TILE),), out_shape=[...  15.8 us
    unnamed x90, local copies, waits for them, and re-layouts  10.2 us
    pallas_call x1, Pallas kernels, middle_back(): pl.pallas_call(functools.partial(middle_back_kernel, len(terms), parts),...  9.91 us
  transfers between devices with their start and end apart: 59, of which 21 were waited for; matrix products, arithmetic and copies ran while one was open for 10% of the time, Pallas kernels for 35%

profile of v4, /device:TPU:0, one launch (start us, length us, event | category | flops | bytes accessed | tf_op | source)
XLA Modules:
  0.0 326.1 jit_solution(10439620808161083213)
XLA Ops:
  9.5 1.1 copy.28
  10.7 3.6 %collective-permute-start.5 = (bf16[1,128,512]{2,1,0:T(8,128)(2,1)S(1)}, bf16[1,128,512]{2,1,0:T(8,128)(2,1)S(1)}, u32[]{:S(2)}, u32[]{:S(2)}) collective-permute-start(bf16[1,128,512]{2,1,0:T(8,128)(2,1)S(1)} %bitcast.71), channel_id=1, source_target_pairs={{0,16},{4,20},{8,24},{12,28},{16,0},{20,4},{24,8},{28,12},{1,17},{... | collective-permute-start | bytes 393224 | tf_op jit(solution)/shard_map/ppermute | solution.py:30
  15.3 1.6 collective-permute-start.8
  16.9 1.8 fusion.8
  18.6 1.7 collective-permute-start.1
  21.1 2.5 unit.1.refs_0_.refs_7_
  25.0 1.6 collective-permute-start.6
  26.6 1.9 collective-permute-done.11
  28.6 1.6 collective-permute-start.12
  30.6 4.1 %collective-permute-done.12 = f32[96,128]{1,0:T(8,128)S(1)} collective-permute-done((f32[96,128]{1,0:T(8,128)S(1)}, f32[96,128]{1,0:T(8,128)S(1)}, u32[]{:S(2)}, u32[]{:S(2)}) %collective-permute-start.12) | collective-permute-done | bytes 49184 | tf_op jit(solution)/shard_map/ppermute | solution.py:30
  34.7 2.7 collective-permute-start.13
  37.5 2.2 collective-permute-start.7
  39.7 4.5 %collective-permute-done.9 = bf16[2,128,512]{2,1,0:T(8,128)(2,1)S(1)} collective-permute-done((bf16[2,128,512]{2,1,0:T(8,128)(2,1)S(1)}, bf16[2,128,512]{2,1,0:T(8,128)(2,1)S(1)}, u32[]{:S(2)}, u32[]{:S(2)}) %collective-permute-start.9) | collective-permute-done | bytes 262176 | tf_op jit(solution)/shard_map/ppermute | solution.py:30
  44.8 3.9 %collective-permute-done.3.refs_2_.refs_9_ = bf16[512,1024]{1,0:T(8,128)(2,1)S(1)} collective-permute-done((bf16[512,1024]{1,0:T(8,128)(2,1)}, bf16[512,1024]{1,0:T(8,128)(2,1)S(1)}, u32[]{:S(2)}, u32[]{:S(2)}) %collective-permute-start.3) | collective-permute-done | bytes 1048608 | tf_op jit(solution)/shard_map/ppermute | solution.py:30
  49.6 1.1 pad_maximum_fusion.refs_4_
  50.7 5.4 %collective-permute-done.10 = bf16[4,128,512]{2,1,0:T(8,128)(2,1)S(1)} collective-permute-done((bf16[4,128,512]{2,1,0:T(8,128)(2,1)S(1)}, bf16[4,128,512]{2,1,0:T(8,128)(2,1)S(1)}, u32[]{:S(2)}, u32[]{:S(2)}) %collective-permute-start.10) | collective-permute-done | bytes 524320 | tf_op jit(solution)/shard_map/ppermute | solution.py:30
  56.1 1.1 pad_maximum_fusion.1.refs_5_.blocks_ref
  59.9 1.6 collective-permute-start.15
  63.2 5.0 %collective-permute-done.15 = bf16[128,1024]{1,0:T(8,128)(2,1)S(1)} collective-permute-done((bf16[128,1024]{1,0:T(8,128)(2,1)S(1)}, bf16[128,1024]{1,0:T(8,128)(2,1)S(1)}, u32[]{:S(2)}, u32[]{:S(2)}) %collective-permute-start.15) | collective-permute-done | bytes 262176 | tf_op jit(solution)/shard_map/ppermute | solution.py:30
  68.2 2.2 placed_rows.1.refs_4_.refs_3_
  70.4 1.6 collective-permute-start.16
  73.6 21.5 %project_attend.1 = (bf16[512,256]{1,0:T(8,128)(2,1)}, bf16[512,256]{1,0:T(8,128)(2,1)}, bf16[512,256]{1,0:T(8,128)(2,1)}, bf16[512,256]{1,0:T(8,128)(2,1)}, bf1...) custom-call(s32[8]{0:T(128)} %broadcast_xor_fusion.1.owner_a, ...), custom_call_target="tpu_custom_call" | custom-call | flops 5368709120 | bytes 10485760 | tf_op jit(solution)/shard_map/project_attend/pallas_call | solution.py:487
  95.8 1.6 collective-permute-start.19
  99.0 6.2 %collective-permute-done.19.refs_2_.refs_9_ = bf16[512,256]{1,0:T(8,128)(2,1)} collective-permute-done((bf16[512,256]{1,0:T(8,128)(2,1)}, bf16[512,256]{1,0:T(8,128)(2,1)}, u32[]{:S(2)}, u32[]{:S(2)}) %collective-permute-start.19) | collective-permute-done | bytes 262176 | tf_op jit(solution)/shard_map/ppermute | solution.py:30
  105.2 4.7 %collective-permute-done.20.refs_3_.refs_10_ = bf16[512,256]{1,0:T(8,128)(2,1)} collective-permute-done((bf16[512,256]{1,0:T(8,128)(2,1)}, bf16[512,256]{1,0:T(8,128)(2,1)}, u32[]{:S(2)}, u32[]{:S(2)}) %collective-permute-start.20) | collective-permute-done | bytes 262176 | tf_op jit(solution)/shard_map/ppermute | solution.py:30
  110.0 5.0 %middle.1 = (bf16[512,1024]{1,0:T(8,128)(2,1)}, bf16[512,1024]{1,0:T(8,128)(2,1)}) custom-call(bf16[512,256]{1,0:T(8,128)(2,1)} %get-tuple-element.140.refs_0_.refs_7_, bf16[512,256]{1,0:T(8,128)(2,1)} %copy-done.12, bf16[512,256]{1,0:T(8,128)(2,1)} %collective-permute-done.19.refs_2_.refs_9_, bf16[512,256]{1,0:T(8,128)(2,1)} %collective-permute-done.20.refs_3_.refs_10_, ...), custom_call_target="tpu_custom_call" | custom-call | flops 1073741824 | bytes 6291456 | tf_op jit(solution)/shard_map/middle/pallas_call | solution.py:839
  117.1 1.7 collective-permute-start.26
  119.8 1.1 constant_dynamic-update-slice_fusion.refs_2_
  121.0 7.3 %all-gather.2.cloned.1.call-done.refs_4_ = bf16[1024,2048]{1,0:T(8,128)(2,1)} async-done(((bf16[128,2048]{1,0:T(8,128)(2,1)}), bf16[1024,2048]{1,0:T(8,128)(2,1)}) %all-gather.2.cloned.1.call-update) | async-done | bytes 4194320 | tf_op jit(solution)/shard_map/all_gather | solution.py:1011
  128.2 14.9 %feed.2 = (bf16[512,1024]{1,0:T(8,128)(2,1)}, bf16[512,1024]{1,0:T(8,128)(2,1)}, bf16[512,1024]{1,0:T(8,128)(2,1)}, bf16[512,1024]{1,0:T(8,128)(2,1)}, bf16[2048...) custom-call(bf16[512,1024]{1,0:T(8,128)(2,1)} %get-tuple-element.146.re, ...), custom_call_target="tpu_custom_call" | custom-call | flops 8589934592 | bytes 20971520 | tf_op jit(solution)/shard_map/feed/pallas_call | solution.py:714
  143.3 2.8 collective-permute-done.27.refs_1_
  146.1 1.0 copy-done.34
  147.1 14.9 %feed.3 = (bf16[512,1024]{1,0:T(8,128)(2,1)}, bf16[512,1024]{1,0:T(8,128)(2,1)}, bf16[512,1024]{1,0:T(8,128)(2,1)}, bf16[512,1024]{1,0:T(8,128)(2,1)}, bf16[2048...) custom-call(bf16[512,1024]{1,0:T(8,128)(2,1)} %collective-permute-do, ...), custom_call_target="tpu_custom_call", output_to_operand_aliasing={{4}: (6, {}), {5}: (7, {}), {6}: (8, {}), {7}: (9, {})} | custom-call | flops 8589934592 | bytes 20971520 | tf_op jit(solution)/shard_map/feed/pallas_call | solution.py:714
  162.7 2.2 collective-permute-done.29
  165.0 2.6 add_convert_fusion.3
  167.6 1.5 collective-permute-start.30
  169.0 15.8 %feed_grads.1 = (bf16[1024,2048]{1,0:T(8,128)(2,1)}, f32[1,1024]{1,0:T(1,128)}) custom-call(bf16[2048,1024]{1,0:T(8,128)(2,1)} %get-tuple-element.164.normed_ref, bf16[2048,1024]{1,0:T(8,128)(2,1)} %get-tuple-element.165.grad_ref, bf16[2048,1024]{1,0:T(8,128)(2,1)} %get-tuple-element.166.grads_ref, bf16[2048,1024]{1,0:T(8,128)(2,1)} %get-tuple-element.167.active_ref), custom_call_target="tpu_custom_call" | custom-call | flops 8589934592 | bytes 16777216 | tf_op jit(solution)/shard_map/feed_grads/pallas_call | solution.py:762
  184.9 1.2 copy-done.11
  186.1 1.6 add_convert_fusion.2
  187.7 1.0 fusion.7
  188.7 4.4 %collective-permute-done.30.refs_2_ = bf16[512,1024]{1,0:T(8,128)(2,1)} collective-permute-done((bf16[512,1024]{1,0:T(8,128)(2,1)}, bf16[512,1024]{1,0:T(8,128)(2,1)}, u32[]{:S(2)}, u32[]{:S(2)}) %collective-permute-start.30) | collective-permute-done | bytes 1048608 | tf_op jit(solution)/shard_map/ppermute | solution.py:30
  193.1 1.5 collective-permute-start.35
  194.6 9.9 %middle_back.1 = (bf16[512,1024]{1,0:T(8,128)(2,1)}, f32[4,1024]{1,0:T(4,128)}, bf16[512,256]{1,0:T(8,128)(2,1)}, bf16[512,256]{1,0:T(8,128)(2,1)}, bf16[512,256...) custom-call(s32[8]{0:T(128)} %broadcast_xor_fusion.owner_b.owner, ...), custom_call_target="tpu_custom_call" | custom-call | flops 2147483648 | bytes 10485760 | tf_op jit(solution)/shard_map/middle_back/pallas_call | solution.py:904
  204.5 1.9 collective-permute-done.35
  207.6 1.5 collective-permute-start.33
  209.8 1.2 add_convert_fusion.5
  211.0 6.0 %collective-permute-done.33.refs_5_ = bf16[512,256]{1,0:T(8,128)(2,1)S(1)} collective-permute-done((bf16[512,256]{1,0:T(8,128)(2,1)}, bf16[512,256]{1,0:T(8,128)(2,1)S(1)}, u32[]{:S(2)}, u32[]{:S(2)}) %collective-permute-start.33) | collective-permute-done | bytes 262176 | tf_op jit(solution)/shard_map/ppermute | solution.py:30
  217.0 3.7 %collective-permute-done.34.refs_6_ = bf16[512,256]{1,0:T(8,128)(2,1)S(1)} collective-permute-done((bf16[512,256]{1,0:T(8,128)(2,1)}, bf16[512,256]{1,0:T(8,128)(2,1)S(1)}, u32[]{:S(2)}, u32[]{:S(2)}) %collective-permute-start.34) | collective-permute-done | bytes 262176 | tf_op jit(solution)/shard_map/ppermute | solution.py:30
  220.8 1.4 collective-permute-start.37
  223.8 37.0 %attend_back.1 = (bf16[4,128,512]{2,1,0:T(8,128)(2,1)}, bf16[4,128,512]{2,1,0:T(8,128)(2,1)}, bf16[4,128,256]{2,1,0:T(8,128)(2,1)S(1)}, bf16[4,128,256]{2,1,0:T(...) custom-call(s32[8]{0:T(128)S(1)} %copy-done.3, ...), custom_call_target="tpu_custom_call" | custom-call | flops 10737418240 | bytes 20971520 | tf_op jit(solution)/shard_map/attend_back/pallas_call | solution.py:615
  263.5 1.6 add_convert_fusion.4
  266.0 1.5 collective-permute-start.49
  268.1 1.5 collective-permute-start.43
  269.6 8.7 %collective-permute-done.49 = f32[104,128]{1,0:T(8,128)S(1)} collective-permute-done((f32[104,128]{1,0:T(8,128)S(1)}, f32[104,128]{1,0:T(8,128)S(1)}, u32[]{:S(2)}, u32[]{:S(2)}) %collective-permute-start.49) | collective-permute-done | bytes 53280 | tf_op jit(solution)/shard_map/ppermute | solution.py:30
  281.5 1.1 collective-permute-start.44
  282.7 1.9 add_convert_fusion
  284.6 1.4 collective-permute-start.46
  286.0 1.6 collective-permute-start.45
  287.7 1.3 collective-permute-start.51
  289.1 13.6 %collective-permute-done.45 = bf16[2,128,512]{2,1,0:T(8,128)(2,1)S(1)} collective-permute-done((bf16[2,128,512]{2,1,0:T(8,128)(2,1)S(1)}, bf16[2,128,512]{2,1,0:T(8,128)(2,1)S(1)}, u32[]{:S(2)}, u32[]{:S(2)}) %collective-permute-start.45) | collective-permute-done | bytes 262176 | tf_op jit(solution)/shard_map/ppermute | solution.py:30
  305.2 4.6 %input_back.1 = bf16[512,1024]{1,0:T(8,128)(2,1)} custom-call(bf16[512,1024]{1,0:T(8,128)(2,1)} %get-tuple-element.222.refs_0_, bf16[512,1024]{1,0:T(8,128)(2,1)} %copy-done.15, bf16[256,1024]{1,0:T(8,128)(2,1)} %copy-done.18, bf16[256,1024]{1,0:T(8,128)(2,1)} %copy-done.20, bf16[512,1024]{1,0:T(8,128)(2,1)} %refs_4_.1, ...), custom_call_target="tpu_custom_call" | custom-call | flops 10485760 | bytes 7340032 | tf_op jit(solution)/shard_map/input_back/pallas_call | solution.py:936
  310.6 1.1 collective-permute-start.54
  311.6 1.0 fusion.1
  317.0 2.1 fusion.9
  (239 shorter events, 37.3 us)
Async XLA Ops:
  7.2 121.0 %all-gather.2.cloned.1.call-start = ((), (), s32[]{:S(2)}) async-start(), calls=%async_computation.1 | async-start | bytes 4718592 | tf_op jit(solution)/shard_map/all_gather | solution.py:1011
  8.9 9.7 %collective-permute-start = (f32[96,128]{1,0:T(8,128)S(1)}, f32[96,128]{1,0:T(8,128)S(1)}, u32[]{:S(2)}, u32[]{:S(2)}) collective-permute-start(f32[96,128]{1,0:T(8,128)S(1)} %maximum_bitcast_fusion.2), channel_id=1, source_target_pairs={{0,1},{1,0},{2,3},{3,2},{4,5},{5,4},{6,7},{7,6},{8,9},{9,8},{10,11... | collective-permute-start | bytes 147464 | tf_op jit(solution)/shard_map/ppermute | solution.py:30
  10.7 14.2 %collective-permute-start.5 = (bf16[1,128,512]{2,1,0:T(8,128)(2,1)S(1)}, bf16[1,128,512]{2,1,0:T(8,128)(2,1)S(1)}, u32[]{:S(2)}, u32[]{:S(2)}) collective-permute-start(bf16[1,128,512]{2,1,0:T(8,128)(2,1)S(1)} %bitcast.71), channel_id=1, source_target_pairs={{0,16},{4,20},{8,24},{12,28},{16,0},{20,4},{24,8},{28,12},{1,17},{... | collective-permute-start | bytes 393224 | tf_op jit(solution)/shard_map/ppermute | solution.py:30
  15.3 14.9 %collective-permute-start.8 = (bf16[1,128,512]{2,1,0:T(8,128)(2,1)S(1)}, bf16[1,128,512]{2,1,0:T(8,128)(2,1)S(1)}, u32[]{:S(2)}, u32[]{:S(2)}) collective-permute-start(bf16[1,128,512]{2,1,0:T(8,128)(2,1)S(1)} %maximum_bitcast_fusion), channel_id=1, source_target_pairs={{0,4},{4,0},{8,12},{12,8},{16,20},{20,16},{24,28},{28,24},{1,5},{5... | collective-permute-start | bytes 393224 | tf_op jit(solution)/shard_map/ppermute | solution.py:30
  18.6 5.0 %collective-permute-start.1 = (f32[96,128]{1,0:T(8,128)S(1)}, f32[96,128]{1,0:T(8,128)S(1)}, u32[]{:S(2)}, u32[]{:S(2)}) collective-permute-start(f32[96,128]{1,0:T(8,128)S(1)} %fusion.4), channel_id=1, source_target_pairs={{0,2},{1,3},{2,0},{3,1},{4,6},{5,7},{6,4},{7,5},{8,10},{9,11},{10,... | collective-permute-start | bytes 147464 | tf_op jit(solution)/shard_map/ppermute | solution.py:30
  23.7 25.0 %collective-permute-start.3 = (bf16[512,1024]{1,0:T(8,128)(2,1)}, bf16[512,1024]{1,0:T(8,128)(2,1)S(1)}, u32[]{:S(2)}, u32[]{:S(2)}) collective-permute-start(bf16[512,1024]{1,0:T(8,128)(2,1)} %unit.1.refs_0_.refs_7_), channel_id=1, source_target_pairs={{0,2},{1,3},{2,0},{3,1},{4,6},{5,7},{6,4},{7,5},{8,10},{9,11},{10,... | collective-permute-start | bytes 3145736 | tf_op jit(solution)/shard_map/ppermute | solution.py:30
  24.5 4.1 %collective-permute-start.11 = (f32[96,128]{1,0:T(8,128)S(1)}, f32[96,128]{1,0:T(8,128)S(1)}, u32[]{:S(2)}, u32[]{:S(2)}) collective-permute-start(f32[96,128]{1,0:T(8,128)S(1)} %bitcast.81), channel_id=1, source_target_pairs={{0,4},{4,0},{8,12},{12,8},{16,20},{20,16},{24,28},{28,24},{1,5},{5... | collective-permute-start | bytes 147464 | tf_op jit(solution)/shard_map/ppermute | solution.py:30
  25.0 12.5 %collective-permute-start.6 = (bf16[2,128,512]{2,1,0:T(8,128)(2,1)S(1)}, bf16[2,128,512]{2,1,0:T(8,128)(2,1)S(1)}, u32[]{:S(2)}, u32[]{:S(2)}) collective-permute-start(bf16[2,128,512]{2,1,0:T(8,128)(2,1)S(1)} %pad_maximum_fusion.8), channel_id=1, source_target_pairs={{0,8},{4,12},{8,0},{12,4},{16,24},{20,28},{24,16},{28,20},{1,9},{5... | collective-permute-start | bytes 786440 | tf_op jit(solution)/shard_map/ppermute | solution.py:30
  28.6 6.1 %collective-permute-start.12 = (f32[96,128]{1,0:T(8,128)S(1)}, f32[96,128]{1,0:T(8,128)S(1)}, u32[]{:S(2)}, u32[]{:S(2)}) collective-permute-start(f32[96,128]{1,0:T(8,128)S(1)} %bitcast_add_fusion), channel_id=1, source_target_pairs={{0,8},{4,12},{8,0},{12,4},{16,24},{20,28},{24,16},{28,20},{1,9},{5... | collective-permute-start | bytes 147464 | tf_op jit(solution)/shard_map/ppermute | solution.py:30
  30.2 14.0 %collective-permute-start.9 = (bf16[2,128,512]{2,1,0:T(8,128)(2,1)S(1)}, bf16[2,128,512]{2,1,0:T(8,128)(2,1)S(1)}, u32[]{:S(2)}, u32[]{:S(2)}) collective-permute-start(bf16[2,128,512]{2,1,0:T(8,128)(2,1)S(1)} %pad_maximum_fusion.9), channel_id=1, source_target_pairs={{0,16},{4,20},{8,24},{12,28},{16,0},{20,4},{24,8},{28,12},{1,17},{... | collective-permute-start | bytes 786440 | tf_op jit(solution)/shard_map/ppermute | solution.py:30
  34.7 10.0 %collective-permute-start.13 = (f32[96,128]{1,0:T(8,128)S(1)}, f32[96,128]{1,0:T(8,128)S(1)}, u32[]{:S(2)}, u32[]{:S(2)}) collective-permute-start(f32[96,128]{1,0:T(8,128)S(1)} %fusion.14), channel_id=1, source_target_pairs={{0,16},{4,20},{8,24},{12,28},{16,0},{20,4},{24,8},{28,12},{1,17},{... | collective-permute-start | bytes 147464 | tf_op jit(solution)/shard_map/ppermute | solution.py:30
  37.5 12.1 %collective-permute-start.7 = (bf16[4,128,512]{2,1,0:T(8,128)(2,1)S(1)}, bf16[4,128,512]{2,1,0:T(8,128)(2,1)S(1)}, u32[]{:S(2)}, u32[]{:S(2)}) collective-permute-start(bf16[4,128,512]{2,1,0:T(8,128)(2,1)S(1)} %pad_maximum_fusion.3), channel_id=1, source_target_pairs={{0,4},{4,0},{8,12},{12,8},{16,20},{20,16},{24,28},{28,24},{1,5},{5... | collective-permute-start | bytes 1572872 | tf_op jit(solution)/shard_map/ppermute | solution.py:30
  44.3 11.8 %collective-permute-start.10 = (bf16[4,128,512]{2,1,0:T(8,128)(2,1)S(1)}, bf16[4,128,512]{2,1,0:T(8,128)(2,1)S(1)}, u32[]{:S(2)}, u32[]{:S(2)}) collective-permute-start(bf16[4,128,512]{2,1,0:T(8,128)(2,1)S(1)} %pad_maximum_fusion.4), channel_id=1, source_target_pairs={{0,8},{4,12},{8,0},{12,4},{16,24},{20,28},{24,16},{28,20},{1,9},{5... | collective-permute-start | bytes 1572872 | tf_op jit(solution)/shard_map/ppermute | solution.py:30
  48.7 8.5 %collective-permute-start.14 = (bf16[128,1024]{1,0:T(8,128)(2,1)S(1)}, bf16[128,1024]{1,0:T(8,128)(2,1)}, u32[]{:S(2)}, u32[]{:S(2)}) collective-permute-start(bf16[128,1024]{1,0:T(8,128)(2,1)S(1)} %copy-done.26), channel_id=1, source_target_pairs={{0,2},{1,3},{2,0},{3,1},{4,6},{5,7},{6,4},{7,5},{8,10},{9,11},{10,... | collective-permute-start | bytes 786440 | tf_op jit(solution)/shard_map/ppermute | solution.py:30
  57.2 259.8 %reduce-scatter.2.cloned.1.call-start = ((), (), s32[]{:S(2)}) async-start(), calls=%async_computation.2 | async-start | bytes 4718592 | tf_op jit(solution)/shard_map/reduce_scatter | solution.py:1066
  57.3 16.3 %collective-permute-start.2 = (bf16[512,1024]{1,0:T(8,128)(2,1)S(1)}, bf16[512,1024]{1,0:T(8,128)(2,1)}, u32[]{:S(2)}, u32[]{:S(2)}) collective-permute-start(bf16[512,1024]{1,0:T(8,128)(2,1)S(1)} %copy-done.13), channel_id=1, source_target_pairs={{0,1},{1,0},{2,3},{3,2},{4,5},{5,4},{6,7},{7,6},{8,9},{9,8},{10,11... | collective-permute-start | bytes 3145736 | tf_op jit(solution)/shard_map/ppermute | solution.py:30
  57.4 16.2 %collective-permute-start.4 = (bf16[512,1024]{1,0:T(8,128)(2,1)}, bf16[512,1024]{1,0:T(8,128)(2,1)}, u32[]{:S(2)}, u32[]{:S(2)}) collective-permute-start(bf16[512,1024]{1,0:T(8,128)(2,1)} %copy-done.32), channel_id=1, source_target_pairs={{0,1},{1,0},{2,3},{3,2},{4,5},{5,4},{6,7},{7,6},{8,9},{9,8},{10,11... | collective-permute-start | bytes 3145736 | tf_op jit(solution)/shard_map/ppermute | solution.py:30
  59.9 8.3 %collective-permute-start.15 = (bf16[128,1024]{1,0:T(8,128)(2,1)S(1)}, bf16[128,1024]{1,0:T(8,128)(2,1)S(1)}, u32[]{:S(2)}, u32[]{:S(2)}) collective-permute-start(bf16[128,1024]{1,0:T(8,128)(2,1)S(1)} %get-tuple-element.129), channel_id=1, source_target_pairs={{0,2},{1,3},{2,0},{3,1},{4,6},{5,7},{6,4},{7,5},{8,10},{9,11},{10,... | collective-permute-start | bytes 786440 | tf_op jit(solution)/shard_map/ppermute | solution.py:30
  70.4 24.8 %collective-permute-start.16 = (bf16[1024,256]{1,0:T(8,128)(2,1)}, bf16[1024,256]{1,0:T(8,128)(2,1)S(1)}, u32[]{:S(2)}, u32[]{:S(2)}) collective-permute-start(bf16[1024,256]{1,0:T(8,128)(2,1)} %placed_rows.1.refs_4_.refs_3_), channel_id=1, source_target_pairs={{0,2},{1,3},{2,0},{3,1},{4,6},{5,7},{6,4},{7,5},{8,10},{9,11},{10,... | collective-permute-start | bytes 1572872 | tf_op jit(solution)/shard_map/ppermute | solution.py:30
  72.0 23.1 %collective-permute-start.17 = (bf16[256,1024]{1,0:T(8,128)(2,1)}, bf16[256,1024]{1,0:T(8,128)(2,1)}, u32[]{:S(2)}, u32[]{:S(2)}) collective-permute-start(bf16[256,1024]{1,0:T(8,128)(2,1)} %slice.188), channel_id=1, source_target_pairs={{0,2},{1,3},{2,0},{3,1},{4,6},{5,7},{6,4},{7,5},{8,10},{9,11},{10,... | collective-permute-start | bytes 1572872 | tf_op jit(solution)/shard_map/ppermute | solution.py:30
  73.6 24.6 %collective-permute-start.21 = (bf16[1024,256]{1,0:T(8,128)(2,1)}, bf16[1024,256]{1,0:T(8,128)(2,1)S(1)}, u32[]{:S(2)}, u32[]{:S(2)}) collective-permute-start(bf16[1024,256]{1,0:T(8,128)(2,1)} %placed_rows.1.refs_4_.refs_3_), channel_id=1, source_target_pairs={{0,1},{1,0},{2,3},{3,2},{4,5},{5,4},{6,7},{7,6},{8,9},{9,8},{10,11... | collective-permute-start | bytes 1572872 | tf_op jit(solution)/shard_map/ppermute | solution.py:30
  95.2 14.8 %collective-permute-start.22 = (bf16[1024,256]{1,0:T(8,128)(2,1)S(1)}, bf16[1024,256]{1,0:T(8,128)(2,1)}, u32[]{:S(2)}, u32[]{:S(2)}) collective-permute-start(bf16[1024,256]{1,0:T(8,128)(2,1)S(1)} %collective-permute-done.16.refs_6_.refs_5_), channel_id=1, source_target_pairs={{0,1},{1,0},{2,3},{3,2},{4,5},{5,4},{6,7},{7,6},{8,9},{9,8},{10,11... | collective-permute-start | bytes 1572872 | tf_op jit(solution)/shard_map/ppermute | solution.py:30
  95.7 3.3 %collective-permute-start.18 = (bf16[512,256]{1,0:T(8,128)(2,1)}, bf16[512,256]{1,0:T(8,128)(2,1)S(1)}, u32[]{:S(2)}, u32[]{:S(2)}) collective-permute-start(bf16[512,256]{1,0:T(8,128)(2,1)} %get-tuple-element.141), channel_id=1, source_target_pairs={{0,1},{1,0},{2,3},{3,2},{4,5},{5,4},{6,7},{7,6},{8,9},{9,8},{10,11... | collective-permute-start | bytes 786440 | tf_op jit(solution)/shard_map/ppermute | solution.py:30
  95.8 9.4 %collective-permute-start.19 = (bf16[512,256]{1,0:T(8,128)(2,1)}, bf16[512,256]{1,0:T(8,128)(2,1)}, u32[]{:S(2)}, u32[]{:S(2)}) collective-permute-start(bf16[512,256]{1,0:T(8,128)(2,1)} %get-tuple-element.142), channel_id=1, source_target_pairs={{0,2},{1,3},{2,0},{3,1},{4,6},{5,7},{6,4},{7,5},{8,10},{9,11},{10,... | collective-permute-start | bytes 786440 | tf_op jit(solution)/shard_map/ppermute | solution.py:30
  97.4 12.5 %collective-permute-start.20 = (bf16[512,256]{1,0:T(8,128)(2,1)}, bf16[512,256]{1,0:T(8,128)(2,1)}, u32[]{:S(2)}, u32[]{:S(2)}) collective-permute-start(bf16[512,256]{1,0:T(8,128)(2,1)} %get-tuple-element.143), channel_id=1, source_target_pairs={{0,3},{1,2},{2,1},{3,0},{4,7},{5,6},{6,5},{7,4},{8,11},{9,10},{10,... | collective-permute-start | bytes 786440 | tf_op jit(solution)/shard_map/ppermute | solution.py:30
  98.2 22.7 %collective-permute-start.24 = (bf16[512,1024]{1,0:T(8,128)(2,1)S(1)}, bf16[512,1024]{1,0:T(8,128)(2,1)}, u32[]{:S(2)}, u32[]{:S(2)}) collective-permute-start(bf16[512,1024]{1,0:T(8,128)(2,1)S(1)} %copy-done.5), channel_id=1, source_target_pairs={{0,1},{1,0},{2,3},{3,2},{4,5},{5,4},{6,7},{7,6},{8,9},{9,8},{10,11... | collective-permute-start | bytes 3145736 | tf_op jit(solution)/shard_map/ppermute | solution.py:30
  114.9 6.0 %collective-permute-start.23 = (bf16[512,1024]{1,0:T(8,128)(2,1)}, bf16[512,1024]{1,0:T(8,128)(2,1)}, u32[]{:S(2)}, u32[]{:S(2)}) collective-permute-start(bf16[512,1024]{1,0:T(8,128)(2,1)} %get-tuple-element.146.refs_0_), channel_id=1, source_target_pairs={{0,1},{1,0},{2,3},{3,2},{4,5},{5,4},{6,7},{7,6},{8,9},{9,8},{10,11... | collective-permute-start | bytes 3145736 | tf_op jit(solution)/shard_map/ppermute | solution.py:30
  117.1 26.1 %collective-permute-start.26 = (bf16[512,1024]{1,0:T(8,128)(2,1)}, bf16[512,1024]{1,0:T(8,128)(2,1)}, u32[]{:S(2)}, u32[]{:S(2)}) collective-permute-start(bf16[512,1024]{1,0:T(8,128)(2,1)} %get-tuple-element.146.refs_0_), channel_id=1, source_target_pairs={{0,2},{1,3},{2,0},{3,1},{4,6},{5,7},{6,4},{7,5},{8,10},{9,11},{10,... | collective-permute-start | bytes 3145736 | tf_op jit(solution)/shard_map/ppermute | solution.py:30
  120.8 22.4 %collective-permute-start.28 = (bf16[512,1024]{1,0:T(8,128)(2,1)S(1)}, bf16[512,1024]{1,0:T(8,128)(2,1)}, u32[]{:S(2)}, u32[]{:S(2)}) collective-permute-start(bf16[512,1024]{1,0:T(8,128)(2,1)S(1)} %constant_dynamic-update-slice_fusion.refs_2_), channel_id=1, source_target_pairs={{0,1},{1,0},{2,3},{3,2},{4,5},{5,4},{6,7},{7,6},{8,9},{9,8},{10,11... | collective-permute-start | bytes 3145736 | tf_op jit(solution)/shard_map/ppermute | solution.py:30
  143.2 2.9 collective-permute-start.27
  162.0 2.9 collective-permute-start.29
  162.2 26.5 %collective-permute-start.25 = (bf16[512,1024]{1,0:T(8,128)(2,1)}, bf16[512,1024]{1,0:T(8,128)(2,1)S(1)}, u32[]{:S(2)}, u32[]{:S(2)}) collective-permute-start(bf16[512,1024]{1,0:T(8,128)(2,1)} %get-tuple-element.149), channel_id=1, source_target_pairs={{0,1},{1,0},{2,3},{3,2},{4,5},{5,4},{6,7},{7,6},{8,9},{9,8},{10,11... | collective-permute-start | bytes 3145736 | tf_op jit(solution)/shard_map/ppermute | solution.py:30
  162.6 22.3 %collective-permute-start.31 = (bf16[512,1024]{1,0:T(8,128)(2,1)}, bf16[512,1024]{1,0:T(8,128)(2,1)}, u32[]{:S(2)}, u32[]{:S(2)}) collective-permute-start(bf16[512,1024]{1,0:T(8,128)(2,1)} %get-tuple-element.170), channel_id=1, source_target_pairs={{0,1},{1,0},{2,3},{3,2},{4,5},{5,4},{6,7},{7,6},{8,9},{9,8},{10,11... | collective-permute-start | bytes 3145736 | tf_op jit(solution)/shard_map/ppermute | solution.py:30
  167.6 25.5 %collective-permute-start.30 = (bf16[512,1024]{1,0:T(8,128)(2,1)}, bf16[512,1024]{1,0:T(8,128)(2,1)}, u32[]{:S(2)}, u32[]{:S(2)}) collective-permute-start(bf16[512,1024]{1,0:T(8,128)(2,1)} %add_convert_fusion.3), channel_id=1, source_target_pairs={{0,2},{1,3},{2,0},{3,1},{4,6},{5,7},{6,4},{7,5},{8,10},{9,11},{10,... | collective-permute-start | bytes 3145736 | tf_op jit(solution)/shard_map/ppermute | solution.py:30
  193.1 13.3 %collective-permute-start.35 = (bf16[256,1024]{1,0:T(8,128)(2,1)}, bf16[256,1024]{1,0:T(8,128)(2,1)S(1)}, u32[]{:S(2)}, u32[]{:S(2)}) collective-permute-start(bf16[256,1024]{1,0:T(8,128)(2,1)} %get-tuple-element.183), channel_id=1, source_target_pairs={{0,2},{1,3},{2,0},{3,1},{4,6},{5,7},{6,4},{7,5},{8,10},{9,11},{10,... | collective-permute-start | bytes 1572872 | tf_op jit(solution)/shard_map/ppermute | solution.py:30
  194.6 28.2 %copy-start.1 = (s32[418]{0:T(512)S(1)}, s32[418]{0:T(512)}, u32[]{:S(2)}) copy-start(s32[418]{0:T(512)} %pad_add_fusion.facts) | copy-start | bytes 5020
  194.6 28.2 %copy-start.3 = (s32[8]{0:T(128)S(1)}, s32[8]{0:T(128)}, u32[]{:S(2)}) copy-start(s32[8]{0:T(128)} %broadcast_xor_fusion.1.owner_a) | copy-start | bytes 100
  194.6 28.2 %copy-start.4 = (f32[32,256]{1,0:T(8,128)S(1)}, f32[32,256]{1,0:T(8,128)}, u32[]{:S(2)}) copy-start(f32[32,256]{1,0:T(8,128)} %get-tuple-element.133.refs_1_) | copy-start | bytes 98308
  206.4 3.3 %collective-permute-start.36 = (bf16[8,128,256]{2,1,0:T(8,128)(2,1)}, bf16[8,128,256]{2,1,0:T(8,128)(2,1)S(1)}, u32[]{:S(2)}, u32[]{:S(2)}) collective-permute-start(bf16[8,128,256]{2,1,0:T(8,128)(2,1)} %get-tuple-element.185), channel_id=1, source_target_pairs={{0,1},{1,0},{2,3},{3,2},{4,5},{5,4},{6,7},{7,6},{8,9},{9,8},{10,11... | collective-permute-start | bytes 1572872 | tf_op jit(solution)/shard_map/ppermute | solution.py:30
  207.1 3.8 %collective-permute-start.32 = (bf16[512,256]{1,0:T(8,128)(2,1)}, bf16[512,256]{1,0:T(8,128)(2,1)S(1)}, u32[]{:S(2)}, u32[]{:S(2)}) collective-permute-start(bf16[512,256]{1,0:T(8,128)(2,1)} %get-tuple-element.176), channel_id=1, source_target_pairs={{0,1},{1,0},{2,3},{3,2},{4,5},{5,4},{6,7},{7,6},{8,9},{9,8},{10,11... | collective-permute-start | bytes 786440 | tf_op jit(solution)/shard_map/ppermute | solution.py:30
  207.6 9.4 %collective-permute-start.33 = (bf16[512,256]{1,0:T(8,128)(2,1)}, bf16[512,256]{1,0:T(8,128)(2,1)S(1)}, u32[]{:S(2)}, u32[]{:S(2)}) collective-permute-start(bf16[512,256]{1,0:T(8,128)(2,1)} %get-tuple-element.177), channel_id=1, source_target_pairs={{0,2},{1,3},{2,0},{3,1},{4,6},{5,7},{6,4},{7,5},{8,10},{9,11},{10,... | collective-permute-start | bytes 786440 | tf_op jit(solution)/shard_map/ppermute | solution.py:30
  209.1 11.7 %collective-permute-start.34 = (bf16[512,256]{1,0:T(8,128)(2,1)}, bf16[512,256]{1,0:T(8,128)(2,1)S(1)}, u32[]{:S(2)}, u32[]{:S(2)}) collective-permute-start(bf16[512,256]{1,0:T(8,128)(2,1)} %get-tuple-element.178), channel_id=1, source_target_pairs={{0,3},{1,2},{2,1},{3,0},{4,7},{5,6},{6,5},{7,4},{8,11},{9,10},{10,... | collective-permute-start | bytes 786440 | tf_op jit(solution)/shard_map/ppermute | solution.py:30
  209.1 51.7 %collective-permute-start.38 = (bf16[8,128,256]{2,1,0:T(8,128)(2,1)}, bf16[8,128,256]{2,1,0:T(8,128)(2,1)S(1)}, u32[]{:S(2)}, u32[]{:S(2)}) collective-permute-start(bf16[8,128,256]{2,1,0:T(8,128)(2,1)} %get-tuple-element.195), channel_id=1, source_target_pairs={{0,1},{1,0},{2,3},{3,2},{4,5},{5,4},{6,7},{7,6},{8,9},{9,8},{10,11... | collective-permute-start | bytes 1572872 | tf_op jit(solution)/shard_map/ppermute | solution.py:30
  220.8 40.0 %collective-permute-start.37 = (bf16[256,1024]{1,0:T(8,128)(2,1)}, bf16[256,1024]{1,0:T(8,128)(2,1)S(1)}, u32[]{:S(2)}, u32[]{:S(2)}) collective-permute-start(bf16[256,1024]{1,0:T(8,128)(2,1)} %get-tuple-element.193), channel_id=1, source_target_pairs={{0,2},{1,3},{2,0},{3,1},{4,6},{5,7},{6,4},{7,5},{8,10},{9,11},{10,... | collective-permute-start | bytes 1572872 | tf_op jit(solution)/shard_map/ppermute | solution.py:30
  222.2 38.6 %collective-permute-start.39 = (bf16[8,128,256]{2,1,0:T(8,128)(2,1)S(1)}, bf16[8,128,256]{2,1,0:T(8,128)(2,1)S(1)}, u32[]{:S(2)}, u32[]{:S(2)}) collective-permute-start(bf16[8,128,256]{2,1,0:T(8,128)(2,1)S(1)} %add_convert_fusion.5), channel_id=1, source_target_pairs={{0,2},{1,3},{2,0},{3,1},{4,6},{5,7},{6,4},{7,5},{8,10},{9,11},{10,... | collective-permute-start | bytes 1572872 | tf_op jit(solution)/shard_map/ppermute | solution.py:30
  223.8 38.6 %copy-start.28 = (f32[4,1024]{1,0:T(4,128)S(1)}, f32[4,1024]{1,0:T(4,128)}, u32[]{:S(2)}) copy-start(f32[4,1024]{1,0:T(4,128)} %get-tuple-element.228) | copy-start | bytes 49156
  223.8 38.6 %copy-start.30 = (f32[1,1024]{1,0:T(1,128)S(1)}, f32[1,1024]{1,0:T(1,128)}, u32[]{:S(2)}) copy-start(f32[1,1024]{1,0:T(1,128)} %get-tuple-element.230) | copy-start | bytes 12292
  261.6 6.0 %collective-permute-start.40 = (bf16[512,1024]{1,0:T(8,128)(2,1)}, bf16[512,1024]{1,0:T(8,128)(2,1)S(1)}, u32[]{:S(2)}, u32[]{:S(2)}) collective-permute-start(bf16[512,1024]{1,0:T(8,128)(2,1)} %get-tuple-element.202), channel_id=1, source_target_pairs={{0,1},{1,0},{2,3},{3,2},{4,5},{5,4},{6,7},{7,6},{8,9},{9,8},{10,11... | collective-permute-start | bytes 3145736 | tf_op jit(solution)/shard_map/ppermute | solution.py:30
  262.1 20.5 %collective-permute-start.47 = (bf16[512,1024]{1,0:T(8,128)(2,1)}, bf16[512,1024]{1,0:T(8,128)(2,1)S(1)}, u32[]{:S(2)}, u32[]{:S(2)}) collective-permute-start(bf16[512,1024]{1,0:T(8,128)(2,1)} %get-tuple-element.218), channel_id=1, source_target_pairs={{0,1},{1,0},{2,3},{3,2},{4,5},{5,4},{6,7},{7,6},{8,9},{9,8},{10,11... | collective-permute-start | bytes 3145736 | tf_op jit(solution)/shard_map/ppermute | solution.py:30
  262.8 16.5 %collective-permute-start.41 = (bf16[4,128,512]{2,1,0:T(8,128)(2,1)}, bf16[4,128,512]{2,1,0:T(8,128)(2,1)S(1)}, u32[]{:S(2)}, u32[]{:S(2)}) collective-permute-start(bf16[4,128,512]{2,1,0:T(8,128)(2,1)} %get-tuple-element.211), channel_id=1, source_target_pairs={{0,4},{4,0},{8,12},{12,8},{16,20},{20,16},{24,28},{28,24},{1,5},{5... | collective-permute-start | bytes 1572872 | tf_op jit(solution)/shard_map/ppermute | solution.py:30
  265.1 15.2 %collective-permute-start.42 = (bf16[4,128,512]{2,1,0:T(8,128)(2,1)S(1)}, bf16[4,128,512]{2,1,0:T(8,128)(2,1)S(1)}, u32[]{:S(2)}, u32[]{:S(2)}) collective-permute-start(bf16[4,128,512]{2,1,0:T(8,128)(2,1)S(1)} %pad_maximum_fusion.6), channel_id=1, source_target_pairs={{0,8},{4,12},{8,0},{12,4},{16,24},{20,28},{24,16},{28,20},{1,9},{5... | collective-permute-start | bytes 1572872 | tf_op jit(solution)/shard_map/ppermute | solution.py:30
  266.0 12.3 %collective-permute-start.49 = (f32[104,128]{1,0:T(8,128)S(1)}, f32[104,128]{1,0:T(8,128)S(1)}, u32[]{:S(2)}, u32[]{:S(2)}) collective-permute-start(f32[104,128]{1,0:T(8,128)S(1)} %maximum_bitcast_fusion.1), channel_id=1, source_target_pairs={{0,4},{4,0},{8,12},{12,8},{16,20},{20,16},{24,28},{28,24},{1,5},{5... | collective-permute-start | bytes 159752 | tf_op jit(solution)/shard_map/ppermute | solution.py:30
  268.1 13.3 %collective-permute-start.43 = (bf16[256,1024]{1,0:T(8,128)(2,1)S(1)}, bf16[256,1024]{1,0:T(8,128)(2,1)S(1)}, u32[]{:S(2)}, u32[]{:S(2)}) collective-permute-start(bf16[256,1024]{1,0:T(8,128)(2,1)S(1)} %get-tuple-element.247), channel_id=1, source_target_pairs={{0,2},{1,3},{2,0},{3,1},{4,6},{5,7},{6,4},{7,5},{8,10},{9,11},{10,... | collective-permute-start | bytes 1572872 | tf_op jit(solution)/shard_map/ppermute | solution.py:30
  278.4 9.3 %collective-permute-start.50 = (f32[104,128]{1,0:T(8,128)S(1)}, f32[104,128]{1,0:T(8,128)S(1)}, u32[]{:S(2)}, u32[]{:S(2)}) collective-permute-start(f32[104,128]{1,0:T(8,128)S(1)} %fusion.5), channel_id=1, source_target_pairs={{0,8},{4,12},{8,0},{12,4},{16,24},{20,28},{24,16},{28,20},{1,9},{5... | collective-permute-start | bytes 159752 | tf_op jit(solution)/shard_map/ppermute | solution.py:30
  281.5 7.6 %collective-permute-start.44 = (bf16[2,128,512]{2,1,0:T(8,128)(2,1)S(1)}, bf16[2,128,512]{2,1,0:T(8,128)(2,1)S(1)}, u32[]{:S(2)}, u32[]{:S(2)}) collective-permute-start(bf16[2,128,512]{2,1,0:T(8,128)(2,1)S(1)} %get-tuple-element.215), channel_id=1, source_target_pairs={{0,8},{4,12},{8,0},{12,4},{16,24},{20,28},{24,16},{28,20},{1,9},{5... | collective-permute-start | bytes 786440 | tf_op jit(solution)/shard_map/ppermute | solution.py:30
  284.6 18.9 %collective-permute-start.46 = (bf16[256,1024]{1,0:T(8,128)(2,1)S(1)}, bf16[256,1024]{1,0:T(8,128)(2,1)S(1)}, u32[]{:S(2)}, u32[]{:S(2)}) collective-permute-start(bf16[256,1024]{1,0:T(8,128)(2,1)S(1)} %get-tuple-element.246), channel_id=1, source_target_pairs={{0,2},{1,3},{2,0},{3,1},{4,6},{5,7},{6,4},{7,5},{8,10},{9,11},{10,... | collective-permute-start | bytes 1572872 | tf_op jit(solution)/shard_map/ppermute | solution.py:30
  286.0 18.2 %collective-permute-start.48 = (bf16[512,1024]{1,0:T(8,128)(2,1)S(1)}, bf16[512,1024]{1,0:T(8,128)(2,1)S(1)}, u32[]{:S(2)}, u32[]{:S(2)}) collective-permute-start(bf16[512,1024]{1,0:T(8,128)(2,1)S(1)} %copy-done.33), channel_id=1, source_target_pairs={{0,1},{1,0},{2,3},{3,2},{4,5},{5,4},{6,7},{7,6},{8,9},{9,8},{10,11... | collective-permute-start | bytes 3145736 | tf_op jit(solution)/shard_map/ppermute | solution.py:30
  286.0 16.7 %collective-permute-start.45 = (bf16[2,128,512]{2,1,0:T(8,128)(2,1)S(1)}, bf16[2,128,512]{2,1,0:T(8,128)(2,1)S(1)}, u32[]{:S(2)}, u32[]{:S(2)}) collective-permute-start(bf16[2,128,512]{2,1,0:T(8,128)(2,1)S(1)} %get-tuple-element.216), channel_id=1, source_target_pairs={{0,16},{4,20},{8,24},{12,28},{16,0},{20,4},{24,8},{28,12},{1,17},{... | collective-permute-start | bytes 786440 | tf_op jit(solution)/shard_map/ppermute | solution.py:30
  287.7 16.5 %collective-permute-start.51 = (f32[104,128]{1,0:T(8,128)S(1)}, f32[104,128]{1,0:T(8,128)S(1)}, u32[]{:S(2)}, u32[]{:S(2)}) collective-permute-start(f32[104,128]{1,0:T(8,128)S(1)} %fusion.13), channel_id=1, source_target_pairs={{0,16},{4,20},{8,24},{12,28},{16,0},{20,4},{24,8},{28,12},{1,17},{... | collective-permute-start | bytes 159752 | tf_op jit(solution)/shard_map/ppermute | solution.py:30
  303.5 8.2 %collective-permute-start.52 = (bf16[1,128,512]{2,1,0:T(8,128)(2,1)S(1)}, bf16[1,128,512]{2,1,0:T(8,128)(2,1)}, u32[]{:S(2)}, u32[]{:S(2)}) collective-permute-start(bf16[1,128,512]{2,1,0:T(8,128)(2,1)S(1)} %get-tuple-element.233), channel_id=1, source_target_pairs={{0,16},{4,20},{8,24},{12,28},{16,0},{20,4},{24,8},{28,12},{1,17},{... | collective-permute-start | bytes 393224 | tf_op jit(solution)/shard_map/ppermute | solution.py:30
  303.5 8.2 %collective-permute-start.53 = (bf16[1,128,512]{2,1,0:T(8,128)(2,1)}, bf16[1,128,512]{2,1,0:T(8,128)(2,1)}, u32[]{:S(2)}, u32[]{:S(2)}) collective-permute-start(bf16[1,128,512]{2,1,0:T(8,128)(2,1)} %get-tuple-element.235), channel_id=1, source_target_pairs={{0,4},{4,0},{8,12},{12,8},{16,20},{20,16},{24,28},{28,24},{1,5},{5... | collective-permute-start | bytes 393224 | tf_op jit(solution)/shard_map/ppermute | solution.py:30
  309.8 3.8 %collective-permute-start.56 = (f32[104,128]{1,0:T(8,128)S(1)}, f32[104,128]{1,0:T(8,128)S(1)}, u32[]{:S(2)}, u32[]{:S(2)}) collective-permute-start(f32[104,128]{1,0:T(8,128)S(1)} %bitcast.85), channel_id=1, source_target_pairs={{0,3},{1,2},{2,1},{3,0},{4,7},{5,6},{6,5},{7,4},{8,11},{9,10},{10,... | collective-permute-start | bytes 159752 | tf_op jit(solution)/shard_map/ppermute | solution.py:30
  309.8 4.7 %collective-permute-start.55 = (f32[104,128]{1,0:T(8,128)S(1)}, f32[104,128]{1,0:T(8,128)S(1)}, u32[]{:S(2)}, u32[]{:S(2)}) collective-permute-start(f32[104,128]{1,0:T(8,128)S(1)} %bitcast.86), channel_id=1, source_target_pairs={{0,2},{1,3},{2,0},{3,1},{4,6},{5,7},{6,4},{7,5},{8,10},{9,11},{10,... | collective-permute-start | bytes 159752 | tf_op jit(solution)/shard_map/ppermute | solution.py:30
  310.6 3.9 %collective-permute-start.54 = (f32[104,128]{1,0:T(8,128)S(1)}, f32[104,128]{1,0:T(8,128)S(1)}, u32[]{:S(2)}, u32[]{:S(2)}) collective-permute-start(f32[104,128]{1,0:T(8,128)S(1)} %bitcast.87), channel_id=1, source_target_pairs={{0,1},{1,0},{2,3},{3,2},{4,5},{5,4},{6,7},{7,6},{8,9},{9,8},{10,11... | collective-permute-start | bytes 159752 | tf_op jit(solution)/shard_map/ppermute | solution.py:30
  (35 other events, 317.5 us)
Sparse Core Ops, SparseCore 0:
  57.4 70.8 all-gather.1
  185.0 85.5 reduce-scatter.1

commit v5 on v4

--- a/solution.py
+++ b/solution.py
@@ -989,7 +989,7 @@
 
     bits = bits_of("dp")
     order_a = bits[::-1]
-    order_b = bits[:1] + bits[:0:-1]
+    order_b = bits[-1:] + bits[:1] + bits[-2:0:-1]
     owner_a = block_owners("dp", order_a)
     owner_b = block_owners("dp", order_b)
     split = 2 * width

time: 333 us -> 330 us (level)
  waiting for transfers between devices: 89.8 us -> 86.3 us
    ppermute x57, waiting for transfers between devices: 82.5 us -> 74.8 us  [swapped(): return lax.ppermute(value, axis, [(i, i ^ bit) for i in range(count)])]
    all_gather x1, waiting for transfers between devices: 7.25 us -> 11.5 us  [per_device(): feed_full = lax.all_gather(feed_flat, 'dp', axis=0, tiled=True)]
  transfers between devices with their start and end apart: 59 -> 59, of which waited for: 21 -> 23; matrix products, arithmetic and copies ran while one was open for 10% -> 10% of each run, Pallas kernels for 35% -> 35%
where the time goes in v5:
time: 330 us; the launch traced here: 324 us
  Pallas kernels  128 us (39%)
  waiting for transfers between devices  86.3 us (26%)
  starting transfers between devices  51.4 us (16%)
  local copies, waits for them, and re-layouts  23.6 us (7%)
  other arithmetic  18.7 us (6%)
  between operations  15.7 us (5%)
    ppermute x57, waiting for transfers between devices, swapped(): return lax.ppermute(value, axis, [(i, i ^ bit) for i in range(count)])  74.8 us
    ppermute x57, starting transfers between devices, swapped(): return lax.ppermute(value, axis, [(i, i ^ bit) for i in range(count)])  51.3 us
    pallas_call x1, Pallas kernels, attend_back(): pl.pallas_call(functools.partial(attend_back_kernel, heads, len(unit)), g...  37 us
    pallas_call x2, Pallas kernels, feed(): pl.pallas_call(functools.partial(feed_kernel, here, len(stacks)), grid=(h...  29.9 us
    pallas_call x1, Pallas kernels, project_attend(): pl.pallas_call(functools.partial(project_attend_kernel, heads, len(unit))...  21.5 us
    pallas_call x1, Pallas kernels, feed_grads(): pl.pallas_call(feed_grads_kernel, grid=(rows // (2 * TILE),), out_shape=[...  15.8 us
    all_gather x1, waiting for transfers between devices, per_device(): feed_full = lax.all_gather(feed_flat, 'dp', axis=0, tiled=True)  11.5 us
    unnamed x90, local copies, waits for them, and re-layouts  10.3 us
  transfers between devices with their start and end apart: 59, of which 23 were waited for; matrix products, arithmetic and copies ran while one was open for 10% of the time, Pallas kernels for 35%

profile of v5, /device:TPU:0, one launch (start us, length us, event | category | flops | bytes accessed | tf_op | source)
XLA Modules:
  0.0 324.0 jit_solution(6197443370410809823)
XLA Ops:
  9.5 1.1 copy.28
  10.7 3.6 %collective-permute-start.5 = (bf16[1,128,512]{2,1,0:T(8,128)(2,1)S(1)}, bf16[1,128,512]{2,1,0:T(8,128)(2,1)S(1)}, u32[]{:S(2)}, u32[]{:S(2)}) collective-permute-start(bf16[1,128,512]{2,1,0:T(8,128)(2,1)S(1)} %bitcast.71), channel_id=1, source_target_pairs={{0,16},{4,20},{8,24},{12,28},{16,0},{20,4},{24,8},{28,12},{1,17},{... | collective-permute-start | bytes 393224 | tf_op jit(solution)/shard_map/ppermute | solution.py:30
  15.4 1.8 fusion.8
  17.1 2.0 collective-permute-start.1
  20.0 2.5 unit.1.refs_0_.refs_7_
  23.3 1.5 collective-permute-start.11
  24.8 1.6 collective-permute-start.6
  27.4 1.6 collective-permute-start.12
  29.1 1.6 collective-permute-start.9
  30.6 2.9 collective-permute-done.12
  33.6 2.4 collective-permute-start.13
  36.0 1.6 collective-permute-start.7
  37.7 1.9 collective-permute-start.10
  39.5 8.0 %collective-permute-done.3.refs_2_.refs_9_ = bf16[512,1024]{1,0:T(8,128)(2,1)S(1)} collective-permute-done((bf16[512,1024]{1,0:T(8,128)(2,1)}, bf16[512,1024]{1,0:T(8,128)(2,1)S(1)}, u32[]{:S(2)}, u32[]{:S(2)}) %collective-permute-start.3) | collective-permute-done | bytes 1048608 | tf_op jit(solution)/shard_map/ppermute | solution.py:30
  48.7 1.1 pad_maximum_fusion.refs_4_
  50.3 1.1 pad_maximum_fusion.1.refs_5_.blocks_ref
  51.4 3.3 %collective-permute-done.14 = bf16[128,1024]{1,0:T(8,128)(2,1)} collective-permute-done((bf16[128,1024]{1,0:T(8,128)(2,1)S(1)}, bf16[128,1024]{1,0:T(8,128)(2,1)}, u32[]{:S(2)}, u32[]{:S(2)}) %collective-permute-start.14) | collective-permute-done | bytes 262176 | tf_op jit(solution)/shard_map/ppermute | solution.py:30
  59.3 6.4 %collective-permute-done.15 = bf16[128,1024]{1,0:T(8,128)(2,1)S(1)} collective-permute-done((bf16[128,1024]{1,0:T(8,128)(2,1)S(1)}, bf16[128,1024]{1,0:T(8,128)(2,1)S(1)}, u32[]{:S(2)}, u32[]{:S(2)}) %collective-permute-start.15) | collective-permute-done | bytes 262176 | tf_op jit(solution)/shard_map/ppermute | solution.py:30
  65.7 2.2 placed_rows.1.refs_4_.refs_3_
  68.1 1.7 collective-permute-start.17
  71.1 21.5 %project_attend.1 = (bf16[512,256]{1,0:T(8,128)(2,1)}, bf16[512,256]{1,0:T(8,128)(2,1)}, bf16[512,256]{1,0:T(8,128)(2,1)}, bf16[512,256]{1,0:T(8,128)(2,1)}, bf1...) custom-call(s32[8]{0:T(128)} %broadcast_xor_fusion.1.owner_a, ...), custom_call_target="tpu_custom_call" | custom-call | flops 5368709120 | bytes 10485760 | tf_op jit(solution)/shard_map/project_attend/pallas_call | solution.py:487
  93.6 1.5 collective-permute-start.20
  96.5 6.2 %collective-permute-done.19.refs_2_.refs_9_ = bf16[512,256]{1,0:T(8,128)(2,1)} collective-permute-done((bf16[512,256]{1,0:T(8,128)(2,1)}, bf16[512,256]{1,0:T(8,128)(2,1)}, u32[]{:S(2)}, u32[]{:S(2)}) %collective-permute-start.19) | collective-permute-done | bytes 262176 | tf_op jit(solution)/shard_map/ppermute | solution.py:30
  102.7 4.7 %collective-permute-done.20.refs_3_.refs_10_ = bf16[512,256]{1,0:T(8,128)(2,1)} collective-permute-done((bf16[512,256]{1,0:T(8,128)(2,1)}, bf16[512,256]{1,0:T(8,128)(2,1)}, u32[]{:S(2)}, u32[]{:S(2)}) %collective-permute-start.20) | collective-permute-done | bytes 262176 | tf_op jit(solution)/shard_map/ppermute | solution.py:30
  107.4 5.0 %middle.1 = (bf16[512,1024]{1,0:T(8,128)(2,1)}, bf16[512,1024]{1,0:T(8,128)(2,1)}) custom-call(bf16[512,256]{1,0:T(8,128)(2,1)} %get-tuple-element.140.refs_0_.refs_7_, bf16[512,256]{1,0:T(8,128)(2,1)} %copy-done.12, bf16[512,256]{1,0:T(8,128)(2,1)} %collective-permute-done.19.refs_2_.refs_9_, bf16[512,256]{1,0:T(8,128)(2,1)} %collective-permute-done.20.refs_3_.refs_10_, ...), custom_call_target="tpu_custom_call" | custom-call | flops 1073741824 | bytes 6291456 | tf_op jit(solution)/shard_map/middle/pallas_call | solution.py:839
  115.9 1.1 constant_dynamic-update-slice_fusion.refs_2_
  117.1 11.5 %all-gather.2.cloned.1.call-done.refs_4_ = bf16[1024,2048]{1,0:T(8,128)(2,1)} async-done(((bf16[128,2048]{1,0:T(8,128)(2,1)}), bf16[1024,2048]{1,0:T(8,128)(2,1)}) %all-gather.2.cloned.1.call-update) | async-done | bytes 4194320 | tf_op jit(solution)/shard_map/all_gather | solution.py:1011
  128.6 14.9 %feed.2 = (bf16[512,1024]{1,0:T(8,128)(2,1)}, bf16[512,1024]{1,0:T(8,128)(2,1)}, bf16[512,1024]{1,0:T(8,128)(2,1)}, bf16[512,1024]{1,0:T(8,128)(2,1)}, bf16[2048...) custom-call(bf16[512,1024]{1,0:T(8,128)(2,1)} %get-tuple-element.146.re, ...), custom_call_target="tpu_custom_call" | custom-call | flops 8589934592 | bytes 20971520 | tf_op jit(solution)/shard_map/feed/pallas_call | solution.py:714
  143.6 2.8 collective-permute-done.27.refs_1_
  147.5 14.9 %feed.3 = (bf16[512,1024]{1,0:T(8,128)(2,1)}, bf16[512,1024]{1,0:T(8,128)(2,1)}, bf16[512,1024]{1,0:T(8,128)(2,1)}, bf16[512,1024]{1,0:T(8,128)(2,1)}, bf16[2048...) custom-call(bf16[512,1024]{1,0:T(8,128)(2,1)} %collective-permute-do, ...), custom_call_target="tpu_custom_call", output_to_operand_aliasing={{4}: (6, {}), {5}: (7, {}), {6}: (8, {}), {7}: (9, {})} | custom-call | flops 8589934592 | bytes 20971520 | tf_op jit(solution)/shard_map/feed/pallas_call | solution.py:714
  163.1 2.2 collective-permute-done.29
  165.3 2.6 add_convert_fusion.3
  167.9 1.5 collective-permute-start.30
  169.4 15.8 %feed_grads.1 = (bf16[1024,2048]{1,0:T(8,128)(2,1)}, f32[1,1024]{1,0:T(1,128)}) custom-call(bf16[2048,1024]{1,0:T(8,128)(2,1)} %get-tuple-element.164.normed_ref, bf16[2048,1024]{1,0:T(8,128)(2,1)} %get-tuple-element.165.grad_ref, bf16[2048,1024]{1,0:T(8,128)(2,1)} %get-tuple-element.166.grads_ref, bf16[2048,1024]{1,0:T(8,128)(2,1)} %get-tuple-element.167.active_ref), custom_call_target="tpu_custom_call" | custom-call | flops 8589934592 | bytes 16777216 | tf_op jit(solution)/shard_map/feed_grads/pallas_call | solution.py:762
  185.2 1.2 copy-done.11
  186.4 1.6 add_convert_fusion.2
  188.1 1.0 fusion.7
  189.1 4.4 %collective-permute-done.30.refs_2_ = bf16[512,1024]{1,0:T(8,128)(2,1)} collective-permute-done((bf16[512,1024]{1,0:T(8,128)(2,1)}, bf16[512,1024]{1,0:T(8,128)(2,1)}, u32[]{:S(2)}, u32[]{:S(2)}) %collective-permute-start.30) | collective-permute-done | bytes 1048608 | tf_op jit(solution)/shard_map/ppermute | solution.py:30
  193.5 1.5 collective-permute-start.35
  195.0 9.9 %middle_back.1 = (bf16[512,1024]{1,0:T(8,128)(2,1)}, f32[4,1024]{1,0:T(4,128)}, bf16[512,256]{1,0:T(8,128)(2,1)}, bf16[512,256]{1,0:T(8,128)(2,1)}, bf16[512,256...) custom-call(s32[8]{0:T(128)} %broadcast_xor_fusion.owner_b.owner, ...), custom_call_target="tpu_custom_call" | custom-call | flops 2147483648 | bytes 10485760 | tf_op jit(solution)/shard_map/middle_back/pallas_call | solution.py:904
  204.9 1.9 collective-permute-done.35
  208.0 1.5 collective-permute-start.33
  210.1 1.2 add_convert_fusion.5
  211.4 6.0 %collective-permute-done.33.refs_5_ = bf16[512,256]{1,0:T(8,128)(2,1)S(1)} collective-permute-done((bf16[512,256]{1,0:T(8,128)(2,1)}, bf16[512,256]{1,0:T(8,128)(2,1)S(1)}, u32[]{:S(2)}, u32[]{:S(2)}) %collective-permute-start.33) | collective-permute-done | bytes 262176 | tf_op jit(solution)/shard_map/ppermute | solution.py:30
  217.4 3.7 %collective-permute-done.34.refs_6_ = bf16[512,256]{1,0:T(8,128)(2,1)S(1)} collective-permute-done((bf16[512,256]{1,0:T(8,128)(2,1)}, bf16[512,256]{1,0:T(8,128)(2,1)S(1)}, u32[]{:S(2)}, u32[]{:S(2)}) %collective-permute-start.34) | collective-permute-done | bytes 262176 | tf_op jit(solution)/shard_map/ppermute | solution.py:30
  221.1 1.4 collective-permute-start.37
  224.2 37.0 %attend_back.1 = (bf16[4,128,512]{2,1,0:T(8,128)(2,1)}, bf16[4,128,512]{2,1,0:T(8,128)(2,1)}, bf16[4,128,256]{2,1,0:T(8,128)(2,1)S(1)}, bf16[4,128,256]{2,1,0:T(...) custom-call(s32[8]{0:T(128)S(1)} %copy-done.3, ...), custom_call_target="tpu_custom_call" | custom-call | flops 10737418240 | bytes 20971520 | tf_op jit(solution)/shard_map/attend_back/pallas_call | solution.py:615
  263.8 1.6 add_convert_fusion.4
  266.4 1.5 collective-permute-start.49
  268.5 1.5 collective-permute-start.43
  270.0 8.7 %collective-permute-done.49 = f32[104,128]{1,0:T(8,128)S(1)} collective-permute-done((f32[104,128]{1,0:T(8,128)S(1)}, f32[104,128]{1,0:T(8,128)S(1)}, u32[]{:S(2)}, u32[]{:S(2)}) %collective-permute-start.49) | collective-permute-done | bytes 53280 | tf_op jit(solution)/shard_map/ppermute | solution.py:30
  281.8 1.2 collective-permute-start.44
  283.0 1.9 add_convert_fusion
  284.9 1.4 collective-permute-start.46
  287.0 2.4 collective-permute-start.51
  289.4 5.7 %collective-permute-done.45 = bf16[2,128,512]{2,1,0:T(8,128)(2,1)S(1)} collective-permute-done((bf16[2,128,512]{2,1,0:T(8,128)(2,1)S(1)}, bf16[2,128,512]{2,1,0:T(8,128)(2,1)S(1)}, u32[]{:S(2)}, u32[]{:S(2)}) %collective-permute-start.45) | collective-permute-done | bytes 262176 | tf_op jit(solution)/shard_map/ppermute | solution.py:30
  295.8 1.6 collective-permute-done.46.refs_3_
  297.5 2.3 collective-permute-start.52
  301.4 4.6 %input_back.1 = bf16[512,1024]{1,0:T(8,128)(2,1)} custom-call(bf16[512,1024]{1,0:T(8,128)(2,1)} %get-tuple-element.222.refs_0_, bf16[512,1024]{1,0:T(8,128)(2,1)} %copy-done.15, bf16[256,1024]{1,0:T(8,128)(2,1)} %copy-done.18, bf16[256,1024]{1,0:T(8,128)(2,1)} %copy-done.20, bf16[512,1024]{1,0:T(8,128)(2,1)} %refs_4_.1, ...), custom_call_target="tpu_custom_call" | custom-call | flops 10485760 | bytes 7340032 | tf_op jit(solution)/shard_map/input_back/pallas_call | solution.py:936
  306.0 1.5 collective-permute-start.55
  307.9 1.1 collective-permute-done.52
  309.0 1.4 collective-permute-done.53
  310.4 1.0 fusion.1
  314.9 2.1 fusion.9
  (239 shorter events, 38.4 us)
Async XLA Ops:
  7.2 121.4 %all-gather.2.cloned.1.call-start = ((), (), s32[]{:S(2)}) async-start(), calls=%async_computation.1 | async-start | bytes 4718592 | tf_op jit(solution)/shard_map/all_gather | solution.py:1011
  8.9 8.2 %collective-permute-start = (f32[96,128]{1,0:T(8,128)S(1)}, f32[96,128]{1,0:T(8,128)S(1)}, u32[]{:S(2)}, u32[]{:S(2)}) collective-permute-start(f32[96,128]{1,0:T(8,128)S(1)} %maximum_bitcast_fusion.2), channel_id=1, source_target_pairs={{0,1},{1,0},{2,3},{3,2},{4,5},{5,4},{6,7},{7,6},{8,9},{9,8},{10,11... | collective-permute-start | bytes 147464 | tf_op jit(solution)/shard_map/ppermute | solution.py:30
  10.7 14.1 %collective-permute-start.5 = (bf16[1,128,512]{2,1,0:T(8,128)(2,1)S(1)}, bf16[1,128,512]{2,1,0:T(8,128)(2,1)S(1)}, u32[]{:S(2)}, u32[]{:S(2)}) collective-permute-start(bf16[1,128,512]{2,1,0:T(8,128)(2,1)S(1)} %bitcast.71), channel_id=1, source_target_pairs={{0,16},{4,20},{8,24},{12,28},{16,0},{20,4},{24,8},{28,12},{1,17},{... | collective-permute-start | bytes 393224 | tf_op jit(solution)/shard_map/ppermute | solution.py:30
  15.3 13.7 %collective-permute-start.8 = (bf16[1,128,512]{2,1,0:T(8,128)(2,1)S(1)}, bf16[1,128,512]{2,1,0:T(8,128)(2,1)S(1)}, u32[]{:S(2)}, u32[]{:S(2)}) collective-permute-start(bf16[1,128,512]{2,1,0:T(8,128)(2,1)S(1)} %maximum_bitcast_fusion), channel_id=1, source_target_pairs={{0,16},{4,20},{8,24},{12,28},{16,0},{20,4},{24,8},{28,12},{1,17},{... | collective-permute-start | bytes 393224 | tf_op jit(solution)/shard_map/ppermute | solution.py:30
  17.1 5.3 %collective-permute-start.1 = (f32[96,128]{1,0:T(8,128)S(1)}, f32[96,128]{1,0:T(8,128)S(1)}, u32[]{:S(2)}, u32[]{:S(2)}) collective-permute-start(f32[96,128]{1,0:T(8,128)S(1)} %fusion.4), channel_id=1, source_target_pairs={{0,2},{1,3},{2,0},{3,1},{4,6},{5,7},{6,4},{7,5},{8,10},{9,11},{10,... | collective-permute-start | bytes 147464 | tf_op jit(solution)/shard_map/ppermute | solution.py:30
  22.5 25.0 %collective-permute-start.3 = (bf16[512,1024]{1,0:T(8,128)(2,1)}, bf16[512,1024]{1,0:T(8,128)(2,1)S(1)}, u32[]{:S(2)}, u32[]{:S(2)}) collective-permute-start(bf16[512,1024]{1,0:T(8,128)(2,1)} %unit.1.refs_0_.refs_7_), channel_id=1, source_target_pairs={{0,2},{1,3},{2,0},{3,1},{4,6},{5,7},{6,4},{7,5},{8,10},{9,11},{10,... | collective-permute-start | bytes 3145736 | tf_op jit(solution)/shard_map/ppermute | solution.py:30
  23.3 4.1 %collective-permute-start.11 = (f32[96,128]{1,0:T(8,128)S(1)}, f32[96,128]{1,0:T(8,128)S(1)}, u32[]{:S(2)}, u32[]{:S(2)}) collective-permute-start(f32[96,128]{1,0:T(8,128)S(1)} %bitcast.81), channel_id=1, source_target_pairs={{0,4},{4,0},{8,12},{12,8},{16,20},{20,16},{24,28},{28,24},{1,5},{5... | collective-permute-start | bytes 147464 | tf_op jit(solution)/shard_map/ppermute | solution.py:30
  24.8 11.1 %collective-permute-start.6 = (bf16[2,128,512]{2,1,0:T(8,128)(2,1)S(1)}, bf16[2,128,512]{2,1,0:T(8,128)(2,1)S(1)}, u32[]{:S(2)}, u32[]{:S(2)}) collective-permute-start(bf16[2,128,512]{2,1,0:T(8,128)(2,1)S(1)} %pad_maximum_fusion.8), channel_id=1, source_target_pairs={{0,8},{4,12},{8,0},{12,4},{16,24},{20,28},{24,16},{28,20},{1,9},{5... | collective-permute-start | bytes 786440 | tf_op jit(solution)/shard_map/ppermute | solution.py:30
  27.4 6.2 %collective-permute-start.12 = (f32[96,128]{1,0:T(8,128)S(1)}, f32[96,128]{1,0:T(8,128)S(1)}, u32[]{:S(2)}, u32[]{:S(2)}) collective-permute-start(f32[96,128]{1,0:T(8,128)S(1)} %bitcast_add_fusion), channel_id=1, source_target_pairs={{0,8},{4,12},{8,0},{12,4},{16,24},{20,28},{24,16},{28,20},{1,9},{5... | collective-permute-start | bytes 147464 | tf_op jit(solution)/shard_map/ppermute | solution.py:30
  29.1 8.5 %collective-permute-start.9 = (bf16[2,128,512]{2,1,0:T(8,128)(2,1)S(1)}, bf16[2,128,512]{2,1,0:T(8,128)(2,1)S(1)}, u32[]{:S(2)}, u32[]{:S(2)}) collective-permute-start(bf16[2,128,512]{2,1,0:T(8,128)(2,1)S(1)} %pad_maximum_fusion.9), channel_id=1, source_target_pairs={{0,4},{4,0},{8,12},{12,8},{16,20},{20,16},{24,28},{28,24},{1,5},{5... | collective-permute-start | bytes 786440 | tf_op jit(solution)/shard_map/ppermute | solution.py:30
  33.6 5.9 %collective-permute-start.13 = (f32[96,128]{1,0:T(8,128)S(1)}, f32[96,128]{1,0:T(8,128)S(1)}, u32[]{:S(2)}, u32[]{:S(2)}) collective-permute-start(f32[96,128]{1,0:T(8,128)S(1)} %fusion.14), channel_id=1, source_target_pairs={{0,16},{4,20},{8,24},{12,28},{16,0},{20,4},{24,8},{28,12},{1,17},{... | collective-permute-start | bytes 147464 | tf_op jit(solution)/shard_map/ppermute | solution.py:30
  36.0 12.7 %collective-permute-start.7 = (bf16[4,128,512]{2,1,0:T(8,128)(2,1)S(1)}, bf16[4,128,512]{2,1,0:T(8,128)(2,1)S(1)}, u32[]{:S(2)}, u32[]{:S(2)}) collective-permute-start(bf16[4,128,512]{2,1,0:T(8,128)(2,1)S(1)} %pad_maximum_fusion.3), channel_id=1, source_target_pairs={{0,4},{4,0},{8,12},{12,8},{16,20},{20,16},{24,28},{28,24},{1,5},{5... | collective-permute-start | bytes 1572872 | tf_op jit(solution)/shard_map/ppermute | solution.py:30
  37.7 12.6 %collective-permute-start.10 = (bf16[4,128,512]{2,1,0:T(8,128)(2,1)S(1)}, bf16[4,128,512]{2,1,0:T(8,128)(2,1)S(1)}, u32[]{:S(2)}, u32[]{:S(2)}) collective-permute-start(bf16[4,128,512]{2,1,0:T(8,128)(2,1)S(1)} %pad_maximum_fusion.4), channel_id=1, source_target_pairs={{0,8},{4,12},{8,0},{12,4},{16,24},{20,28},{24,16},{28,20},{1,9},{5... | collective-permute-start | bytes 1572872 | tf_op jit(solution)/shard_map/ppermute | solution.py:30
  47.6 7.1 %collective-permute-start.14 = (bf16[128,1024]{1,0:T(8,128)(2,1)S(1)}, bf16[128,1024]{1,0:T(8,128)(2,1)}, u32[]{:S(2)}, u32[]{:S(2)}) collective-permute-start(bf16[128,1024]{1,0:T(8,128)(2,1)S(1)} %copy-done.26), channel_id=1, source_target_pairs={{0,2},{1,3},{2,0},{3,1},{4,6},{5,7},{6,4},{7,5},{8,10},{9,11},{10,... | collective-permute-start | bytes 786440 | tf_op jit(solution)/shard_map/ppermute | solution.py:30
  54.7 260.2 %reduce-scatter.2.cloned.1.call-start = ((), (), s32[]{:S(2)}) async-start(), calls=%async_computation.2 | async-start | bytes 4718592 | tf_op jit(solution)/shard_map/reduce_scatter | solution.py:1066
  54.8 16.3 %collective-permute-start.2 = (bf16[512,1024]{1,0:T(8,128)(2,1)S(1)}, bf16[512,1024]{1,0:T(8,128)(2,1)}, u32[]{:S(2)}, u32[]{:S(2)}) collective-permute-start(bf16[512,1024]{1,0:T(8,128)(2,1)S(1)} %copy-done.13), channel_id=1, source_target_pairs={{0,1},{1,0},{2,3},{3,2},{4,5},{5,4},{6,7},{7,6},{8,9},{9,8},{10,11... | collective-permute-start | bytes 3145736 | tf_op jit(solution)/shard_map/ppermute | solution.py:30
  54.9 16.2 %collective-permute-start.4 = (bf16[512,1024]{1,0:T(8,128)(2,1)}, bf16[512,1024]{1,0:T(8,128)(2,1)}, u32[]{:S(2)}, u32[]{:S(2)}) collective-permute-start(bf16[512,1024]{1,0:T(8,128)(2,1)} %copy-done.32), channel_id=1, source_target_pairs={{0,1},{1,0},{2,3},{3,2},{4,5},{5,4},{6,7},{7,6},{8,9},{9,8},{10,11... | collective-permute-start | bytes 3145736 | tf_op jit(solution)/shard_map/ppermute | solution.py:30
  57.4 8.3 %collective-permute-start.15 = (bf16[128,1024]{1,0:T(8,128)(2,1)S(1)}, bf16[128,1024]{1,0:T(8,128)(2,1)S(1)}, u32[]{:S(2)}, u32[]{:S(2)}) collective-permute-start(bf16[128,1024]{1,0:T(8,128)(2,1)S(1)} %get-tuple-element.129), channel_id=1, source_target_pairs={{0,2},{1,3},{2,0},{3,1},{4,6},{5,7},{6,4},{7,5},{8,10},{9,11},{10,... | collective-permute-start | bytes 786440 | tf_op jit(solution)/shard_map/ppermute | solution.py:30
  67.8 24.8 %collective-permute-start.16 = (bf16[1024,256]{1,0:T(8,128)(2,1)}, bf16[1024,256]{1,0:T(8,128)(2,1)S(1)}, u32[]{:S(2)}, u32[]{:S(2)}) collective-permute-start(bf16[1024,256]{1,0:T(8,128)(2,1)} %placed_rows.1.refs_4_.refs_3_), channel_id=1, source_target_pairs={{0,2},{1,3},{2,0},{3,1},{4,6},{5,7},{6,4},{7,5},{8,10},{9,11},{10,... | collective-permute-start | bytes 1572872 | tf_op jit(solution)/shard_map/ppermute | solution.py:30
  68.1 24.5 %collective-permute-start.17 = (bf16[256,1024]{1,0:T(8,128)(2,1)}, bf16[256,1024]{1,0:T(8,128)(2,1)}, u32[]{:S(2)}, u32[]{:S(2)}) collective-permute-start(bf16[256,1024]{1,0:T(8,128)(2,1)} %slice.188), channel_id=1, source_target_pairs={{0,2},{1,3},{2,0},{3,1},{4,6},{5,7},{6,4},{7,5},{8,10},{9,11},{10,... | collective-permute-start | bytes 1572872 | tf_op jit(solution)/shard_map/ppermute | solution.py:30
  71.1 24.6 %collective-permute-start.21 = (bf16[1024,256]{1,0:T(8,128)(2,1)}, bf16[1024,256]{1,0:T(8,128)(2,1)S(1)}, u32[]{:S(2)}, u32[]{:S(2)}) collective-permute-start(bf16[1024,256]{1,0:T(8,128)(2,1)} %placed_rows.1.refs_4_.refs_3_), channel_id=1, source_target_pairs={{0,1},{1,0},{2,3},{3,2},{4,5},{5,4},{6,7},{7,6},{8,9},{9,8},{10,11... | collective-permute-start | bytes 1572872 | tf_op jit(solution)/shard_map/ppermute | solution.py:30
  92.7 14.8 %collective-permute-start.22 = (bf16[1024,256]{1,0:T(8,128)(2,1)S(1)}, bf16[1024,256]{1,0:T(8,128)(2,1)}, u32[]{:S(2)}, u32[]{:S(2)}) collective-permute-start(bf16[1024,256]{1,0:T(8,128)(2,1)S(1)} %collective-permute-done.16.refs_6_.refs_5_), channel_id=1, source_target_pairs={{0,1},{1,0},{2,3},{3,2},{4,5},{5,4},{6,7},{7,6},{8,9},{9,8},{10,11... | collective-permute-start | bytes 1572872 | tf_op jit(solution)/shard_map/ppermute | solution.py:30
  93.2 3.3 %collective-permute-start.18 = (bf16[512,256]{1,0:T(8,128)(2,1)}, bf16[512,256]{1,0:T(8,128)(2,1)S(1)}, u32[]{:S(2)}, u32[]{:S(2)}) collective-permute-start(bf16[512,256]{1,0:T(8,128)(2,1)} %get-tuple-element.141), channel_id=1, source_target_pairs={{0,1},{1,0},{2,3},{3,2},{4,5},{5,4},{6,7},{7,6},{8,9},{9,8},{10,11... | collective-permute-start | bytes 786440 | tf_op jit(solution)/shard_map/ppermute | solution.py:30
  93.3 9.4 %collective-permute-start.19 = (bf16[512,256]{1,0:T(8,128)(2,1)}, bf16[512,256]{1,0:T(8,128)(2,1)}, u32[]{:S(2)}, u32[]{:S(2)}) collective-permute-start(bf16[512,256]{1,0:T(8,128)(2,1)} %get-tuple-element.142), channel_id=1, source_target_pairs={{0,2},{1,3},{2,0},{3,1},{4,6},{5,7},{6,4},{7,5},{8,10},{9,11},{10,... | collective-permute-start | bytes 786440 | tf_op jit(solution)/shard_map/ppermute | solution.py:30
  93.6 13.8 %collective-permute-start.20 = (bf16[512,256]{1,0:T(8,128)(2,1)}, bf16[512,256]{1,0:T(8,128)(2,1)}, u32[]{:S(2)}, u32[]{:S(2)}) collective-permute-start(bf16[512,256]{1,0:T(8,128)(2,1)} %get-tuple-element.143), channel_id=1, source_target_pairs={{0,3},{1,2},{2,1},{3,0},{4,7},{5,6},{6,5},{7,4},{8,11},{9,10},{10,... | collective-permute-start | bytes 786440 | tf_op jit(solution)/shard_map/ppermute | solution.py:30
  95.7 21.3 %collective-permute-start.24 = (bf16[512,1024]{1,0:T(8,128)(2,1)S(1)}, bf16[512,1024]{1,0:T(8,128)(2,1)}, u32[]{:S(2)}, u32[]{:S(2)}) collective-permute-start(bf16[512,1024]{1,0:T(8,128)(2,1)S(1)} %copy-done.5), channel_id=1, source_target_pairs={{0,1},{1,0},{2,3},{3,2},{4,5},{5,4},{6,7},{7,6},{8,9},{9,8},{10,11... | collective-permute-start | bytes 3145736 | tf_op jit(solution)/shard_map/ppermute | solution.py:30
  112.4 4.6 %collective-permute-start.23 = (bf16[512,1024]{1,0:T(8,128)(2,1)}, bf16[512,1024]{1,0:T(8,128)(2,1)}, u32[]{:S(2)}, u32[]{:S(2)}) collective-permute-start(bf16[512,1024]{1,0:T(8,128)(2,1)} %get-tuple-element.146.refs_0_), channel_id=1, source_target_pairs={{0,1},{1,0},{2,3},{3,2},{4,5},{5,4},{6,7},{7,6},{8,9},{9,8},{10,11... | collective-permute-start | bytes 3145736 | tf_op jit(solution)/shard_map/ppermute | solution.py:30
  114.6 28.9 %collective-permute-start.26 = (bf16[512,1024]{1,0:T(8,128)(2,1)}, bf16[512,1024]{1,0:T(8,128)(2,1)}, u32[]{:S(2)}, u32[]{:S(2)}) collective-permute-start(bf16[512,1024]{1,0:T(8,128)(2,1)} %get-tuple-element.146.refs_0_), channel_id=1, source_target_pairs={{0,2},{1,3},{2,0},{3,1},{4,6},{5,7},{6,4},{7,5},{8,10},{9,11},{10,... | collective-permute-start | bytes 3145736 | tf_op jit(solution)/shard_map/ppermute | solution.py:30
  117.0 26.6 %collective-permute-start.28 = (bf16[512,1024]{1,0:T(8,128)(2,1)S(1)}, bf16[512,1024]{1,0:T(8,128)(2,1)}, u32[]{:S(2)}, u32[]{:S(2)}) collective-permute-start(bf16[512,1024]{1,0:T(8,128)(2,1)S(1)} %constant_dynamic-update-slice_fusion.refs_2_), channel_id=1, source_target_pairs={{0,1},{1,0},{2,3},{3,2},{4,5},{5,4},{6,7},{7,6},{8,9},{9,8},{10,11... | collective-permute-start | bytes 3145736 | tf_op jit(solution)/shard_map/ppermute | solution.py:30
  143.5 2.9 collective-permute-start.27
  162.4 2.9 collective-permute-start.29
  162.6 26.5 %collective-permute-start.25 = (bf16[512,1024]{1,0:T(8,128)(2,1)}, bf16[512,1024]{1,0:T(8,128)(2,1)S(1)}, u32[]{:S(2)}, u32[]{:S(2)}) collective-permute-start(bf16[512,1024]{1,0:T(8,128)(2,1)} %get-tuple-element.149), channel_id=1, source_target_pairs={{0,1},{1,0},{2,3},{3,2},{4,5},{5,4},{6,7},{7,6},{8,9},{9,8},{10,11... | collective-permute-start | bytes 3145736 | tf_op jit(solution)/shard_map/ppermute | solution.py:30
  163.0 22.3 %collective-permute-start.31 = (bf16[512,1024]{1,0:T(8,128)(2,1)}, bf16[512,1024]{1,0:T(8,128)(2,1)}, u32[]{:S(2)}, u32[]{:S(2)}) collective-permute-start(bf16[512,1024]{1,0:T(8,128)(2,1)} %get-tuple-element.170), channel_id=1, source_target_pairs={{0,1},{1,0},{2,3},{3,2},{4,5},{5,4},{6,7},{7,6},{8,9},{9,8},{10,11... | collective-permute-start | bytes 3145736 | tf_op jit(solution)/shard_map/ppermute | solution.py:30
  167.9 25.5 %collective-permute-start.30 = (bf16[512,1024]{1,0:T(8,128)(2,1)}, bf16[512,1024]{1,0:T(8,128)(2,1)}, u32[]{:S(2)}, u32[]{:S(2)}) collective-permute-start(bf16[512,1024]{1,0:T(8,128)(2,1)} %add_convert_fusion.3), channel_id=1, source_target_pairs={{0,2},{1,3},{2,0},{3,1},{4,6},{5,7},{6,4},{7,5},{8,10},{9,11},{10,... | collective-permute-start | bytes 3145736 | tf_op jit(solution)/shard_map/ppermute | solution.py:30
  193.5 13.3 %collective-permute-start.35 = (bf16[256,1024]{1,0:T(8,128)(2,1)}, bf16[256,1024]{1,0:T(8,128)(2,1)S(1)}, u32[]{:S(2)}, u32[]{:S(2)}) collective-permute-start(bf16[256,1024]{1,0:T(8,128)(2,1)} %get-tuple-element.183), channel_id=1, source_target_pairs={{0,2},{1,3},{2,0},{3,1},{4,6},{5,7},{6,4},{7,5},{8,10},{9,11},{10,... | collective-permute-start | bytes 1572872 | tf_op jit(solution)/shard_map/ppermute | solution.py:30
  194.9 28.2 %copy-start.1 = (s32[418]{0:T(512)S(1)}, s32[418]{0:T(512)}, u32[]{:S(2)}) copy-start(s32[418]{0:T(512)} %pad_add_fusion.facts) | copy-start | bytes 5020
  194.9 28.2 %copy-start.3 = (s32[8]{0:T(128)S(1)}, s32[8]{0:T(128)}, u32[]{:S(2)}) copy-start(s32[8]{0:T(128)} %broadcast_xor_fusion.1.owner_a) | copy-start | bytes 100
  194.9 28.2 %copy-start.4 = (f32[32,256]{1,0:T(8,128)S(1)}, f32[32,256]{1,0:T(8,128)}, u32[]{:S(2)}) copy-start(f32[32,256]{1,0:T(8,128)} %get-tuple-element.133.refs_1_) | copy-start | bytes 98308
  206.8 3.3 %collective-permute-start.36 = (bf16[8,128,256]{2,1,0:T(8,128)(2,1)}, bf16[8,128,256]{2,1,0:T(8,128)(2,1)S(1)}, u32[]{:S(2)}, u32[]{:S(2)}) collective-permute-start(bf16[8,128,256]{2,1,0:T(8,128)(2,1)} %get-tuple-element.185), channel_id=1, source_target_pairs={{0,1},{1,0},{2,3},{3,2},{4,5},{5,4},{6,7},{7,6},{8,9},{9,8},{10,11... | collective-permute-start | bytes 1572872 | tf_op jit(solution)/shard_map/ppermute | solution.py:30
  207.5 3.8 %collective-permute-start.32 = (bf16[512,256]{1,0:T(8,128)(2,1)}, bf16[512,256]{1,0:T(8,128)(2,1)S(1)}, u32[]{:S(2)}, u32[]{:S(2)}) collective-permute-start(bf16[512,256]{1,0:T(8,128)(2,1)} %get-tuple-element.176), channel_id=1, source_target_pairs={{0,1},{1,0},{2,3},{3,2},{4,5},{5,4},{6,7},{7,6},{8,9},{9,8},{10,11... | collective-permute-start | bytes 786440 | tf_op jit(solution)/shard_map/ppermute | solution.py:30
  208.0 9.4 %collective-permute-start.33 = (bf16[512,256]{1,0:T(8,128)(2,1)}, bf16[512,256]{1,0:T(8,128)(2,1)S(1)}, u32[]{:S(2)}, u32[]{:S(2)}) collective-permute-start(bf16[512,256]{1,0:T(8,128)(2,1)} %get-tuple-element.177), channel_id=1, source_target_pairs={{0,2},{1,3},{2,0},{3,1},{4,6},{5,7},{6,4},{7,5},{8,10},{9,11},{10,... | collective-permute-start | bytes 786440 | tf_op jit(solution)/shard_map/ppermute | solution.py:30
  209.5 11.7 %collective-permute-start.34 = (bf16[512,256]{1,0:T(8,128)(2,1)}, bf16[512,256]{1,0:T(8,128)(2,1)S(1)}, u32[]{:S(2)}, u32[]{:S(2)}) collective-permute-start(bf16[512,256]{1,0:T(8,128)(2,1)} %get-tuple-element.178), channel_id=1, source_target_pairs={{0,3},{1,2},{2,1},{3,0},{4,7},{5,6},{6,5},{7,4},{8,11},{9,10},{10,... | collective-permute-start | bytes 786440 | tf_op jit(solution)/shard_map/ppermute | solution.py:30
  209.5 51.7 %collective-permute-start.38 = (bf16[8,128,256]{2,1,0:T(8,128)(2,1)}, bf16[8,128,256]{2,1,0:T(8,128)(2,1)S(1)}, u32[]{:S(2)}, u32[]{:S(2)}) collective-permute-start(bf16[8,128,256]{2,1,0:T(8,128)(2,1)} %get-tuple-element.195), channel_id=1, source_target_pairs={{0,1},{1,0},{2,3},{3,2},{4,5},{5,4},{6,7},{7,6},{8,9},{9,8},{10,11... | collective-permute-start | bytes 1572872 | tf_op jit(solution)/shard_map/ppermute | solution.py:30
  221.1 40.0 %collective-permute-start.37 = (bf16[256,1024]{1,0:T(8,128)(2,1)}, bf16[256,1024]{1,0:T(8,128)(2,1)S(1)}, u32[]{:S(2)}, u32[]{:S(2)}) collective-permute-start(bf16[256,1024]{1,0:T(8,128)(2,1)} %get-tuple-element.193), channel_id=1, source_target_pairs={{0,2},{1,3},{2,0},{3,1},{4,6},{5,7},{6,4},{7,5},{8,10},{9,11},{10,... | collective-permute-start | bytes 1572872 | tf_op jit(solution)/shard_map/ppermute | solution.py:30
  222.5 38.7 %collective-permute-start.39 = (bf16[8,128,256]{2,1,0:T(8,128)(2,1)S(1)}, bf16[8,128,256]{2,1,0:T(8,128)(2,1)S(1)}, u32[]{:S(2)}, u32[]{:S(2)}) collective-permute-start(bf16[8,128,256]{2,1,0:T(8,128)(2,1)S(1)} %add_convert_fusion.5), channel_id=1, source_target_pairs={{0,2},{1,3},{2,0},{3,1},{4,6},{5,7},{6,4},{7,5},{8,10},{9,11},{10,... | collective-permute-start | bytes 1572872 | tf_op jit(solution)/shard_map/ppermute | solution.py:30
  224.2 38.6 %copy-start.28 = (f32[4,1024]{1,0:T(4,128)S(1)}, f32[4,1024]{1,0:T(4,128)}, u32[]{:S(2)}) copy-start(f32[4,1024]{1,0:T(4,128)} %get-tuple-element.228) | copy-start | bytes 49156
  224.2 38.6 %copy-start.30 = (f32[1,1024]{1,0:T(1,128)S(1)}, f32[1,1024]{1,0:T(1,128)}, u32[]{:S(2)}) copy-start(f32[1,1024]{1,0:T(1,128)} %get-tuple-element.230) | copy-start | bytes 12292
  262.0 5.9 %collective-permute-start.40 = (bf16[512,1024]{1,0:T(8,128)(2,1)}, bf16[512,1024]{1,0:T(8,128)(2,1)S(1)}, u32[]{:S(2)}, u32[]{:S(2)}) collective-permute-start(bf16[512,1024]{1,0:T(8,128)(2,1)} %get-tuple-element.202), channel_id=1, source_target_pairs={{0,1},{1,0},{2,3},{3,2},{4,5},{5,4},{6,7},{7,6},{8,9},{9,8},{10,11... | collective-permute-start | bytes 3145736 | tf_op jit(solution)/shard_map/ppermute | solution.py:30
  262.5 20.5 %collective-permute-start.47 = (bf16[512,1024]{1,0:T(8,128)(2,1)}, bf16[512,1024]{1,0:T(8,128)(2,1)S(1)}, u32[]{:S(2)}, u32[]{:S(2)}) collective-permute-start(bf16[512,1024]{1,0:T(8,128)(2,1)} %get-tuple-element.218), channel_id=1, source_target_pairs={{0,1},{1,0},{2,3},{3,2},{4,5},{5,4},{6,7},{7,6},{8,9},{9,8},{10,11... | collective-permute-start | bytes 3145736 | tf_op jit(solution)/shard_map/ppermute | solution.py:30
  263.2 16.5 %collective-permute-start.41 = (bf16[4,128,512]{2,1,0:T(8,128)(2,1)}, bf16[4,128,512]{2,1,0:T(8,128)(2,1)S(1)}, u32[]{:S(2)}, u32[]{:S(2)}) collective-permute-start(bf16[4,128,512]{2,1,0:T(8,128)(2,1)} %get-tuple-element.211), channel_id=1, source_target_pairs={{0,4},{4,0},{8,12},{12,8},{16,20},{20,16},{24,28},{28,24},{1,5},{5... | collective-permute-start | bytes 1572872 | tf_op jit(solution)/shard_map/ppermute | solution.py:30
  265.5 15.3 %collective-permute-start.42 = (bf16[4,128,512]{2,1,0:T(8,128)(2,1)S(1)}, bf16[4,128,512]{2,1,0:T(8,128)(2,1)S(1)}, u32[]{:S(2)}, u32[]{:S(2)}) collective-permute-start(bf16[4,128,512]{2,1,0:T(8,128)(2,1)S(1)} %pad_maximum_fusion.6), channel_id=1, source_target_pairs={{0,8},{4,12},{8,0},{12,4},{16,24},{20,28},{24,16},{28,20},{1,9},{5... | collective-permute-start | bytes 1572872 | tf_op jit(solution)/shard_map/ppermute | solution.py:30
  266.4 12.3 %collective-permute-start.49 = (f32[104,128]{1,0:T(8,128)S(1)}, f32[104,128]{1,0:T(8,128)S(1)}, u32[]{:S(2)}, u32[]{:S(2)}) collective-permute-start(f32[104,128]{1,0:T(8,128)S(1)} %maximum_bitcast_fusion.1), channel_id=1, source_target_pairs={{0,4},{4,0},{8,12},{12,8},{16,20},{20,16},{24,28},{28,24},{1,5},{5... | collective-permute-start | bytes 159752 | tf_op jit(solution)/shard_map/ppermute | solution.py:30
  268.5 13.4 %collective-permute-start.43 = (bf16[256,1024]{1,0:T(8,128)(2,1)S(1)}, bf16[256,1024]{1,0:T(8,128)(2,1)S(1)}, u32[]{:S(2)}, u32[]{:S(2)}) collective-permute-start(bf16[256,1024]{1,0:T(8,128)(2,1)S(1)} %get-tuple-element.247), channel_id=1, source_target_pairs={{0,2},{1,3},{2,0},{3,1},{4,6},{5,7},{6,4},{7,5},{8,10},{9,11},{10,... | collective-permute-start | bytes 1572872 | tf_op jit(solution)/shard_map/ppermute | solution.py:30
  278.7 8.2 %collective-permute-start.50 = (f32[104,128]{1,0:T(8,128)S(1)}, f32[104,128]{1,0:T(8,128)S(1)}, u32[]{:S(2)}, u32[]{:S(2)}) collective-permute-start(f32[104,128]{1,0:T(8,128)S(1)} %fusion.5), channel_id=1, source_target_pairs={{0,8},{4,12},{8,0},{12,4},{16,24},{20,28},{24,16},{28,20},{1,9},{5... | collective-permute-start | bytes 159752 | tf_op jit(solution)/shard_map/ppermute | solution.py:30
  281.8 7.5 %collective-permute-start.44 = (bf16[2,128,512]{2,1,0:T(8,128)(2,1)S(1)}, bf16[2,128,512]{2,1,0:T(8,128)(2,1)S(1)}, u32[]{:S(2)}, u32[]{:S(2)}) collective-permute-start(bf16[2,128,512]{2,1,0:T(8,128)(2,1)S(1)} %get-tuple-element.215), channel_id=1, source_target_pairs={{0,8},{4,12},{8,0},{12,4},{16,24},{20,28},{24,16},{28,20},{1,9},{5... | collective-permute-start | bytes 786440 | tf_op jit(solution)/shard_map/ppermute | solution.py:30
  284.9 12.5 %collective-permute-start.46 = (bf16[256,1024]{1,0:T(8,128)(2,1)S(1)}, bf16[256,1024]{1,0:T(8,128)(2,1)S(1)}, u32[]{:S(2)}, u32[]{:S(2)}) collective-permute-start(bf16[256,1024]{1,0:T(8,128)(2,1)S(1)} %get-tuple-element.246), channel_id=1, source_target_pairs={{0,2},{1,3},{2,0},{3,1},{4,6},{5,7},{6,4},{7,5},{8,10},{9,11},{10,... | collective-permute-start | bytes 1572872 | tf_op jit(solution)/shard_map/ppermute | solution.py:30
  286.4 14.0 %collective-permute-start.48 = (bf16[512,1024]{1,0:T(8,128)(2,1)S(1)}, bf16[512,1024]{1,0:T(8,128)(2,1)S(1)}, u32[]{:S(2)}, u32[]{:S(2)}) collective-permute-start(bf16[512,1024]{1,0:T(8,128)(2,1)S(1)} %copy-done.33), channel_id=1, source_target_pairs={{0,1},{1,0},{2,3},{3,2},{4,5},{5,4},{6,7},{7,6},{8,9},{9,8},{10,11... | collective-permute-start | bytes 3145736 | tf_op jit(solution)/shard_map/ppermute | solution.py:30
  286.4 8.7 %collective-permute-start.45 = (bf16[2,128,512]{2,1,0:T(8,128)(2,1)S(1)}, bf16[2,128,512]{2,1,0:T(8,128)(2,1)S(1)}, u32[]{:S(2)}, u32[]{:S(2)}) collective-permute-start(bf16[2,128,512]{2,1,0:T(8,128)(2,1)S(1)} %get-tuple-element.216), channel_id=1, source_target_pairs={{0,4},{4,0},{8,12},{12,8},{16,20},{20,16},{24,28},{28,24},{1,5},{5... | collective-permute-start | bytes 786440 | tf_op jit(solution)/shard_map/ppermute | solution.py:30
  287.0 13.4 %collective-permute-start.51 = (f32[104,128]{1,0:T(8,128)S(1)}, f32[104,128]{1,0:T(8,128)S(1)}, u32[]{:S(2)}, u32[]{:S(2)}) collective-permute-start(f32[104,128]{1,0:T(8,128)S(1)} %fusion.13), channel_id=1, source_target_pairs={{0,16},{4,20},{8,24},{12,28},{16,0},{20,4},{24,8},{28,12},{1,17},{... | collective-permute-start | bytes 159752 | tf_op jit(solution)/shard_map/ppermute | solution.py:30
  297.5 11.5 %collective-permute-start.52 = (bf16[1,128,512]{2,1,0:T(8,128)(2,1)S(1)}, bf16[1,128,512]{2,1,0:T(8,128)(2,1)}, u32[]{:S(2)}, u32[]{:S(2)}) collective-permute-start(bf16[1,128,512]{2,1,0:T(8,128)(2,1)S(1)} %get-tuple-element.233), channel_id=1, source_target_pairs={{0,16},{4,20},{8,24},{12,28},{16,0},{20,4},{24,8},{28,12},{1,17},{... | collective-permute-start | bytes 393224 | tf_op jit(solution)/shard_map/ppermute | solution.py:30
  299.8 10.7 %collective-permute-start.53 = (bf16[1,128,512]{2,1,0:T(8,128)(2,1)}, bf16[1,128,512]{2,1,0:T(8,128)(2,1)}, u32[]{:S(2)}, u32[]{:S(2)}) collective-permute-start(bf16[1,128,512]{2,1,0:T(8,128)(2,1)} %get-tuple-element.235), channel_id=1, source_target_pairs={{0,16},{4,20},{8,24},{12,28},{16,0},{20,4},{24,8},{28,12},{1,17},{... | collective-permute-start | bytes 393224 | tf_op jit(solution)/shard_map/ppermute | solution.py:30
  306.0 6.3 %collective-permute-start.56 = (f32[104,128]{1,0:T(8,128)S(1)}, f32[104,128]{1,0:T(8,128)S(1)}, u32[]{:S(2)}, u32[]{:S(2)}) collective-permute-start(f32[104,128]{1,0:T(8,128)S(1)} %bitcast.85), channel_id=1, source_target_pairs={{0,3},{1,2},{2,1},{3,0},{4,7},{5,6},{6,5},{7,4},{8,11},{9,10},{10,... | collective-permute-start | bytes 159752 | tf_op jit(solution)/shard_map/ppermute | solution.py:30
  306.0 6.3 %collective-permute-start.55 = (f32[104,128]{1,0:T(8,128)S(1)}, f32[104,128]{1,0:T(8,128)S(1)}, u32[]{:S(2)}, u32[]{:S(2)}) collective-permute-start(f32[104,128]{1,0:T(8,128)S(1)} %bitcast.86), channel_id=1, source_target_pairs={{0,2},{1,3},{2,0},{3,1},{4,6},{5,7},{6,4},{7,5},{8,10},{9,11},{10,... | collective-permute-start | bytes 159752 | tf_op jit(solution)/shard_map/ppermute | solution.py:30
  307.5 4.8 %collective-permute-start.54 = (f32[104,128]{1,0:T(8,128)S(1)}, f32[104,128]{1,0:T(8,128)S(1)}, u32[]{:S(2)}, u32[]{:S(2)}) collective-permute-start(f32[104,128]{1,0:T(8,128)S(1)} %bitcast.87), channel_id=1, source_target_pairs={{0,1},{1,0},{2,3},{3,2},{4,5},{5,4},{6,7},{7,6},{8,9},{9,8},{10,11... | collective-permute-start | bytes 159752 | tf_op jit(solution)/shard_map/ppermute | solution.py:30
  (35 other events, 310.9 us)
Sparse Core Ops, SparseCore 0:
  54.8 73.6 all-gather.1
  185.4 85.5 reduce-scatter.1

commit v6 on v5

--- a/solution.py
+++ b/solution.py
@@ -999,9 +999,9 @@
     last_blocks = doubled(last_flat, "dp", order_b)
     packed = summed_everywhere(packed, ("dp",))
     feed_flat = jnp.concatenate([up_weight, down_weight], axis=1)
-    piece_rows = near // 4
-    first_going, next_going = output_cotangent[:piece_rows], output_cotangent[piece_rows:]
-    next_going, last_going = next_going[:piece_rows], next_going[piece_rows:]
+    first_going = output_cotangent[: near // 8]
+    next_going = output_cotangent[near // 8 : near // 2]
+    last_going = output_cotangent[near // 2 :]
     first_going, unit_far = together(first_going, unit_far)
     cotangent_first = far(first_going, "tensor")
     feed_flat, first_blocks, last_blocks, packed, cotangent_first, next_going = together(

time: 330 us -> 332 us (level)
  starting transfers between devices: 51.4 us -> 57.5 us
  waiting for transfers between devices: 86.3 us -> 82.8 us
    ppermute x57, starting transfers between devices: 51.3 us -> 57.4 us  [swapped(): return lax.ppermute(value, axis, [(i, i ^ bit) for i in range(count)])]
    all_gather x1, waiting for transfers between devices: 11.5 us -> 6.2 us  [per_device(): feed_full = lax.all_gather(feed_flat, 'dp', axis=0, tiled=True)]
    unnamed x90 -> x94, local copies, waits for them, and re-layouts: 10.3 us -> 8.83 us
  transfers between devices with their start and end apart: 59 -> 59, of which waited for: 23 -> 21; matrix products, arithmetic and copies ran while one was open for 10% -> 10% of each run, Pallas kernels for 35% -> 35%
where the time goes in v6:
time: 332 us; the launch traced here: 327 us
  Pallas kernels  128 us (39%)
  waiting for transfers between devices  82.8 us (25%)
  starting transfers between devices  57.5 us (17%)
  other arithmetic  21.3 us (6%)
  local copies, waits for them, and re-layouts  21.1 us (6%)
  between operations  15.7 us (5%)
    ppermute x57, waiting for transfers between devices, swapped(): return lax.ppermute(value, axis, [(i, i ^ bit) for i in range(count)])  76.6 us
    ppermute x57, starting transfers between devices, swapped(): return lax.ppermute(value, axis, [(i, i ^ bit) for i in range(count)])  57.4 us
    pallas_call x1, Pallas kernels, attend_back(): pl.pallas_call(functools.partial(attend_back_kernel, heads, len(unit)), g...  36.9 us
    pallas_call x2, Pallas kernels, feed(): pl.pallas_call(functools.partial(feed_kernel, here, len(stacks)), grid=(h...  29.9 us
    pallas_call x1, Pallas kernels, project_attend(): pl.pallas_call(functools.partial(project_attend_kernel, heads, len(unit))...  21.5 us
    pallas_call x1, Pallas kernels, feed_grads(): pl.pallas_call(feed_grads_kernel, grid=(rows // (2 * TILE),), out_shape=[...  15.8 us
    pallas_call x1, Pallas kernels, middle_back(): pl.pallas_call(functools.partial(middle_back_kernel, len(terms), parts),...  9.9 us
    unnamed x94, local copies, waits for them, and re-layouts  8.83 us
  transfers between devices with their start and end apart: 59, of which 21 were waited for; matrix products, arithmetic and copies ran while one was open for 10% of the time, Pallas kernels for 35%

profile of v6, /device:TPU:0, one launch (start us, length us, event | category | flops | bytes accessed | tf_op | source)
XLA Modules:
  0.0 326.6 jit_solution(12308105762264091847)
XLA Ops:
  9.5 1.1 copy.28
  10.8 3.6 %collective-permute-start.5 = (bf16[1,128,512]{2,1,0:T(8,128)(2,1)S(1)}, bf16[1,128,512]{2,1,0:T(8,128)(2,1)S(1)}, u32[]{:S(2)}, u32[]{:S(2)}) collective-permute-start(bf16[1,128,512]{2,1,0:T(8,128)(2,1)S(1)} %bitcast.71), channel_id=1, source_target_pairs={{0,16},{4,20},{8,24},{12,28},{16,0},{20,4},{24,8},{28,12},{1,17},{... | collective-permute-start | bytes 393224 | tf_op jit(solution)/shard_map/ppermute | solution.py:30
  16.0 1.9 collective-permute-start.1
  17.9 1.9 pad_maximum_fusion.2
  20.5 2.5 unit.1.refs_0_.refs_7_
  24.1 1.8 collective-permute-start.11
  25.9 1.6 collective-permute-start.6
  28.2 1.9 collective-permute-start.12
  30.1 1.6 collective-permute-start.9
  31.7 2.6 collective-permute-done.12
  34.4 2.7 collective-permute-start.13
  37.7 1.8 collective-permute-start.10
  39.6 9.3 %collective-permute-done.7 = bf16[4,128,512]{2,1,0:T(8,128)(2,1)S(1)} collective-permute-done((bf16[4,128,512]{2,1,0:T(8,128)(2,1)S(1)}, bf16[4,128,512]{2,1,0:T(8,128)(2,1)S(1)}, u32[]{:S(2)}, u32[]{:S(2)}) %collective-permute-start.7) | collective-permute-done | bytes 524320 | tf_op jit(solution)/shard_map/ppermute | solution.py:30
  48.9 1.1 pad_maximum_fusion.refs_4_
  50.0 1.7 collective-permute-start.14
  52.8 2.3 collective-permute-done.14
  58.7 1.6 collective-permute-start.15
  61.0 8.8 %collective-permute-done.15 = bf16[192,1024]{1,0:T(8,128)(2,1)S(1)} collective-permute-done((bf16[192,1024]{1,0:T(8,128)(2,1)S(1)}, bf16[192,1024]{1,0:T(8,128)(2,1)S(1)}, u32[]{:S(2)}, u32[]{:S(2)}) %collective-permute-start.15) | collective-permute-done | bytes 393248 | tf_op jit(solution)/shard_map/ppermute | solution.py:30
  69.8 2.2 placed_rows.1.refs_4_.refs_3_
  72.0 1.6 collective-permute-start.16
  75.3 21.5 %project_attend.1 = (bf16[512,256]{1,0:T(8,128)(2,1)}, bf16[512,256]{1,0:T(8,128)(2,1)}, bf16[512,256]{1,0:T(8,128)(2,1)}, bf16[512,256]{1,0:T(8,128)(2,1)}, bf1...) custom-call(s32[8]{0:T(128)} %broadcast_xor_fusion.1.owner_a, ...), custom_call_target="tpu_custom_call" | custom-call | flops 5368709120 | bytes 10485760 | tf_op jit(solution)/shard_map/project_attend/pallas_call | solution.py:487
  97.5 1.6 collective-permute-start.19
  100.7 6.2 %collective-permute-done.19.refs_2_.refs_9_ = bf16[512,256]{1,0:T(8,128)(2,1)} collective-permute-done((bf16[512,256]{1,0:T(8,128)(2,1)}, bf16[512,256]{1,0:T(8,128)(2,1)}, u32[]{:S(2)}, u32[]{:S(2)}) %collective-permute-start.19) | collective-permute-done | bytes 262176 | tf_op jit(solution)/shard_map/ppermute | solution.py:30
  106.9 4.7 %collective-permute-done.20.refs_3_.refs_10_ = bf16[512,256]{1,0:T(8,128)(2,1)} collective-permute-done((bf16[512,256]{1,0:T(8,128)(2,1)}, bf16[512,256]{1,0:T(8,128)(2,1)}, u32[]{:S(2)}, u32[]{:S(2)}) %collective-permute-start.20) | collective-permute-done | bytes 262176 | tf_op jit(solution)/shard_map/ppermute | solution.py:30
  111.6 5.0 %middle.1 = (bf16[512,1024]{1,0:T(8,128)(2,1)}, bf16[512,1024]{1,0:T(8,128)(2,1)}) custom-call(bf16[512,256]{1,0:T(8,128)(2,1)} %get-tuple-element.140.refs_0_.refs_7_, bf16[512,256]{1,0:T(8,128)(2,1)} %copy-done.12, bf16[512,256]{1,0:T(8,128)(2,1)} %collective-permute-done.19.refs_2_.refs_9_, bf16[512,256]{1,0:T(8,128)(2,1)} %collective-permute-done.20.refs_3_.refs_10_, ...), custom_call_target="tpu_custom_call" | custom-call | flops 1073741824 | bytes 6291456 | tf_op jit(solution)/shard_map/middle/pallas_call | solution.py:839
  117.8 1.7 collective-permute-start.26
  121.8 6.2 %all-gather.2.cloned.1.call-done.refs_4_ = bf16[1024,2048]{1,0:T(8,128)(2,1)} async-done(((bf16[128,2048]{1,0:T(8,128)(2,1)}), bf16[1024,2048]{1,0:T(8,128)(2,1)}) %all-gather.2.cloned.1.call-update) | async-done | bytes 4194320 | tf_op jit(solution)/shard_map/all_gather | solution.py:1011
  128.0 14.9 %feed.2 = (bf16[512,1024]{1,0:T(8,128)(2,1)}, bf16[512,1024]{1,0:T(8,128)(2,1)}, bf16[512,1024]{1,0:T(8,128)(2,1)}, bf16[512,1024]{1,0:T(8,128)(2,1)}, bf16[2048...) custom-call(bf16[512,1024]{1,0:T(8,128)(2,1)} %get-tuple-element.146.re, ...), custom_call_target="tpu_custom_call" | custom-call | flops 8589934592 | bytes 20971520 | tf_op jit(solution)/shard_map/feed/pallas_call | solution.py:714
  143.3 2.9 collective-permute-done.27.refs_1_
  147.2 14.9 %feed.3 = (bf16[512,1024]{1,0:T(8,128)(2,1)}, bf16[512,1024]{1,0:T(8,128)(2,1)}, bf16[512,1024]{1,0:T(8,128)(2,1)}, bf16[512,1024]{1,0:T(8,128)(2,1)}, bf16[2048...) custom-call(bf16[512,1024]{1,0:T(8,128)(2,1)} %collective-permute-do, ...), custom_call_target="tpu_custom_call", output_to_operand_aliasing={{4}: (6, {}), {5}: (7, {}), {6}: (8, {}), {7}: (9, {})} | custom-call | flops 8589934592 | bytes 20971520 | tf_op jit(solution)/shard_map/feed/pallas_call | solution.py:714
  162.8 2.2 collective-permute-done.29
  165.0 2.6 add_convert_fusion.3
  167.6 1.6 collective-permute-start.30
  169.3 15.8 %feed_grads.1 = (bf16[1024,2048]{1,0:T(8,128)(2,1)}, f32[1,1024]{1,0:T(1,128)}) custom-call(bf16[2048,1024]{1,0:T(8,128)(2,1)} %get-tuple-element.164.normed_ref, bf16[2048,1024]{1,0:T(8,128)(2,1)} %get-tuple-element.165.grad_ref, bf16[2048,1024]{1,0:T(8,128)(2,1)} %get-tuple-element.166.grads_ref, bf16[2048,1024]{1,0:T(8,128)(2,1)} %get-tuple-element.167.active_ref), custom_call_target="tpu_custom_call" | custom-call | flops 8589934592 | bytes 16777216 | tf_op jit(solution)/shard_map/feed_grads/pallas_call | solution.py:762
  185.1 1.2 copy-done.11
  186.3 1.6 add_convert_fusion.2
  188.9 4.2 %collective-permute-done.30.refs_2_ = bf16[512,1024]{1,0:T(8,128)(2,1)} collective-permute-done((bf16[512,1024]{1,0:T(8,128)(2,1)}, bf16[512,1024]{1,0:T(8,128)(2,1)}, u32[]{:S(2)}, u32[]{:S(2)}) %collective-permute-start.30) | collective-permute-done | bytes 1048608 | tf_op jit(solution)/shard_map/ppermute | solution.py:30
  193.1 1.6 collective-permute-start.35
  194.8 9.9 %middle_back.1 = (bf16[512,1024]{1,0:T(8,128)(2,1)}, f32[4,1024]{1,0:T(4,128)}, bf16[512,256]{1,0:T(8,128)(2,1)}, bf16[512,256]{1,0:T(8,128)(2,1)}, bf16[512,256...) custom-call(s32[8]{0:T(128)} %broadcast_xor_fusion.owner_b.owner, ...), custom_call_target="tpu_custom_call" | custom-call | flops 2147483648 | bytes 10485760 | tf_op jit(solution)/shard_map/middle_back/pallas_call | solution.py:904
  204.7 1.8 collective-permute-done.35
  207.7 1.7 collective-permute-start.33
  209.8 1.2 add_convert_fusion.5
  211.0 6.0 %collective-permute-done.33.refs_5_ = bf16[512,256]{1,0:T(8,128)(2,1)S(1)} collective-permute-done((bf16[512,256]{1,0:T(8,128)(2,1)}, bf16[512,256]{1,0:T(8,128)(2,1)S(1)}, u32[]{:S(2)}, u32[]{:S(2)}) %collective-permute-start.33) | collective-permute-done | bytes 262176 | tf_op jit(solution)/shard_map/ppermute | solution.py:30
  217.0 3.9 %collective-permute-done.34.refs_6_ = bf16[512,256]{1,0:T(8,128)(2,1)S(1)} collective-permute-done((bf16[512,256]{1,0:T(8,128)(2,1)}, bf16[512,256]{1,0:T(8,128)(2,1)S(1)}, u32[]{:S(2)}, u32[]{:S(2)}) %collective-permute-start.34) | collective-permute-done | bytes 262176 | tf_op jit(solution)/shard_map/ppermute | solution.py:30
  221.0 1.4 collective-permute-start.37
  224.0 36.9 %attend_back.1 = (bf16[4,128,512]{2,1,0:T(8,128)(2,1)}, bf16[4,128,512]{2,1,0:T(8,128)(2,1)}, bf16[4,128,256]{2,1,0:T(8,128)(2,1)S(1)}, bf16[4,128,256]{2,1,0:T(...) custom-call(s32[8]{0:T(128)S(1)} %copy-done.3, ...), custom_call_target="tpu_custom_call" | custom-call | flops 10737418240 | bytes 20971520 | tf_op jit(solution)/shard_map/attend_back/pallas_call | solution.py:615
  263.4 1.6 add_convert_fusion.4
  265.1 2.1 collective-permute-start.42
  267.2 1.1 collective-permute-start.49
  268.9 1.8 collective-permute-start.43
  270.6 7.6 %collective-permute-done.49 = f32[104,128]{1,0:T(8,128)S(1)} collective-permute-done((f32[104,128]{1,0:T(8,128)S(1)}, f32[104,128]{1,0:T(8,128)S(1)}, u32[]{:S(2)}, u32[]{:S(2)}) %collective-permute-start.49) | collective-permute-done | bytes 53280 | tf_op jit(solution)/shard_map/ppermute | solution.py:30
  278.2 1.7 collective-permute-start.50
  280.1 2.1 collective-permute-done.42
  283.2 1.9 add_convert_fusion
  285.1 1.7 collective-permute-start.46
  286.8 1.5 collective-permute-start.45
  288.3 2.6 collective-permute-start.51
  291.0 4.5 %collective-permute-done.45 = bf16[2,128,512]{2,1,0:T(8,128)(2,1)S(1)} collective-permute-done((bf16[2,128,512]{2,1,0:T(8,128)(2,1)S(1)}, bf16[2,128,512]{2,1,0:T(8,128)(2,1)S(1)}, u32[]{:S(2)}, u32[]{:S(2)}) %collective-permute-start.45) | collective-permute-done | bytes 262176 | tf_op jit(solution)/shard_map/ppermute | solution.py:30
  296.2 2.7 collective-permute-done.46.refs_3_
  299.0 2.1 collective-permute-start.52
  303.0 4.6 %input_back.1 = bf16[512,1024]{1,0:T(8,128)(2,1)} custom-call(bf16[512,1024]{1,0:T(8,128)(2,1)} %get-tuple-element.222.refs_0_, bf16[512,1024]{1,0:T(8,128)(2,1)} %copy-done.15, bf16[256,1024]{1,0:T(8,128)(2,1)} %copy-done.18, bf16[256,1024]{1,0:T(8,128)(2,1)} %copy-done.20, bf16[512,1024]{1,0:T(8,128)(2,1)} %refs_4_.1, ...), custom_call_target="tpu_custom_call" | custom-call | flops 10485760 | bytes 7340032 | tf_op jit(solution)/shard_map/input_back/pallas_call | solution.py:936
  307.5 1.5 collective-permute-start.55
  310.4 2.5 collective-permute-done.53
  317.5 2.1 fusion.8
  (245 shorter events, 38.3 us)
Async XLA Ops:
  7.2 120.8 %all-gather.2.cloned.1.call-start = ((), (), s32[]{:S(2)}) async-start(), calls=%async_computation.1 | async-start | bytes 4718592 | tf_op jit(solution)/shard_map/all_gather | solution.py:1011
  8.9 6.5 %collective-permute-start = (f32[96,128]{1,0:T(8,128)S(1)}, f32[96,128]{1,0:T(8,128)S(1)}, u32[]{:S(2)}, u32[]{:S(2)}) collective-permute-start(f32[96,128]{1,0:T(8,128)S(1)} %maximum_bitcast_fusion.2), channel_id=1, source_target_pairs={{0,1},{1,0},{2,3},{3,2},{4,5},{5,4},{6,7},{7,6},{8,9},{9,8},{10,11... | collective-permute-start | bytes 147464 | tf_op jit(solution)/shard_map/ppermute | solution.py:30
  10.8 15.1 %collective-permute-start.5 = (bf16[1,128,512]{2,1,0:T(8,128)(2,1)S(1)}, bf16[1,128,512]{2,1,0:T(8,128)(2,1)S(1)}, u32[]{:S(2)}, u32[]{:S(2)}) collective-permute-start(bf16[1,128,512]{2,1,0:T(8,128)(2,1)S(1)} %bitcast.71), channel_id=1, source_target_pairs={{0,16},{4,20},{8,24},{12,28},{16,0},{20,4},{24,8},{28,12},{1,17},{... | collective-permute-start | bytes 393224 | tf_op jit(solution)/shard_map/ppermute | solution.py:30
  15.3 14.8 %collective-permute-start.8 = (bf16[1,128,512]{2,1,0:T(8,128)(2,1)S(1)}, bf16[1,128,512]{2,1,0:T(8,128)(2,1)S(1)}, u32[]{:S(2)}, u32[]{:S(2)}) collective-permute-start(bf16[1,128,512]{2,1,0:T(8,128)(2,1)S(1)} %maximum_bitcast_fusion), channel_id=1, source_target_pairs={{0,16},{4,20},{8,24},{12,28},{16,0},{20,4},{24,8},{28,12},{1,17},{... | collective-permute-start | bytes 393224 | tf_op jit(solution)/shard_map/ppermute | solution.py:30
  16.0 7.0 %collective-permute-start.1 = (f32[96,128]{1,0:T(8,128)}, f32[96,128]{1,0:T(8,128)}, u32[]{:S(2)}, u32[]{:S(2)}) collective-permute-start(f32[96,128]{1,0:T(8,128)} %fusion.4), channel_id=1, source_target_pairs={{0,2},{1,3},{2,0},{3,1},{4,6},{5,7},{6,4},{7,5},{8,10},{9,11},{10,... | collective-permute-start | bytes 147464 | tf_op jit(solution)/shard_map/ppermute | solution.py:30
  23.9 26.1 %collective-permute-start.3 = (bf16[512,1024]{1,0:T(8,128)(2,1)}, bf16[512,1024]{1,0:T(8,128)(2,1)S(1)}, u32[]{:S(2)}, u32[]{:S(2)}) collective-permute-start(bf16[512,1024]{1,0:T(8,128)(2,1)} %unit.1.refs_0_.refs_7_), channel_id=1, source_target_pairs={{0,2},{1,3},{2,0},{3,1},{4,6},{5,7},{6,4},{7,5},{8,10},{9,11},{10,... | collective-permute-start | bytes 3145736 | tf_op jit(solution)/shard_map/ppermute | solution.py:30
  24.1 4.1 %collective-permute-start.11 = (f32[96,128]{1,0:T(8,128)S(1)}, f32[96,128]{1,0:T(8,128)S(1)}, u32[]{:S(2)}, u32[]{:S(2)}) collective-permute-start(f32[96,128]{1,0:T(8,128)S(1)} %bitcast.81), channel_id=1, source_target_pairs={{0,4},{4,0},{8,12},{12,8},{16,20},{20,16},{24,28},{28,24},{1,5},{5... | collective-permute-start | bytes 147464 | tf_op jit(solution)/shard_map/ppermute | solution.py:30
  25.9 11.1 %collective-permute-start.6 = (bf16[2,128,512]{2,1,0:T(8,128)(2,1)S(1)}, bf16[2,128,512]{2,1,0:T(8,128)(2,1)S(1)}, u32[]{:S(2)}, u32[]{:S(2)}) collective-permute-start(bf16[2,128,512]{2,1,0:T(8,128)(2,1)S(1)} %pad_maximum_fusion.8), channel_id=1, source_target_pairs={{0,8},{4,12},{8,0},{12,4},{16,24},{20,28},{24,16},{28,20},{1,9},{5... | collective-permute-start | bytes 786440 | tf_op jit(solution)/shard_map/ppermute | solution.py:30
  28.2 6.2 %collective-permute-start.12 = (f32[96,128]{1,0:T(8,128)S(1)}, f32[96,128]{1,0:T(8,128)S(1)}, u32[]{:S(2)}, u32[]{:S(2)}) collective-permute-start(f32[96,128]{1,0:T(8,128)S(1)} %bitcast_add_fusion), channel_id=1, source_target_pairs={{0,8},{4,12},{8,0},{12,4},{16,24},{20,28},{24,16},{28,20},{1,9},{5... | collective-permute-start | bytes 147464 | tf_op jit(solution)/shard_map/ppermute | solution.py:30
  30.1 7.5 %collective-permute-start.9 = (bf16[2,128,512]{2,1,0:T(8,128)(2,1)S(1)}, bf16[2,128,512]{2,1,0:T(8,128)(2,1)S(1)}, u32[]{:S(2)}, u32[]{:S(2)}) collective-permute-start(bf16[2,128,512]{2,1,0:T(8,128)(2,1)S(1)} %pad_maximum_fusion.9), channel_id=1, source_target_pairs={{0,4},{4,0},{8,12},{12,8},{16,20},{20,16},{24,28},{28,24},{1,5},{5... | collective-permute-start | bytes 786440 | tf_op jit(solution)/shard_map/ppermute | solution.py:30
  34.4 5.2 %collective-permute-start.13 = (f32[96,128]{1,0:T(8,128)S(1)}, f32[96,128]{1,0:T(8,128)S(1)}, u32[]{:S(2)}, u32[]{:S(2)}) collective-permute-start(f32[96,128]{1,0:T(8,128)S(1)} %fusion.13), channel_id=1, source_target_pairs={{0,16},{4,20},{8,24},{12,28},{16,0},{20,4},{24,8},{28,12},{1,17},{... | collective-permute-start | bytes 147464 | tf_op jit(solution)/shard_map/ppermute | solution.py:30
  37.1 11.8 %collective-permute-start.7 = (bf16[4,128,512]{2,1,0:T(8,128)(2,1)S(1)}, bf16[4,128,512]{2,1,0:T(8,128)(2,1)S(1)}, u32[]{:S(2)}, u32[]{:S(2)}) collective-permute-start(bf16[4,128,512]{2,1,0:T(8,128)(2,1)S(1)} %pad_maximum_fusion.3), channel_id=1, source_target_pairs={{0,4},{4,0},{8,12},{12,8},{16,20},{20,16},{24,28},{28,24},{1,5},{5... | collective-permute-start | bytes 1572872 | tf_op jit(solution)/shard_map/ppermute | solution.py:30
  37.7 13.9 %collective-permute-start.10 = (bf16[4,128,512]{2,1,0:T(8,128)(2,1)S(1)}, bf16[4,128,512]{2,1,0:T(8,128)(2,1)S(1)}, u32[]{:S(2)}, u32[]{:S(2)}) collective-permute-start(bf16[4,128,512]{2,1,0:T(8,128)(2,1)S(1)} %pad_maximum_fusion.4), channel_id=1, source_target_pairs={{0,8},{4,12},{8,0},{12,4},{16,24},{20,28},{24,16},{28,20},{1,9},{5... | collective-permute-start | bytes 1572872 | tf_op jit(solution)/shard_map/ppermute | solution.py:30
  39.6 34.5 %copy-start.24 = (f32[12288]{0:T(1024)}, f32[12288]{0:T(1024)S(1)}, u32[]{:S(2)}) copy-start(f32[12288]{0:T(1024)S(1)} %add_bitcast_fusion.1) | copy-start | bytes 147460
  50.0 5.0 %collective-permute-start.14 = (bf16[64,1024]{1,0:T(8,128)(2,1)S(1)}, bf16[64,1024]{1,0:T(8,128)(2,1)S(1)}, u32[]{:S(2)}, u32[]{:S(2)}) collective-permute-start(bf16[64,1024]{1,0:T(8,128)(2,1)S(1)} %copy-done.28), channel_id=1, source_target_pairs={{0,2},{1,3},{2,0},{3,1},{4,6},{5,7},{6,4},{7,5},{8,10},{9,11},{10,... | collective-permute-start | bytes 393224 | tf_op jit(solution)/shard_map/ppermute | solution.py:30
  55.1 262.4 %reduce-scatter.2.cloned.1.call-start = ((), (), s32[]{:S(2)}) async-start(), calls=%async_computation.2 | async-start | bytes 4718592 | tf_op jit(solution)/shard_map/reduce_scatter | solution.py:1066
  55.1 20.1 %collective-permute-start.2 = (bf16[512,1024]{1,0:T(8,128)(2,1)S(1)}, bf16[512,1024]{1,0:T(8,128)(2,1)}, u32[]{:S(2)}, u32[]{:S(2)}) collective-permute-start(bf16[512,1024]{1,0:T(8,128)(2,1)S(1)} %copy-done.13), channel_id=1, source_target_pairs={{0,1},{1,0},{2,3},{3,2},{4,5},{5,4},{6,7},{7,6},{8,9},{9,8},{10,11... | collective-permute-start | bytes 3145736 | tf_op jit(solution)/shard_map/ppermute | solution.py:30
  55.2 20.0 %collective-permute-start.4 = (bf16[512,1024]{1,0:T(8,128)(2,1)}, bf16[512,1024]{1,0:T(8,128)(2,1)}, u32[]{:S(2)}, u32[]{:S(2)}) collective-permute-start(bf16[512,1024]{1,0:T(8,128)(2,1)} %copy-done.34), channel_id=1, source_target_pairs={{0,1},{1,0},{2,3},{3,2},{4,5},{5,4},{6,7},{7,6},{8,9},{9,8},{10,11... | collective-permute-start | bytes 3145736 | tf_op jit(solution)/shard_map/ppermute | solution.py:30
  58.7 11.1 %collective-permute-start.15 = (bf16[192,1024]{1,0:T(8,128)(2,1)S(1)}, bf16[192,1024]{1,0:T(8,128)(2,1)S(1)}, u32[]{:S(2)}, u32[]{:S(2)}) collective-permute-start(bf16[192,1024]{1,0:T(8,128)(2,1)S(1)} %slice.180), channel_id=1, source_target_pairs={{0,2},{1,3},{2,0},{3,1},{4,6},{5,7},{6,4},{7,5},{8,10},{9,11},{10,... | collective-permute-start | bytes 1179656 | tf_op jit(solution)/shard_map/ppermute | solution.py:30
  72.0 24.8 %collective-permute-start.16 = (bf16[1024,256]{1,0:T(8,128)(2,1)}, bf16[1024,256]{1,0:T(8,128)(2,1)S(1)}, u32[]{:S(2)}, u32[]{:S(2)}) collective-permute-start(bf16[1024,256]{1,0:T(8,128)(2,1)} %placed_rows.1.refs_4_.refs_3_), channel_id=1, source_target_pairs={{0,2},{1,3},{2,0},{3,1},{4,6},{5,7},{6,4},{7,5},{8,10},{9,11},{10,... | collective-permute-start | bytes 1572872 | tf_op jit(solution)/shard_map/ppermute | solution.py:30
  73.6 23.2 %collective-permute-start.17 = (bf16[256,1024]{1,0:T(8,128)(2,1)}, bf16[256,1024]{1,0:T(8,128)(2,1)}, u32[]{:S(2)}, u32[]{:S(2)}) collective-permute-start(bf16[256,1024]{1,0:T(8,128)(2,1)} %slice.185), channel_id=1, source_target_pairs={{0,2},{1,3},{2,0},{3,1},{4,6},{5,7},{6,4},{7,5},{8,10},{9,11},{10,... | collective-permute-start | bytes 1572872 | tf_op jit(solution)/shard_map/ppermute | solution.py:30
  75.2 24.7 %collective-permute-start.21 = (bf16[1024,256]{1,0:T(8,128)(2,1)}, bf16[1024,256]{1,0:T(8,128)(2,1)S(1)}, u32[]{:S(2)}, u32[]{:S(2)}) collective-permute-start(bf16[1024,256]{1,0:T(8,128)(2,1)} %placed_rows.1.refs_4_.refs_3_), channel_id=1, source_target_pairs={{0,1},{1,0},{2,3},{3,2},{4,5},{5,4},{6,7},{7,6},{8,9},{9,8},{10,11... | collective-permute-start | bytes 1572872 | tf_op jit(solution)/shard_map/ppermute | solution.py:30
  96.8 14.8 %collective-permute-start.22 = (bf16[1024,256]{1,0:T(8,128)(2,1)S(1)}, bf16[1024,256]{1,0:T(8,128)(2,1)}, u32[]{:S(2)}, u32[]{:S(2)}) collective-permute-start(bf16[1024,256]{1,0:T(8,128)(2,1)S(1)} %collective-permute-done.16.refs_6_.refs_5_), channel_id=1, source_target_pairs={{0,1},{1,0},{2,3},{3,2},{4,5},{5,4},{6,7},{7,6},{8,9},{9,8},{10,11... | collective-permute-start | bytes 1572872 | tf_op jit(solution)/shard_map/ppermute | solution.py:30
  97.4 3.3 %collective-permute-start.18 = (bf16[512,256]{1,0:T(8,128)(2,1)}, bf16[512,256]{1,0:T(8,128)(2,1)S(1)}, u32[]{:S(2)}, u32[]{:S(2)}) collective-permute-start(bf16[512,256]{1,0:T(8,128)(2,1)} %get-tuple-element.141), channel_id=1, source_target_pairs={{0,1},{1,0},{2,3},{3,2},{4,5},{5,4},{6,7},{7,6},{8,9},{9,8},{10,11... | collective-permute-start | bytes 786440 | tf_op jit(solution)/shard_map/ppermute | solution.py:30
  97.5 9.4 %collective-permute-start.19 = (bf16[512,256]{1,0:T(8,128)(2,1)}, bf16[512,256]{1,0:T(8,128)(2,1)}, u32[]{:S(2)}, u32[]{:S(2)}) collective-permute-start(bf16[512,256]{1,0:T(8,128)(2,1)} %get-tuple-element.142), channel_id=1, source_target_pairs={{0,2},{1,3},{2,0},{3,1},{4,6},{5,7},{6,4},{7,5},{8,10},{9,11},{10,... | collective-permute-start | bytes 786440 | tf_op jit(solution)/shard_map/ppermute | solution.py:30
  99.1 12.5 %collective-permute-start.20 = (bf16[512,256]{1,0:T(8,128)(2,1)}, bf16[512,256]{1,0:T(8,128)(2,1)}, u32[]{:S(2)}, u32[]{:S(2)}) collective-permute-start(bf16[512,256]{1,0:T(8,128)(2,1)} %get-tuple-element.143), channel_id=1, source_target_pairs={{0,3},{1,2},{2,1},{3,0},{4,7},{5,6},{6,5},{7,4},{8,11},{9,10},{10,... | collective-permute-start | bytes 786440 | tf_op jit(solution)/shard_map/ppermute | solution.py:30
  99.9 21.8 %collective-permute-start.24 = (bf16[512,1024]{1,0:T(8,128)(2,1)S(1)}, bf16[512,1024]{1,0:T(8,128)(2,1)}, u32[]{:S(2)}, u32[]{:S(2)}) collective-permute-start(bf16[512,1024]{1,0:T(8,128)(2,1)S(1)} %copy-done.5), channel_id=1, source_target_pairs={{0,1},{1,0},{2,3},{3,2},{4,5},{5,4},{6,7},{7,6},{8,9},{9,8},{10,11... | collective-permute-start | bytes 3145736 | tf_op jit(solution)/shard_map/ppermute | solution.py:30
  116.6 5.1 %collective-permute-start.23 = (bf16[512,1024]{1,0:T(8,128)(2,1)}, bf16[512,1024]{1,0:T(8,128)(2,1)}, u32[]{:S(2)}, u32[]{:S(2)}) collective-permute-start(bf16[512,1024]{1,0:T(8,128)(2,1)} %get-tuple-element.146.refs_0_), channel_id=1, source_target_pairs={{0,1},{1,0},{2,3},{3,2},{4,5},{5,4},{6,7},{7,6},{8,9},{9,8},{10,11... | collective-permute-start | bytes 3145736 | tf_op jit(solution)/shard_map/ppermute | solution.py:30
  117.8 25.5 %collective-permute-start.26 = (bf16[512,1024]{1,0:T(8,128)(2,1)}, bf16[512,1024]{1,0:T(8,128)(2,1)}, u32[]{:S(2)}, u32[]{:S(2)}) collective-permute-start(bf16[512,1024]{1,0:T(8,128)(2,1)} %get-tuple-element.146.refs_0_), channel_id=1, source_target_pairs={{0,2},{1,3},{2,0},{3,1},{4,6},{5,7},{6,4},{7,5},{8,10},{9,11},{10,... | collective-permute-start | bytes 3145736 | tf_op jit(solution)/shard_map/ppermute | solution.py:30
  121.7 21.7 %collective-permute-start.28 = (bf16[512,1024]{1,0:T(8,128)(2,1)S(1)}, bf16[512,1024]{1,0:T(8,128)(2,1)}, u32[]{:S(2)}, u32[]{:S(2)}) collective-permute-start(bf16[512,1024]{1,0:T(8,128)(2,1)S(1)} %constant_dynamic-update-slice_fusion.refs_2_), channel_id=1, source_target_pairs={{0,1},{1,0},{2,3},{3,2},{4,5},{5,4},{6,7},{7,6},{8,9},{9,8},{10,11... | collective-permute-start | bytes 3145736 | tf_op jit(solution)/shard_map/ppermute | solution.py:30
  143.3 2.9 collective-permute-start.27
  162.1 2.9 collective-permute-start.29
  162.3 26.6 %collective-permute-start.25 = (bf16[512,1024]{1,0:T(8,128)(2,1)}, bf16[512,1024]{1,0:T(8,128)(2,1)S(1)}, u32[]{:S(2)}, u32[]{:S(2)}) collective-permute-start(bf16[512,1024]{1,0:T(8,128)(2,1)} %get-tuple-element.149), channel_id=1, source_target_pairs={{0,1},{1,0},{2,3},{3,2},{4,5},{5,4},{6,7},{7,6},{8,9},{9,8},{10,11... | collective-permute-start | bytes 3145736 | tf_op jit(solution)/shard_map/ppermute | solution.py:30
  162.6 22.4 %collective-permute-start.31 = (bf16[512,1024]{1,0:T(8,128)(2,1)}, bf16[512,1024]{1,0:T(8,128)(2,1)}, u32[]{:S(2)}, u32[]{:S(2)}) collective-permute-start(bf16[512,1024]{1,0:T(8,128)(2,1)} %get-tuple-element.170), channel_id=1, source_target_pairs={{0,1},{1,0},{2,3},{3,2},{4,5},{5,4},{6,7},{7,6},{8,9},{9,8},{10,11... | collective-permute-start | bytes 3145736 | tf_op jit(solution)/shard_map/ppermute | solution.py:30
  167.6 25.5 %collective-permute-start.30 = (bf16[512,1024]{1,0:T(8,128)(2,1)}, bf16[512,1024]{1,0:T(8,128)(2,1)}, u32[]{:S(2)}, u32[]{:S(2)}) collective-permute-start(bf16[512,1024]{1,0:T(8,128)(2,1)} %add_convert_fusion.3), channel_id=1, source_target_pairs={{0,2},{1,3},{2,0},{3,1},{4,6},{5,7},{6,4},{7,5},{8,10},{9,11},{10,... | collective-permute-start | bytes 3145736 | tf_op jit(solution)/shard_map/ppermute | solution.py:30
  193.1 13.3 %collective-permute-start.35 = (bf16[256,1024]{1,0:T(8,128)(2,1)}, bf16[256,1024]{1,0:T(8,128)(2,1)S(1)}, u32[]{:S(2)}, u32[]{:S(2)}) collective-permute-start(bf16[256,1024]{1,0:T(8,128)(2,1)} %get-tuple-element.183), channel_id=1, source_target_pairs={{0,2},{1,3},{2,0},{3,1},{4,6},{5,7},{6,4},{7,5},{8,10},{9,11},{10,... | collective-permute-start | bytes 1572872 | tf_op jit(solution)/shard_map/ppermute | solution.py:30
  194.8 28.2 %copy-start.3 = (s32[8]{0:T(128)S(1)}, s32[8]{0:T(128)}, u32[]{:S(2)}) copy-start(s32[8]{0:T(128)} %broadcast_xor_fusion.1.owner_a) | copy-start | bytes 100
  194.8 28.2 %copy-start.4 = (f32[32,256]{1,0:T(8,128)S(1)}, f32[32,256]{1,0:T(8,128)}, u32[]{:S(2)}) copy-start(f32[32,256]{1,0:T(8,128)} %get-tuple-element.133.refs_1_) | copy-start | bytes 98308
  206.5 3.3 %collective-permute-start.36 = (bf16[8,128,256]{2,1,0:T(8,128)(2,1)}, bf16[8,128,256]{2,1,0:T(8,128)(2,1)S(1)}, u32[]{:S(2)}, u32[]{:S(2)}) collective-permute-start(bf16[8,128,256]{2,1,0:T(8,128)(2,1)} %get-tuple-element.185), channel_id=1, source_target_pairs={{0,1},{1,0},{2,3},{3,2},{4,5},{5,4},{6,7},{7,6},{8,9},{9,8},{10,11... | collective-permute-start | bytes 1572872 | tf_op jit(solution)/shard_map/ppermute | solution.py:30
  207.1 3.8 %collective-permute-start.32 = (bf16[512,256]{1,0:T(8,128)(2,1)}, bf16[512,256]{1,0:T(8,128)(2,1)S(1)}, u32[]{:S(2)}, u32[]{:S(2)}) collective-permute-start(bf16[512,256]{1,0:T(8,128)(2,1)} %get-tuple-element.176), channel_id=1, source_target_pairs={{0,1},{1,0},{2,3},{3,2},{4,5},{5,4},{6,7},{7,6},{8,9},{9,8},{10,11... | collective-permute-start | bytes 786440 | tf_op jit(solution)/shard_map/ppermute | solution.py:30
  207.7 9.4 %collective-permute-start.33 = (bf16[512,256]{1,0:T(8,128)(2,1)}, bf16[512,256]{1,0:T(8,128)(2,1)S(1)}, u32[]{:S(2)}, u32[]{:S(2)}) collective-permute-start(bf16[512,256]{1,0:T(8,128)(2,1)} %get-tuple-element.177), channel_id=1, source_target_pairs={{0,2},{1,3},{2,0},{3,1},{4,6},{5,7},{6,4},{7,5},{8,10},{9,11},{10,... | collective-permute-start | bytes 786440 | tf_op jit(solution)/shard_map/ppermute | solution.py:30
  209.3 11.7 %collective-permute-start.34 = (bf16[512,256]{1,0:T(8,128)(2,1)}, bf16[512,256]{1,0:T(8,128)(2,1)S(1)}, u32[]{:S(2)}, u32[]{:S(2)}) collective-permute-start(bf16[512,256]{1,0:T(8,128)(2,1)} %get-tuple-element.178), channel_id=1, source_target_pairs={{0,3},{1,2},{2,1},{3,0},{4,7},{5,6},{6,5},{7,4},{8,11},{9,10},{10,... | collective-permute-start | bytes 786440 | tf_op jit(solution)/shard_map/ppermute | solution.py:30
  209.3 51.6 %collective-permute-start.38 = (bf16[8,128,256]{2,1,0:T(8,128)(2,1)}, bf16[8,128,256]{2,1,0:T(8,128)(2,1)S(1)}, u32[]{:S(2)}, u32[]{:S(2)}) collective-permute-start(bf16[8,128,256]{2,1,0:T(8,128)(2,1)} %get-tuple-element.195), channel_id=1, source_target_pairs={{0,1},{1,0},{2,3},{3,2},{4,5},{5,4},{6,7},{7,6},{8,9},{9,8},{10,11... | collective-permute-start | bytes 1572872 | tf_op jit(solution)/shard_map/ppermute | solution.py:30
  221.0 40.0 %collective-permute-start.37 = (bf16[256,1024]{1,0:T(8,128)(2,1)}, bf16[256,1024]{1,0:T(8,128)(2,1)S(1)}, u32[]{:S(2)}, u32[]{:S(2)}) collective-permute-start(bf16[256,1024]{1,0:T(8,128)(2,1)} %get-tuple-element.193), channel_id=1, source_target_pairs={{0,2},{1,3},{2,0},{3,1},{4,6},{5,7},{6,4},{7,5},{8,10},{9,11},{10,... | collective-permute-start | bytes 1572872 | tf_op jit(solution)/shard_map/ppermute | solution.py:30
  222.4 38.6 %collective-permute-start.39 = (bf16[8,128,256]{2,1,0:T(8,128)(2,1)S(1)}, bf16[8,128,256]{2,1,0:T(8,128)(2,1)S(1)}, u32[]{:S(2)}, u32[]{:S(2)}) collective-permute-start(bf16[8,128,256]{2,1,0:T(8,128)(2,1)S(1)} %add_convert_fusion.5), channel_id=1, source_target_pairs={{0,2},{1,3},{2,0},{3,1},{4,6},{5,7},{6,4},{7,5},{8,10},{9,11},{10,... | collective-permute-start | bytes 1572872 | tf_op jit(solution)/shard_map/ppermute | solution.py:30
  224.0 38.4 %copy-start.30 = (f32[4,1024]{1,0:T(4,128)S(1)}, f32[4,1024]{1,0:T(4,128)}, u32[]{:S(2)}) copy-start(f32[4,1024]{1,0:T(4,128)} %get-tuple-element.228) | copy-start | bytes 49156
  224.0 38.4 %copy-start.32 = (f32[1,1024]{1,0:T(1,128)S(1)}, f32[1,1024]{1,0:T(1,128)}, u32[]{:S(2)}) copy-start(f32[1,1024]{1,0:T(1,128)} %get-tuple-element.230) | copy-start | bytes 12292
  261.0 7.3 %collective-permute-start.40 = (bf16[512,1024]{1,0:T(8,128)(2,1)}, bf16[512,1024]{1,0:T(8,128)(2,1)S(1)}, u32[]{:S(2)}, u32[]{:S(2)}) collective-permute-start(bf16[512,1024]{1,0:T(8,128)(2,1)} %get-tuple-element.202), channel_id=1, source_target_pairs={{0,1},{1,0},{2,3},{3,2},{4,5},{5,4},{6,7},{7,6},{8,9},{9,8},{10,11... | collective-permute-start | bytes 3145736 | tf_op jit(solution)/shard_map/ppermute | solution.py:30
  262.1 21.0 %collective-permute-start.47 = (bf16[512,1024]{1,0:T(8,128)(2,1)}, bf16[512,1024]{1,0:T(8,128)(2,1)S(1)}, u32[]{:S(2)}, u32[]{:S(2)}) collective-permute-start(bf16[512,1024]{1,0:T(8,128)(2,1)} %get-tuple-element.218), channel_id=1, source_target_pairs={{0,1},{1,0},{2,3},{3,2},{4,5},{5,4},{6,7},{7,6},{8,9},{9,8},{10,11... | collective-permute-start | bytes 3145736 | tf_op jit(solution)/shard_map/ppermute | solution.py:30
  262.8 17.1 %collective-permute-start.41 = (bf16[4,128,512]{2,1,0:T(8,128)(2,1)}, bf16[4,128,512]{2,1,0:T(8,128)(2,1)S(1)}, u32[]{:S(2)}, u32[]{:S(2)}) collective-permute-start(bf16[4,128,512]{2,1,0:T(8,128)(2,1)} %get-tuple-element.211), channel_id=1, source_target_pairs={{0,4},{4,0},{8,12},{12,8},{16,20},{20,16},{24,28},{28,24},{1,5},{5... | collective-permute-start | bytes 1572872 | tf_op jit(solution)/shard_map/ppermute | solution.py:30
  265.1 17.1 %collective-permute-start.42 = (bf16[4,128,512]{2,1,0:T(8,128)(2,1)S(1)}, bf16[4,128,512]{2,1,0:T(8,128)(2,1)S(1)}, u32[]{:S(2)}, u32[]{:S(2)}) collective-permute-start(bf16[4,128,512]{2,1,0:T(8,128)(2,1)S(1)} %pad_maximum_fusion.6), channel_id=1, source_target_pairs={{0,8},{4,12},{8,0},{12,4},{16,24},{20,28},{24,16},{28,20},{1,9},{5... | collective-permute-start | bytes 1572872 | tf_op jit(solution)/shard_map/ppermute | solution.py:30
  267.2 11.0 %collective-permute-start.49 = (f32[104,128]{1,0:T(8,128)S(1)}, f32[104,128]{1,0:T(8,128)S(1)}, u32[]{:S(2)}, u32[]{:S(2)}) collective-permute-start(f32[104,128]{1,0:T(8,128)S(1)} %maximum_bitcast_fusion.1), channel_id=1, source_target_pairs={{0,4},{4,0},{8,12},{12,8},{16,20},{20,16},{24,28},{28,24},{1,5},{5... | collective-permute-start | bytes 159752 | tf_op jit(solution)/shard_map/ppermute | solution.py:30
  268.9 13.5 %collective-permute-start.43 = (bf16[256,1024]{1,0:T(8,128)(2,1)S(1)}, bf16[256,1024]{1,0:T(8,128)(2,1)S(1)}, u32[]{:S(2)}, u32[]{:S(2)}) collective-permute-start(bf16[256,1024]{1,0:T(8,128)(2,1)S(1)} %get-tuple-element.247), channel_id=1, source_target_pairs={{0,2},{1,3},{2,0},{3,1},{4,6},{5,7},{6,4},{7,5},{8,10},{9,11},{10,... | collective-permute-start | bytes 1572872 | tf_op jit(solution)/shard_map/ppermute | solution.py:30
  278.2 10.0 %collective-permute-start.50 = (f32[104,128]{1,0:T(8,128)S(1)}, f32[104,128]{1,0:T(8,128)S(1)}, u32[]{:S(2)}, u32[]{:S(2)}) collective-permute-start(f32[104,128]{1,0:T(8,128)S(1)} %fusion.5), channel_id=1, source_target_pairs={{0,8},{4,12},{8,0},{12,4},{16,24},{20,28},{24,16},{28,20},{1,9},{5... | collective-permute-start | bytes 159752 | tf_op jit(solution)/shard_map/ppermute | solution.py:30
  282.4 8.5 %collective-permute-start.44 = (bf16[2,128,512]{2,1,0:T(8,128)(2,1)S(1)}, bf16[2,128,512]{2,1,0:T(8,128)(2,1)S(1)}, u32[]{:S(2)}, u32[]{:S(2)}) collective-permute-start(bf16[2,128,512]{2,1,0:T(8,128)(2,1)S(1)} %get-tuple-element.215), channel_id=1, source_target_pairs={{0,8},{4,12},{8,0},{12,4},{16,24},{20,28},{24,16},{28,20},{1,9},{5... | collective-permute-start | bytes 786440 | tf_op jit(solution)/shard_map/ppermute | solution.py:30
  285.1 13.9 %collective-permute-start.46 = (bf16[256,1024]{1,0:T(8,128)(2,1)S(1)}, bf16[256,1024]{1,0:T(8,128)(2,1)S(1)}, u32[]{:S(2)}, u32[]{:S(2)}) collective-permute-start(bf16[256,1024]{1,0:T(8,128)(2,1)S(1)} %get-tuple-element.246), channel_id=1, source_target_pairs={{0,2},{1,3},{2,0},{3,1},{4,6},{5,7},{6,4},{7,5},{8,10},{9,11},{10,... | collective-permute-start | bytes 1572872 | tf_op jit(solution)/shard_map/ppermute | solution.py:30
  286.8 15.1 %collective-permute-start.48 = (bf16[512,1024]{1,0:T(8,128)(2,1)S(1)}, bf16[512,1024]{1,0:T(8,128)(2,1)S(1)}, u32[]{:S(2)}, u32[]{:S(2)}) collective-permute-start(bf16[512,1024]{1,0:T(8,128)(2,1)S(1)} %copy-done.35), channel_id=1, source_target_pairs={{0,1},{1,0},{2,3},{3,2},{4,5},{5,4},{6,7},{7,6},{8,9},{9,8},{10,11... | collective-permute-start | bytes 3145736 | tf_op jit(solution)/shard_map/ppermute | solution.py:30
  286.8 8.7 %collective-permute-start.45 = (bf16[2,128,512]{2,1,0:T(8,128)(2,1)S(1)}, bf16[2,128,512]{2,1,0:T(8,128)(2,1)S(1)}, u32[]{:S(2)}, u32[]{:S(2)}) collective-permute-start(bf16[2,128,512]{2,1,0:T(8,128)(2,1)S(1)} %get-tuple-element.216), channel_id=1, source_target_pairs={{0,4},{4,0},{8,12},{12,8},{16,20},{20,16},{24,28},{28,24},{1,5},{5... | collective-permute-start | bytes 786440 | tf_op jit(solution)/shard_map/ppermute | solution.py:30
  288.3 13.6 %collective-permute-start.51 = (f32[104,128]{1,0:T(8,128)S(1)}, f32[104,128]{1,0:T(8,128)S(1)}, u32[]{:S(2)}, u32[]{:S(2)}) collective-permute-start(f32[104,128]{1,0:T(8,128)S(1)} %fusion.12), channel_id=1, source_target_pairs={{0,16},{4,20},{8,24},{12,28},{16,0},{20,4},{24,8},{28,12},{1,17},{... | collective-permute-start | bytes 159752 | tf_op jit(solution)/shard_map/ppermute | solution.py:30
  299.0 11.5 %collective-permute-start.52 = (bf16[1,128,512]{2,1,0:T(8,128)(2,1)S(1)}, bf16[1,128,512]{2,1,0:T(8,128)(2,1)}, u32[]{:S(2)}, u32[]{:S(2)}) collective-permute-start(bf16[1,128,512]{2,1,0:T(8,128)(2,1)S(1)} %get-tuple-element.233), channel_id=1, source_target_pairs={{0,16},{4,20},{8,24},{12,28},{16,0},{20,4},{24,8},{28,12},{1,17},{... | collective-permute-start | bytes 393224 | tf_op jit(solution)/shard_map/ppermute | solution.py:30
  301.1 11.9 %collective-permute-start.53 = (bf16[1,128,512]{2,1,0:T(8,128)(2,1)}, bf16[1,128,512]{2,1,0:T(8,128)(2,1)}, u32[]{:S(2)}, u32[]{:S(2)}) collective-permute-start(bf16[1,128,512]{2,1,0:T(8,128)(2,1)} %get-tuple-element.235), channel_id=1, source_target_pairs={{0,16},{4,20},{8,24},{12,28},{16,0},{20,4},{24,8},{28,12},{1,17},{... | collective-permute-start | bytes 393224 | tf_op jit(solution)/shard_map/ppermute | solution.py:30
  307.5 7.4 %collective-permute-start.56 = (f32[104,128]{1,0:T(8,128)S(1)}, f32[104,128]{1,0:T(8,128)S(1)}, u32[]{:S(2)}, u32[]{:S(2)}) collective-permute-start(f32[104,128]{1,0:T(8,128)S(1)} %bitcast.85), channel_id=1, source_target_pairs={{0,3},{1,2},{2,1},{3,0},{4,7},{5,6},{6,5},{7,4},{8,11},{9,10},{10,... | collective-permute-start | bytes 159752 | tf_op jit(solution)/shard_map/ppermute | solution.py:30
  307.5 7.4 %collective-permute-start.55 = (f32[104,128]{1,0:T(8,128)S(1)}, f32[104,128]{1,0:T(8,128)S(1)}, u32[]{:S(2)}, u32[]{:S(2)}) collective-permute-start(f32[104,128]{1,0:T(8,128)S(1)} %bitcast.86), channel_id=1, source_target_pairs={{0,2},{1,3},{2,0},{3,1},{4,6},{5,7},{6,4},{7,5},{8,10},{9,11},{10,... | collective-permute-start | bytes 159752 | tf_op jit(solution)/shard_map/ppermute | solution.py:30
  309.0 5.9 %collective-permute-start.54 = (f32[104,128]{1,0:T(8,128)S(1)}, f32[104,128]{1,0:T(8,128)S(1)}, u32[]{:S(2)}, u32[]{:S(2)}) collective-permute-start(f32[104,128]{1,0:T(8,128)S(1)} %bitcast.87), channel_id=1, source_target_pairs={{0,1},{1,0},{2,3},{3,2},{4,5},{5,4},{6,7},{7,6},{8,9},{9,8},{10,11... | collective-permute-start | bytes 159752 | tf_op jit(solution)/shard_map/ppermute | solution.py:30
  (38 other events, 363.2 us)
Sparse Core Ops, SparseCore 0:
  55.2 72.7 all-gather.1
  185.2 88.1 reduce-scatter.1

commit v7 on v5

--- a/solution.py
+++ b/solution.py
@@ -369,12 +369,12 @@
         out_ref[here, :width] = grad_queries.astype(BF16)
 
     def step(group, carry):
-        for part in range(6):
-            item(1 + group * 6 + part)
+        for part in range(10):
+            item(1 + group * 10 + part)
         return carry
 
-    lax.fori_loop(0, (count - 1) // 6, step, 0)
-    for number in range(1 + (count - 1) // 6 * 6, count):
+    lax.fori_loop(0, (count - 1) // 10, step, 0)
+    for number in range(1 + (count - 1) // 10 * 10, count):
         item(number)
 
     row = lax.broadcasted_iota(jnp.int32, (BLOCK, 1), 0)
@@ -878,12 +878,15 @@
 
     @pl.when(first)
     def _():
-        sum_ref[...] = jnp.zeros_like(sum_ref)
-        found_ref[...] = jnp.zeros_like(found_ref)
-
-    sum_ref[...] += sums
-    for k, context_ref in enumerate(context_refs):
-        found_ref[:, k * width : (k + 1) * width] += matmul(low, context_ref[...], TN)
+        sum_ref[...] = sums
+        for k, context_ref in enumerate(context_refs):
+            found_ref[:, k * width : (k + 1) * width] = matmul(low, context_ref[...], TN)
+
+    @pl.when(pl.program_id(0) > 0)
+    def _():
+        sum_ref[...] += sums
+        for k, context_ref in enumerate(context_refs):
+            found_ref[:, k * width : (k + 1) * width] += matmul(low, context_ref[...], TN)
 
     @pl.when(last)
     def _():

time: 330 us -> 330 us (level)
  no operation moved by 1% of the time
where the time goes in v7:
time: 330 us; the launch traced here: 324 us
  Pallas kernels  128 us (39%)
  waiting for transfers between devices  86.6 us (26%)
  starting transfers between devices  51.6 us (16%)
  local copies, waits for them, and re-layouts  23.6 us (7%)
  other arithmetic  18.7 us (6%)
  between operations  15.8 us (5%)
    ppermute x57, waiting for transfers between devices, swapped(): return lax.ppermute(value, axis, [(i, i ^ bit) for i in range(count)])  75.2 us
    ppermute x57, starting transfers between devices, swapped(): return lax.ppermute(value, axis, [(i, i ^ bit) for i in range(count)])  51.5 us
    pallas_call x1, Pallas kernels, attend_back(): pl.pallas_call(functools.partial(attend_back_kernel, heads, len(unit)), g...  36.7 us
    pallas_call x2, Pallas kernels, feed(): pl.pallas_call(functools.partial(feed_kernel, here, len(stacks)), grid=(h...  29.9 us
    pallas_call x1, Pallas kernels, project_attend(): pl.pallas_call(functools.partial(project_attend_kernel, heads, len(unit))...  21.6 us
    pallas_call x1, Pallas kernels, feed_grads(): pl.pallas_call(feed_grads_kernel, grid=(rows // (2 * TILE),), out_shape=[...  15.9 us
    all_gather x1, waiting for transfers between devices, per_device(): feed_full = lax.all_gather(feed_flat, 'dp', axis=0, tiled=True)  11.4 us
    unnamed x90, local copies, waits for them, and re-layouts  10.3 us
  transfers between devices with their start and end apart: 59, of which 23 were waited for; matrix products, arithmetic and copies ran while one was open for 10% of the time, Pallas kernels for 35%

profile of v7, /device:TPU:0, one launch (start us, length us, event | category | flops | bytes accessed | tf_op | source)
XLA Modules:
  0.0 324.2 jit_solution(1335355332238655221)
XLA Ops:
  9.5 1.1 copy.28
  10.7 3.6 %collective-permute-start.5 = (bf16[1,128,512]{2,1,0:T(8,128)(2,1)S(1)}, bf16[1,128,512]{2,1,0:T(8,128)(2,1)S(1)}, u32[]{:S(2)}, u32[]{:S(2)}) collective-permute-start(bf16[1,128,512]{2,1,0:T(8,128)(2,1)S(1)} %bitcast.71), channel_id=1, source_target_pairs={{0,16},{4,20},{8,24},{12,28},{16,0},{20,4},{24,8},{28,12},{1,17},{... | collective-permute-start | bytes 393224 | tf_op jit(solution)/shard_map/ppermute | solution.py:30
  15.4 1.8 fusion.8
  17.1 2.0 collective-permute-start.1
  20.0 2.5 unit.1.refs_0_.refs_7_
  23.3 1.5 collective-permute-start.11
  24.8 1.6 collective-permute-start.6
  27.4 1.6 collective-permute-start.12
  29.1 1.6 collective-permute-start.9
  30.6 2.9 collective-permute-done.12
  33.6 2.4 collective-permute-start.13
  36.0 1.6 collective-permute-start.7
  37.7 1.9 collective-permute-start.10
  39.5 8.0 %collective-permute-done.3.refs_2_.refs_9_ = bf16[512,1024]{1,0:T(8,128)(2,1)S(1)} collective-permute-done((bf16[512,1024]{1,0:T(8,128)(2,1)}, bf16[512,1024]{1,0:T(8,128)(2,1)S(1)}, u32[]{:S(2)}, u32[]{:S(2)}) %collective-permute-start.3) | collective-permute-done | bytes 1048608 | tf_op jit(solution)/shard_map/ppermute | solution.py:30
  48.7 1.1 pad_maximum_fusion.refs_4_
  50.3 1.1 pad_maximum_fusion.1.refs_5_.blocks_ref
  51.4 3.3 %collective-permute-done.14 = bf16[128,1024]{1,0:T(8,128)(2,1)} collective-permute-done((bf16[128,1024]{1,0:T(8,128)(2,1)S(1)}, bf16[128,1024]{1,0:T(8,128)(2,1)}, u32[]{:S(2)}, u32[]{:S(2)}) %collective-permute-start.14) | collective-permute-done | bytes 262176 | tf_op jit(solution)/shard_map/ppermute | solution.py:30
  59.3 6.4 %collective-permute-done.15 = bf16[128,1024]{1,0:T(8,128)(2,1)S(1)} collective-permute-done((bf16[128,1024]{1,0:T(8,128)(2,1)S(1)}, bf16[128,1024]{1,0:T(8,128)(2,1)S(1)}, u32[]{:S(2)}, u32[]{:S(2)}) %collective-permute-start.15) | collective-permute-done | bytes 262176 | tf_op jit(solution)/shard_map/ppermute | solution.py:30
  65.7 2.2 placed_rows.1.refs_4_.refs_3_
  68.1 1.7 collective-permute-start.17
  71.1 21.6 %project_attend.1 = (bf16[512,256]{1,0:T(8,128)(2,1)}, bf16[512,256]{1,0:T(8,128)(2,1)}, bf16[512,256]{1,0:T(8,128)(2,1)}, bf16[512,256]{1,0:T(8,128)(2,1)}, bf1...) custom-call(s32[8]{0:T(128)} %broadcast_xor_fusion.1.owner_a, ...), custom_call_target="tpu_custom_call" | custom-call | flops 5368709120 | bytes 10485760 | tf_op jit(solution)/shard_map/project_attend/pallas_call | solution.py:487
  93.7 1.5 collective-permute-start.20
  96.6 6.2 %collective-permute-done.19.refs_2_.refs_9_ = bf16[512,256]{1,0:T(8,128)(2,1)} collective-permute-done((bf16[512,256]{1,0:T(8,128)(2,1)}, bf16[512,256]{1,0:T(8,128)(2,1)}, u32[]{:S(2)}, u32[]{:S(2)}) %collective-permute-start.19) | collective-permute-done | bytes 262176 | tf_op jit(solution)/shard_map/ppermute | solution.py:30
  102.8 4.7 %collective-permute-done.20.refs_3_.refs_10_ = bf16[512,256]{1,0:T(8,128)(2,1)} collective-permute-done((bf16[512,256]{1,0:T(8,128)(2,1)}, bf16[512,256]{1,0:T(8,128)(2,1)}, u32[]{:S(2)}, u32[]{:S(2)}) %collective-permute-start.20) | collective-permute-done | bytes 262176 | tf_op jit(solution)/shard_map/ppermute | solution.py:30
  107.6 5.0 %middle.1 = (bf16[512,1024]{1,0:T(8,128)(2,1)}, bf16[512,1024]{1,0:T(8,128)(2,1)}) custom-call(bf16[512,256]{1,0:T(8,128)(2,1)} %get-tuple-element.140.refs_0_.refs_7_, bf16[512,256]{1,0:T(8,128)(2,1)} %copy-done.12, bf16[512,256]{1,0:T(8,128)(2,1)} %collective-permute-done.19.refs_2_.refs_9_, bf16[512,256]{1,0:T(8,128)(2,1)} %collective-permute-done.20.refs_3_.refs_10_, ...), custom_call_target="tpu_custom_call" | custom-call | flops 1073741824 | bytes 6291456 | tf_op jit(solution)/shard_map/middle/pallas_call | solution.py:839
  116.0 1.1 constant_dynamic-update-slice_fusion.refs_2_
  117.2 11.4 %all-gather.2.cloned.1.call-done.refs_4_ = bf16[1024,2048]{1,0:T(8,128)(2,1)} async-done(((bf16[128,2048]{1,0:T(8,128)(2,1)}), bf16[1024,2048]{1,0:T(8,128)(2,1)}) %all-gather.2.cloned.1.call-update) | async-done | bytes 4194320 | tf_op jit(solution)/shard_map/all_gather | solution.py:1014
  128.6 14.9 %feed.2 = (bf16[512,1024]{1,0:T(8,128)(2,1)}, bf16[512,1024]{1,0:T(8,128)(2,1)}, bf16[512,1024]{1,0:T(8,128)(2,1)}, bf16[512,1024]{1,0:T(8,128)(2,1)}, bf16[2048...) custom-call(bf16[512,1024]{1,0:T(8,128)(2,1)} %get-tuple-element.146.re, ...), custom_call_target="tpu_custom_call" | custom-call | flops 8589934592 | bytes 20971520 | tf_op jit(solution)/shard_map/feed/pallas_call | solution.py:714
  143.6 2.8 collective-permute-done.27.refs_1_
  147.5 14.9 %feed.3 = (bf16[512,1024]{1,0:T(8,128)(2,1)}, bf16[512,1024]{1,0:T(8,128)(2,1)}, bf16[512,1024]{1,0:T(8,128)(2,1)}, bf16[512,1024]{1,0:T(8,128)(2,1)}, bf16[2048...) custom-call(bf16[512,1024]{1,0:T(8,128)(2,1)} %collective-permute-do, ...), custom_call_target="tpu_custom_call", output_to_operand_aliasing={{4}: (6, {}), {5}: (7, {}), {6}: (8, {}), {7}: (9, {})} | custom-call | flops 8589934592 | bytes 20971520 | tf_op jit(solution)/shard_map/feed/pallas_call | solution.py:714
  163.1 2.2 collective-permute-done.29
  165.3 2.6 add_convert_fusion.3
  168.0 1.5 collective-permute-start.30
  169.4 15.9 %feed_grads.1 = (bf16[1024,2048]{1,0:T(8,128)(2,1)}, f32[1,1024]{1,0:T(1,128)}) custom-call(bf16[2048,1024]{1,0:T(8,128)(2,1)} %get-tuple-element.164.normed_ref, bf16[2048,1024]{1,0:T(8,128)(2,1)} %get-tuple-element.165.grad_ref, bf16[2048,1024]{1,0:T(8,128)(2,1)} %get-tuple-element.166.grads_ref, bf16[2048,1024]{1,0:T(8,128)(2,1)} %get-tuple-element.167.active_ref), custom_call_target="tpu_custom_call" | custom-call | flops 8589934592 | bytes 16777216 | tf_op jit(solution)/shard_map/feed_grads/pallas_call | solution.py:762
  185.4 1.2 copy-done.11
  186.6 1.6 add_convert_fusion.2
  189.2 4.3 %collective-permute-done.30.refs_2_ = bf16[512,1024]{1,0:T(8,128)(2,1)} collective-permute-done((bf16[512,1024]{1,0:T(8,128)(2,1)}, bf16[512,1024]{1,0:T(8,128)(2,1)}, u32[]{:S(2)}, u32[]{:S(2)}) %collective-permute-start.30) | collective-permute-done | bytes 1048608 | tf_op jit(solution)/shard_map/ppermute | solution.py:30
  193.5 1.5 collective-permute-start.35
  195.0 9.6 %middle_back.1 = (bf16[512,1024]{1,0:T(8,128)(2,1)}, f32[4,1024]{1,0:T(4,128)}, bf16[512,256]{1,0:T(8,128)(2,1)}, bf16[512,256]{1,0:T(8,128)(2,1)}, bf16[512,256...) custom-call(s32[8]{0:T(128)} %broadcast_xor_fusion.owner_b.owner, ...), custom_call_target="tpu_custom_call" | custom-call | flops 2147483648 | bytes 10485760 | tf_op jit(solution)/shard_map/middle_back/pallas_call | solution.py:907
  204.6 2.2 collective-permute-done.35
  208.0 1.5 collective-permute-start.33
  210.1 1.2 add_convert_fusion.5
  211.3 6.0 %collective-permute-done.33.refs_5_ = bf16[512,256]{1,0:T(8,128)(2,1)S(1)} collective-permute-done((bf16[512,256]{1,0:T(8,128)(2,1)}, bf16[512,256]{1,0:T(8,128)(2,1)S(1)}, u32[]{:S(2)}, u32[]{:S(2)}) %collective-permute-start.33) | collective-permute-done | bytes 262176 | tf_op jit(solution)/shard_map/ppermute | solution.py:30
  217.4 3.7 %collective-permute-done.34.refs_6_ = bf16[512,256]{1,0:T(8,128)(2,1)S(1)} collective-permute-done((bf16[512,256]{1,0:T(8,128)(2,1)}, bf16[512,256]{1,0:T(8,128)(2,1)S(1)}, u32[]{:S(2)}, u32[]{:S(2)}) %collective-permute-start.34) | collective-permute-done | bytes 262176 | tf_op jit(solution)/shard_map/ppermute | solution.py:30
  221.1 1.4 collective-permute-start.37
  224.2 36.7 %attend_back.1 = (bf16[4,128,512]{2,1,0:T(8,128)(2,1)}, bf16[4,128,512]{2,1,0:T(8,128)(2,1)}, bf16[4,128,256]{2,1,0:T(8,128)(2,1)S(1)}, bf16[4,128,256]{2,1,0:T(...) custom-call(s32[8]{0:T(128)S(1)} %copy-done.3, ...), custom_call_target="tpu_custom_call" | custom-call | flops 10737418240 | bytes 20971520 | tf_op jit(solution)/shard_map/attend_back/pallas_call | solution.py:615
  263.6 1.6 add_convert_fusion.4
  266.1 1.5 collective-permute-start.49
  268.2 1.6 collective-permute-start.43
  269.7 8.7 %collective-permute-done.49 = f32[104,128]{1,0:T(8,128)S(1)} collective-permute-done((f32[104,128]{1,0:T(8,128)S(1)}, f32[104,128]{1,0:T(8,128)S(1)}, u32[]{:S(2)}, u32[]{:S(2)}) %collective-permute-start.49) | collective-permute-done | bytes 53280 | tf_op jit(solution)/shard_map/ppermute | solution.py:30
  279.5 1.3 collective-permute-done.42
  281.5 1.2 collective-permute-start.44
  282.8 1.9 add_convert_fusion
  284.7 1.4 collective-permute-start.46
  286.7 2.6 collective-permute-start.51
  289.4 5.4 %collective-permute-done.45 = bf16[2,128,512]{2,1,0:T(8,128)(2,1)S(1)} collective-permute-done((bf16[2,128,512]{2,1,0:T(8,128)(2,1)S(1)}, bf16[2,128,512]{2,1,0:T(8,128)(2,1)S(1)}, u32[]{:S(2)}, u32[]{:S(2)}) %collective-permute-start.45) | collective-permute-done | bytes 262176 | tf_op jit(solution)/shard_map/ppermute | solution.py:30
  295.6 1.9 collective-permute-done.46.refs_3_
  297.5 2.2 collective-permute-start.52
  301.5 4.6 %input_back.1 = bf16[512,1024]{1,0:T(8,128)(2,1)} custom-call(bf16[512,1024]{1,0:T(8,128)(2,1)} %get-tuple-element.222.refs_0_, bf16[512,1024]{1,0:T(8,128)(2,1)} %copy-done.15, bf16[256,1024]{1,0:T(8,128)(2,1)} %copy-done.18, bf16[256,1024]{1,0:T(8,128)(2,1)} %copy-done.20, bf16[512,1024]{1,0:T(8,128)(2,1)} %refs_4_.1, ...), custom_call_target="tpu_custom_call" | custom-call | flops 10485760 | bytes 7340032 | tf_op jit(solution)/shard_map/input_back/pallas_call | solution.py:939
  306.0 1.5 collective-permute-start.55
  307.9 1.3 collective-permute-done.52
  309.1 1.4 collective-permute-done.53
  310.6 1.0 fusion.1
  315.1 2.1 fusion.9
  (239 shorter events, 38.1 us)
Async XLA Ops:
  7.2 121.4 %all-gather.2.cloned.1.call-start = ((), (), s32[]{:S(2)}) async-start(), calls=%async_computation.1 | async-start | bytes 4718592 | tf_op jit(solution)/shard_map/all_gather | solution.py:1014
  8.9 8.2 %collective-permute-start = (f32[96,128]{1,0:T(8,128)S(1)}, f32[96,128]{1,0:T(8,128)S(1)}, u32[]{:S(2)}, u32[]{:S(2)}) collective-permute-start(f32[96,128]{1,0:T(8,128)S(1)} %maximum_bitcast_fusion.2), channel_id=1, source_target_pairs={{0,1},{1,0},{2,3},{3,2},{4,5},{5,4},{6,7},{7,6},{8,9},{9,8},{10,11... | collective-permute-start | bytes 147464 | tf_op jit(solution)/shard_map/ppermute | solution.py:30
  10.7 14.1 %collective-permute-start.5 = (bf16[1,128,512]{2,1,0:T(8,128)(2,1)S(1)}, bf16[1,128,512]{2,1,0:T(8,128)(2,1)S(1)}, u32[]{:S(2)}, u32[]{:S(2)}) collective-permute-start(bf16[1,128,512]{2,1,0:T(8,128)(2,1)S(1)} %bitcast.71), channel_id=1, source_target_pairs={{0,16},{4,20},{8,24},{12,28},{16,0},{20,4},{24,8},{28,12},{1,17},{... | collective-permute-start | bytes 393224 | tf_op jit(solution)/shard_map/ppermute | solution.py:30
  15.3 13.7 %collective-permute-start.8 = (bf16[1,128,512]{2,1,0:T(8,128)(2,1)S(1)}, bf16[1,128,512]{2,1,0:T(8,128)(2,1)S(1)}, u32[]{:S(2)}, u32[]{:S(2)}) collective-permute-start(bf16[1,128,512]{2,1,0:T(8,128)(2,1)S(1)} %maximum_bitcast_fusion), channel_id=1, source_target_pairs={{0,16},{4,20},{8,24},{12,28},{16,0},{20,4},{24,8},{28,12},{1,17},{... | collective-permute-start | bytes 393224 | tf_op jit(solution)/shard_map/ppermute | solution.py:30
  17.1 5.3 %collective-permute-start.1 = (f32[96,128]{1,0:T(8,128)S(1)}, f32[96,128]{1,0:T(8,128)S(1)}, u32[]{:S(2)}, u32[]{:S(2)}) collective-permute-start(f32[96,128]{1,0:T(8,128)S(1)} %fusion.4), channel_id=1, source_target_pairs={{0,2},{1,3},{2,0},{3,1},{4,6},{5,7},{6,4},{7,5},{8,10},{9,11},{10,... | collective-permute-start | bytes 147464 | tf_op jit(solution)/shard_map/ppermute | solution.py:30
  22.5 25.0 %collective-permute-start.3 = (bf16[512,1024]{1,0:T(8,128)(2,1)}, bf16[512,1024]{1,0:T(8,128)(2,1)S(1)}, u32[]{:S(2)}, u32[]{:S(2)}) collective-permute-start(bf16[512,1024]{1,0:T(8,128)(2,1)} %unit.1.refs_0_.refs_7_), channel_id=1, source_target_pairs={{0,2},{1,3},{2,0},{3,1},{4,6},{5,7},{6,4},{7,5},{8,10},{9,11},{10,... | collective-permute-start | bytes 3145736 | tf_op jit(solution)/shard_map/ppermute | solution.py:30
  23.3 4.1 %collective-permute-start.11 = (f32[96,128]{1,0:T(8,128)S(1)}, f32[96,128]{1,0:T(8,128)S(1)}, u32[]{:S(2)}, u32[]{:S(2)}) collective-permute-start(f32[96,128]{1,0:T(8,128)S(1)} %bitcast.81), channel_id=1, source_target_pairs={{0,4},{4,0},{8,12},{12,8},{16,20},{20,16},{24,28},{28,24},{1,5},{5... | collective-permute-start | bytes 147464 | tf_op jit(solution)/shard_map/ppermute | solution.py:30
  24.8 11.1 %collective-permute-start.6 = (bf16[2,128,512]{2,1,0:T(8,128)(2,1)S(1)}, bf16[2,128,512]{2,1,0:T(8,128)(2,1)S(1)}, u32[]{:S(2)}, u32[]{:S(2)}) collective-permute-start(bf16[2,128,512]{2,1,0:T(8,128)(2,1)S(1)} %pad_maximum_fusion.8), channel_id=1, source_target_pairs={{0,8},{4,12},{8,0},{12,4},{16,24},{20,28},{24,16},{28,20},{1,9},{5... | collective-permute-start | bytes 786440 | tf_op jit(solution)/shard_map/ppermute | solution.py:30
  27.4 6.2 %collective-permute-start.12 = (f32[96,128]{1,0:T(8,128)S(1)}, f32[96,128]{1,0:T(8,128)S(1)}, u32[]{:S(2)}, u32[]{:S(2)}) collective-permute-start(f32[96,128]{1,0:T(8,128)S(1)} %bitcast_add_fusion), channel_id=1, source_target_pairs={{0,8},{4,12},{8,0},{12,4},{16,24},{20,28},{24,16},{28,20},{1,9},{5... | collective-permute-start | bytes 147464 | tf_op jit(solution)/shard_map/ppermute | solution.py:30
  29.1 8.5 %collective-permute-start.9 = (bf16[2,128,512]{2,1,0:T(8,128)(2,1)S(1)}, bf16[2,128,512]{2,1,0:T(8,128)(2,1)S(1)}, u32[]{:S(2)}, u32[]{:S(2)}) collective-permute-start(bf16[2,128,512]{2,1,0:T(8,128)(2,1)S(1)} %pad_maximum_fusion.9), channel_id=1, source_target_pairs={{0,4},{4,0},{8,12},{12,8},{16,20},{20,16},{24,28},{28,24},{1,5},{5... | collective-permute-start | bytes 786440 | tf_op jit(solution)/shard_map/ppermute | solution.py:30
  33.6 5.9 %collective-permute-start.13 = (f32[96,128]{1,0:T(8,128)S(1)}, f32[96,128]{1,0:T(8,128)S(1)}, u32[]{:S(2)}, u32[]{:S(2)}) collective-permute-start(f32[96,128]{1,0:T(8,128)S(1)} %fusion.14), channel_id=1, source_target_pairs={{0,16},{4,20},{8,24},{12,28},{16,0},{20,4},{24,8},{28,12},{1,17},{... | collective-permute-start | bytes 147464 | tf_op jit(solution)/shard_map/ppermute | solution.py:30
  36.0 12.7 %collective-permute-start.7 = (bf16[4,128,512]{2,1,0:T(8,128)(2,1)S(1)}, bf16[4,128,512]{2,1,0:T(8,128)(2,1)S(1)}, u32[]{:S(2)}, u32[]{:S(2)}) collective-permute-start(bf16[4,128,512]{2,1,0:T(8,128)(2,1)S(1)} %pad_maximum_fusion.3), channel_id=1, source_target_pairs={{0,4},{4,0},{8,12},{12,8},{16,20},{20,16},{24,28},{28,24},{1,5},{5... | collective-permute-start | bytes 1572872 | tf_op jit(solution)/shard_map/ppermute | solution.py:30
  37.7 12.6 %collective-permute-start.10 = (bf16[4,128,512]{2,1,0:T(8,128)(2,1)S(1)}, bf16[4,128,512]{2,1,0:T(8,128)(2,1)S(1)}, u32[]{:S(2)}, u32[]{:S(2)}) collective-permute-start(bf16[4,128,512]{2,1,0:T(8,128)(2,1)S(1)} %pad_maximum_fusion.4), channel_id=1, source_target_pairs={{0,8},{4,12},{8,0},{12,4},{16,24},{20,28},{24,16},{28,20},{1,9},{5... | collective-permute-start | bytes 1572872 | tf_op jit(solution)/shard_map/ppermute | solution.py:30
  47.6 7.1 %collective-permute-start.14 = (bf16[128,1024]{1,0:T(8,128)(2,1)S(1)}, bf16[128,1024]{1,0:T(8,128)(2,1)}, u32[]{:S(2)}, u32[]{:S(2)}) collective-permute-start(bf16[128,1024]{1,0:T(8,128)(2,1)S(1)} %copy-done.26), channel_id=1, source_target_pairs={{0,2},{1,3},{2,0},{3,1},{4,6},{5,7},{6,4},{7,5},{8,10},{9,11},{10,... | collective-permute-start | bytes 786440 | tf_op jit(solution)/shard_map/ppermute | solution.py:30
  54.7 260.3 %reduce-scatter.2.cloned.1.call-start = ((), (), s32[]{:S(2)}) async-start(), calls=%async_computation.2 | async-start | bytes 4718592 | tf_op jit(solution)/shard_map/reduce_scatter | solution.py:1069
  54.8 16.3 %collective-permute-start.2 = (bf16[512,1024]{1,0:T(8,128)(2,1)S(1)}, bf16[512,1024]{1,0:T(8,128)(2,1)}, u32[]{:S(2)}, u32[]{:S(2)}) collective-permute-start(bf16[512,1024]{1,0:T(8,128)(2,1)S(1)} %copy-done.13), channel_id=1, source_target_pairs={{0,1},{1,0},{2,3},{3,2},{4,5},{5,4},{6,7},{7,6},{8,9},{9,8},{10,11... | collective-permute-start | bytes 3145736 | tf_op jit(solution)/shard_map/ppermute | solution.py:30
  54.9 16.2 %collective-permute-start.4 = (bf16[512,1024]{1,0:T(8,128)(2,1)}, bf16[512,1024]{1,0:T(8,128)(2,1)}, u32[]{:S(2)}, u32[]{:S(2)}) collective-permute-start(bf16[512,1024]{1,0:T(8,128)(2,1)} %copy-done.32), channel_id=1, source_target_pairs={{0,1},{1,0},{2,3},{3,2},{4,5},{5,4},{6,7},{7,6},{8,9},{9,8},{10,11... | collective-permute-start | bytes 3145736 | tf_op jit(solution)/shard_map/ppermute | solution.py:30
  57.4 8.3 %collective-permute-start.15 = (bf16[128,1024]{1,0:T(8,128)(2,1)S(1)}, bf16[128,1024]{1,0:T(8,128)(2,1)S(1)}, u32[]{:S(2)}, u32[]{:S(2)}) collective-permute-start(bf16[128,1024]{1,0:T(8,128)(2,1)S(1)} %get-tuple-element.129), channel_id=1, source_target_pairs={{0,2},{1,3},{2,0},{3,1},{4,6},{5,7},{6,4},{7,5},{8,10},{9,11},{10,... | collective-permute-start | bytes 786440 | tf_op jit(solution)/shard_map/ppermute | solution.py:30
  67.8 24.9 %collective-permute-start.16 = (bf16[1024,256]{1,0:T(8,128)(2,1)}, bf16[1024,256]{1,0:T(8,128)(2,1)S(1)}, u32[]{:S(2)}, u32[]{:S(2)}) collective-permute-start(bf16[1024,256]{1,0:T(8,128)(2,1)} %placed_rows.1.refs_4_.refs_3_), channel_id=1, source_target_pairs={{0,2},{1,3},{2,0},{3,1},{4,6},{5,7},{6,4},{7,5},{8,10},{9,11},{10,... | collective-permute-start | bytes 1572872 | tf_op jit(solution)/shard_map/ppermute | solution.py:30
  68.1 24.6 %collective-permute-start.17 = (bf16[256,1024]{1,0:T(8,128)(2,1)}, bf16[256,1024]{1,0:T(8,128)(2,1)}, u32[]{:S(2)}, u32[]{:S(2)}) collective-permute-start(bf16[256,1024]{1,0:T(8,128)(2,1)} %slice.188), channel_id=1, source_target_pairs={{0,2},{1,3},{2,0},{3,1},{4,6},{5,7},{6,4},{7,5},{8,10},{9,11},{10,... | collective-permute-start | bytes 1572872 | tf_op jit(solution)/shard_map/ppermute | solution.py:30
  71.1 24.8 %collective-permute-start.21 = (bf16[1024,256]{1,0:T(8,128)(2,1)}, bf16[1024,256]{1,0:T(8,128)(2,1)S(1)}, u32[]{:S(2)}, u32[]{:S(2)}) collective-permute-start(bf16[1024,256]{1,0:T(8,128)(2,1)} %placed_rows.1.refs_4_.refs_3_), channel_id=1, source_target_pairs={{0,1},{1,0},{2,3},{3,2},{4,5},{5,4},{6,7},{7,6},{8,9},{9,8},{10,11... | collective-permute-start | bytes 1572872 | tf_op jit(solution)/shard_map/ppermute | solution.py:30
  92.8 14.8 %collective-permute-start.22 = (bf16[1024,256]{1,0:T(8,128)(2,1)S(1)}, bf16[1024,256]{1,0:T(8,128)(2,1)}, u32[]{:S(2)}, u32[]{:S(2)}) collective-permute-start(bf16[1024,256]{1,0:T(8,128)(2,1)S(1)} %collective-permute-done.16.refs_6_.refs_5_), channel_id=1, source_target_pairs={{0,1},{1,0},{2,3},{3,2},{4,5},{5,4},{6,7},{7,6},{8,9},{9,8},{10,11... | collective-permute-start | bytes 1572872 | tf_op jit(solution)/shard_map/ppermute | solution.py:30
  93.3 3.3 %collective-permute-start.18 = (bf16[512,256]{1,0:T(8,128)(2,1)}, bf16[512,256]{1,0:T(8,128)(2,1)S(1)}, u32[]{:S(2)}, u32[]{:S(2)}) collective-permute-start(bf16[512,256]{1,0:T(8,128)(2,1)} %get-tuple-element.141), channel_id=1, source_target_pairs={{0,1},{1,0},{2,3},{3,2},{4,5},{5,4},{6,7},{7,6},{8,9},{9,8},{10,11... | collective-permute-start | bytes 786440 | tf_op jit(solution)/shard_map/ppermute | solution.py:30
  93.4 9.4 %collective-permute-start.19 = (bf16[512,256]{1,0:T(8,128)(2,1)}, bf16[512,256]{1,0:T(8,128)(2,1)}, u32[]{:S(2)}, u32[]{:S(2)}) collective-permute-start(bf16[512,256]{1,0:T(8,128)(2,1)} %get-tuple-element.142), channel_id=1, source_target_pairs={{0,2},{1,3},{2,0},{3,1},{4,6},{5,7},{6,4},{7,5},{8,10},{9,11},{10,... | collective-permute-start | bytes 786440 | tf_op jit(solution)/shard_map/ppermute | solution.py:30
  93.7 13.8 %collective-permute-start.20 = (bf16[512,256]{1,0:T(8,128)(2,1)}, bf16[512,256]{1,0:T(8,128)(2,1)}, u32[]{:S(2)}, u32[]{:S(2)}) collective-permute-start(bf16[512,256]{1,0:T(8,128)(2,1)} %get-tuple-element.143), channel_id=1, source_target_pairs={{0,3},{1,2},{2,1},{3,0},{4,7},{5,6},{6,5},{7,4},{8,11},{9,10},{10,... | collective-permute-start | bytes 786440 | tf_op jit(solution)/shard_map/ppermute | solution.py:30
  95.8 21.4 %collective-permute-start.24 = (bf16[512,1024]{1,0:T(8,128)(2,1)S(1)}, bf16[512,1024]{1,0:T(8,128)(2,1)}, u32[]{:S(2)}, u32[]{:S(2)}) collective-permute-start(bf16[512,1024]{1,0:T(8,128)(2,1)S(1)} %copy-done.5), channel_id=1, source_target_pairs={{0,1},{1,0},{2,3},{3,2},{4,5},{5,4},{6,7},{7,6},{8,9},{9,8},{10,11... | collective-permute-start | bytes 3145736 | tf_op jit(solution)/shard_map/ppermute | solution.py:30
  112.6 4.6 %collective-permute-start.23 = (bf16[512,1024]{1,0:T(8,128)(2,1)}, bf16[512,1024]{1,0:T(8,128)(2,1)}, u32[]{:S(2)}, u32[]{:S(2)}) collective-permute-start(bf16[512,1024]{1,0:T(8,128)(2,1)} %get-tuple-element.146.refs_0_), channel_id=1, source_target_pairs={{0,1},{1,0},{2,3},{3,2},{4,5},{5,4},{6,7},{7,6},{8,9},{9,8},{10,11... | collective-permute-start | bytes 3145736 | tf_op jit(solution)/shard_map/ppermute | solution.py:30
  114.7 28.8 %collective-permute-start.26 = (bf16[512,1024]{1,0:T(8,128)(2,1)}, bf16[512,1024]{1,0:T(8,128)(2,1)}, u32[]{:S(2)}, u32[]{:S(2)}) collective-permute-start(bf16[512,1024]{1,0:T(8,128)(2,1)} %get-tuple-element.146.refs_0_), channel_id=1, source_target_pairs={{0,2},{1,3},{2,0},{3,1},{4,6},{5,7},{6,4},{7,5},{8,10},{9,11},{10,... | collective-permute-start | bytes 3145736 | tf_op jit(solution)/shard_map/ppermute | solution.py:30
  117.1 26.5 %collective-permute-start.28 = (bf16[512,1024]{1,0:T(8,128)(2,1)S(1)}, bf16[512,1024]{1,0:T(8,128)(2,1)}, u32[]{:S(2)}, u32[]{:S(2)}) collective-permute-start(bf16[512,1024]{1,0:T(8,128)(2,1)S(1)} %constant_dynamic-update-slice_fusion.refs_2_), channel_id=1, source_target_pairs={{0,1},{1,0},{2,3},{3,2},{4,5},{5,4},{6,7},{7,6},{8,9},{9,8},{10,11... | collective-permute-start | bytes 3145736 | tf_op jit(solution)/shard_map/ppermute | solution.py:30
  143.5 2.9 collective-permute-start.27
  162.4 2.9 collective-permute-start.29
  162.6 26.6 %collective-permute-start.25 = (bf16[512,1024]{1,0:T(8,128)(2,1)}, bf16[512,1024]{1,0:T(8,128)(2,1)S(1)}, u32[]{:S(2)}, u32[]{:S(2)}) collective-permute-start(bf16[512,1024]{1,0:T(8,128)(2,1)} %get-tuple-element.149), channel_id=1, source_target_pairs={{0,1},{1,0},{2,3},{3,2},{4,5},{5,4},{6,7},{7,6},{8,9},{9,8},{10,11... | collective-permute-start | bytes 3145736 | tf_op jit(solution)/shard_map/ppermute | solution.py:30
  163.0 22.4 %collective-permute-start.31 = (bf16[512,1024]{1,0:T(8,128)(2,1)}, bf16[512,1024]{1,0:T(8,128)(2,1)}, u32[]{:S(2)}, u32[]{:S(2)}) collective-permute-start(bf16[512,1024]{1,0:T(8,128)(2,1)} %get-tuple-element.170), channel_id=1, source_target_pairs={{0,1},{1,0},{2,3},{3,2},{4,5},{5,4},{6,7},{7,6},{8,9},{9,8},{10,11... | collective-permute-start | bytes 3145736 | tf_op jit(solution)/shard_map/ppermute | solution.py:30
  168.0 25.5 %collective-permute-start.30 = (bf16[512,1024]{1,0:T(8,128)(2,1)}, bf16[512,1024]{1,0:T(8,128)(2,1)}, u32[]{:S(2)}, u32[]{:S(2)}) collective-permute-start(bf16[512,1024]{1,0:T(8,128)(2,1)} %add_convert_fusion.3), channel_id=1, source_target_pairs={{0,2},{1,3},{2,0},{3,1},{4,6},{5,7},{6,4},{7,5},{8,10},{9,11},{10,... | collective-permute-start | bytes 3145736 | tf_op jit(solution)/shard_map/ppermute | solution.py:30
  193.5 13.3 %collective-permute-start.35 = (bf16[256,1024]{1,0:T(8,128)(2,1)}, bf16[256,1024]{1,0:T(8,128)(2,1)S(1)}, u32[]{:S(2)}, u32[]{:S(2)}) collective-permute-start(bf16[256,1024]{1,0:T(8,128)(2,1)} %get-tuple-element.183), channel_id=1, source_target_pairs={{0,2},{1,3},{2,0},{3,1},{4,6},{5,7},{6,4},{7,5},{8,10},{9,11},{10,... | collective-permute-start | bytes 1572872 | tf_op jit(solution)/shard_map/ppermute | solution.py:30
  194.9 28.2 %copy-start.1 = (s32[418]{0:T(512)S(1)}, s32[418]{0:T(512)}, u32[]{:S(2)}) copy-start(s32[418]{0:T(512)} %pad_add_fusion.facts) | copy-start | bytes 5020
  194.9 28.2 %copy-start.3 = (s32[8]{0:T(128)S(1)}, s32[8]{0:T(128)}, u32[]{:S(2)}) copy-start(s32[8]{0:T(128)} %broadcast_xor_fusion.1.owner_a) | copy-start | bytes 100
  194.9 28.2 %copy-start.4 = (f32[32,256]{1,0:T(8,128)S(1)}, f32[32,256]{1,0:T(8,128)}, u32[]{:S(2)}) copy-start(f32[32,256]{1,0:T(8,128)} %get-tuple-element.133.refs_1_) | copy-start | bytes 98308
  206.8 3.3 %collective-permute-start.36 = (bf16[8,128,256]{2,1,0:T(8,128)(2,1)}, bf16[8,128,256]{2,1,0:T(8,128)(2,1)S(1)}, u32[]{:S(2)}, u32[]{:S(2)}) collective-permute-start(bf16[8,128,256]{2,1,0:T(8,128)(2,1)} %get-tuple-element.185), channel_id=1, source_target_pairs={{0,1},{1,0},{2,3},{3,2},{4,5},{5,4},{6,7},{7,6},{8,9},{9,8},{10,11... | collective-permute-start | bytes 1572872 | tf_op jit(solution)/shard_map/ppermute | solution.py:30
  207.5 3.8 %collective-permute-start.32 = (bf16[512,256]{1,0:T(8,128)(2,1)}, bf16[512,256]{1,0:T(8,128)(2,1)S(1)}, u32[]{:S(2)}, u32[]{:S(2)}) collective-permute-start(bf16[512,256]{1,0:T(8,128)(2,1)} %get-tuple-element.176), channel_id=1, source_target_pairs={{0,1},{1,0},{2,3},{3,2},{4,5},{5,4},{6,7},{7,6},{8,9},{9,8},{10,11... | collective-permute-start | bytes 786440 | tf_op jit(solution)/shard_map/ppermute | solution.py:30
  208.0 9.4 %collective-permute-start.33 = (bf16[512,256]{1,0:T(8,128)(2,1)}, bf16[512,256]{1,0:T(8,128)(2,1)S(1)}, u32[]{:S(2)}, u32[]{:S(2)}) collective-permute-start(bf16[512,256]{1,0:T(8,128)(2,1)} %get-tuple-element.177), channel_id=1, source_target_pairs={{0,2},{1,3},{2,0},{3,1},{4,6},{5,7},{6,4},{7,5},{8,10},{9,11},{10,... | collective-permute-start | bytes 786440 | tf_op jit(solution)/shard_map/ppermute | solution.py:30
  209.5 11.7 %collective-permute-start.34 = (bf16[512,256]{1,0:T(8,128)(2,1)}, bf16[512,256]{1,0:T(8,128)(2,1)S(1)}, u32[]{:S(2)}, u32[]{:S(2)}) collective-permute-start(bf16[512,256]{1,0:T(8,128)(2,1)} %get-tuple-element.178), channel_id=1, source_target_pairs={{0,3},{1,2},{2,1},{3,0},{4,7},{5,6},{6,5},{7,4},{8,11},{9,10},{10,... | collective-permute-start | bytes 786440 | tf_op jit(solution)/shard_map/ppermute | solution.py:30
  209.5 51.4 %collective-permute-start.38 = (bf16[8,128,256]{2,1,0:T(8,128)(2,1)}, bf16[8,128,256]{2,1,0:T(8,128)(2,1)S(1)}, u32[]{:S(2)}, u32[]{:S(2)}) collective-permute-start(bf16[8,128,256]{2,1,0:T(8,128)(2,1)} %get-tuple-element.195), channel_id=1, source_target_pairs={{0,1},{1,0},{2,3},{3,2},{4,5},{5,4},{6,7},{7,6},{8,9},{9,8},{10,11... | collective-permute-start | bytes 1572872 | tf_op jit(solution)/shard_map/ppermute | solution.py:30
  221.1 39.8 %collective-permute-start.37 = (bf16[256,1024]{1,0:T(8,128)(2,1)}, bf16[256,1024]{1,0:T(8,128)(2,1)S(1)}, u32[]{:S(2)}, u32[]{:S(2)}) collective-permute-start(bf16[256,1024]{1,0:T(8,128)(2,1)} %get-tuple-element.193), channel_id=1, source_target_pairs={{0,2},{1,3},{2,0},{3,1},{4,6},{5,7},{6,4},{7,5},{8,10},{9,11},{10,... | collective-permute-start | bytes 1572872 | tf_op jit(solution)/shard_map/ppermute | solution.py:30
  222.5 38.4 %collective-permute-start.39 = (bf16[8,128,256]{2,1,0:T(8,128)(2,1)S(1)}, bf16[8,128,256]{2,1,0:T(8,128)(2,1)S(1)}, u32[]{:S(2)}, u32[]{:S(2)}) collective-permute-start(bf16[8,128,256]{2,1,0:T(8,128)(2,1)S(1)} %add_convert_fusion.5), channel_id=1, source_target_pairs={{0,2},{1,3},{2,0},{3,1},{4,6},{5,7},{6,4},{7,5},{8,10},{9,11},{10,... | collective-permute-start | bytes 1572872 | tf_op jit(solution)/shard_map/ppermute | solution.py:30
  224.2 38.4 %copy-start.28 = (f32[4,1024]{1,0:T(4,128)S(1)}, f32[4,1024]{1,0:T(4,128)}, u32[]{:S(2)}) copy-start(f32[4,1024]{1,0:T(4,128)} %get-tuple-element.228) | copy-start | bytes 49156
  224.2 38.4 %copy-start.30 = (f32[1,1024]{1,0:T(1,128)S(1)}, f32[1,1024]{1,0:T(1,128)}, u32[]{:S(2)}) copy-start(f32[1,1024]{1,0:T(1,128)} %get-tuple-element.230) | copy-start | bytes 12292
  261.7 5.9 %collective-permute-start.40 = (bf16[512,1024]{1,0:T(8,128)(2,1)}, bf16[512,1024]{1,0:T(8,128)(2,1)S(1)}, u32[]{:S(2)}, u32[]{:S(2)}) collective-permute-start(bf16[512,1024]{1,0:T(8,128)(2,1)} %get-tuple-element.202), channel_id=1, source_target_pairs={{0,1},{1,0},{2,3},{3,2},{4,5},{5,4},{6,7},{7,6},{8,9},{9,8},{10,11... | collective-permute-start | bytes 3145736 | tf_op jit(solution)/shard_map/ppermute | solution.py:30
  262.2 20.5 %collective-permute-start.47 = (bf16[512,1024]{1,0:T(8,128)(2,1)}, bf16[512,1024]{1,0:T(8,128)(2,1)S(1)}, u32[]{:S(2)}, u32[]{:S(2)}) collective-permute-start(bf16[512,1024]{1,0:T(8,128)(2,1)} %get-tuple-element.218), channel_id=1, source_target_pairs={{0,1},{1,0},{2,3},{3,2},{4,5},{5,4},{6,7},{7,6},{8,9},{9,8},{10,11... | collective-permute-start | bytes 3145736 | tf_op jit(solution)/shard_map/ppermute | solution.py:30
  262.9 16.4 %collective-permute-start.41 = (bf16[4,128,512]{2,1,0:T(8,128)(2,1)}, bf16[4,128,512]{2,1,0:T(8,128)(2,1)S(1)}, u32[]{:S(2)}, u32[]{:S(2)}) collective-permute-start(bf16[4,128,512]{2,1,0:T(8,128)(2,1)} %get-tuple-element.211), channel_id=1, source_target_pairs={{0,4},{4,0},{8,12},{12,8},{16,20},{20,16},{24,28},{28,24},{1,5},{5... | collective-permute-start | bytes 1572872 | tf_op jit(solution)/shard_map/ppermute | solution.py:30
  265.2 15.6 %collective-permute-start.42 = (bf16[4,128,512]{2,1,0:T(8,128)(2,1)S(1)}, bf16[4,128,512]{2,1,0:T(8,128)(2,1)S(1)}, u32[]{:S(2)}, u32[]{:S(2)}) collective-permute-start(bf16[4,128,512]{2,1,0:T(8,128)(2,1)S(1)} %pad_maximum_fusion.6), channel_id=1, source_target_pairs={{0,8},{4,12},{8,0},{12,4},{16,24},{20,28},{24,16},{28,20},{1,9},{5... | collective-permute-start | bytes 1572872 | tf_op jit(solution)/shard_map/ppermute | solution.py:30
  266.1 12.4 %collective-permute-start.49 = (f32[104,128]{1,0:T(8,128)S(1)}, f32[104,128]{1,0:T(8,128)S(1)}, u32[]{:S(2)}, u32[]{:S(2)}) collective-permute-start(f32[104,128]{1,0:T(8,128)S(1)} %maximum_bitcast_fusion.1), channel_id=1, source_target_pairs={{0,4},{4,0},{8,12},{12,8},{16,20},{20,16},{24,28},{28,24},{1,5},{5... | collective-permute-start | bytes 159752 | tf_op jit(solution)/shard_map/ppermute | solution.py:30
  268.2 13.4 %collective-permute-start.43 = (bf16[256,1024]{1,0:T(8,128)(2,1)S(1)}, bf16[256,1024]{1,0:T(8,128)(2,1)S(1)}, u32[]{:S(2)}, u32[]{:S(2)}) collective-permute-start(bf16[256,1024]{1,0:T(8,128)(2,1)S(1)} %get-tuple-element.247), channel_id=1, source_target_pairs={{0,2},{1,3},{2,0},{3,1},{4,6},{5,7},{6,4},{7,5},{8,10},{9,11},{10,... | collective-permute-start | bytes 1572872 | tf_op jit(solution)/shard_map/ppermute | solution.py:30
  278.5 8.2 %collective-permute-start.50 = (f32[104,128]{1,0:T(8,128)S(1)}, f32[104,128]{1,0:T(8,128)S(1)}, u32[]{:S(2)}, u32[]{:S(2)}) collective-permute-start(f32[104,128]{1,0:T(8,128)S(1)} %fusion.5), channel_id=1, source_target_pairs={{0,8},{4,12},{8,0},{12,4},{16,24},{20,28},{24,16},{28,20},{1,9},{5... | collective-permute-start | bytes 159752 | tf_op jit(solution)/shard_map/ppermute | solution.py:30
  281.5 7.8 %collective-permute-start.44 = (bf16[2,128,512]{2,1,0:T(8,128)(2,1)S(1)}, bf16[2,128,512]{2,1,0:T(8,128)(2,1)S(1)}, u32[]{:S(2)}, u32[]{:S(2)}) collective-permute-start(bf16[2,128,512]{2,1,0:T(8,128)(2,1)S(1)} %get-tuple-element.215), channel_id=1, source_target_pairs={{0,8},{4,12},{8,0},{12,4},{16,24},{20,28},{24,16},{28,20},{1,9},{5... | collective-permute-start | bytes 786440 | tf_op jit(solution)/shard_map/ppermute | solution.py:30
  284.7 12.8 %collective-permute-start.46 = (bf16[256,1024]{1,0:T(8,128)(2,1)S(1)}, bf16[256,1024]{1,0:T(8,128)(2,1)S(1)}, u32[]{:S(2)}, u32[]{:S(2)}) collective-permute-start(bf16[256,1024]{1,0:T(8,128)(2,1)S(1)} %get-tuple-element.246), channel_id=1, source_target_pairs={{0,2},{1,3},{2,0},{3,1},{4,6},{5,7},{6,4},{7,5},{8,10},{9,11},{10,... | collective-permute-start | bytes 1572872 | tf_op jit(solution)/shard_map/ppermute | solution.py:30
  286.1 14.3 %collective-permute-start.48 = (bf16[512,1024]{1,0:T(8,128)(2,1)S(1)}, bf16[512,1024]{1,0:T(8,128)(2,1)S(1)}, u32[]{:S(2)}, u32[]{:S(2)}) collective-permute-start(bf16[512,1024]{1,0:T(8,128)(2,1)S(1)} %copy-done.33), channel_id=1, source_target_pairs={{0,1},{1,0},{2,3},{3,2},{4,5},{5,4},{6,7},{7,6},{8,9},{9,8},{10,11... | collective-permute-start | bytes 3145736 | tf_op jit(solution)/shard_map/ppermute | solution.py:30
  286.1 8.7 %collective-permute-start.45 = (bf16[2,128,512]{2,1,0:T(8,128)(2,1)S(1)}, bf16[2,128,512]{2,1,0:T(8,128)(2,1)S(1)}, u32[]{:S(2)}, u32[]{:S(2)}) collective-permute-start(bf16[2,128,512]{2,1,0:T(8,128)(2,1)S(1)} %get-tuple-element.216), channel_id=1, source_target_pairs={{0,4},{4,0},{8,12},{12,8},{16,20},{20,16},{24,28},{28,24},{1,5},{5... | collective-permute-start | bytes 786440 | tf_op jit(solution)/shard_map/ppermute | solution.py:30
  286.7 13.7 %collective-permute-start.51 = (f32[104,128]{1,0:T(8,128)S(1)}, f32[104,128]{1,0:T(8,128)S(1)}, u32[]{:S(2)}, u32[]{:S(2)}) collective-permute-start(f32[104,128]{1,0:T(8,128)S(1)} %fusion.13), channel_id=1, source_target_pairs={{0,16},{4,20},{8,24},{12,28},{16,0},{20,4},{24,8},{28,12},{1,17},{... | collective-permute-start | bytes 159752 | tf_op jit(solution)/shard_map/ppermute | solution.py:30
  297.5 11.7 %collective-permute-start.52 = (bf16[1,128,512]{2,1,0:T(8,128)(2,1)S(1)}, bf16[1,128,512]{2,1,0:T(8,128)(2,1)}, u32[]{:S(2)}, u32[]{:S(2)}) collective-permute-start(bf16[1,128,512]{2,1,0:T(8,128)(2,1)S(1)} %get-tuple-element.233), channel_id=1, source_target_pairs={{0,16},{4,20},{8,24},{12,28},{16,0},{20,4},{24,8},{28,12},{1,17},{... | collective-permute-start | bytes 393224 | tf_op jit(solution)/shard_map/ppermute | solution.py:30
  299.7 10.9 %collective-permute-start.53 = (bf16[1,128,512]{2,1,0:T(8,128)(2,1)}, bf16[1,128,512]{2,1,0:T(8,128)(2,1)}, u32[]{:S(2)}, u32[]{:S(2)}) collective-permute-start(bf16[1,128,512]{2,1,0:T(8,128)(2,1)} %get-tuple-element.235), channel_id=1, source_target_pairs={{0,16},{4,20},{8,24},{12,28},{16,0},{20,4},{24,8},{28,12},{1,17},{... | collective-permute-start | bytes 393224 | tf_op jit(solution)/shard_map/ppermute | solution.py:30
  306.0 6.5 %collective-permute-start.56 = (f32[104,128]{1,0:T(8,128)S(1)}, f32[104,128]{1,0:T(8,128)S(1)}, u32[]{:S(2)}, u32[]{:S(2)}) collective-permute-start(f32[104,128]{1,0:T(8,128)S(1)} %bitcast.85), channel_id=1, source_target_pairs={{0,3},{1,2},{2,1},{3,0},{4,7},{5,6},{6,5},{7,4},{8,11},{9,10},{10,... | collective-permute-start | bytes 159752 | tf_op jit(solution)/shard_map/ppermute | solution.py:30
  306.0 6.5 %collective-permute-start.55 = (f32[104,128]{1,0:T(8,128)S(1)}, f32[104,128]{1,0:T(8,128)S(1)}, u32[]{:S(2)}, u32[]{:S(2)}) collective-permute-start(f32[104,128]{1,0:T(8,128)S(1)} %bitcast.86), channel_id=1, source_target_pairs={{0,2},{1,3},{2,0},{3,1},{4,6},{5,7},{6,4},{7,5},{8,10},{9,11},{10,... | collective-permute-start | bytes 159752 | tf_op jit(solution)/shard_map/ppermute | solution.py:30
  307.5 5.0 %collective-permute-start.54 = (f32[104,128]{1,0:T(8,128)S(1)}, f32[104,128]{1,0:T(8,128)S(1)}, u32[]{:S(2)}, u32[]{:S(2)}) collective-permute-start(f32[104,128]{1,0:T(8,128)S(1)} %bitcast.87), channel_id=1, source_target_pairs={{0,1},{1,0},{2,3},{3,2},{4,5},{5,4},{6,7},{7,6},{8,9},{9,8},{10,11... | collective-permute-start | bytes 159752 | tf_op jit(solution)/shard_map/ppermute | solution.py:30
  (35 other events, 311.0 us)
Sparse Core Ops, SparseCore 0:
  54.8 73.6 all-gather.1
  185.5 85.5 reduce-scatter.1
